TPU v7x, 32 devices: a whole 2x2x4 slice. The times are simulated.
32 devices in a mesh: tm: 8 (over y, x, core), mp: 4 (over z).
Axes of the slice: x: 2, y: 2, z: 4, core: 2. Of those that a mesh axis runs over, the one named last changes fastest.
Arguments:
- frames: bfloat16 [4096, 1024], P(('tm', 'mp')), may hold values from -6 to 6
- block_ids: int32 [4096], replicated, may hold values from 0 to 203, never falling along the last dimension, each value on 1 to 40 neighbouring positions
- valid_counts: int32 [8], replicated, may hold values from 1 to 512, as said below
- norm_attn: float32 [1024], replicated, may hold values from 0.25 to 1.75
- w_qkv: bfloat16 [1024, 3072], replicated, may hold values from -1 to 1
- w_attn_out: bfloat16 [1024, 1024], replicated, may hold values from -0.1875 to 0.1875
- norm_conv: float32 [1024], replicated, may hold values from 0.25 to 1.75
- w_point_in: bfloat16 [1024, 2048], replicated, may hold values from -0.1875 to 0.1875
- w_depth: bfloat16 [31, 1024], replicated, may hold values from -1 to 1
- w_point_out: bfloat16 [1024, 1024], replicated, may hold values from -0.1875 to 0.1875
- w_adapter: bfloat16 [1024, 8192], P('tm', 'mp'), may hold values from -1 to 1
- llm_gain: float32 [8192], replicated, may hold values from 0.25 to 1.75
- w_query: bfloat16 [8192, 8192], P('tm', 'mp'), may hold values from -1 to 1
- w_key: bfloat16 [8192, 1024], P('tm', 'mp'), may hold values from -1 to 1
- w_value: bfloat16 [8192, 1024], P('tm', 'mp'), may hold values from -0.0625 to 0.0625
Outputs:
- conf_out: bfloat16 [4096, 1024], P(('tm', 'mp'))
- attended: bfloat16 [1024, 8192], P('tm', 'mp')
Inputs may be any that keep to these rules, and one draw needn't show every extreme that they name: `block_ids`: block numbers never fall along the recording, and one block holds 1 to 40 frames. Every time shard but the last holds 512 real frames; the frames after the first valid_counts[t] of time shard t are padding.
All inputs are finite; a program needn't handle non-finite values.
Results may differ from a plain program's by a relative error of at most 0.014.
Values may be sent and summed in bfloat16 or wider, within the bound.
No kernel may reach another device: no remote copies, remote signals or barrier semaphores. Data moves between devices by JAX's collectives and lax.ppermute only.
A program may use at most 192 MiB of HBM per device.

v0:
```python
import math

import jax
import jax.numpy as jnp
from jax import lax
from jax.sharding import PartitionSpec as P

CH = 16
HDIM = 128


eps_conf = 1e-05
eps_llm = 1e-06
rope_base = 1000000.0
masked_score = -1e30


def passed_along(value, axis, by):
    length = lax.axis_size(axis)
    pairs = [(i, i + by) for i in range(length) if 0 <= i + by < length]
    return lax.ppermute(value, axis, pairs)


def shard_count(index, valid_counts, shard_len):
    shard = index // shard_len
    table = jnp.arange(valid_counts.shape[0], dtype=jnp.int32)
    hit = shard[:, None] == table[None, :]
    count = jnp.sum(jnp.where(hit, valid_counts[None, :], 0), axis=1)
    return (index - shard * shard_len, count)


def layer_norm(field, gain):
    center = field - jnp.mean(field, axis=-1, keepdims=True)
    spread = jnp.mean(center * center, axis=-1, keepdims=True)
    return center * lax.rsqrt(spread + eps_conf) * gain


def rotary(field, positions):
    half = field.shape[-1] // 2
    freq = rope_base ** (-(jnp.arange(half, dtype=jnp.float32) * 2.0) / field.shape[-1])
    angle = positions.astype(jnp.float32)[:, None] * freq[None, :]
    cosine = jnp.concatenate([jnp.cos(angle), jnp.cos(angle)], axis=-1)[:, None, :]
    sine = jnp.concatenate([jnp.sin(angle), jnp.sin(angle)], axis=-1)[:, None, :]
    turned = jnp.concatenate([-field[..., half:], field[..., :half]], axis=-1)
    return field * cosine + turned * sine


def on_device(
    frames,
    block_ids,
    valid_counts,
    norm_attn,
    w_qkv,
    w_attn_out,
    norm_conv,
    w_point_in,
    w_depth,
    w_point_out,
    w_adapter,
    llm_gain,
    w_query,
    w_key,
    w_value,
):
    mp_count = lax.axis_size("mp")
    frame_rows, width = frames.shape
    heads = CH
    head_size = width // heads
    shard_frames = frame_rows * mp_count
    time_place = lax.axis_index("tm")
    model_place = lax.axis_index("mp")
    first = (time_place * mp_count + model_place) * frame_rows
    inputs = frames.astype(jnp.float32)
    own_index = first + jnp.arange(frame_rows, dtype=jnp.int32)
    own_place, own_count = shard_count(own_index, valid_counts, shard_frames)
    frame_real = own_place < own_count
    normed = layer_norm(inputs, norm_attn).astype(jnp.bfloat16)
    projected = jnp.dot(normed, w_qkv, preferred_element_type=jnp.float32).astype(jnp.bfloat16)
    queries = projected[:, :width]
    own_keys = projected[:, width : 2 * width]
    own_values = projected[:, 2 * width :]
    prior_keys, prior_values = passed_along((own_keys, own_values), ("tm", "mp"), 1)
    keys = jnp.concatenate([prior_keys, own_keys], axis=0).reshape(2 * frame_rows, heads, head_size)
    values = jnp.concatenate([prior_values, own_values], axis=0).reshape(
        2 * frame_rows, heads, head_size
    )
    key_index = first - frame_rows + jnp.arange(2 * frame_rows, dtype=jnp.int32)
    key_place, key_count = shard_count(key_index, valid_counts, shard_frames)
    key_real = key_place < key_count
    prior_ids = lax.dynamic_slice_in_dim(
        block_ids, jnp.maximum(first - frame_rows, 0), frame_rows, 0
    )
    query_ids = lax.dynamic_slice_in_dim(block_ids, first, frame_rows, 0)
    key_ids = jnp.concatenate([prior_ids, query_ids], axis=0)
    same = key_index[None, :] == own_index[:, None]
    visible = (
        (key_index[None, :] <= own_index[:, None])
        & (key_ids[None, :] >= query_ids[:, None] - 2)
        & (key_real[None, :] | same)
    )
    query_heads = queries.reshape(frame_rows, heads, head_size)
    scores = jnp.einsum(
        "qhd,khd->hqk", query_heads, keys, preferred_element_type=jnp.float32
    ) / jnp.sqrt(jnp.float32(head_size))
    scores = jnp.where(visible[None], scores, masked_score)
    top = jnp.max(scores, axis=-1, keepdims=True)
    weights = jnp.where(visible[None], jnp.exp(scores - top), 0.0)
    total = jnp.sum(weights, axis=-1)
    summed = jnp.einsum(
        "hqk,khd->qhd", weights.astype(jnp.bfloat16), values, preferred_element_type=jnp.float32
    )
    conf_context = (
        (summed / jnp.transpose(total)[:, :, None]).reshape(frame_rows, width).astype(jnp.bfloat16)
    )
    mid = inputs + jnp.dot(conf_context, w_attn_out, preferred_element_type=jnp.float32)
    conv_in = layer_norm(mid, norm_conv).astype(jnp.bfloat16)
    both = jnp.dot(conv_in, w_point_in, preferred_element_type=jnp.float32)
    glu = both[:, :width] * jax.nn.sigmoid(both[:, width:])
    glu = jnp.where(frame_real[:, None], glu, 0.0).astype(jnp.bfloat16)
    taps = w_depth.shape[0]
    rim = passed_along(glu[frame_rows - (taps - 1) :], ("tm", "mp"), 1)
    padded = jnp.concatenate([rim, glu], axis=0).astype(jnp.float32)
    kernel = w_depth.astype(jnp.float32)
    depth = jnp.zeros((frame_rows, width), jnp.float32)
    for tap in range(taps):
        depth = depth + kernel[tap][None, :] * padded[taps - 1 - tap : taps - 1 - tap + frame_rows]
    activated = jax.nn.silu(depth).astype(jnp.bfloat16)
    final = mid + jnp.dot(activated, w_point_out, preferred_element_type=jnp.float32)
    conf_out = jnp.where(frame_real[:, None], final, 0.0).astype(jnp.bfloat16)
    pooled = (
        jnp.sum(conf_out.astype(jnp.float32).reshape(frame_rows // 4, 4, width), axis=1) * 0.25
    ).astype(jnp.bfloat16)
    shard_pooled = lax.all_gather(pooled, "mp", axis=0, tiled=True)
    shard_tokens = shard_pooled.shape[0]
    adapter_part = lax.all_gather(w_adapter, "tm", axis=0, tiled=True)
    adapter_full = lax.all_gather(adapter_part, "mp", axis=1, tiled=True)
    adapted = jnp.dot(shard_pooled, adapter_full, preferred_element_type=jnp.float32)
    llm_in = (
        adapted
        * lax.rsqrt(jnp.mean(adapted * adapted, axis=-1, keepdims=True) + eps_llm)
        * llm_gain
    ).astype(jnp.bfloat16)
    query_cols = w_query.shape[1]
    key_cols = w_key.shape[1]
    raw_query = jnp.dot(
        llm_in,
        lax.all_gather(w_query, "tm", axis=0, tiled=True),
        preferred_element_type=jnp.float32,
    )
    raw_keys = jnp.dot(
        llm_in, lax.all_gather(w_key, "tm", axis=0, tiled=True), preferred_element_type=jnp.float32
    )
    raw_values = jnp.dot(
        llm_in,
        lax.all_gather(w_value, "tm", axis=0, tiled=True),
        preferred_element_type=jnp.float32,
    )
    llm_size = HDIM
    query_heads_dev = query_cols // llm_size
    kv_heads = key_cols // llm_size
    group = query_heads_dev // kv_heads
    token_index = time_place * shard_tokens + jnp.arange(shard_tokens, dtype=jnp.int32)
    llm_query = rotary(
        raw_query.reshape(shard_tokens, query_heads_dev, llm_size), token_index
    ).astype(jnp.bfloat16)
    llm_query = llm_query.reshape(shard_tokens, kv_heads, group, llm_size)
    llm_keys = (
        rotary(raw_keys.reshape(shard_tokens, kv_heads, llm_size), token_index)
        .astype(jnp.bfloat16)
        .reshape(shard_tokens, key_cols)
    )
    llm_values = raw_values.astype(jnp.bfloat16)
    score_scale = 1.0 / jnp.sqrt(jnp.float32(llm_size))
    start_state = (
        jnp.full((kv_heads, group, shard_tokens), masked_score, jnp.float32),
        jnp.zeros((kv_heads, group, shard_tokens), jnp.float32),
        jnp.zeros((kv_heads, group, shard_tokens, llm_size), jnp.float32),
    )
    key_piece = lax.all_gather(llm_keys, "tm", axis=0, tiled=True)
    value_piece = lax.all_gather(llm_values, "tm", axis=0, tiled=True)
    piece_rows = key_piece.shape[0]
    step_rows = math.gcd(piece_rows, 512)

    def one_step(block, state):
        best, total_weight, accum = state
        key_block = lax.dynamic_slice_in_dim(key_piece, block * step_rows, step_rows, 0).reshape(
            step_rows, kv_heads, llm_size
        )
        value_block = lax.dynamic_slice_in_dim(
            value_piece, block * step_rows, step_rows, 0
        ).reshape(step_rows, kv_heads, llm_size)
        block_index = block * step_rows + jnp.arange(step_rows, dtype=jnp.int32)
        block_place, block_count = shard_count(block_index, valid_counts, shard_tokens)
        block_real = block_place * 4 < block_count
        matches = block_index[None, :] == token_index[:, None]
        seen = (block_index[None, :] <= token_index[:, None]) & (block_real[None, :] | matches)
        block_scores = (
            jnp.einsum("qhgd,khd->hgqk", llm_query, key_block, preferred_element_type=jnp.float32)
            * score_scale
        )
        block_scores = jnp.where(seen[None, None], block_scores, masked_score)
        new_best = jnp.maximum(best, jnp.max(block_scores, axis=-1))
        block_weights = jnp.where(
            seen[None, None], jnp.exp(block_scores - new_best[..., None]), 0.0
        )
        fade = jnp.exp(best - new_best)
        total_weight = total_weight * fade + jnp.sum(block_weights, axis=-1)
        accum = accum * fade[..., None] + jnp.einsum(
            "hgqk,khd->hgqd",
            block_weights.astype(jnp.bfloat16),
            value_block,
            preferred_element_type=jnp.float32,
        )
        return (new_best, total_weight, accum)

    best, total_weight, accum = lax.fori_loop(0, piece_rows // step_rows, one_step, start_state)
    result = accum / total_weight[..., None]
    attended = (
        jnp.transpose(result, (2, 0, 1, 3)).reshape(shard_tokens, query_cols).astype(jnp.bfloat16)
    )
    return (conf_out, attended)


def solution(mesh):
    placed = (
        P(("tm", "mp"), None),
        P(),
        P(),
        P(),
        P(),
        P(),
        P(),
        P(),
        P(),
        P(),
        P("tm", "mp"),
        P(),
        P("tm", "mp"),
        P("tm", "mp"),
        P("tm", "mp"),
    )
    return jax.shard_map(
        on_device,
        mesh=mesh,
        in_specs=placed,
        out_specs=(P(("tm", "mp"), None), P("tm", "mp")),
        check_vma=False,
    )
```

profile of v0, /device:TPU:0, one launch (start us, length us, event | category | flops | bytes accessed | tf_op | source)
XLA Modules:
  0.0 644.8 jit_solution(2328061743884182033)
XLA Ops:
  7.2 0.7 all-gather.6.cloned.1.call-update
  8.0 41.4 %all-gather.6.cloned.1.call-done = bf16[1024,2048]{1,0:T(8,128)(2,1)} async-done(((bf16[128,2048]{1,0:T(8,128)(2,1)}), bf16[1024,2048]{1,0:T(8,128)(2,1)}) %all-gather.6.cloned.1.call-update) | async-done | bytes 4194320 | tf_op jit(solution)/shard_map/all_gather | solution.py:135
  49.4 0.7 all-gather.10.cloned.1.call-update
  50.2 0.5 all-gather.14.cloned.1.call-update
  50.7 0.5 all-gather.12.cloned.1.call-update
  51.4 0.2 fusion.32
  51.7 3.9 convolution_convert_fusion
  55.6 0.8 fusion.92
  56.3 3.4 collective-permute-start.1
  59.7 4.1 collective-permute-start
  63.9 0.9 broadcast_add_fusion
  64.9 0.7 or_and_fusion.1
  65.6 0.7 fusion.94
  66.2 0.7 fusion.93
  66.9 0.3 multiply_cosine_fusion
  67.3 0.8 copy.53
  68.2 0.6 subtract_compare_fusion.1
  68.7 0.6 collective-permute-done.1
  69.6 10.4 %collective-permute-done = bf16[128,1024]{1,0:T(8,128)(2,1)} collective-permute-done((bf16[128,1024]{1,0:T(8,128)(2,1)}, bf16[128,1024]{1,0:T(8,128)(2,1)}, u32[]{:S(2)}, u32[]{:S(2)}) %collective-permute-start) | collective-permute-done | bytes 262176 | tf_op jit(solution)/shard_map/ppermute | solution.py:21
  80.0 1.1 pad_maximum_fusion
  81.1 1.0 copy.52
  82.1 2.0 fusion.95
  84.1 1.8 fusion.97
  86.0 3.9 fusion.22
  89.9 0.5 fusion.96
  90.4 0.2 multiply_reduce_fusion.1
  91.0 3.1 fusion.72
  94.3 13.2 %collective-permute-start.2 = (bf16[30,1024]{1,0:T(8,128)(2,1)S(1)}, bf16[30,1024]{1,0:T(8,128)(2,1)S(1)}, u32[]{:S(2)}, u32[]{:S(2)}) collective-permute-start(bf16[30,1024]{1,0:T(8,128)(2,1)S(1)} %slice.294), channel_id=1, source_target_pairs={{0,1},{1,2},{2,3},{3,4},{4,5},{5,6},{6,7},{7,8},{8,9},{9,10},{10,1... | collective-permute-start | bytes 184328 | tf_op jit(solution)/shard_map/ppermute | solution.py:21
  107.6 3.0 collective-permute-done.2
  111.1 2.5 fusion.23
  113.8 0.3 reduce_sum.120
  114.1 36.5 %all_gather.24 = bf16[128,1024]{1,0:T(8,128)(2,1)S(1)} all-gather(bf16[32,1024]{1,0:T(8,128)(2,1)S(1)} %multiply_convert_fusion.5), channel_id=1, replica_groups=mesh['tm'=8,'mp'=4] {'mp'}, dimensions={0}, use_global_device_ids=true | all-gather | bytes 327680 | tf_op jit(solution)/shard_map/all_gather | solution.py:133
  150.6 200.2 %all-gather.8.cloned.1.call-done = bf16[1024,8192]{1,0:T(8,128)(2,1)} async-done(((bf16[1024,2048]{1,0:T(8,128)(2,1)}), bf16[1024,8192]{1,0:T(8,128)(2,1)}) %all-gather.8.cloned.1.call-update) | async-done | bytes 16777232 | tf_op jit(solution)/shard_map/all_gather | solution.py:136
  350.8 8.2 %multiply_reduce_fusion = (f32[128]{0:T(128)S(1)}, f32[128,8192]{1,0:T(8,128)S(1)}) fusion(bf16[128,1024]{1,0:T(8,128)(2,1)S(1)} %all_gather.24, bf16[1024,8192]{1,0:T(8,128)(2,1)} %all-gather.8.cloned.1.call-done), kind=kOutput, calls=%fused_computation.35 | convolution fusion | flops 2149580800 | bytes 21234176 | tf_op jit(solution)/shard_map/dot_general | solution.py:137
  359.0 0.5 multiply_convert_fusion
  359.5 27.4 %all-gather.10.cloned.1.call-done = bf16[8192,256]{1,0:T(8,128)(2,1)} async-done(((bf16[1024,256]{1,0:T(8,128)(2,1)}), bf16[8192,256]{1,0:T(8,128)(2,1)}) %all-gather.10.cloned.1.call-update) | async-done | bytes 4194320 | tf_op jit(solution)/shard_map/all_gather | solution.py:151
  386.9 2.9 fusion.98
  389.9 0.2 slice_negate_fusion.2
  390.1 0.2 maximum_multiply_fusion.1
  390.4 12.2 %all_gather.28 = bf16[1024,256]{1,0:T(8,128)(2,1)} all-gather(bf16[128,256]{1,0:T(8,128)(2,1)S(1)} %fusion.82), channel_id=1, replica_groups=mesh['tm'=8,'mp'=4] {'tm'}, dimensions={0}, use_global_device_ids=true | all-gather | bytes 589824 | tf_op jit(solution)/shard_map/all_gather | solution.py:179
  402.6 23.5 %all-gather.14.cloned.1.call-done = bf16[8192,256]{1,0:T(8,128)(2,1)} async-done(((bf16[1024,256]{1,0:T(8,128)(2,1)}), bf16[8192,256]{1,0:T(8,128)(2,1)}) %all-gather.14.cloned.1.call-update) | async-done | bytes 4194320 | tf_op jit(solution)/shard_map/all_gather | solution.py:155
  426.1 2.9 convolution_convert_fusion.1
  429.0 10.8 %all_gather.31 = bf16[1024,256]{1,0:T(8,128)(2,1)} all-gather(bf16[128,256]{1,0:T(8,128)(2,1)S(1)} %convolution_convert_fusion.1), channel_id=1, replica_groups=mesh['tm'=8,'mp'=4] {'tm'}, dimensions={0}, use_global_device_ids=true | all-gather | bytes 589824 | tf_op jit(solution)/shard_map/all_gather | solution.py:180
  439.8 148.9 %all-gather.12.cloned.1.call-done = bf16[8192,2048]{1,0:T(8,128)(2,1)} async-done(((bf16[1024,2048]{1,0:T(8,128)(2,1)}), bf16[8192,2048]{1,0:T(8,128)(2,1)}) %all-gather.12.cloned.1.call-update) | async-done | bytes 33554448 | tf_op jit(solution)/shard_map/all_gather | solution.py:147
  588.7 12.9 %fusion.99 = f32[128,2048]{1,0:T(8,128)S(1)} fusion(bf16[128,8192]{1,0:T(8,128)(2,1)S(1)} %multiply_convert_fusion, bf16[8192,2048]{1,0:T(8,128)(2,1)} %all-gather.12.cloned.1.call-done), kind=kOutput, calls=%fused_computation.199 | convolution fusion | flops 4294967296 | bytes 36700160 | tf_op jit(solution)/shard_map/dot_general | solution.py:145
  601.6 0.3 copy.56
  601.9 1.1 slice_negate_fusion
  603.0 2.4 copy.57
  605.4 2.4 copy.58
  608.0 2.2 fusion.25
  610.2 25.0 %while.20 = (s32[]{:T(128)}, f32[2,8,128]{2,1,0:T(8,128)S(1)}, f32[2,8,128]{2,1,0:T(8,128)S(1)}, f32[2,8,128,128]{3,2,1,0:T(8,128)}, s32[8]{0:T(128)S(1)}, /*ind...) while((s32[]{:T(128)}, f32[2,8,128]{2,1,0:T(8,128)S(1)}, ...), condition=%wide.region_14.15_spmd.clone, body=%wide.region_10.14_spmd.clone.sunk | while | flops 551591552 | bytes 26622240 | solution.py:216
  610.6 1.0 constant_dynamic-slice_fusion.3
  611.7 2.8 fusion.133
  614.6 3.2 fusion.134
  617.9 3.9 fusion.136
  621.8 0.9 copy-done.5
  623.1 1.0 constant_dynamic-slice_fusion.3
  624.3 2.8 fusion.133
  627.1 3.2 fusion.134
  630.4 3.9 fusion.136
  634.3 0.9 copy-done.5
  635.3 1.7 fusion.70
  637.0 0.3 copy.61
  637.4 0.9 copy.81
  (152 shorter events, 3.2 us)
Async XLA Ops:
  7.2 82.7 %copy-start = (bf16[1024,1024]{1,0:T(8,128)(2,1)S(1)}, bf16[1024,1024]{1,0:T(8,128)(2,1)}, u32[]{:S(2)}) copy-start(bf16[1024,1024]{1,0:T(8,128)(2,1)} %param.22) | copy-start | bytes 6291460
  7.2 42.2 %all-gather.6.cloned.1.call-start = ((), (), s32[]{:S(2)}) async-start(), calls=%async_computation | async-start | bytes 4718592 | tf_op jit(solution)/shard_map/all_gather | solution.py:135
  7.9 342.8 %all-gather.8.cloned.1.call-start = ((), (), s32[]{:S(2)}) async-start(), calls=%async_computation.1 | async-start | bytes 20971520 | tf_op jit(solution)/shard_map/all_gather | solution.py:136
  49.4 1.9 copy-start.3
  49.4 2.3 copy-start.9
  49.4 337.5 %all-gather.10.cloned.1.call-start = ((), (), s32[]{:S(2)}) async-start(), calls=%async_computation.2 | async-start | bytes 4718592 | tf_op jit(solution)/shard_map/all_gather | solution.py:151
  50.1 376.0 %all-gather.14.cloned.1.call-start = ((), (), s32[]{:S(2)}) async-start(), calls=%async_computation.4 | async-start | bytes 4718592 | tf_op jit(solution)/shard_map/all_gather | solution.py:155
  50.7 538.0 %all-gather.12.cloned.1.call-start = ((), (), s32[]{:S(2)}) async-start(), calls=%async_computation.3 | async-start | bytes 37748736 | tf_op jit(solution)/shard_map/all_gather | solution.py:147
  51.7 13.1 %copy-start.11 = (s32[8]{0:T(128)S(1)}, s32[8]{0:T(128)}, u32[]{:S(2)}) copy-start(s32[8]{0:T(128)} %param.19) | copy-start | bytes 100
  51.7 13.9 %copy-start.8 = (bf16[31,1024]{1,0:T(8,128)(2,1)S(1)}, bf16[31,1024]{1,0:T(8,128)(2,1)}, u32[]{:S(2)}) copy-start(bf16[31,1024]{1,0:T(8,128)(2,1)} %param.25) | copy-start | bytes 190468
  56.3 13.0 %collective-permute-start.1 = (bf16[128,1024]{1,0:T(8,128)(2,1)S(1)}, bf16[128,1024]{1,0:T(8,128)(2,1)S(1)}, u32[]{:S(2)}, u32[]{:S(2)}) collective-permute-start(bf16[128,1024]{1,0:T(8,128)(2,1)S(1)} %get-tuple-element.316), channel_id=1, source_target_pairs={{0,1},{1,2},{2,3},{3,4},{4,5},{5,6},{6,7},{7,8},{8,9},{9,10},{10,1... | collective-permute-start | bytes 786440 | tf_op jit(solution)/shard_map/ppermute | solution.py:21
  59.7 20.3 %collective-permute-start = (bf16[128,1024]{1,0:T(8,128)(2,1)}, bf16[128,1024]{1,0:T(8,128)(2,1)}, u32[]{:S(2)}, u32[]{:S(2)}) collective-permute-start(bf16[128,1024]{1,0:T(8,128)(2,1)} %get-tuple-element.318), channel_id=1, source_target_pairs={{0,1},{1,2},{2,3},{3,4},{4,5},{5,6},{6,7},{7,8},{8,9},{9,10},{10,1... | collective-permute-start | bytes 786440 | tf_op jit(solution)/shard_map/ppermute | solution.py:21
  82.1 2.0 copy-start.6
  86.0 4.7 copy-start.44
  89.8 4.3 copy-start.45
  90.6 20.1 %copy-start.13 = (f32[1,1024]{1,0:T(1,128)S(1)}, f32[1,1024]{1,0:T(1,128)}, u32[]{:S(2)}) copy-start(f32[1,1024]{1,0:T(1,128)} %get-tuple-element.340) | copy-start | bytes 12292
  90.7 20.1 %copy-start.14 = (f32[1,1024]{1,0:T(1,128)S(1)}, f32[1,1024]{1,0:T(1,128)}, u32[]{:S(2)}) copy-start(f32[1,1024]{1,0:T(1,128)} %get-tuple-element.341) | copy-start | bytes 12292
  90.7 20.1 %copy-start.15 = (f32[1,1024]{1,0:T(1,128)S(1)}, f32[1,1024]{1,0:T(1,128)}, u32[]{:S(2)}) copy-start(f32[1,1024]{1,0:T(1,128)} %get-tuple-element.342) | copy-start | bytes 12292
  90.7 20.1 %copy-start.16 = (f32[1,1024]{1,0:T(1,128)S(1)}, f32[1,1024]{1,0:T(1,128)}, u32[]{:S(2)}) copy-start(f32[1,1024]{1,0:T(1,128)} %get-tuple-element.343) | copy-start | bytes 12292
  90.7 20.1 %copy-start.17 = (f32[1,1024]{1,0:T(1,128)S(1)}, f32[1,1024]{1,0:T(1,128)}, u32[]{:S(2)}) copy-start(f32[1,1024]{1,0:T(1,128)} %get-tuple-element.344) | copy-start | bytes 12292
  90.7 20.1 %copy-start.18 = (f32[1,1024]{1,0:T(1,128)S(1)}, f32[1,1024]{1,0:T(1,128)}, u32[]{:S(2)}) copy-start(f32[1,1024]{1,0:T(1,128)} %get-tuple-element.345) | copy-start | bytes 12292
  90.7 20.1 %copy-start.19 = (f32[1,1024]{1,0:T(1,128)S(1)}, f32[1,1024]{1,0:T(1,128)}, u32[]{:S(2)}) copy-start(f32[1,1024]{1,0:T(1,128)} %get-tuple-element.346) | copy-start | bytes 12292
  90.7 20.1 %copy-start.20 = (f32[1,1024]{1,0:T(1,128)S(1)}, f32[1,1024]{1,0:T(1,128)}, u32[]{:S(2)}) copy-start(f32[1,1024]{1,0:T(1,128)} %get-tuple-element.347) | copy-start | bytes 12292
  90.7 20.1 %copy-start.21 = (f32[1,1024]{1,0:T(1,128)S(1)}, f32[1,1024]{1,0:T(1,128)}, u32[]{:S(2)}) copy-start(f32[1,1024]{1,0:T(1,128)} %get-tuple-element.348) | copy-start | bytes 12292
  90.7 20.1 %copy-start.22 = (f32[1,1024]{1,0:T(1,128)S(1)}, f32[1,1024]{1,0:T(1,128)}, u32[]{:S(2)}) copy-start(f32[1,1024]{1,0:T(1,128)} %get-tuple-element.349) | copy-start | bytes 12292
  90.7 20.1 %copy-start.23 = (f32[1,1024]{1,0:T(1,128)S(1)}, f32[1,1024]{1,0:T(1,128)}, u32[]{:S(2)}) copy-start(f32[1,1024]{1,0:T(1,128)} %get-tuple-element.350) | copy-start | bytes 12292
  90.8 20.1 %copy-start.24 = (f32[1,1024]{1,0:T(1,128)S(1)}, f32[1,1024]{1,0:T(1,128)}, u32[]{:S(2)}) copy-start(f32[1,1024]{1,0:T(1,128)} %get-tuple-element.351) | copy-start | bytes 12292
  90.8 20.1 %copy-start.25 = (f32[1,1024]{1,0:T(1,128)S(1)}, f32[1,1024]{1,0:T(1,128)}, u32[]{:S(2)}) copy-start(f32[1,1024]{1,0:T(1,128)} %get-tuple-element.321) | copy-start | bytes 12292
  90.8 20.1 %copy-start.26 = (f32[1,1024]{1,0:T(1,128)S(1)}, f32[1,1024]{1,0:T(1,128)}, u32[]{:S(2)}) copy-start(f32[1,1024]{1,0:T(1,128)} %get-tuple-element.322) | copy-start | bytes 12292
  90.8 20.1 %copy-start.27 = (f32[1,1024]{1,0:T(1,128)S(1)}, f32[1,1024]{1,0:T(1,128)}, u32[]{:S(2)}) copy-start(f32[1,1024]{1,0:T(1,128)} %get-tuple-element.323) | copy-start | bytes 12292
  90.8 20.1 %copy-start.28 = (f32[1,1024]{1,0:T(1,128)S(1)}, f32[1,1024]{1,0:T(1,128)}, u32[]{:S(2)}) copy-start(f32[1,1024]{1,0:T(1,128)} %get-tuple-element.324) | copy-start | bytes 12292
  90.8 20.1 %copy-start.29 = (f32[1,1024]{1,0:T(1,128)S(1)}, f32[1,1024]{1,0:T(1,128)}, u32[]{:S(2)}) copy-start(f32[1,1024]{1,0:T(1,128)} %get-tuple-element.325) | copy-start | bytes 12292
  90.8 20.1 %copy-start.30 = (f32[1,1024]{1,0:T(1,128)S(1)}, f32[1,1024]{1,0:T(1,128)}, u32[]{:S(2)}) copy-start(f32[1,1024]{1,0:T(1,128)} %get-tuple-element.326) | copy-start | bytes 12292
  90.8 20.1 %copy-start.31 = (f32[1,1024]{1,0:T(1,128)S(1)}, f32[1,1024]{1,0:T(1,128)}, u32[]{:S(2)}) copy-start(f32[1,1024]{1,0:T(1,128)} %get-tuple-element.327) | copy-start | bytes 12292
  90.8 20.1 %copy-start.32 = (f32[1,1024]{1,0:T(1,128)S(1)}, f32[1,1024]{1,0:T(1,128)}, u32[]{:S(2)}) copy-start(f32[1,1024]{1,0:T(1,128)} %get-tuple-element.328) | copy-start | bytes 12292
  90.8 20.1 %copy-start.33 = (f32[1,1024]{1,0:T(1,128)S(1)}, f32[1,1024]{1,0:T(1,128)}, u32[]{:S(2)}) copy-start(f32[1,1024]{1,0:T(1,128)} %get-tuple-element.329) | copy-start | bytes 12292
  90.9 20.1 %copy-start.34 = (f32[1,1024]{1,0:T(1,128)S(1)}, f32[1,1024]{1,0:T(1,128)}, u32[]{:S(2)}) copy-start(f32[1,1024]{1,0:T(1,128)} %get-tuple-element.330) | copy-start | bytes 12292
  90.9 20.1 %copy-start.35 = (f32[1,1024]{1,0:T(1,128)S(1)}, f32[1,1024]{1,0:T(1,128)}, u32[]{:S(2)}) copy-start(f32[1,1024]{1,0:T(1,128)} %get-tuple-element.331) | copy-start | bytes 12292
  90.9 20.1 %copy-start.36 = (f32[1,1024]{1,0:T(1,128)S(1)}, f32[1,1024]{1,0:T(1,128)}, u32[]{:S(2)}) copy-start(f32[1,1024]{1,0:T(1,128)} %get-tuple-element.332) | copy-start | bytes 12292
  90.9 20.1 %copy-start.37 = (f32[1,1024]{1,0:T(1,128)S(1)}, f32[1,1024]{1,0:T(1,128)}, u32[]{:S(2)}) copy-start(f32[1,1024]{1,0:T(1,128)} %get-tuple-element.333) | copy-start | bytes 12292
  90.9 20.1 %copy-start.38 = (f32[1,1024]{1,0:T(1,128)S(1)}, f32[1,1024]{1,0:T(1,128)}, u32[]{:S(2)}) copy-start(f32[1,1024]{1,0:T(1,128)} %get-tuple-element.334) | copy-start | bytes 12292
  90.9 20.1 %copy-start.39 = (f32[1,1024]{1,0:T(1,128)S(1)}, f32[1,1024]{1,0:T(1,128)}, u32[]{:S(2)}) copy-start(f32[1,1024]{1,0:T(1,128)} %get-tuple-element.335) | copy-start | bytes 12292
  90.9 20.1 %copy-start.40 = (f32[1,1024]{1,0:T(1,128)S(1)}, f32[1,1024]{1,0:T(1,128)}, u32[]{:S(2)}) copy-start(f32[1,1024]{1,0:T(1,128)} %get-tuple-element.336) | copy-start | bytes 12292
  90.9 20.1 %copy-start.41 = (f32[1,1024]{1,0:T(1,128)S(1)}, f32[1,1024]{1,0:T(1,128)}, u32[]{:S(2)}) copy-start(f32[1,1024]{1,0:T(1,128)} %get-tuple-element.337) | copy-start | bytes 12292
  90.9 20.1 %copy-start.42 = (f32[1,1024]{1,0:T(1,128)S(1)}, f32[1,1024]{1,0:T(1,128)}, u32[]{:S(2)}) copy-start(f32[1,1024]{1,0:T(1,128)} %get-tuple-element.338) | copy-start | bytes 12292
  90.9 20.1 %copy-start.43 = (f32[1,1024]{1,0:T(1,128)S(1)}, f32[1,1024]{1,0:T(1,128)}, u32[]{:S(2)}) copy-start(f32[1,1024]{1,0:T(1,128)} %get-tuple-element.339) | copy-start | bytes 12292
  91.0 20.1 %copy-start.46 = (bf16[1024,1024]{1,0:T(8,128)(2,1)S(1)}, bf16[1024,1024]{1,0:T(8,128)(2,1)}, u32[]{:S(2)}) copy-start(bf16[1024,1024]{1,0:T(8,128)(2,1)} %param.26) | copy-start | bytes 6291460
  94.3 16.3 %collective-permute-start.2 = (bf16[30,1024]{1,0:T(8,128)(2,1)S(1)}, bf16[30,1024]{1,0:T(8,128)(2,1)S(1)}, u32[]{:S(2)}, u32[]{:S(2)}) collective-permute-start(bf16[30,1024]{1,0:T(8,128)(2,1)S(1)} %slice.294), channel_id=1, source_target_pairs={{0,1},{1,2},{2,3},{3,4},{4,5},{5,6},{6,7},{7,8},{8,9},{9,10},{10,1... | collective-permute-start | bytes 184328 | tf_op jit(solution)/shard_map/ppermute | solution.py:21
  113.6 245.4 %copy-start.7 = (bf16[128,1024]{1,0:T(8,128)(2,1)}, bf16[128,1024]{1,0:T(8,128)(2,1)S(1)}, u32[]{:S(2)}) copy-start(bf16[128,1024]{1,0:T(8,128)(2,1)S(1)} %fusion.23) | copy-start | bytes 786436
  150.6 208.4 %copy-start.10 = (f32[8192]{0:T(1024)S(1)}, f32[8192]{0:T(1024)}, u32[]{:S(2)}) copy-start(f32[8192]{0:T(1024)} %param.28) | copy-start | bytes 98308
  603.0 7.2 %copy-start.2 = (bf16[1024,256]{1,0:T(8,128)(2,1)S(1)}, bf16[1024,256]{1,0:T(8,128)(2,1)}, u32[]{:S(2)}) copy-start(bf16[1024,256]{1,0:T(8,128)(2,1)} %all_gather.28) | copy-start | bytes 1572868
  603.0 7.2 %copy-start.12 = (s32[8]{0:T(128)S(1)}, s32[8]{0:T(128)}, u32[]{:S(2)}) copy-start(s32[8]{0:T(128)} %param.19) | copy-start | bytes 100
  611.7 6.2 copy-start.4
  621.8 1.0 copy-start.5
  624.2 6.2 copy-start.4
  634.3 1.0 copy-start.5
  635.3 3.0 copy-start.1
Sparse Core Ops, SparseCore 0:
  9.9 39.4 all-gather.5
  50.9 299.7 all-gather.7
  352.7 34.2 all-gather.9
  388.7 37.3 all-gather.13
  427.8 160.7 all-gather.11
where the time goes:
time: 646 us; the launch traced here: 645 us
  waiting for transfers between devices  458 us (71%)
  blocking collectives  59.4 us (9%)
  matrix products  58.1 us (9%)
  starting transfers between devices  20.9 us (3%)
  other arithmetic  18.1 us (3%)
  local copies, waits for them, and re-layouts  15.7 us (2%)
  between operations  14.7 us (2%)
    all_gather x1, waiting for transfers between devices, on_device(): adapter_full = lax.all_gather(adapter_part, 'mp', axis=1, tiled=True)  200 us
    all_gather x1, waiting for transfers between devices, on_device(): lax.all_gather(w_query, 'tm', axis=0, tiled=True)  149 us
    all_gather x1, waiting for transfers between devices, on_device(): adapter_part = lax.all_gather(w_adapter, 'tm', axis=0, tiled=True)  41.4 us
    all_gather x1, blocking collectives, on_device(): shard_pooled = lax.all_gather(pooled, 'mp', axis=0, tiled=True)  36.5 us
    all_gather x1, waiting for transfers between devices, on_device(): lax.all_gather(w_key, 'tm', axis=0, tiled=True)  27.4 us
    all_gather x1, waiting for transfers between devices, on_device(): lax.all_gather(w_value, 'tm', axis=0, tiled=True)  23.5 us
    ppermute x3, starting transfers between devices, passed_along(): return lax.ppermute(value, axis, pairs)  20.7 us
    ppermute x3, waiting for transfers between devices, passed_along(): return lax.ppermute(value, axis, pairs)  14.1 us
  transfers between devices with their start and end apart: 8, of which 8 were waited for; matrix products, arithmetic and copies ran while one was open for 7% of the time, Pallas kernels for 0%

commit v1 on v0

v1 whole, which is shorter than its diff:
```python
import jax
import jax.numpy as jnp
from jax import lax
from jax.experimental import pallas as pl
from jax.experimental.pallas import tpu as pltpu
from jax.sharding import PartitionSpec as P

CH = 16
HDIM = 128
SPAN = 40


eps_conf = 1e-05
eps_llm = 1e-06
rope_base = 1000000.0
masked_score = -1e30


def shifted(value, axis, by):
    length = lax.axis_size(axis)
    return lax.ppermute(value, axis, [(i, i + by) for i in range(length - by)])


def swapped(value, bits):
    length = lax.axis_size("tm")
    return lax.ppermute(value, "tm", [(i, i ^ bits) for i in range(length)])


def rotated(value, by):
    length = lax.axis_size("mp")
    return lax.ppermute(value, "mp", [(i, (i + by) % length) for i in range(length)])


def shard_count(index, valid_counts, shard_len):
    shard = index // shard_len
    table = jnp.arange(valid_counts.shape[0], dtype=jnp.int32)
    hit = shard[:, None] == table[None, :]
    count = jnp.sum(jnp.where(hit, valid_counts[None, :], 0), axis=1)
    return (index - shard * shard_len, count)


def layer_norm(field, gain):
    center = field - jnp.mean(field, axis=-1, keepdims=True)
    spread = jnp.mean(center * center, axis=-1, keepdims=True)
    return center * lax.rsqrt(spread + eps_conf) * gain


def rotary_tables(positions, size):
    half = size // 2
    freq = rope_base ** (-(jnp.arange(half, dtype=jnp.float32) * 2.0) / size)
    angle = positions.astype(jnp.float32)[:, None] * freq[None, :]
    cosine = jnp.concatenate([jnp.cos(angle), jnp.cos(angle)], axis=-1)
    sine = jnp.concatenate([-jnp.sin(angle), jnp.sin(angle)], axis=-1)
    return cosine, sine


def turn(field, cosine, sine):
    return field * cosine + pltpu.roll(field, HDIM // 2, 1) * sine


def total_of(refs, columns):
    parts = [ref[:, columns].astype(jnp.float32) for ref in refs]
    while len(parts) > 1:
        parts = [sum(parts[i : i + 2]) for i in range(0, len(parts), 2)]
    return parts[0]


def finish_keys(parts, cosine, sine, key_cols, width):
    rows = cosine.shape[0]

    def kernel(*refs):
        part_refs, (cos_ref, sin_ref, kv_ref, scale_ref) = refs[: len(parts)], refs[len(parts) :]
        squares = total_of(part_refs, pl.ds(2 * key_cols, HDIM))
        power = (
            squares[:, 0:1] + squares[:, 32:33] + squares[:, 64:65] + squares[:, 96:97]
        ) * (1.0 / width)
        scale = lax.rsqrt(power + eps_llm)
        scale_ref[...] = jnp.broadcast_to(scale, scale_ref.shape)
        for head in range(key_cols // HDIM):
            columns = pl.ds(head * HDIM, HDIM)
            raw = total_of(part_refs, columns) * scale
            kv_ref[:, columns] = turn(raw, cos_ref[...], sin_ref[...]).astype(jnp.bfloat16)
        columns = pl.ds(key_cols, key_cols)
        kv_ref[:, columns] = (total_of(part_refs, columns) * scale).astype(jnp.bfloat16)

    return pl.pallas_call(
        kernel,
        out_shape=(
            jax.ShapeDtypeStruct((rows, 2 * key_cols), jnp.bfloat16),
            jax.ShapeDtypeStruct((rows, HDIM), jnp.float32),
        ),
        name="finish_keys",
    )(*parts, cosine, sine)


def attend(parts, kv, scale, cosine, sine, query_place, key_place, key_real, kv_heads):
    rows, query_cols = parts[0].shape
    tokens = kv.shape[0]
    group = query_cols // HDIM // kv_heads
    step = 2 if group % 2 == 0 and tokens <= 2048 else 1
    factor = HDIM**-0.5

    def kernel(*refs):
        part_refs = refs[: len(parts)]
        scale_ref, cos_ref, sin_ref, at_ref, place_ref, real_ref, key_ref, value_ref, out_ref = refs[
            len(parts) :
        ]
        at, place = at_ref[...], place_ref[...]
        seen = (place <= at) & ((real_ref[...] > 0) | (place == at))
        bias = jnp.where(seen, 0.0, masked_score)
        bias = jnp.concatenate([bias] * step, axis=0)
        keys, values = key_ref[...], value_ref[...]
        for first in range(0, group, step):
            queries = []
            for head in range(first, first + step):
                raw = total_of(part_refs, pl.ds(head * HDIM, HDIM)) * scale_ref[...]
                queries.append(turn(raw, cos_ref[...], sin_ref[...]).astype(jnp.bfloat16))
            query = jnp.concatenate(queries, axis=0)
            scores = lax.dot_general(
                query, keys, (((1,), (1,)), ((), ())), preferred_element_type=jnp.float32
            )
            scores = scores * factor + bias
            top = jnp.max(scores, axis=-1, keepdims=True)
            weights = jnp.exp(scores - top)
            total = jnp.sum(weights, axis=-1, keepdims=True)
            summed = jnp.dot(
                weights.astype(jnp.bfloat16), values, preferred_element_type=jnp.float32
            )
            result = (summed / total).astype(jnp.bfloat16)
            for i in range(step):
                out_ref[:, pl.ds((first + i) * HDIM, HDIM)] = result[i * rows : (i + 1) * rows]

    whole = lambda shape: pl.BlockSpec(shape, lambda h: (0, 0))
    return pl.pallas_call(
        kernel,
        grid=(kv_heads,),
        in_specs=[pl.BlockSpec((rows, group * HDIM), lambda h: (0, h))] * len(parts)
        + [
            whole((rows, HDIM)),
            whole((rows, HDIM)),
            whole((rows, HDIM)),
            whole((rows, 1)),
            whole((1, tokens)),
            whole((1, tokens)),
            pl.BlockSpec((tokens, HDIM), lambda h: (0, h)),
            pl.BlockSpec((tokens, HDIM), lambda h: (0, kv_heads + h)),
        ],
        out_specs=pl.BlockSpec((rows, group * HDIM), lambda h: (0, h)),
        out_shape=jax.ShapeDtypeStruct((rows, query_cols), jnp.bfloat16),
        compiler_params=pltpu.CompilerParams(vmem_limit_bytes=48 << 20),
        name="attend",
    )(*parts, scale, cosine, sine, query_place, key_place, key_real, kv, kv)


def conformer(
    frames, near, far, first, block_ids, valid_counts, shard_frames, norm_attn, w_qkv, w_attn_out,
    norm_conv, w_point_in, w_depth, w_point_out,
):
    frame_rows, width = frames.shape
    heads, head_size = CH, width // CH
    extra = far.shape[0]
    before = near.shape[0] + extra
    held = jnp.concatenate([far, near, frames], axis=0).astype(jnp.float32)
    key_rows, query_rows = before + frame_rows, extra + frame_rows
    lead = key_rows - query_rows
    normed = layer_norm(held, norm_attn).astype(jnp.bfloat16)
    projected = jnp.dot(normed, w_qkv, preferred_element_type=jnp.float32).astype(jnp.bfloat16)
    queries = projected[lead:, :width].reshape(query_rows, heads, head_size)
    keys = projected[:, width : 2 * width].reshape(key_rows, heads, head_size)
    values = projected[:, 2 * width :].reshape(key_rows, heads, head_size)
    key_index = first - before + jnp.arange(key_rows, dtype=jnp.int32)
    key_place, key_count = shard_count(key_index, valid_counts, shard_frames)
    key_real = (key_place < key_count) & (key_index >= 0)
    padded_ids = jnp.concatenate([jnp.full((before,), -100, jnp.int32), block_ids])
    key_ids = lax.dynamic_slice_in_dim(padded_ids, first, key_rows, 0)
    query_index, query_ids, real = key_index[lead:], key_ids[lead:], key_real[lead:]
    same = key_index[None, :] == query_index[:, None]
    visible = (
        (key_index[None, :] <= query_index[:, None])
        & (key_ids[None, :] >= query_ids[:, None] - 2)
        & (key_real[None, :] | same)
    )
    scores = jnp.einsum("qhd,khd->hqk", queries, keys, preferred_element_type=jnp.float32) / jnp.sqrt(
        jnp.float32(head_size)
    )
    scores = jnp.where(visible[None], scores, masked_score)
    top = jnp.max(scores, axis=-1, keepdims=True)
    weights = jnp.where(visible[None], jnp.exp(scores - top), 0.0)
    total = jnp.sum(weights, axis=-1)
    summed = jnp.einsum(
        "hqk,khd->qhd", weights.astype(jnp.bfloat16), values, preferred_element_type=jnp.float32
    )
    context = (
        (summed / jnp.transpose(total)[:, :, None]).reshape(query_rows, width).astype(jnp.bfloat16)
    )
    mid = held[lead:] + jnp.dot(context, w_attn_out, preferred_element_type=jnp.float32)
    conv_in = layer_norm(mid, norm_conv).astype(jnp.bfloat16)
    both = jnp.dot(conv_in, w_point_in, preferred_element_type=jnp.float32)
    glu = both[:, :width] * jax.nn.sigmoid(both[:, width:])
    glu = jnp.where(real[:, None], glu, 0.0).astype(jnp.bfloat16).astype(jnp.float32)
    taps = w_depth.shape[0]
    kernel = w_depth.astype(jnp.float32)
    depth = jnp.zeros((frame_rows, width), jnp.float32)
    for tap in range(taps):
        depth = depth + kernel[tap][None, :] * glu[extra - tap : extra - tap + frame_rows]
    activated = jax.nn.silu(depth).astype(jnp.bfloat16)
    final = mid[extra:] + jnp.dot(activated, w_point_out, preferred_element_type=jnp.float32)
    conf_out = jnp.where(real[extra:, None], final, 0.0).astype(jnp.bfloat16)
    pooled = (
        jnp.sum(conf_out.astype(jnp.float32).reshape(frame_rows // 4, 4, width), axis=1) * 0.25
    ).astype(jnp.bfloat16)
    return conf_out, pooled


def own_adapter_columns(w_adapter):
    tm_count, mp_count = lax.axis_size("tm"), lax.axis_size("mp")
    time_place, model_place = lax.axis_index("tm"), lax.axis_index("mp")
    rows, cols = w_adapter.shape
    pieces = [w_adapter] + [rotated(w_adapter, by) for by in range(1, mp_count)]
    stacked = jnp.stack(pieces)
    kept = {}
    for other in range(0, tm_count, 2):
        wanted = (time_place ^ other) // 2
        piece = lax.dynamic_index_in_dim(
            stacked, (model_place - wanted) % mp_count, 0, keepdims=False
        )
        kept[other] = swapped(piece, other) if other else piece
    near = jnp.stack([kept[other] for other in range(0, tm_count, 2)])
    half = cols // 2
    core = time_place % 2
    mine = lax.dynamic_slice_in_dim(near, core * half, half, 2)
    given = lax.dynamic_slice_in_dim(near, (1 - core) * half, half, 2)
    taken = swapped(given, 1)
    result = jnp.zeros((tm_count, rows, half), w_adapter.dtype)
    for i in range(tm_count // 2):
        result = lax.dynamic_update_index_in_dim(result, mine[i], time_place ^ (2 * i), 0)
        result = lax.dynamic_update_index_in_dim(result, taken[i], time_place ^ (2 * i + 1), 0)
    return result.reshape(tm_count * rows, half)


def spread(value):
    tm_count = lax.axis_size("tm")
    blocks = [value] + [swapped(value, other) for other in range(2, tm_count, 2)]
    even = jnp.concatenate(blocks, axis=0)
    return jnp.concatenate([even, swapped(even, 1)], axis=0)


def gathered_parts(value):
    tm_count = lax.axis_size("tm")
    half = value.shape[0] // 2
    rows = value.shape[0] // tm_count
    other = swapped(value[half:], 1)
    chip = (value[:half].astype(jnp.float32) + other.astype(jnp.float32)).astype(jnp.bfloat16)
    return [chip[:rows]] + [
        swapped(chip[i * rows : (i + 1) * rows], 2 * i) for i in range(1, tm_count // 2)
    ]


def on_device(
    frames,
    block_ids,
    valid_counts,
    norm_attn,
    w_qkv,
    w_attn_out,
    norm_conv,
    w_point_in,
    w_depth,
    w_point_out,
    w_adapter,
    llm_gain,
    w_query,
    w_key,
    w_value,
):
    tm_count, mp_count = lax.axis_size("tm"), lax.axis_size("mp")
    time_place, model_place = lax.axis_index("tm"), lax.axis_index("mp")
    frame_rows, width = frames.shape
    shard_frames = frame_rows * mp_count
    first = (time_place * mp_count + model_place) * frame_rows
    near = shifted(frames, ("tm", "mp"), 1)
    far = shifted(frames[frame_rows - 32 :], ("tm", "mp"), 2)
    adapter = own_adapter_columns(w_adapter)
    conf_out, pooled = conformer(
        frames, near, far, first, block_ids, valid_counts, shard_frames, norm_attn, w_qkv,
        w_attn_out, norm_conv, w_point_in, w_depth, w_point_out,
    )
    piece = pooled.shape[0]
    shard_tokens = piece * mp_count
    cycle = [rotated(pooled, by) for by in range(mp_count - 1, 0, -1)] + [pooled]
    shard_pooled = lax.dynamic_slice_in_dim(
        jnp.concatenate(cycle + cycle, axis=0), (mp_count - 1 - model_place) * piece, shard_tokens, 0
    )
    all_pooled = spread(shard_pooled)
    tokens = all_pooled.shape[0]
    adapted = jnp.dot(all_pooled, adapter, preferred_element_type=jnp.float32)
    block = adapter.shape[1]
    gain = lax.dynamic_slice_in_dim(llm_gain, time_place * block, block, 0)
    scaled = (adapted * gain).astype(jnp.bfloat16)
    squares = jnp.sum(adapted * adapted, axis=-1, keepdims=True)
    high = lax.reduce_precision(squares, 8, 7)
    lane = jnp.arange(HDIM, dtype=jnp.int32)[None, :] // 32 - 2 * (time_place % 2)
    words = jnp.where(lane == 0, high, jnp.where(lane == 1, squares - high, 0.0)).astype(jnp.bfloat16)
    raw_keys = jnp.dot(scaled, w_key, preferred_element_type=jnp.float32).astype(jnp.bfloat16)
    raw_values = jnp.dot(scaled, w_value, preferred_element_type=jnp.float32).astype(jnp.bfloat16)
    raw_query = jnp.dot(scaled, w_query, preferred_element_type=jnp.float32).astype(jnp.bfloat16)
    key_cols = w_key.shape[1]
    kv_parts = gathered_parts(jnp.concatenate([raw_keys, raw_values, words], axis=1))
    query_parts = gathered_parts(raw_query)
    order = list(range(0, tm_count, 2)) + list(range(1, tm_count, 2))
    within = jnp.arange(shard_tokens, dtype=jnp.int32)
    own_place = time_place * shard_tokens + within
    cosine, sine = rotary_tables(own_place, HDIM)
    kv, scale = finish_keys(kv_parts, cosine, sine, key_cols, block * tm_count)
    all_kv = spread(kv)
    key_place = jnp.concatenate([(time_place ^ other) * shard_tokens + within for other in order])
    place_in, counts = shard_count(key_place, valid_counts, shard_tokens)
    key_real = (place_in * 4 < counts).astype(jnp.int32)
    attended = attend(
        query_parts, all_kv, scale, cosine, sine, own_place[:, None], key_place[None, :],
        key_real[None, :], key_cols // HDIM,
    )
    return (conf_out, attended)


def solution(mesh):
    placed = (
        P(("tm", "mp"), None),
        P(),
        P(),
        P(),
        P(),
        P(),
        P(),
        P(),
        P(),
        P(),
        P("tm", "mp"),
        P(),
        P("tm", "mp"),
        P("tm", "mp"),
        P("tm", "mp"),
    )
    return jax.shard_map(
        on_device,
        mesh=mesh,
        in_specs=placed,
        out_specs=(P(("tm", "mp"), None), P("tm", "mp")),
        check_vma=False,
    )
```

time: 646 us -> 220 us (0.34)
  waiting for transfers between devices: 458 us -> 96 us
  blocking collectives: 59.4 us -> 0 us
  matrix products: 58.1 us -> 25.1 us
  starting transfers between devices: 20.9 us -> 50.7 us
  between operations: 14.7 us -> 1.85 us
  Pallas kernels: 0 us -> 7.72 us
  local copies, waits for them, and re-layouts: 15.7 us -> 22.7 us
    all_gather x5 -> x0, waiting for transfers between devices: 441 us -> none  [the longest x1 200 us: on_device(): adapter_full = lax.all_gather(adapter_part, 'mp', axis=1, tiled=True)]
    ppermute x3 -> x28, waiting for transfers between devices: 14.1 us -> 96 us  [the longest x20 64.3 us: swapped(): return lax.ppermute(value, 'tm', [(i, i ^ bits) for i in range(length)])]
    all_gather x3 -> x0, blocking collectives: 59.4 us -> none  [the longest x1 36.5 us: on_device(): shard_pooled = lax.all_gather(pooled, 'mp', axis=0, tiled=True)]
    dot_general x14 -> x9, matrix products: 56.1 us -> 20.5 us  [the longest x1 4.99 us: conformer(): jnp.dot(normed, w_qkv, preferred_element_type=jnp.float32)]
    ppermute x3 -> x28, starting transfers between devices: 20.7 us -> 50.7 us  [the longest x6 24.2 us: rotated(): lax.ppermute(value, 'mp', [(i, (i + by) % length) for i in range(length)])]
    slice x5 -> x14, local copies, waits for them, and re-layouts: 2.95 us -> 11.1 us  [the longest x2 3.36 us: conformer(): kernel[tap][None, :] * glu[extra - tap:extra - tap + frame_rows]]
    pallas_call x0 -> x2, Pallas kernels: none -> 7.72 us  [the longest x1 5.6 us: attend(): pl.pallas_call(kernel, grid=(kv_heads,), in_specs=[pl.BlockSpec((rows, gr...]
  transfers between devices with their start and end apart: 8 -> 28, of which waited for: 8 -> 13; matrix products, arithmetic and copies ran while one was open for 7% -> 21% of each run, Pallas kernels for 0% -> 1%
where the time goes in v1:
time: 220 us
  waiting for transfers between devices  96 us (44%)
  starting transfers between devices  50.7 us (23%)
  matrix products  25.1 us (11%)
  local copies, waits for them, and re-layouts  22.7 us (10%)
  other arithmetic  15.7 us (7%)
  Pallas kernels  7.72 us (4%)
    ppermute x20, waiting for transfers between devices, swapped(): return lax.ppermute(value, 'tm', [(i, i ^ bits) for i in range(length)])  64.3 us
    ppermute x6, starting transfers between devices, rotated(): lax.ppermute(value, 'mp', [(i, (i + by) % length) for i in range(length)])  24.2 us
    ppermute x2, waiting for transfers between devices, shifted(): return lax.ppermute(value, axis, [(i, i + by) for i in range(length - by)])  23.3 us
    ppermute x20, starting transfers between devices, swapped(): return lax.ppermute(value, 'tm', [(i, i ^ bits) for i in range(length)])  21.7 us
    ppermute x6, waiting for transfers between devices, rotated(): lax.ppermute(value, 'mp', [(i, (i + by) % length) for i in range(length)])  8.38 us
    unnamed x132, local copies, waits for them, and re-layouts  6.97 us
    pallas_call x1, Pallas kernels, attend(): pl.pallas_call(kernel, grid=(kv_heads,), in_specs=[pl.BlockSpec((rows, gr...  5.6 us
    dot_general x1, matrix products, conformer(): jnp.dot(normed, w_qkv, preferred_element_type=jnp.float32)  4.99 us
  transfers between devices with their start and end apart: 28, of which 13 were waited for; matrix products, arithmetic and copies ran while one was open for 21% of the time, Pallas kernels for 1%

profile of v1, /device:TPU:0, one launch (start us, length us, event | category | flops | bytes accessed | tf_op | source)
XLA Modules:
  0.0 219.7 jit_solution(15601228479152077801)
XLA Ops:
  0.6 3.1 %collective-permute-start.9 = (bf16[128,2048]{1,0:T(8,128)(2,1)}, bf16[128,2048]{1,0:T(8,128)(2,1)}, u32[]{:S(2)}, u32[]{:S(2)}) collective-permute-start(bf16[128,2048]{1,0:T(8,128)(2,1)} %param.25), channel_id=1, source_target_pairs={{0,1},{1,2},{2,3},{3,0},{4,5},{5,6},{6,7},{7,4},{8,9},{9,10},{10,1... | collective-permute-start | bytes 1572872 | tf_op jit(solution)/shard_map/ppermute | solution.py:31
  3.7 2.6 %collective-permute-start.10 = (bf16[128,2048]{1,0:T(8,128)(2,1)}, bf16[128,2048]{1,0:T(8,128)(2,1)}, u32[]{:S(2)}, u32[]{:S(2)}) collective-permute-start(bf16[128,2048]{1,0:T(8,128)(2,1)} %param.25), channel_id=1, source_target_pairs={{0,2},{1,3},{2,0},{3,1},{4,6},{5,7},{6,4},{7,5},{8,10},{9,11},{10,... | collective-permute-start | bytes 1572872 | tf_op jit(solution)/shard_map/ppermute | solution.py:31
  6.3 1.3 collective-permute-start.11
  7.7 2.6 %collective-permute-start.1 = (bf16[128,1024]{1,0:T(8,128)(2,1)}, bf16[128,1024]{1,0:T(8,128)(2,1)S(1)}, u32[]{:S(2)}, u32[]{:S(2)}) collective-permute-start(bf16[128,1024]{1,0:T(8,128)(2,1)} %param.15), channel_id=1, source_target_pairs={{0,1},{1,2},{2,3},{3,4},{4,5},{5,6},{6,7},{7,8},{8,9},{9,10},{10,1... | collective-permute-start | bytes 786440 | tf_op jit(solution)/shard_map/ppermute | solution.py:21
  10.3 0.9 slice.284
  11.1 2.2 collective-permute-start
  13.3 1.7 fusion.82
  15.1 1.6 fusion.83
  17.3 0.8 pad_dynamic-slice_fusion
  19.4 0.8 or_and_fusion
  21.4 23.3 %collective-permute-done = bf16[32,1024]{1,0:T(8,128)(2,1)S(1)} collective-permute-done((bf16[32,1024]{1,0:T(8,128)(2,1)S(1)}, bf16[32,1024]{1,0:T(8,128)(2,1)S(1)}, u32[]{:S(2)}, u32[]{:S(2)}) %collective-permute-start) | collective-permute-done | bytes 65568 | tf_op jit(solution)/shard_map/ppermute | solution.py:21
  44.7 1.1 convert_reduce_fusion
  45.8 1.3 multiply_reduce_fusion.1
  47.1 5.0 %convolution_convert_fusion = bf16[288,3072]{1,0:T(8,128)(2,1)S(1)} fusion(bf16[1024,3072]{1,0:T(8,128)(2,1)} %param.19, f32[1024]{0:T(1024)} %param.18, f32[288]{0:T(512)S(1)} %add_rsqrt_fusion, f32[288]{0:T(512)S(1)} %broadcast_multiply_fusion, bf16[128,1024]{1,0:T(8,128)(2,1)} %param.15, bf16[128,1024]{1,0:T(8,128)(2,1)S(1)} %collective-permute-done.1, ...), kind=kOutput, calls=%fused_computation.4 | convolution fusion | flops 1815773184 | bytes 8657152 | tf_op jit(solution)/shard_map/dot_general | solution.py:167
  52.2 0.7 slice.379
  53.0 1.2 copy.28
  54.1 2.0 copy.34
  56.1 1.2 copy.27
  57.3 4.6 %fusion.85 = (f32[16,160]{1,0:T(8,128)S(1)}, bf16[16,160,288]{2,1,0:T(8,128)(2,1)}) fusion(pred[160,288]{1,0:T(8,128)(4,1)S(1)} %copy-done.17, bf16[160,16,64]{0,2,1:T(8,128)(2,1)} %bitcast.98, bf16[288,16,64]{0,2,1:T(8,128)(2,1)} %bitcast.95), kind=kOutput, calls=%fused_computation.233 | convolution fusion | flops 98795808 | bytes 2448384 | tf_op jit(solution)/shard_map/sub | solution.py:188
  61.8 2.6 %fusion.13 = bf16[160,16,64]{0,2,1:T(8,128)(2,1)S(1)} fusion(bf16[288,16,64]{0,2,1:T(8,128)(2,1)S(1)} %bitcast.96, bf16[16,160,288]{2,1,0:T(8,128)(2,1)} %get-tuple-element.63, f32[160,16]{0,1:T(8,128)S(1)} %bitcast.133), kind=kOutput, calls=%fused_computation.22 | convolution fusion | flops 94699520 | bytes 2402304 | tf_op jit(solution)/shard_map/hqk,khd->qhd/dot_general | solution.py:190
  65.5 1.3 copy-done.6
  67.0 0.9 fusion.57
  68.6 2.5 %fusion.17 = bf16[128,1024]{1,0:T(8,128)(2,1)S(1)} fusion(bf16[1024,1024]{1,0:T(8,128)(2,1)S(1)} %copy-done.55, f32[160,1024]{1,0:T(8,128)S(1)} %get-tuple-element.9, pred[128]{0:T(512)(128)(4,1)S(1)} %copy-done.58, f32[160,1024]{1,0:T(8,128)S(1)} %fusion.61, f32[1024]{0:T(1024)S(1)} %bitcast.132, f32[1024]{0:T(1024)S(1)} %bitcast.131, ...), kind=kOutput, calls=%fused_computation.25 | convolution fusion | flops 277479424 | bytes 19264000 | tf_op jit(solution)/shard_map/dot_general | solution.py:207
  71.6 17.2 %collective-permute-start.2 = (bf16[32,1024]{1,0:T(8,128)(2,1)S(1)}, bf16[32,1024]{1,0:T(8,128)(2,1)S(1)}, u32[]{:S(2)}, u32[]{:S(2)}) collective-permute-start(bf16[32,1024]{1,0:T(8,128)(2,1)S(1)} %multiply_convert_fusion.7), channel_id=1, source_target_pairs={{0,3},{1,0},{2,1},{3,2},{4,7},{5,4},{6,5},{7,6},{8,11},{9,8},{10,9... | collective-permute-start | bytes 196616 | tf_op jit(solution)/shard_map/ppermute | solution.py:31
  88.9 1.9 collective-permute-done.2
  90.8 3.3 %collective-permute-done.3 = bf16[32,1024]{1,0:T(8,128)(2,1)S(1)} collective-permute-done((bf16[32,1024]{1,0:T(8,128)(2,1)S(1)}, bf16[32,1024]{1,0:T(8,128)(2,1)S(1)}, u32[]{:S(2)}, u32[]{:S(2)}) %collective-permute-start.3) | collective-permute-done | bytes 65568 | tf_op jit(solution)/shard_map/ppermute | solution.py:31
  94.0 3.2 %collective-permute-done.4 = bf16[32,1024]{1,0:T(8,128)(2,1)S(1)} collective-permute-done((bf16[32,1024]{1,0:T(8,128)(2,1)S(1)}, bf16[32,1024]{1,0:T(8,128)(2,1)S(1)}, u32[]{:S(2)}, u32[]{:S(2)}) %collective-permute-start.4) | collective-permute-done | bytes 65568 | tf_op jit(solution)/shard_map/ppermute | solution.py:31
  97.3 0.7 constant_dynamic-update-slice_fusion.12
  98.1 2.4 %collective-permute-start.5 = (bf16[128,1024]{1,0:T(8,128)(2,1)S(1)}, bf16[128,1024]{1,0:T(8,128)(2,1)S(1)}, u32[]{:S(2)}, u32[]{:S(2)}) collective-permute-start(bf16[128,1024]{1,0:T(8,128)(2,1)S(1)} %get-tuple-element.7), channel_id=1, source_target_pairs={{0,8},{4,12},{8,0},{12,4},{16,24},{20,28},{24,16},{28,20},{1,9},{5... | collective-permute-start | bytes 786440 | tf_op jit(solution)/shard_map/ppermute | solution.py:26
  100.5 1.6 pad_maximum_fusion
  102.2 1.0 constant_dynamic-slice_fusion.1
  103.1 2.3 %collective-permute-start.13 = (bf16[128,2048]{1,0:T(8,128)(2,1)S(1)}, bf16[128,2048]{1,0:T(8,128)(2,1)}, u32[]{:S(2)}, u32[]{:S(2)}) collective-permute-start(bf16[128,2048]{1,0:T(8,128)(2,1)S(1)} %get-tuple-element.18), channel_id=1, source_target_pairs={{0,16},{4,20},{8,24},{12,28},{16,0},{20,4},{24,8},{28,12},{1,17},{... | collective-permute-start | bytes 1572872 | tf_op jit(solution)/shard_map/ppermute | solution.py:26
  105.5 1.2 collective-permute-start.14
  106.6 1.5 collective-permute-start.6
  108.1 2.4 %collective-permute-start.7 = (bf16[128,1024]{1,0:T(8,128)(2,1)S(1)}, bf16[128,1024]{1,0:T(8,128)(2,1)S(1)}, u32[]{:S(2)}, u32[]{:S(2)}) collective-permute-start(bf16[128,1024]{1,0:T(8,128)(2,1)S(1)} %get-tuple-element.7), channel_id=1, source_target_pairs={{0,24},{4,28},{8,16},{12,20},{16,8},{20,12},{24,0},{28,4},{1,25},{... | collective-permute-start | bytes 786440 | tf_op jit(solution)/shard_map/ppermute | solution.py:26
  110.6 25.8 %collective-permute-done.6 = bf16[128,1024]{1,0:T(8,128)(2,1)S(1)} collective-permute-done((bf16[128,1024]{1,0:T(8,128)(2,1)S(1)}, bf16[128,1024]{1,0:T(8,128)(2,1)S(1)}, u32[]{:S(2)}, u32[]{:S(2)}) %collective-permute-start.6) | collective-permute-done | bytes 262176 | tf_op jit(solution)/shard_map/ppermute | solution.py:26
  136.6 1.5 pad_maximum_fusion.1
  138.8 0.9 copy-done.18
  140.1 0.9 collective-permute-done.15
  141.3 2.6 %multiply_reduce_fusion = (f32[1024]{0:T(1024)S(1)}, bf16[1024,1024]{0,1:T(8,128)(2,1)S(1)}) fusion(f32[1024]{0:T(1024)S(1)} %dynamic-slice-done, bf16[1024,1024]{1,0:T(8,128)(2,1)S(1)} %constant_dynamic-update-slice_fusion.8, bf16[1024,1024]{1,0:T(8,128)(2,1)S(1)} %bitcast.94), kind=kOutput, calls=%fused_computation.1 | convolution fusion | flops 2151676928 | bytes 6299648 | tf_op jit(solution)/shard_map/dot_general | solution.py:296
  143.9 0.8 convolution_convert_fusion.2
  144.9 0.8 convolution_convert_fusion.3
  145.7 1.4 copy-done.54
  147.1 4.9 %convolution_convert_fusion.1 = bf16[1024,2048]{1,0:T(8,128)(2,1)S(1)} fusion(bf16[1024,1024]{0,1:T(8,128)(2,1)S(1)} %get-tuple-element.11, bf16[1024,2048]{1,0:T(8,128)(2,1)S(1)} %copy-done.54), kind=kOutput, calls=%fused_computation.7 | convolution fusion | flops 4297064448 | bytes 10485760 | tf_op jit(solution)/shard_map/dot_general | solution.py:306
  152.0 1.6 slice.451
  153.6 1.1 copy-done.5
  157.6 2.2 %collective-permute-done.20 = bf16[512,640]{1,0:T(8,128)(2,1)S(1)} collective-permute-done((bf16[512,640]{1,0:T(8,128)(2,1)S(1)}, bf16[512,640]{1,0:T(8,128)(2,1)S(1)}, u32[]{:S(2)}, u32[]{:S(2)}) %collective-permute-start.20) | collective-permute-done | bytes 655392 | tf_op jit(solution)/shard_map/ppermute | solution.py:26
  160.7 1.6 collective-permute-start.21
  163.0 1.3 collective-permute-start.23
  164.3 3.4 %collective-permute-done.21.refs_1_ = bf16[128,640]{1,0:T(8,128)(2,1)S(1)} collective-permute-done((bf16[128,640]{1,0:T(8,128)(2,1)S(1)}, bf16[128,640]{1,0:T(8,128)(2,1)S(1)}, u32[]{:S(2)}, u32[]{:S(2)}) %collective-permute-start.21) | collective-permute-done | bytes 163872 | tf_op jit(solution)/shard_map/ppermute | solution.py:26
  167.8 4.3 %collective-permute-done.22.refs_2_ = bf16[128,640]{1,0:T(8,128)(2,1)S(1)} collective-permute-done((bf16[128,640]{1,0:T(8,128)(2,1)S(1)}, bf16[128,640]{1,0:T(8,128)(2,1)S(1)}, u32[]{:S(2)}, u32[]{:S(2)}) %collective-permute-start.22) | collective-permute-done | bytes 163872 | tf_op jit(solution)/shard_map/ppermute | solution.py:26
  172.8 2.1 finish_keys.1
  175.3 1.8 collective-permute-start.25
  177.1 1.3 collective-permute-start.26
  178.4 2.9 %collective-permute-done.24 = bf16[128,512]{1,0:T(8,128)(2,1)S(1)} collective-permute-done((bf16[128,512]{1,0:T(8,128)(2,1)}, bf16[128,512]{1,0:T(8,128)(2,1)S(1)}, u32[]{:S(2)}, u32[]{:S(2)}) %collective-permute-start.24) | collective-permute-done | bytes 131104 | tf_op jit(solution)/shard_map/ppermute | solution.py:26
  181.3 1.9 collective-permute-done.25
  183.2 0.9 pad_maximum_fusion.5
  184.3 3.0 %add_convert_fusion = bf16[512,2048]{1,0:T(8,128)(2,1)S(1)} fusion(bf16[512,2048]{1,0:T(8,128)(2,1)} %collective-permute-done.16, bf16[1024,2048]{1,0:T(8,128)(2,1)} %copy-done.5), kind=kLoop, calls=%fused_computation.2 | loop fusion | flops 4194304 | bytes 6291456 | tf_op jit(solution)/shard_map/convert_element_type | solution.py:253
  187.5 1.3 collective-permute-start.17
  188.8 1.1 collective-permute-start.18
  189.9 1.2 collective-permute-start.19
  191.2 11.1 %collective-permute-done.17.refs_1_ = bf16[128,2048]{1,0:T(8,128)(2,1)S(1)} collective-permute-done((bf16[128,2048]{1,0:T(8,128)(2,1)S(1)}, bf16[128,2048]{1,0:T(8,128)(2,1)S(1)}, u32[]{:S(2)}, u32[]{:S(2)}) %collective-permute-start.17) | collective-permute-done | bytes 524320 | tf_op jit(solution)/shard_map/ppermute | solution.py:26
  202.3 11.8 %collective-permute-done.18.refs_2_ = bf16[128,2048]{1,0:T(8,128)(2,1)S(1)} collective-permute-done((bf16[128,2048]{1,0:T(8,128)(2,1)S(1)}, bf16[128,2048]{1,0:T(8,128)(2,1)S(1)}, u32[]{:S(2)}, u32[]{:S(2)}) %collective-permute-start.18) | collective-permute-done | bytes 524320 | tf_op jit(solution)/shard_map/ppermute | solution.py:26
  214.1 5.6 %attend.1 = bf16[128,2048]{1,0:T(8,128)(2,1)} custom-call(bf16[128,2048]{1,0:T(8,128)(2,1)S(1)} %get-tuple-element.15.refs_0_, bf16[128,2048]{1,0:T(8,128)(2,1)S(1)} %collective-permute-done.17.refs_1_, bf16[128,2048]{1,0:T(8,128)(2,1)S(1)} %collective-permute-done.18.refs_2_, bf16[128,2048]{1,0:T(8,128)(2,1)S(1)} %collective-permute-done.19.refs_3_, ...), custom_call_target="tpu_custom_call" | custom-call | tf_op jit(solution)/shard_map/attend/pallas_call | solution.py:134
  (221 shorter events, 13.0 us)
Async XLA Ops:
  0.6 63.9 %copy-start = (bf16[1024,1024]{1,0:T(8,128)(2,1)S(1)}, bf16[1024,1024]{1,0:T(8,128)(2,1)}, u32[]{:S(2)}) copy-start(bf16[1024,1024]{1,0:T(8,128)(2,1)} %param.20) | copy-start | bytes 6291460
  0.6 99.8 %collective-permute-start.9 = (bf16[128,2048]{1,0:T(8,128)(2,1)}, bf16[128,2048]{1,0:T(8,128)(2,1)}, u32[]{:S(2)}, u32[]{:S(2)}) collective-permute-start(bf16[128,2048]{1,0:T(8,128)(2,1)} %param.25), channel_id=1, source_target_pairs={{0,1},{1,2},{2,3},{3,0},{4,5},{5,6},{6,7},{7,4},{8,9},{9,10},{10,1... | collective-permute-start | bytes 1572872 | tf_op jit(solution)/shard_map/ppermute | solution.py:31
  3.7 96.8 %collective-permute-start.10 = (bf16[128,2048]{1,0:T(8,128)(2,1)}, bf16[128,2048]{1,0:T(8,128)(2,1)}, u32[]{:S(2)}, u32[]{:S(2)}) collective-permute-start(bf16[128,2048]{1,0:T(8,128)(2,1)} %param.25), channel_id=1, source_target_pairs={{0,2},{1,3},{2,0},{3,1},{4,6},{5,7},{6,4},{7,5},{8,10},{9,11},{10,... | collective-permute-start | bytes 1572872 | tf_op jit(solution)/shard_map/ppermute | solution.py:31
  6.3 94.2 %collective-permute-start.11 = (bf16[128,2048]{1,0:T(8,128)(2,1)}, bf16[128,2048]{1,0:T(8,128)(2,1)}, u32[]{:S(2)}, u32[]{:S(2)}) collective-permute-start(bf16[128,2048]{1,0:T(8,128)(2,1)} %param.25), channel_id=1, source_target_pairs={{0,3},{1,0},{2,1},{3,2},{4,7},{5,4},{6,5},{7,6},{8,11},{9,8},{10,9... | collective-permute-start | bytes 1572872 | tf_op jit(solution)/shard_map/ppermute | solution.py:31
  7.7 37.0 %collective-permute-start.1 = (bf16[128,1024]{1,0:T(8,128)(2,1)}, bf16[128,1024]{1,0:T(8,128)(2,1)S(1)}, u32[]{:S(2)}, u32[]{:S(2)}) collective-permute-start(bf16[128,1024]{1,0:T(8,128)(2,1)} %param.15), channel_id=1, source_target_pairs={{0,1},{1,2},{2,3},{3,4},{4,5},{5,6},{6,7},{7,8},{8,9},{9,10},{10,1... | collective-permute-start | bytes 786440 | tf_op jit(solution)/shard_map/ppermute | solution.py:21
  11.1 33.5 %collective-permute-start = (bf16[32,1024]{1,0:T(8,128)(2,1)S(1)}, bf16[32,1024]{1,0:T(8,128)(2,1)S(1)}, u32[]{:S(2)}, u32[]{:S(2)}) collective-permute-start(bf16[32,1024]{1,0:T(8,128)(2,1)S(1)} %slice.284), channel_id=1, source_target_pairs={{0,2},{1,3},{2,4},{3,5},{4,6},{5,7},{6,8},{7,9},{8,10},{9,11},{10,... | collective-permute-start | bytes 196616 | tf_op jit(solution)/shard_map/ppermute | solution.py:21
  21.4 25.7 %copy-start.48 = (s32[1,1024]{1,0:T(1,128)}, s32[1,1024]{1,0:T(1,128)S(1)}, u32[]{:S(2)}) copy-start(s32[1,1024]{1,0:T(1,128)S(1)} %constant_dynamic-update-slice_fusion.19) | copy-start | bytes 12292
  44.7 2.5 %copy-start.9 = (bf16[32,1024]{1,0:T(8,128)(2,1)}, bf16[32,1024]{1,0:T(8,128)(2,1)S(1)}, u32[]{:S(2)}) copy-start(bf16[32,1024]{1,0:T(8,128)(2,1)S(1)} %collective-permute-done) | copy-start | bytes 196612
  54.1 3.1 %copy-start.17 = (pred[160,288]{1,0:T(8,128)(4,1)S(1)}, pred[160,288]{1,0:T(8,128)(4,1)}, u32[]{:S(2)}) copy-start(pred[160,288]{1,0:T(8,128)(4,1)} %or_and_fusion) | copy-start | bytes 138244
  57.3 4.6 %copy-start.8 = (bf16[288,1024]{0,1:T(8,128)(2,1)S(1)}, bf16[288,1024]{0,1:T(8,128)(2,1)}, u32[]{:S(2)}) copy-start(bf16[288,1024]{0,1:T(8,128)(2,1)} %copy.27) | copy-start | bytes 1769476
  61.8 2.6 %copy-start.7 = (bf16[128,1024]{1,0:T(8,128)(2,1)S(1)}, bf16[128,1024]{1,0:T(8,128)(2,1)}, u32[]{:S(2)}) copy-start(bf16[128,1024]{1,0:T(8,128)(2,1)} %param.15) | copy-start | bytes 786436
  61.8 2.6 %copy-start.10 = (bf16[32,1024]{1,0:T(8,128)(2,1)S(1)}, bf16[32,1024]{1,0:T(8,128)(2,1)}, u32[]{:S(2)}) copy-start(bf16[32,1024]{1,0:T(8,128)(2,1)} %copy-done.9) | copy-start | bytes 196612
  64.5 2.2 copy-start.6
  64.6 2.2 copy-start.19
  66.7 1.4 copy-start.22
  66.8 1.4 copy-start.23
  66.8 1.4 copy-start.24
  66.8 1.4 copy-start.25
  66.8 1.4 copy-start.26
  66.8 1.4 copy-start.27
  66.8 1.4 copy-start.28
  66.8 1.4 copy-start.29
  66.8 1.4 copy-start.30
  66.8 1.4 copy-start.31
  66.8 1.4 copy-start.32
  67.0 1.6 copy-start.55
  67.0 1.6 copy-start.58
  68.6 20.2 %copy-start.49 = (s32[1,1024]{1,0:T(1,128)S(1)}, s32[1,1024]{1,0:T(1,128)}, u32[]{:S(2)}) copy-start(s32[1,1024]{1,0:T(1,128)} %copy-done.48) | copy-start | bytes 12292
  71.1 31.1 %copy-start.13 = (bf16[128,1024]{1,0:T(8,128)(2,1)}, bf16[128,1024]{1,0:T(8,128)(2,1)S(1)}, u32[]{:S(2)}) copy-start(bf16[128,1024]{1,0:T(8,128)(2,1)S(1)} %fusion.17) | copy-start | bytes 786436
  71.1 29.4 %copy-start.12 = (bf16[128,2048]{1,0:T(8,128)(2,1)S(1)}, bf16[128,2048]{1,0:T(8,128)(2,1)}, u32[]{:S(2)}) copy-start(bf16[128,2048]{1,0:T(8,128)(2,1)} %param.25) | copy-start | bytes 1572868
  71.6 19.1 %collective-permute-start.2 = (bf16[32,1024]{1,0:T(8,128)(2,1)S(1)}, bf16[32,1024]{1,0:T(8,128)(2,1)S(1)}, u32[]{:S(2)}, u32[]{:S(2)}) collective-permute-start(bf16[32,1024]{1,0:T(8,128)(2,1)S(1)} %multiply_convert_fusion.7), channel_id=1, source_target_pairs={{0,3},{1,0},{2,1},{3,2},{4,7},{5,4},{6,5},{7,6},{8,11},{9,8},{10,9... | collective-permute-start | bytes 196616 | tf_op jit(solution)/shard_map/ppermute | solution.py:31
  88.9 5.2 %collective-permute-start.3 = (bf16[32,1024]{1,0:T(8,128)(2,1)S(1)}, bf16[32,1024]{1,0:T(8,128)(2,1)S(1)}, u32[]{:S(2)}, u32[]{:S(2)}) collective-permute-start(bf16[32,1024]{1,0:T(8,128)(2,1)S(1)} %multiply_convert_fusion.7), channel_id=1, source_target_pairs={{0,2},{1,3},{2,0},{3,1},{4,6},{5,7},{6,4},{7,5},{8,10},{9,11},{10,... | collective-permute-start | bytes 196616 | tf_op jit(solution)/shard_map/ppermute | solution.py:31
  90.8 6.5 %collective-permute-start.4 = (bf16[32,1024]{1,0:T(8,128)(2,1)S(1)}, bf16[32,1024]{1,0:T(8,128)(2,1)S(1)}, u32[]{:S(2)}, u32[]{:S(2)}) collective-permute-start(bf16[32,1024]{1,0:T(8,128)(2,1)S(1)} %multiply_convert_fusion.7), channel_id=1, source_target_pairs={{0,1},{1,2},{2,3},{3,0},{4,5},{5,6},{6,7},{7,4},{8,9},{9,10},{10,1... | collective-permute-start | bytes 196616 | tf_op jit(solution)/shard_map/ppermute | solution.py:31
  98.1 10.1 %collective-permute-start.5 = (bf16[128,1024]{1,0:T(8,128)(2,1)S(1)}, bf16[128,1024]{1,0:T(8,128)(2,1)S(1)}, u32[]{:S(2)}, u32[]{:S(2)}) collective-permute-start(bf16[128,1024]{1,0:T(8,128)(2,1)S(1)} %get-tuple-element.7), channel_id=1, source_target_pairs={{0,8},{4,12},{8,0},{12,4},{16,24},{20,28},{24,16},{28,20},{1,9},{5... | collective-permute-start | bytes 786440 | tf_op jit(solution)/shard_map/ppermute | solution.py:26
  103.1 33.5 %collective-permute-start.12 = (bf16[128,2048]{1,0:T(8,128)(2,1)}, bf16[128,2048]{1,0:T(8,128)(2,1)S(1)}, u32[]{:S(2)}, u32[]{:S(2)}) collective-permute-start(bf16[128,2048]{1,0:T(8,128)(2,1)} %get-tuple-element.19), channel_id=1, source_target_pairs={{0,8},{4,12},{8,0},{12,4},{16,24},{20,28},{24,16},{28,20},{1,9},{5... | collective-permute-start | bytes 1572872 | tf_op jit(solution)/shard_map/ppermute | solution.py:26
  103.1 33.5 %collective-permute-start.13 = (bf16[128,2048]{1,0:T(8,128)(2,1)S(1)}, bf16[128,2048]{1,0:T(8,128)(2,1)}, u32[]{:S(2)}, u32[]{:S(2)}) collective-permute-start(bf16[128,2048]{1,0:T(8,128)(2,1)S(1)} %get-tuple-element.18), channel_id=1, source_target_pairs={{0,16},{4,20},{8,24},{12,28},{16,0},{20,4},{24,8},{28,12},{1,17},{... | collective-permute-start | bytes 1572872 | tf_op jit(solution)/shard_map/ppermute | solution.py:26
  105.5 31.1 %collective-permute-start.14 = (bf16[128,2048]{1,0:T(8,128)(2,1)S(1)}, bf16[128,2048]{1,0:T(8,128)(2,1)}, u32[]{:S(2)}, u32[]{:S(2)}) collective-permute-start(bf16[128,2048]{1,0:T(8,128)(2,1)S(1)} %get-tuple-element.17), channel_id=1, source_target_pairs={{0,24},{4,28},{8,16},{12,20},{16,8},{20,12},{24,0},{28,4},{1,25},{... | collective-permute-start | bytes 1572872 | tf_op jit(solution)/shard_map/ppermute | solution.py:26
  106.6 29.8 %collective-permute-start.6 = (bf16[128,1024]{1,0:T(8,128)(2,1)S(1)}, bf16[128,1024]{1,0:T(8,128)(2,1)S(1)}, u32[]{:S(2)}, u32[]{:S(2)}) collective-permute-start(bf16[128,1024]{1,0:T(8,128)(2,1)S(1)} %get-tuple-element.7), channel_id=1, source_target_pairs={{0,16},{4,20},{8,24},{12,28},{16,0},{20,4},{24,8},{28,12},{1,17},{... | collective-permute-start | bytes 786440 | tf_op jit(solution)/shard_map/ppermute | solution.py:26
  108.1 28.3 %collective-permute-start.7 = (bf16[128,1024]{1,0:T(8,128)(2,1)S(1)}, bf16[128,1024]{1,0:T(8,128)(2,1)S(1)}, u32[]{:S(2)}, u32[]{:S(2)}) collective-permute-start(bf16[128,1024]{1,0:T(8,128)(2,1)S(1)} %get-tuple-element.7), channel_id=1, source_target_pairs={{0,24},{4,28},{8,16},{12,20},{16,8},{20,12},{24,0},{28,4},{1,25},{... | collective-permute-start | bytes 786440 | tf_op jit(solution)/shard_map/ppermute | solution.py:26
  136.5 3.5 %collective-permute-start.8 = (bf16[512,1024]{1,0:T(8,128)(2,1)S(1)}, bf16[512,1024]{1,0:T(8,128)(2,1)S(1)}, u32[]{:S(2)}, u32[]{:S(2)}) collective-permute-start(bf16[512,1024]{1,0:T(8,128)(2,1)S(1)} %pad_maximum_fusion.3), channel_id=1, source_target_pairs={{0,4},{4,0},{8,12},{12,8},{16,20},{20,16},{24,28},{28,24},{1,5},{5... | collective-permute-start | bytes 3145736 | tf_op jit(solution)/shard_map/ppermute | solution.py:26
  138.1 1.6 copy-start.18
  138.2 2.8 %collective-permute-start.15 = (bf16[4,128,1024]{2,1,0:T(8,128)(2,1)S(1)}, bf16[4,128,1024]{2,1,0:T(8,128)(2,1)S(1)}, u32[]{:S(2)}, u32[]{:S(2)}) collective-permute-start(bf16[4,128,1024]{2,1,0:T(8,128)(2,1)S(1)} %constant_dynamic-slice_fusion), channel_id=1, source_target_pairs={{0,4},{4,0},{8,12},{12,8},{16,20},{20,16},{24,28},{28,24},{1,5},{5... | collective-permute-start | bytes 3145736 | tf_op jit(solution)/shard_map/ppermute | solution.py:26
  141.3 2.6 %copy-start.56 = (bf16[1024,256]{1,0:T(8,128)(2,1)S(1)}, bf16[1024,256]{1,0:T(8,128)(2,1)}, u32[]{:S(2)}) copy-start(bf16[1024,256]{1,0:T(8,128)(2,1)} %param.29) | copy-start | bytes 1572868
  144.9 2.2 copy-start.54
  152.0 2.8 %copy-start.5 = (bf16[1024,2048]{1,0:T(8,128)(2,1)}, bf16[1024,2048]{1,0:T(8,128)(2,1)S(1)}, u32[]{:S(2)}) copy-start(bf16[1024,2048]{1,0:T(8,128)(2,1)S(1)} %convolution_convert_fusion.1) | copy-start | bytes 12582916
  154.7 29.5 %collective-permute-start.16 = (bf16[512,2048]{1,0:T(8,128)(2,1)}, bf16[512,2048]{1,0:T(8,128)(2,1)}, u32[]{:S(2)}, u32[]{:S(2)}) collective-permute-start(bf16[512,2048]{1,0:T(8,128)(2,1)} %slice.451), channel_id=1, source_target_pairs={{0,4},{4,0},{8,12},{12,8},{16,20},{20,16},{24,28},{28,24},{1,5},{5... | collective-permute-start | bytes 6291464 | tf_op jit(solution)/shard_map/ppermute | solution.py:26
  155.6 8.6 %copy-start.50 = (s32[8]{0:T(128)S(1)}, s32[8]{0:T(128)}, u32[]{:S(2)}) copy-start(s32[8]{0:T(128)} %param.17) | copy-start | bytes 100
  155.7 4.2 %collective-permute-start.20 = (bf16[512,640]{1,0:T(8,128)(2,1)S(1)}, bf16[512,640]{1,0:T(8,128)(2,1)S(1)}, u32[]{:S(2)}, u32[]{:S(2)}) collective-permute-start(bf16[512,640]{1,0:T(8,128)(2,1)S(1)} %slice.457), channel_id=1, source_target_pairs={{0,4},{4,0},{8,12},{12,8},{16,20},{20,16},{24,28},{28,24},{1,5},{5... | collective-permute-start | bytes 1966088 | tf_op jit(solution)/shard_map/ppermute | solution.py:26
  160.7 7.0 %collective-permute-start.21 = (bf16[128,640]{1,0:T(8,128)(2,1)S(1)}, bf16[128,640]{1,0:T(8,128)(2,1)S(1)}, u32[]{:S(2)}, u32[]{:S(2)}) collective-permute-start(bf16[128,640]{1,0:T(8,128)(2,1)S(1)} %get-tuple-element.24), channel_id=1, source_target_pairs={{0,8},{4,12},{8,0},{12,4},{16,24},{20,28},{24,16},{28,20},{1,9},{5... | collective-permute-start | bytes 491528 | tf_op jit(solution)/shard_map/ppermute | solution.py:26
  162.3 9.7 %collective-permute-start.22 = (bf16[128,640]{1,0:T(8,128)(2,1)S(1)}, bf16[128,640]{1,0:T(8,128)(2,1)S(1)}, u32[]{:S(2)}, u32[]{:S(2)}) collective-permute-start(bf16[128,640]{1,0:T(8,128)(2,1)S(1)} %get-tuple-element.23), channel_id=1, source_target_pairs={{0,16},{4,20},{8,24},{12,28},{16,0},{20,4},{24,8},{28,12},{1,17},{... | collective-permute-start | bytes 491528 | tf_op jit(solution)/shard_map/ppermute | solution.py:26
  163.0 9.1 %collective-permute-start.23 = (bf16[128,640]{1,0:T(8,128)(2,1)S(1)}, bf16[128,640]{1,0:T(8,128)(2,1)S(1)}, u32[]{:S(2)}, u32[]{:S(2)}) collective-permute-start(bf16[128,640]{1,0:T(8,128)(2,1)S(1)} %get-tuple-element.22), channel_id=1, source_target_pairs={{0,24},{4,28},{8,16},{12,20},{16,8},{20,12},{24,0},{28,4},{1,25},{... | collective-permute-start | bytes 491528 | tf_op jit(solution)/shard_map/ppermute | solution.py:26
  167.8 4.3 %copy-start.14 = (bf16[128,640]{1,0:T(8,128)(2,1)}, bf16[128,640]{1,0:T(8,128)(2,1)S(1)}, u32[]{:S(2)}) copy-start(bf16[128,640]{1,0:T(8,128)(2,1)S(1)} %collective-permute-done.21.refs_1_) | copy-start | bytes 491524
  174.9 6.4 %collective-permute-start.24 = (bf16[128,512]{1,0:T(8,128)(2,1)}, bf16[128,512]{1,0:T(8,128)(2,1)S(1)}, u32[]{:S(2)}, u32[]{:S(2)}) collective-permute-start(bf16[128,512]{1,0:T(8,128)(2,1)} %get-tuple-element.5), channel_id=1, source_target_pairs={{0,8},{4,12},{8,0},{12,4},{16,24},{20,28},{24,16},{28,20},{1,9},{5... | collective-permute-start | bytes 393224 | tf_op jit(solution)/shard_map/ppermute | solution.py:26
  175.3 8.0 %collective-permute-start.25 = (bf16[128,512]{1,0:T(8,128)(2,1)}, bf16[128,512]{1,0:T(8,128)(2,1)S(1)}, u32[]{:S(2)}, u32[]{:S(2)}) collective-permute-start(bf16[128,512]{1,0:T(8,128)(2,1)} %get-tuple-element.5), channel_id=1, source_target_pairs={{0,16},{4,20},{8,24},{12,28},{16,0},{20,4},{24,8},{28,12},{1,17},{... | collective-permute-start | bytes 393224 | tf_op jit(solution)/shard_map/ppermute | solution.py:26
  177.1 6.2 %collective-permute-start.26 = (bf16[128,512]{1,0:T(8,128)(2,1)}, bf16[128,512]{1,0:T(8,128)(2,1)S(1)}, u32[]{:S(2)}, u32[]{:S(2)}) collective-permute-start(bf16[128,512]{1,0:T(8,128)(2,1)} %get-tuple-element.5), channel_id=1, source_target_pairs={{0,24},{4,28},{8,16},{12,20},{16,8},{20,12},{24,0},{28,4},{1,25},{... | collective-permute-start | bytes 393224 | tf_op jit(solution)/shard_map/ppermute | solution.py:26
  184.2 7.0 %collective-permute-start.27 = (bf16[512,512]{1,0:T(8,128)(2,1)S(1)}, bf16[512,512]{1,0:T(8,128)(2,1)S(1)}, u32[]{:S(2)}, u32[]{:S(2)}) collective-permute-start(bf16[512,512]{1,0:T(8,128)(2,1)S(1)} %pad_maximum_fusion.5), channel_id=1, source_target_pairs={{0,4},{4,0},{8,12},{12,8},{16,20},{20,16},{24,28},{28,24},{1,5},{5... | collective-permute-start | bytes 1572872 | tf_op jit(solution)/shard_map/ppermute | solution.py:26
  187.3 3.8 %copy-start.11 = (bf16[128,512]{1,0:T(8,128)(2,1)S(1)}, bf16[128,512]{1,0:T(8,128)(2,1)}, u32[]{:S(2)}) copy-start(bf16[128,512]{1,0:T(8,128)(2,1)} %get-tuple-element.5) | copy-start | bytes 393220
  187.5 26.6 %copy-start.2 = (f32[128,128]{1,0:T(8,128)S(1)}, f32[128,128]{1,0:T(8,128)}, u32[]{:S(2)}) copy-start(f32[128,128]{1,0:T(8,128)} %pad_maximum_fusion.7.refs_5_.refs_6_) | copy-start | bytes 196612
  187.5 26.6 %copy-start.3 = (f32[128,128]{1,0:T(8,128)S(1)}, f32[128,128]{1,0:T(8,128)}, u32[]{:S(2)}) copy-start(f32[128,128]{1,0:T(8,128)} %pad_maximum_fusion.6.refs_4_.refs_5_) | copy-start | bytes 196612
  187.5 26.6 %copy-start.4 = (f32[128,128]{1,0:T(8,128)S(1)}, f32[128,128]{1,0:T(8,128)}, u32[]{:S(2)}) copy-start(f32[128,128]{1,0:T(8,128)} %get-tuple-element.4.refs_4_) | copy-start | bytes 196612
  187.5 14.8 %collective-permute-start.17 = (bf16[128,2048]{1,0:T(8,128)(2,1)S(1)}, bf16[128,2048]{1,0:T(8,128)(2,1)S(1)}, u32[]{:S(2)}, u32[]{:S(2)}) collective-permute-start(bf16[128,2048]{1,0:T(8,128)(2,1)S(1)} %get-tuple-element.14), channel_id=1, source_target_pairs={{0,8},{4,12},{8,0},{12,4},{16,24},{20,28},{24,16},{28,20},{1,9},{5... | collective-permute-start | bytes 1572872 | tf_op jit(solution)/shard_map/ppermute | solution.py:26
  188.8 25.3 %collective-permute-start.18 = (bf16[128,2048]{1,0:T(8,128)(2,1)S(1)}, bf16[128,2048]{1,0:T(8,128)(2,1)S(1)}, u32[]{:S(2)}, u32[]{:S(2)}) collective-permute-start(bf16[128,2048]{1,0:T(8,128)(2,1)S(1)} %get-tuple-element.13), channel_id=1, source_target_pairs={{0,16},{4,20},{8,24},{12,28},{16,0},{20,4},{24,8},{28,12},{1,17},{... | collective-permute-start | bytes 1572872 | tf_op jit(solution)/shard_map/ppermute | solution.py:26
  189.9 24.2 %collective-permute-start.19 = (bf16[128,2048]{1,0:T(8,128)(2,1)S(1)}, bf16[128,2048]{1,0:T(8,128)(2,1)S(1)}, u32[]{:S(2)}, u32[]{:S(2)}) collective-permute-start(bf16[128,2048]{1,0:T(8,128)(2,1)S(1)} %get-tuple-element.12), channel_id=1, source_target_pairs={{0,24},{4,28},{8,16},{12,20},{16,8},{20,12},{24,0},{28,4},{1,25},{... | collective-permute-start | bytes 1572872 | tf_op jit(solution)/shard_map/ppermute | solution.py:26
  214.1 5.6 %copy-start.1 = (bf16[1024,1024]{1,0:T(8,128)(2,1)S(1)}, bf16[1024,1024]{1,0:T(8,128)(2,1)}, u32[]{:S(2)}) copy-start(bf16[1024,1024]{1,0:T(8,128)(2,1)} %param.20) | copy-start | bytes 6291460
  (24 other events, 30.9 us)

commit v2 on v1

v2 whole, which is shorter than its diff:
```python
import jax
import jax.numpy as jnp
from jax import lax
from jax.experimental import pallas as pl
from jax.experimental.pallas import tpu as pltpu
from jax.sharding import PartitionSpec as P

CH = 16
HDIM = 128
SPAN = 40


eps_conf = 1e-05
eps_llm = 1e-06
rope_base = 1000000.0
masked_score = -1e30


def shifted(value, axis, by):
    length = lax.axis_size(axis)
    return lax.ppermute(value, axis, [(i, i + by) for i in range(length - by)])


def swapped(value, bits):
    length = lax.axis_size("tm")
    return lax.ppermute(value, "tm", [(i, i ^ bits) for i in range(length)])


def rotated(value, by):
    length = lax.axis_size("mp")
    return lax.ppermute(value, "mp", [(i, (i + by) % length) for i in range(length)])


def shard_count(index, valid_counts, shard_len):
    shard = index // shard_len
    table = jnp.arange(valid_counts.shape[0], dtype=jnp.int32)
    hit = shard[:, None] == table[None, :]
    count = jnp.sum(jnp.where(hit, valid_counts[None, :], 0), axis=1)
    return (index - shard * shard_len, count)


def layer_norm(field, gain):
    center = field - jnp.mean(field, axis=-1, keepdims=True)
    spread = jnp.mean(center * center, axis=-1, keepdims=True)
    return center * lax.rsqrt(spread + eps_conf) * gain


def rotary_tables(positions, size):
    half = size // 2
    freq = rope_base ** (-(jnp.arange(half, dtype=jnp.float32) * 2.0) / size)
    angle = positions.astype(jnp.float32)[:, None] * freq[None, :]
    cosine = jnp.concatenate([jnp.cos(angle), jnp.cos(angle)], axis=-1)
    sine = jnp.concatenate([-jnp.sin(angle), jnp.sin(angle)], axis=-1)
    return cosine, sine


def turn(field, cosine, sine):
    return field * cosine + pltpu.roll(field, HDIM // 2, 1) * sine


def total_of(refs, columns):
    parts = [ref[:, columns].astype(jnp.float32) for ref in refs]
    while len(parts) > 1:
        parts = [sum(parts[i : i + 2]) for i in range(0, len(parts), 2)]
    return parts[0]


def finish_keys(parts, cosine, sine, key_cols, width):
    rows = cosine.shape[0]

    def kernel(*refs):
        part_refs, (cos_ref, sin_ref, kv_ref, scale_ref) = refs[: len(parts)], refs[len(parts) :]
        squares = total_of(part_refs, pl.ds(2 * key_cols, HDIM))
        power = (
            squares[:, 0:1] + squares[:, 32:33] + squares[:, 64:65] + squares[:, 96:97]
        ) * (1.0 / width)
        scale = lax.rsqrt(power + eps_llm)
        scale_ref[...] = jnp.broadcast_to(scale, scale_ref.shape)
        for head in range(key_cols // HDIM):
            columns = pl.ds(head * HDIM, HDIM)
            raw = total_of(part_refs, columns) * scale
            kv_ref[:, columns] = turn(raw, cos_ref[...], sin_ref[...]).astype(jnp.bfloat16)
        columns = pl.ds(key_cols, key_cols)
        kv_ref[:, columns] = (total_of(part_refs, columns) * scale).astype(jnp.bfloat16)

    return pl.pallas_call(
        kernel,
        out_shape=(
            jax.ShapeDtypeStruct((rows, 2 * key_cols), jnp.bfloat16),
            jax.ShapeDtypeStruct((rows, HDIM), jnp.float32),
        ),
        name="finish_keys",
    )(*parts, cosine, sine)


def attend(chunks, kv, scale, cosine, sine, query_place, key_place, key_real, kv_heads):
    count, each = len(chunks), len(chunks[0])
    rows, chunk_cols = chunks[0][0].shape
    tokens = kv.shape[0]
    chunk_heads = chunk_cols // HDIM
    group = count * chunk_heads // kv_heads
    step = 2 if chunk_heads % 2 == 0 and tokens <= 2048 else 1
    factor = HDIM**-0.5

    def kernel(*refs):
        part_refs = refs[: count * each]
        scale_ref, cos_ref, sin_ref, at_ref, place_ref, real_ref, kv_ref, out_ref = refs[count * each :]
        at, place = at_ref[...], place_ref[...]
        seen = (place <= at) & ((real_ref[...] > 0) | (place == at))
        bias = jnp.where(seen, 0.0, masked_score)
        bias = jnp.concatenate([bias] * step, axis=0)
        for first in range(0, count * chunk_heads, step):
            refs_here = part_refs[first // chunk_heads * each : (first // chunk_heads + 1) * each]
            kv_head = first // group
            queries = []
            for head in range(first % chunk_heads, first % chunk_heads + step):
                raw = total_of(refs_here, pl.ds(head * HDIM, HDIM)) * scale_ref[...]
                queries.append(turn(raw, cos_ref[...], sin_ref[...]).astype(jnp.bfloat16))
            scores = lax.dot_general(
                jnp.concatenate(queries, axis=0),
                kv_ref[:, pl.ds(kv_head * HDIM, HDIM)],
                (((1,), (1,)), ((), ())),
                preferred_element_type=jnp.float32,
            )
            scores = scores * factor + bias
            top = jnp.max(scores, axis=-1, keepdims=True)
            weights = jnp.exp(scores - top)
            total = jnp.sum(weights, axis=-1, keepdims=True)
            summed = jnp.dot(
                weights.astype(jnp.bfloat16),
                kv_ref[:, pl.ds((kv_heads + kv_head) * HDIM, HDIM)],
                preferred_element_type=jnp.float32,
            )
            result = (summed / total).astype(jnp.bfloat16)
            for i in range(step):
                out_ref[:, pl.ds((first + i) * HDIM, HDIM)] = result[i * rows : (i + 1) * rows]

    flat = [part for chunk in chunks for part in chunk]
    return pl.pallas_call(
        kernel,
        out_shape=jax.ShapeDtypeStruct((rows, count * chunk_cols), jnp.bfloat16),
        compiler_params=pltpu.CompilerParams(vmem_limit_bytes=40 << 20),
        name="attend",
    )(*flat, scale, cosine, sine, query_place, key_place, key_real, kv)


def project(held, gain, w_qkv):
    rows, width = held.shape
    wide = w_qkv.shape[1]
    step = width

    def kernel(held_ref, gain_ref, weight_ref, out_ref, normed_ref):
        @pl.when(pl.program_id(0) == 0)
        def _():
            normed_ref[...] = layer_norm(held_ref[...].astype(jnp.float32), gain_ref[...]).astype(
                jnp.bfloat16
            )

        out_ref[...] = jnp.dot(
            normed_ref[...], weight_ref[...], preferred_element_type=jnp.float32
        ).astype(jnp.bfloat16)

    return pl.pallas_call(
        kernel,
        grid=(wide // step,),
        in_specs=[
            pl.BlockSpec((rows, width), lambda i: (0, 0)),
            pl.BlockSpec((1, width), lambda i: (0, 0)),
            pl.BlockSpec((width, step), lambda i: (0, i)),
        ],
        out_specs=pl.BlockSpec((rows, step), lambda i: (0, i)),
        out_shape=jax.ShapeDtypeStruct((rows, wide), jnp.bfloat16),
        scratch_shapes=[pltpu.VMEM((rows, width), jnp.bfloat16)],
        compiler_params=pltpu.CompilerParams(vmem_limit_bytes=16 << 20),
        cost_estimate=pl.CostEstimate(
            flops=2 * rows * width * wide, bytes_accessed=2 * width * wide, transcendentals=0
        ),
        name="project",
    )(held, gain[None, :], w_qkv)


def convolve(
    frames, near, own_proj, before_proj, key_index, key_ids, key_real, w_attn_out, norm_conv,
    w_point_in, w_depth, w_point_out,
):
    frame_rows, width = frames.shape
    before = before_proj.shape[0]
    key_rows = before + frame_rows
    near_rows = near.shape[0]
    extra = before - near_rows
    query_rows = extra + frame_rows
    lead = key_rows - query_rows
    head_size = width // CH
    pooled_rows = frame_rows // 4
    taps = w_depth.shape[0]
    lanes = 2 * head_size

    def kernel(
        frames_ref, near_ref, own_ref, before_ref, key_row_ref, query_col_ref, gain_ref, depth_ref,
        attn_hbm, in_hbm, out_hbm, conf_ref, pooled_ref,
        attn_w, in_w, out_w, context_ref, glu_ref, active_ref, sems,
    ):
        copies = [
            pltpu.make_async_copy(source, target, sems.at[i])
            for i, (source, target) in enumerate(
                ((attn_hbm, attn_w), (in_hbm, in_w), (out_hbm, out_w))
            )
        ]
        for copy in copies:
            copy.start()
        key_at, key_id, key_live = key_row_ref[0:1], key_row_ref[1:2], key_row_ref[2:3]
        at, ids, live = query_col_ref[:, 0:1], query_col_ref[:, 1:2], query_col_ref[:, 2:3]
        seen = (key_at <= at) & (key_id >= ids - 2) & ((key_live > 0) | (key_at == at))
        bias = jnp.where(seen, 0.0, masked_score)
        bias = jnp.concatenate([bias, bias], axis=0)
        left = lax.broadcasted_iota(jnp.int32, (query_rows, lanes), 1) < head_size
        for pair in range(width // lanes):

            def both_rows(offset):
                columns = pl.ds(offset + pair * lanes, lanes)
                return jnp.concatenate([before_ref[:, columns], own_ref[:, columns]], axis=0)

            query = both_rows(0)[lead:]
            none = jnp.zeros_like(query)
            query = jnp.concatenate(
                [jnp.where(left, query, none), jnp.where(left, none, query)], axis=0
            )
            scores = lax.dot_general(
                query, both_rows(width), (((1,), (1,)), ((), ())), preferred_element_type=jnp.float32
            )
            scores = scores * head_size**-0.5 + bias
            top = jnp.max(scores, axis=-1, keepdims=True)
            weights = jnp.exp(scores - top)
            total = jnp.sum(weights, axis=-1, keepdims=True)
            summed = jnp.dot(
                weights.astype(jnp.bfloat16), both_rows(2 * width), preferred_element_type=jnp.float32
            )
            context = summed / total
            context_ref[:, pl.ds(pair * lanes, lanes)] = jnp.where(
                left, context[:query_rows], context[query_rows:]
            ).astype(jnp.bfloat16)
        inputs = jnp.concatenate([near_ref[near_rows - extra :], frames_ref[...]], axis=0)
        copies[0].wait()
        mid = inputs.astype(jnp.float32) + jnp.dot(
            context_ref[...], attn_w[...], preferred_element_type=jnp.float32
        )
        conv_in = layer_norm(mid, gain_ref[...]).astype(jnp.bfloat16)
        copies[1].wait()
        part = 256
        for start in range(0, width, part):
            value = jnp.dot(
                conv_in, in_w[:, pl.ds(start, part)], preferred_element_type=jnp.float32
            )
            gate = jnp.dot(
                conv_in, in_w[:, pl.ds(width + start, part)], preferred_element_type=jnp.float32
            )
            glu = jnp.where(live > 0, value * jax.nn.sigmoid(gate), 0.0)
            glu_ref[:, pl.ds(start, part)] = glu.astype(jnp.bfloat16).astype(jnp.float32)
        for start in range(0, width, 128):
            columns = pl.ds(start, 128)
            depth = jnp.zeros((frame_rows, 128), jnp.float32)
            for tap in range(taps):
                depth = depth + depth_ref[tap : tap + 1, columns] * glu_ref[
                    pl.ds(extra - tap, frame_rows), columns
                ]
            active_ref[:, columns] = jax.nn.silu(depth).astype(jnp.bfloat16)
        copies[2].wait()
        final = mid[extra:] + jnp.dot(
            active_ref[...], out_w[...], preferred_element_type=jnp.float32
        )
        conf = jnp.where(live[extra:] > 0, final, 0.0).astype(jnp.bfloat16)
        conf_ref[...] = conf
        row = lax.broadcasted_iota(jnp.int32, (pooled_rows, frame_rows), 0)
        column = lax.broadcasted_iota(jnp.int32, (pooled_rows, frame_rows), 1)
        mean = jnp.where(column // 4 == row, 0.25, 0.0).astype(jnp.bfloat16)
        pooled_ref[...] = jnp.dot(mean, conf, preferred_element_type=jnp.float32).astype(
            jnp.bfloat16
        )

    key_row = jnp.stack([key_index, key_ids, key_real.astype(jnp.int32)])
    query_col = jnp.transpose(key_row[:, lead:])
    plain = pl.BlockSpec(memory_space=pltpu.VMEM)
    apart = pl.BlockSpec(memory_space=pl.ANY)
    flops = 2 * query_rows * width * 4 * width
    return pl.pallas_call(
        kernel,
        in_specs=[plain] * 8 + [apart] * 3,
        out_specs=(plain, plain),
        out_shape=(
            jax.ShapeDtypeStruct((frame_rows, width), jnp.bfloat16),
            jax.ShapeDtypeStruct((pooled_rows, width), jnp.bfloat16),
        ),
        scratch_shapes=[
            pltpu.VMEM(w_attn_out.shape, jnp.bfloat16),
            pltpu.VMEM(w_point_in.shape, jnp.bfloat16),
            pltpu.VMEM(w_point_out.shape, jnp.bfloat16),
            pltpu.VMEM((query_rows, width), jnp.bfloat16),
            pltpu.VMEM((query_rows, width), jnp.float32),
            pltpu.VMEM((frame_rows, width), jnp.bfloat16),
            pltpu.SemaphoreType.DMA((3,)),
        ],
        compiler_params=pltpu.CompilerParams(vmem_limit_bytes=32 << 20),
        cost_estimate=pl.CostEstimate(
            flops=flops, bytes_accessed=8 * width * width, transcendentals=CH * query_rows * key_rows
        ),
        name="convolve",
    )(
        frames, near, own_proj, before_proj, key_row, query_col, norm_conv[None, :],
        w_depth.astype(jnp.float32), w_attn_out, w_point_in, w_point_out,
    )


def conformer(
    frames, own_proj, near, far, first, block_ids, valid_counts, shard_frames, norm_attn, w_qkv,
    w_attn_out, norm_conv, w_point_in, w_depth, w_point_out,
):
    frame_rows = frames.shape[0]
    before = near.shape[0] + far.shape[0]
    key_rows = before + frame_rows
    before_proj = project(jnp.concatenate([far, near], axis=0), norm_attn, w_qkv)
    key_index = first - before + jnp.arange(key_rows, dtype=jnp.int32)
    key_place, key_count = shard_count(key_index, valid_counts, shard_frames)
    key_real = (key_place < key_count) & (key_index >= 0)
    padded_ids = jnp.concatenate([jnp.full((before,), -100, jnp.int32), block_ids])
    key_ids = lax.dynamic_slice_in_dim(padded_ids, first, key_rows, 0)
    return convolve(
        frames, near, own_proj, before_proj, key_index, key_ids, key_real, w_attn_out, norm_conv,
        w_point_in, w_depth, w_point_out,
    )


def line_pieces(value, beside):
    mp_count, place = lax.axis_size("mp"), lax.axis_index("mp")
    if mp_count != 4:
        pieces = [value] + [rotated(value, by) for by in range(1, mp_count)]
        return [jnp.stack(pieces)], lambda source: (place - source) % mp_count, beside
    below = lax.ppermute(value, "mp", [(0, 1), (1, 2), (2, 3)])
    above = lax.ppermute(value, "mp", [(1, 0), (2, 1), (3, 2)])
    value, below, above, beside = lax.optimization_barrier((value, below, above, beside))
    half = value.shape[0] // 2
    chunks, waiting = [], (value, below, above)
    for start in (0, half):
        mine, lower, upper = [array[start : start + half] for array in waiting]
        far = lax.ppermute(mine, "mp", [(0, 3), (3, 0)])
        lower_2 = lax.ppermute(lower, "mp", [(1, 2), (2, 3)])
        upper_2 = lax.ppermute(upper, "mp", [(2, 1), (1, 0)])
        if start == 0:
            far, lower_2, upper_2, waiting = lax.optimization_barrier(
                (far, lower_2, upper_2, waiting)
            )
        chunks.append(jnp.stack([far, lower_2, lower, mine, upper, upper_2]))
    return chunks, lambda source: (source - place + 3) % 6, beside


def chip_adapter_columns(stacked, row_of):
    tm_count = lax.axis_size("tm")
    time_place = lax.axis_index("tm")
    kept = []
    for other in range(0, tm_count, 2):
        wanted = (time_place ^ other) // 2
        piece = lax.dynamic_index_in_dim(stacked, row_of(wanted), 0, keepdims=False)
        kept.append(swapped(piece, other) if other else piece)
    return kept


def adapt(pooled, near, gain):
    tm_count, time_place = lax.axis_size("tm"), lax.axis_index("tm")
    part, cols = near[0][0].shape
    half = cols // 2
    tokens, depth = pooled.shape
    flat = [array for chunk in near for array in chunk]
    place_word = time_place.reshape(1).astype(jnp.int32)
    plain = pl.BlockSpec(memory_space=pltpu.VMEM)
    scalar = pl.BlockSpec(memory_space=pltpu.SMEM)

    def other_half(place_ref, *refs):
        columns = pl.ds(pl.multiple_of((1 - place_ref[0] % 2) * half, 128), half)
        for i, ref in enumerate(refs[:-1]):
            refs[-1][i * part : (i + 1) * part, :] = ref[:, columns]

    given = pl.pallas_call(
        other_half,
        in_specs=[scalar] + [plain] * len(flat),
        out_specs=plain,
        out_shape=jax.ShapeDtypeStruct((len(flat) * part, half), jnp.bfloat16),
        compiler_params=pltpu.CompilerParams(vmem_limit_bytes=16 << 20),
        name="other_half",
    )(place_word, *flat)
    taken = swapped(given, 1)
    step = min(256, tokens)

    def kernel(place_ref, *refs):
        near_refs = refs[: len(flat)]
        taken_ref, pooled_ref, gain_ref, out_ref, word_ref, weight_ref = refs[len(flat) :]
        place = place_ref[0]
        columns = pl.ds(pl.multiple_of((place % 2) * half, 128), half)
        for i, ref in enumerate(near_refs):
            chunk, other = i // (tm_count // 2), 2 * (i % (tm_count // 2))
            for shift in (0, 1):
                source = place ^ (other + shift)
                row = pl.multiple_of(source * (part * len(near)) + chunk * part, part)
                if shift:
                    weight_ref[pl.ds(row, part), :] = taken_ref[i * part : (i + 1) * part]
                else:
                    weight_ref[pl.ds(row, part), :] = ref[:, columns]
        lane = lax.broadcasted_iota(jnp.int32, (step, HDIM), 1) // 32 - 2 * (place % 2)
        for start in range(0, tokens, step):
            rows = pl.ds(start, step)
            adapted = jnp.dot(
                pooled_ref[rows, :], weight_ref[...], preferred_element_type=jnp.float32
            )
            out_ref[rows, :] = (adapted * gain_ref[...]).astype(jnp.bfloat16)
            squares = jnp.sum(adapted * adapted, axis=-1, keepdims=True)
            high = squares.astype(jnp.bfloat16).astype(jnp.float32)
            words = jnp.where(lane == 0, high, jnp.where(lane == 1, squares - high, 0.0))
            word_ref[rows, :] = words.astype(jnp.bfloat16)

    return pl.pallas_call(
        kernel,
        in_specs=[scalar] + [plain] * (len(flat) + 3),
        out_specs=(plain, plain),
        out_shape=(
            jax.ShapeDtypeStruct((tokens, half), jnp.bfloat16),
            jax.ShapeDtypeStruct((tokens, HDIM), jnp.bfloat16),
        ),
        scratch_shapes=[pltpu.VMEM((depth, half), jnp.bfloat16)],
        compiler_params=pltpu.CompilerParams(vmem_limit_bytes=48 << 20),
        name="adapt",
    )(place_word, *flat, taken, pooled, gain[None, :])


def spread_even(value):
    tm_count = lax.axis_size("tm")
    blocks = [value] + [swapped(value, other) for other in range(2, tm_count, 2)]
    return jnp.concatenate(blocks, axis=0)


def spread(even):
    return jnp.concatenate([even, swapped(even, 1)], axis=0)


def both_sum(one, other):
    return (one.astype(jnp.float32) + other.astype(jnp.float32)).astype(jnp.bfloat16)


def direct_parts(value):
    tm_count = lax.axis_size("tm")
    half = value.shape[0] // 2
    rows = value.shape[0] // tm_count
    chip = both_sum(value[:half], swapped(value[half:], 1))
    return [chip[:rows]] + [
        swapped(chip[i * rows : (i + 1) * rows], 2 * i) for i in range(1, tm_count // 2)
    ]


def chip_sum(left, right, weight):
    def product(rows):
        return jnp.dot(rows, weight, preferred_element_type=jnp.float32)

    other = swapped(product(right).astype(jnp.bfloat16), 1)
    return (product(left) + other.astype(jnp.float32)).astype(jnp.bfloat16)


def halved(held, bit, axes):
    axis = axes.index(bit)
    keep = lax.index_in_dim(held, 0, axis, keepdims=False)
    given = lax.index_in_dim(held, 1, axis, keepdims=False)
    return keep, swapped(given, 2 << bit), axes[:axis] + axes[axis + 1 :]


def on_device(
    frames,
    block_ids,
    valid_counts,
    norm_attn,
    w_qkv,
    w_attn_out,
    norm_conv,
    w_point_in,
    w_depth,
    w_point_out,
    w_adapter,
    llm_gain,
    w_query,
    w_key,
    w_value,
):
    tm_count, mp_count = lax.axis_size("tm"), lax.axis_size("mp")
    time_place, model_place = lax.axis_index("tm"), lax.axis_index("mp")
    frame_rows, width = frames.shape
    shard_frames = frame_rows * mp_count
    first = (time_place * mp_count + model_place) * frame_rows
    near = shifted(frames, ("tm", "mp"), 1)
    far = shifted(frames[frame_rows - 32 :], ("tm", "mp"), 2)
    own_proj = project(frames, norm_attn, w_qkv)
    stacked, row_of, (near, far, own_proj) = line_pieces(w_adapter, (near, far, own_proj))
    conf_out, pooled = conformer(
        frames, own_proj, near, far, first, block_ids, valid_counts, shard_frames, norm_attn, w_qkv,
        w_attn_out, norm_conv, w_point_in, w_depth, w_point_out,
    )
    pooled, stacked[0] = lax.optimization_barrier((pooled, stacked[0]))
    piece = pooled.shape[0]
    shard_tokens = piece * mp_count
    cycle = [rotated(pooled, by) for by in range(mp_count - 1, 0, -1)] + [pooled]
    shard_pooled = lax.dynamic_slice_in_dim(
        jnp.concatenate(cycle + cycle, axis=0), (mp_count - 1 - model_place) * piece, shard_tokens, 0
    )
    all_pooled, near_columns = lax.optimization_barrier(
        (
            spread(spread_even(shard_pooled)),
            [chip_adapter_columns(chunk, row_of) for chunk in stacked],
        )
    )
    tokens = all_pooled.shape[0]
    block = w_adapter.shape[1] * mp_count // tm_count
    gain = lax.dynamic_slice_in_dim(llm_gain, time_place * block, block, 0)
    scaled, words = adapt(all_pooled, near_columns, gain)
    raw_keys = jnp.dot(scaled, w_key, preferred_element_type=jnp.float32).astype(jnp.bfloat16)
    raw_values = jnp.dot(scaled, w_value, preferred_element_type=jnp.float32).astype(jnp.bfloat16)
    key_cols, half_cols = w_key.shape[1], w_query.shape[1] // 2
    kv_raw, scaled = lax.optimization_barrier(
        (jnp.concatenate([raw_keys, raw_values, words], axis=1), scaled)
    )
    kv_parts = direct_parts(kv_raw)
    bits = list(range(tm_count.bit_length() - 2))
    left, right = scaled[: tokens // 2], scaled[tokens // 2 :]
    sums = [
        chip_sum(left, right, w_query[:, :half_cols]),
        chip_sum(left, right, w_query[:, half_cols:]),
    ]
    kv_parts, _ = lax.optimization_barrier((kv_parts, sums))
    query_chunks, rest = [], [bits, bits[::-1]]
    for held, turns in zip(sums, rest):
        held = held.reshape((2,) * len(bits) + (shard_tokens, half_cols))
        keep, taken, left_axes = halved(held, turns[0], bits[::-1])
        for turn_bit in turns[1:]:
            keep, taken, left_axes = halved(both_sum(keep, taken), turn_bit, left_axes)
        query_chunks.append((keep, taken))
    order = list(range(0, tm_count, 2)) + list(range(1, tm_count, 2))
    within = jnp.arange(shard_tokens, dtype=jnp.int32)
    own_place = time_place * shard_tokens + within
    cosine, sine = rotary_tables(own_place, HDIM)
    kv, scale = finish_keys(kv_parts, cosine, sine, key_cols, block * tm_count)
    all_kv = spread(spread_even(kv))
    key_place = jnp.concatenate([(time_place ^ other) * shard_tokens + within for other in order])
    place_in, counts = shard_count(key_place, valid_counts, shard_tokens)
    key_real = (place_in * 4 < counts).astype(jnp.int32)
    attended = attend(
        query_chunks, all_kv, scale, cosine, sine, own_place[:, None], key_place[None, :],
        key_real[None, :], key_cols // HDIM,
    )
    return (conf_out, attended)


def solution(mesh):
    placed = (
        P(("tm", "mp"), None),
        P(),
        P(),
        P(),
        P(),
        P(),
        P(),
        P(),
        P(),
        P(),
        P("tm", "mp"),
        P(),
        P("tm", "mp"),
        P("tm", "mp"),
        P("tm", "mp"),
    )
    return jax.shard_map(
        on_device,
        mesh=mesh,
        in_specs=placed,
        out_specs=(P(("tm", "mp"), None), P("tm", "mp")),
        check_vma=False,
    )
```

time: 220 us -> 171 us (0.78)
  waiting for transfers between devices: 96 us -> 52.3 us
  matrix products: 25.1 us -> 6.47 us
  Pallas kernels: 7.72 us -> 24.6 us
  other arithmetic: 15.7 us -> 4.46 us
  starting transfers between devices: 50.7 us -> 61.6 us
  local copies, waits for them, and re-layouts: 22.7 us -> 18.9 us
    ppermute x2, waiting for transfers between devices: 23.3 us -> 0.01 us  [shifted(): return lax.ppermute(value, axis, [(i, i + by) for i in range(length - by)])]
    ppermute x0 -> x8, starting transfers between devices: none -> 21.2 us  [the longest x2 10.8 us: line_pieces(): far = lax.ppermute(mine, 'mp', [(0, 3), (3, 0)])]
    ppermute x6 -> x3, starting transfers between devices: 24.2 us -> 4.73 us  [rotated(): lax.ppermute(value, 'mp', [(i, (i + by) % length) for i in range(length)])]
    pallas_call x1 -> x6, Pallas kernels: 5.6 us -> 22.5 us  [the longest x1 8.42 us: convolve(): pl.pallas_call(kernel, in_specs=[plain] * 8 + [apart] * 3, out_specs=(pla...]
    ppermute x20 -> x25, waiting for transfers between devices: 64.3 us -> 47.5 us  [swapped(): return lax.ppermute(value, 'tm', [(i, i ^ bits) for i in range(length)])]
    dot_general x7 -> x4, matrix products: 19 us -> 5.05 us  [product(): return jnp.dot(rows, weight, preferred_element_type=jnp.float32)]
    slice x13 -> x11, local copies, waits for them, and re-layouts: 10.3 us -> 1.08 us  [the longest x1 0.73 us: direct_parts(): chip[i * rows:(i + 1) * rows]]
    unnamed x132 -> x89, local copies, waits for them, and re-layouts: 6.97 us -> 15 us
  transfers between devices with their start and end apart: 28 -> 38, of which waited for: 13 -> 19; matrix products, arithmetic and copies ran while one was open for 21% -> 8% of each run, Pallas kernels for 1% -> 8%
where the time goes in v2:
time: 171 us; the launch traced here: 170 us
  starting transfers between devices  61.6 us (36%)
  waiting for transfers between devices  52.3 us (31%)
  Pallas kernels  24.6 us (14%)
  local copies, waits for them, and re-layouts  18.9 us (11%)
  matrix products  6.47 us (4%)
  other arithmetic  4.46 us (3%)
  between operations  1.83 us (1%)
    ppermute x25, waiting for transfers between devices, swapped(): return lax.ppermute(value, 'tm', [(i, i ^ bits) for i in range(length)])  47.5 us
    ppermute x25, starting transfers between devices, swapped(): return lax.ppermute(value, 'tm', [(i, i ^ bits) for i in range(length)])  26.6 us
    unnamed x89, local copies, waits for them, and re-layouts  15 us
    ppermute x2, starting transfers between devices, line_pieces(): far = lax.ppermute(mine, 'mp', [(0, 3), (3, 0)])  10.8 us
    ppermute x2, starting transfers between devices, shifted(): return lax.ppermute(value, axis, [(i, i + by) for i in range(length - by)])  9.01 us
    pallas_call x1, Pallas kernels, convolve(): pl.pallas_call(kernel, in_specs=[plain] * 8 + [apart] * 3, out_specs=(pla...  8.42 us
    pallas_call x1, Pallas kernels, attend(): pl.pallas_call(kernel, out_shape=jax.ShapeDtypeStruct((rows, count * chun...  5.31 us
    ppermute x1, starting transfers between devices, line_pieces(): below = lax.ppermute(value, 'mp', [(0, 1), (1, 2), (2, 3)])  5.09 us
  transfers between devices with their start and end apart: 38, of which 19 were waited for; matrix products, arithmetic and copies ran while one was open for 8% of the time, Pallas kernels for 8%

profile of v2, /device:TPU:0, one launch (start us, length us, event | category | flops | bytes accessed | tf_op | source)
XLA Modules:
  0.0 170.1 jit_solution(2518188734157187997)
XLA Ops:
  0.6 5.1 %collective-permute-start = (bf16[128,2048]{1,0:T(8,128)(2,1)}, bf16[128,2048]{1,0:T(8,128)(2,1)S(1)}, u32[]{:S(2)}, u32[]{:S(2)}) collective-permute-start(bf16[128,2048]{1,0:T(8,128)(2,1)} %param.25), channel_id=1, source_target_pairs={{0,1},{1,2},{2,3},{4,5},{5,6},{6,7},{8,9},{9,10},{10,11},{12,13},{... | collective-permute-start | bytes 1572872 | tf_op jit(solution)/shard_map/ppermute | solution.py:337
  5.7 1.3 collective-permute-start.1
  7.0 4.6 %collective-permute-start.2 = (bf16[128,1024]{1,0:T(8,128)(2,1)}, bf16[128,1024]{1,0:T(8,128)(2,1)S(1)}, u32[]{:S(2)}, u32[]{:S(2)}) collective-permute-start(bf16[128,1024]{1,0:T(8,128)(2,1)} %frames_ref.1), channel_id=1, source_target_pairs={{0,1},{1,2},{2,3},{3,4},{4,5},{5,6},{6,7},{7,8},{8,9},{9,10},{10,1... | collective-permute-start | bytes 786440 | tf_op jit(solution)/shard_map/ppermute | solution.py:21
  11.6 0.9 slice.80
  12.5 4.4 %collective-permute-start.3 = (bf16[32,1024]{1,0:T(8,128)(2,1)S(1)}, bf16[32,1024]{1,0:T(8,128)(2,1)S(1)}, u32[]{:S(2)}, u32[]{:S(2)}) collective-permute-start(bf16[32,1024]{1,0:T(8,128)(2,1)S(1)} %slice.80), channel_id=1, source_target_pairs={{0,2},{1,3},{2,4},{3,5},{4,6},{5,7},{6,8},{7,9},{8,10},{9,11},{10,... | collective-permute-start | bytes 196616 | tf_op jit(solution)/shard_map/ppermute | solution.py:21
  17.2 0.8 pad_dynamic-slice_fusion
  18.0 0.7 select_reduce_fusion.1
  19.1 0.9 convert_element_type.88.depth_ref
  20.0 2.8 %copy-done.1 = bf16[1024,3072]{1,0:T(8,128)(2,1)S(1)} copy-done((bf16[1024,3072]{1,0:T(8,128)(2,1)S(1)}, bf16[1024,3072]{1,0:T(8,128)(2,1)}, u32[]{:S(2)}) %copy-start.1) | copy-done | bytes 6291480
  22.8 0.9 copy-done.6
  24.4 2.1 %project.2.own_ref = bf16[128,3072]{1,0:T(8,128)(2,1)S(1)} custom-call(bf16[128,1024]{1,0:T(8,128)(2,1)S(1)} %copy-done.6, f32[1,1024]{1,0:T(1,128)S(1)} %bitcast.91, bf16[1024,3072]{1,0:T(8,128)(2,1)S(1)} %copy-done.1), custom_call_target="tpu_custom_call" | custom-call | flops 805306368 | bytes 6291456 | tf_op jit(solution)/shard_map/project/pallas_call | solution.py:163
  26.7 1.4 collective-permute-start.6
  28.8 5.2 %collective-permute-start.4 = (bf16[64,2048]{1,0:T(8,128)(2,1)S(1)}, bf16[64,2048]{1,0:T(8,128)(2,1)S(1)}, u32[]{:S(2)}, u32[]{:S(2)}) collective-permute-start(bf16[64,2048]{1,0:T(8,128)(2,1)S(1)} %slice.82), channel_id=1, source_target_pairs={{0,3},{3,0},{4,7},{7,4},{8,11},{11,8},{12,15},{15,12},{16,19},{19,... | collective-permute-start | bytes 786440 | tf_op jit(solution)/shard_map/ppermute | solution.py:344
  34.1 2.3 %project.3.before_ref = bf16[160,3072]{1,0:T(8,128)(2,1)S(1)} custom-call(bf16[160,1024]{1,0:T(8,128)(2,1)S(1)} %pad_maximum_fusion.3.held_ref, f32[1,1024]{1,0:T(1,128)S(1)} %bitcast.92, bf16[1024,3072]{1,0:T(8,128)(2,1)S(1)} %copy-done.2), custom_call_target="tpu_custom_call" | custom-call | flops 1006632960 | bytes 6291456 | tf_op jit(solution)/shard_map/project/pallas_call | solution.py:163
  37.0 8.4 %convolve.1 = (bf16[128,1024]{1,0:T(8,128)(2,1)}, bf16[32,1024]{1,0:T(8,128)(2,1)S(1)}) custom-call(bf16[128,1024]{1,0:T(8,128)(2,1)S(1)} %copy-done.7, bf16[128,1024]{1,0:T(8,128)(2,1)S(1)} %collective-permute-done.2.near_ref, bf16[128,3072]{1,0:T(8,128)(2,1)S(1)} %project.2.own_ref, bf16[160,3072]{1,0:T(8,128)(2,1)S(1)} %project.3.before_ref, ...), custom_call_target="tpu_custom_call" | custom-call | flops 1342177280 | bytes 8388608 | tf_op jit(solution)/shard_map/convolve/pallas_call | solution.py:285
  45.6 1.0 collective-permute-start.9
  46.6 0.9 collective-permute-start.8
  47.5 2.8 %collective-permute-start.7 = (bf16[32,1024]{1,0:T(8,128)(2,1)S(1)}, bf16[32,1024]{1,0:T(8,128)(2,1)S(1)}, u32[]{:S(2)}, u32[]{:S(2)}) collective-permute-start(bf16[32,1024]{1,0:T(8,128)(2,1)S(1)} %get-tuple-element.48), channel_id=1, source_target_pairs={{0,3},{1,0},{2,1},{3,2},{4,7},{5,4},{6,5},{7,6},{8,11},{9,8},{10,9... | collective-permute-start | bytes 196616 | tf_op jit(solution)/shard_map/ppermute | solution.py:31
  50.4 1.3 collective-permute-start.19
  52.5 0.7 collective-permute-done.7
  53.2 5.5 %collective-permute-start.17 = (bf16[64,2048]{1,0:T(8,128)(2,1)S(1)}, bf16[64,2048]{1,0:T(8,128)(2,1)S(1)}, u32[]{:S(2)}, u32[]{:S(2)}) collective-permute-start(bf16[64,2048]{1,0:T(8,128)(2,1)S(1)} %slice.85), channel_id=1, source_target_pairs={{0,3},{3,0},{4,7},{7,4},{8,11},{11,8},{12,15},{15,12},{16,19},{19,... | collective-permute-start | bytes 786440 | tf_op jit(solution)/shard_map/ppermute | solution.py:344
  58.8 2.2 %collective-permute-start.16 = (bf16[64,2048]{1,0:T(8,128)(2,1)S(1)}, bf16[64,2048]{1,0:T(8,128)(2,1)S(1)}, u32[]{:S(2)}, u32[]{:S(2)}) collective-permute-start(bf16[64,2048]{1,0:T(8,128)(2,1)S(1)} %get-tuple-element.78), channel_id=1, source_target_pairs={{0,24},{4,28},{8,16},{12,20},{16,8},{20,12},{24,0},{28,4},{1,25},{... | collective-permute-start | bytes 786440 | tf_op jit(solution)/shard_map/ppermute | solution.py:26
  61.2 0.8 collective-permute-start.12
  62.0 4.0 %collective-permute-done.17 = bf16[64,2048]{1,0:T(8,128)(2,1)S(1)} collective-permute-done((bf16[64,2048]{1,0:T(8,128)(2,1)S(1)}, bf16[64,2048]{1,0:T(8,128)(2,1)S(1)}, u32[]{:S(2)}, u32[]{:S(2)}) %collective-permute-start.17) | collective-permute-done | bytes 262176 | tf_op jit(solution)/shard_map/ppermute | solution.py:344
  66.0 1.7 %collective-permute-start.11 = (bf16[128,1024]{1,0:T(8,128)(2,1)S(1)}, bf16[128,1024]{1,0:T(8,128)(2,1)S(1)}, u32[]{:S(2)}, u32[]{:S(2)}) collective-permute-start(bf16[128,1024]{1,0:T(8,128)(2,1)S(1)} %get-tuple-element.73), channel_id=1, source_target_pairs={{0,16},{4,20},{8,24},{12,28},{16,0},{20,4},{24,8},{28,12},{1,17},{... | collective-permute-start | bytes 786440 | tf_op jit(solution)/shard_map/ppermute | solution.py:26
  68.4 6.3 %collective-permute-done.12 = bf16[128,1024]{1,0:T(8,128)(2,1)S(1)} collective-permute-done((bf16[128,1024]{1,0:T(8,128)(2,1)S(1)}, bf16[128,1024]{1,0:T(8,128)(2,1)S(1)}, u32[]{:S(2)}, u32[]{:S(2)}) %collective-permute-start.12) | collective-permute-done | bytes 262176 | tf_op jit(solution)/shard_map/ppermute | solution.py:26
  74.7 3.5 %collective-permute-start.15 = (bf16[64,2048]{1,0:T(8,128)(2,1)S(1)}, bf16[64,2048]{1,0:T(8,128)(2,1)S(1)}, u32[]{:S(2)}, u32[]{:S(2)}) collective-permute-start(bf16[64,2048]{1,0:T(8,128)(2,1)S(1)} %get-tuple-element.79), channel_id=1, source_target_pairs={{0,16},{4,20},{8,24},{12,28},{16,0},{20,4},{24,8},{28,12},{1,17},{... | collective-permute-start | bytes 786440 | tf_op jit(solution)/shard_map/ppermute | solution.py:26
  78.8 2.4 %collective-permute-start.14 = (bf16[64,2048]{1,0:T(8,128)(2,1)S(1)}, bf16[64,2048]{1,0:T(8,128)(2,1)S(1)}, u32[]{:S(2)}, u32[]{:S(2)}) collective-permute-start(bf16[64,2048]{1,0:T(8,128)(2,1)S(1)} %get-tuple-element.80), channel_id=1, source_target_pairs={{0,8},{4,12},{8,0},{12,4},{16,24},{20,28},{24,16},{28,20},{1,9},{5... | collective-permute-start | bytes 786440 | tf_op jit(solution)/shard_map/ppermute | solution.py:26
  81.5 1.4 collective-permute-start.22
  83.1 0.8 collective-permute-done.13
  84.0 1.2 collective-permute-start.20
  85.3 3.0 %collective-permute-done.14.refs_1_ = bf16[64,2048]{1,0:T(8,128)(2,1)S(1)} collective-permute-done((bf16[64,2048]{1,0:T(8,128)(2,1)S(1)}, bf16[64,2048]{1,0:T(8,128)(2,1)S(1)}, u32[]{:S(2)}, u32[]{:S(2)}) %collective-permute-start.14) | collective-permute-done | bytes 262176 | tf_op jit(solution)/shard_map/ppermute | solution.py:26
  88.3 7.0 %collective-permute-done.22.refs_7_ = bf16[64,2048]{1,0:T(8,128)(2,1)S(1)} collective-permute-done((bf16[64,2048]{1,0:T(8,128)(2,1)S(1)}, bf16[64,2048]{1,0:T(8,128)(2,1)S(1)}, u32[]{:S(2)}, u32[]{:S(2)}) %collective-permute-start.22) | collective-permute-done | bytes 262176 | tf_op jit(solution)/shard_map/ppermute | solution.py:26
  95.3 1.7 %collective-permute-done.21.refs_6_ = bf16[64,2048]{1,0:T(8,128)(2,1)S(1)} collective-permute-done((bf16[64,2048]{1,0:T(8,128)(2,1)S(1)}, bf16[64,2048]{1,0:T(8,128)(2,1)S(1)}, u32[]{:S(2)}, u32[]{:S(2)}) %collective-permute-start.21) | collective-permute-done | bytes 262176 | tf_op jit(solution)/shard_map/ppermute | solution.py:26
  97.0 1.8 %collective-permute-done.20.refs_5_ = bf16[64,2048]{1,0:T(8,128)(2,1)S(1)} collective-permute-done((bf16[64,2048]{1,0:T(8,128)(2,1)S(1)}, bf16[64,2048]{1,0:T(8,128)(2,1)S(1)}, u32[]{:S(2)}, u32[]{:S(2)}) %collective-permute-start.20) | collective-permute-done | bytes 262176 | tf_op jit(solution)/shard_map/ppermute | solution.py:26
  98.9 0.7 copy-done.8
  103.0 1.5 collective-permute-done.23.refs_8_
  104.4 0.9 copy-done.9
  105.4 0.9 copy-done.11
  106.3 0.9 copy-done.13
  107.3 0.9 copy-done.15
  108.2 0.9 copy-done.17
  109.2 4.2 %adapt.1 = (bf16[1024,1024]{1,0:T(8,128)(2,1)S(1)}, bf16[1024,128]{1,0:T(8,128)(2,1)S(1)}) custom-call(s32[1]{0:T(128)} %bitcast.3.place_ref, bf16[64,2048]{1,0:T(8,128)(2,1)S(1)} %get-tuple-element.53.refs_0_, bf16[64,2048]{1,0:T(8,128)(2,1)S(1)} %copy-done.11, bf16[64,2048]{1,0:T(8,128)(2,1)S(1)} %copy-done.9, ...), custom_call_target="tpu_custom_call" | custom-call | tf_op jit(solution)/shard_map/adapt/pallas_call | solution.py:418
  115.5 1.1 copy-done.30
  116.6 1.3 fusion.8
  118.8 1.3 fusion.11
  121.4 0.7 fusion.32
  122.1 1.3 collective-permute-start.33
  123.4 1.9 %collective-permute-start.32 = (bf16[128,640]{1,0:T(8,128)(2,1)S(1)}, bf16[128,640]{1,0:T(8,128)(2,1)S(1)}, u32[]{:S(2)}, u32[]{:S(2)}) collective-permute-start(bf16[128,640]{1,0:T(8,128)(2,1)S(1)} %get-tuple-element.85), channel_id=1, source_target_pairs={{0,16},{4,20},{8,24},{12,28},{16,0},{20,4},{24,8},{28,12},{1,17},{... | collective-permute-start | bytes 491528 | tf_op jit(solution)/shard_map/ppermute | solution.py:26
  125.6 1.3 add_convert_fusion.1
  126.9 1.3 add_convert_fusion
  128.2 1.9 %collective-permute-done.33.refs_3_ = bf16[128,640]{1,0:T(8,128)(2,1)S(1)} collective-permute-done((bf16[128,640]{1,0:T(8,128)(2,1)S(1)}, bf16[128,640]{1,0:T(8,128)(2,1)S(1)}, u32[]{:S(2)}, u32[]{:S(2)}) %collective-permute-start.33) | collective-permute-done | bytes 163872 | tf_op jit(solution)/shard_map/ppermute | solution.py:26
  130.1 2.7 %collective-permute-done.32.refs_2_ = bf16[128,640]{1,0:T(8,128)(2,1)S(1)} collective-permute-done((bf16[128,640]{1,0:T(8,128)(2,1)S(1)}, bf16[128,640]{1,0:T(8,128)(2,1)S(1)}, u32[]{:S(2)}, u32[]{:S(2)}) %collective-permute-start.32) | collective-permute-done | bytes 163872 | tf_op jit(solution)/shard_map/ppermute | solution.py:26
  133.6 2.1 %finish_keys.1 = (bf16[128,512]{1,0:T(8,128)(2,1)}, f32[128,128]{1,0:T(8,128)}) custom-call(bf16[128,640]{1,0:T(8,128)(2,1)} %get-tuple-element.66.refs_0_, bf16[128,640]{1,0:T(8,128)(2,1)} %copy-done.28, bf16[128,640]{1,0:T(8,128)(2,1)} %copy-done.27, bf16[128,640]{1,0:T(8,128)(2,1)} %copy-done.26, f32[128,128]{1,0:T(8,128)} %pad_maximum_fusion.4.refs_4_.refs_5_, ...), custom_call_target="tpu_custom_call" | custom-call | tf_op jit(solution)/shard_map/finish_keys/pallas_call | solution.py:86
  135.7 1.6 collective-permute-start.36
  137.3 1.5 collective-permute-start.35
  139.3 1.7 collective-permute-start.25
  141.6 1.6 collective-permute-done.36
  143.2 1.8 %collective-permute-done.35 = bf16[128,512]{1,0:T(8,128)(2,1)S(1)} collective-permute-done((bf16[128,512]{1,0:T(8,128)(2,1)}, bf16[128,512]{1,0:T(8,128)(2,1)S(1)}, u32[]{:S(2)}, u32[]{:S(2)}) %collective-permute-start.35) | collective-permute-done | bytes 131104 | tf_op jit(solution)/shard_map/ppermute | solution.py:26
  145.1 1.0 collective-permute-done.34
  146.2 10.2 %collective-permute-done.25 = bf16[2,128,1024]{2,1,0:T(8,128)(2,1)S(1)} collective-permute-done((bf16[2,128,1024]{2,1,0:T(8,128)(2,1)S(1)}, bf16[2,128,1024]{2,1,0:T(8,128)(2,1)S(1)}, u32[]{:S(2)}, u32[]{:S(2)}) %collective-permute-start.25) | collective-permute-done | bytes 524320 | tf_op jit(solution)/shard_map/ppermute | solution.py:26
  157.3 1.8 %collective-permute-start.29 = (bf16[128,1024]{1,0:T(8,128)(2,1)S(1)}, bf16[128,1024]{1,0:T(8,128)(2,1)S(1)}, u32[]{:S(2)}, u32[]{:S(2)}) collective-permute-start(bf16[128,1024]{1,0:T(8,128)(2,1)S(1)} %get-tuple-element.88), channel_id=1, source_target_pairs={{0,8},{4,12},{8,0},{12,4},{16,24},{20,28},{24,16},{28,20},{1,9},{5... | collective-permute-start | bytes 786440 | tf_op jit(solution)/shard_map/ppermute | solution.py:26
  159.2 4.8 %collective-permute-done.26.refs_1_ = bf16[128,1024]{1,0:T(8,128)(2,1)S(1)} collective-permute-done((bf16[128,1024]{1,0:T(8,128)(2,1)S(1)}, bf16[128,1024]{1,0:T(8,128)(2,1)S(1)}, u32[]{:S(2)}, u32[]{:S(2)}) %collective-permute-start.26) | collective-permute-done | bytes 262176 | tf_op jit(solution)/shard_map/ppermute | solution.py:26
  164.7 5.3 %attend.1 = bf16[128,2048]{1,0:T(8,128)(2,1)} custom-call(bf16[128,1024]{1,0:T(8,128)(2,1)S(1)} %get-tuple-element.91.refs_0_, bf16[128,1024]{1,0:T(8,128)(2,1)S(1)} %collective-permute-done.26.refs_1_, bf16[128,1024]{1,0:T(8,128)(2,1)S(1)} %get-tuple-element.89.refs_2_, bf16[128,1024]{1,0:T(8,128)(2,1)S(1)} %collective-permute-done.29.refs_3_, ...), custom_call_target="tpu_custom_call" | custom-call | tf_op jit(solution)/shard_map/attend/pallas_call | solution.py:139
  (177 shorter events, 17.1 us)
Async XLA Ops:
  0.6 112.7 %copy-start = (bf16[1024,256]{1,0:T(8,128)(2,1)S(1)}, bf16[1024,256]{1,0:T(8,128)(2,1)}, u32[]{:S(2)}) copy-start(bf16[1024,256]{1,0:T(8,128)(2,1)} %param.29) | copy-start | bytes 1572868
  0.6 25.9 %collective-permute-start = (bf16[128,2048]{1,0:T(8,128)(2,1)}, bf16[128,2048]{1,0:T(8,128)(2,1)S(1)}, u32[]{:S(2)}, u32[]{:S(2)}) collective-permute-start(bf16[128,2048]{1,0:T(8,128)(2,1)} %param.25), channel_id=1, source_target_pairs={{0,1},{1,2},{2,3},{4,5},{5,6},{6,7},{8,9},{9,10},{10,11},{12,13},{... | collective-permute-start | bytes 1572872 | tf_op jit(solution)/shard_map/ppermute | solution.py:337
  5.7 20.8 %collective-permute-start.1 = (bf16[128,2048]{1,0:T(8,128)(2,1)}, bf16[128,2048]{1,0:T(8,128)(2,1)S(1)}, u32[]{:S(2)}, u32[]{:S(2)}) collective-permute-start(bf16[128,2048]{1,0:T(8,128)(2,1)} %param.25), channel_id=1, source_target_pairs={{1,0},{2,1},{3,2},{5,4},{6,5},{7,6},{9,8},{10,9},{11,10},{13,12},{... | collective-permute-start | bytes 1572872 | tf_op jit(solution)/shard_map/ppermute | solution.py:338
  7.0 19.5 %collective-permute-start.2 = (bf16[128,1024]{1,0:T(8,128)(2,1)}, bf16[128,1024]{1,0:T(8,128)(2,1)S(1)}, u32[]{:S(2)}, u32[]{:S(2)}) collective-permute-start(bf16[128,1024]{1,0:T(8,128)(2,1)} %frames_ref.1), channel_id=1, source_target_pairs={{0,1},{1,2},{2,3},{3,4},{4,5},{5,6},{6,7},{7,8},{8,9},{9,10},{10,1... | collective-permute-start | bytes 786440 | tf_op jit(solution)/shard_map/ppermute | solution.py:21
  12.5 14.1 %collective-permute-start.3 = (bf16[32,1024]{1,0:T(8,128)(2,1)S(1)}, bf16[32,1024]{1,0:T(8,128)(2,1)S(1)}, u32[]{:S(2)}, u32[]{:S(2)}) collective-permute-start(bf16[32,1024]{1,0:T(8,128)(2,1)S(1)} %slice.80), channel_id=1, source_target_pairs={{0,2},{1,3},{2,4},{3,5},{4,6},{5,7},{6,8},{7,9},{8,10},{9,11},{10,... | collective-permute-start | bytes 196616 | tf_op jit(solution)/shard_map/ppermute | solution.py:21
  20.0 2.8 %copy-start.1 = (bf16[1024,3072]{1,0:T(8,128)(2,1)S(1)}, bf16[1024,3072]{1,0:T(8,128)(2,1)}, u32[]{:S(2)}) copy-start(bf16[1024,3072]{1,0:T(8,128)(2,1)} %weight_ref.3) | copy-start | bytes 18874372
  22.8 0.9 copy-start.6
  24.4 2.2 %copy-start.24 = (bf16[128,2048]{1,0:T(8,128)(2,1)S(1)}, bf16[128,2048]{1,0:T(8,128)(2,1)}, u32[]{:S(2)}) copy-start(bf16[128,2048]{1,0:T(8,128)(2,1)} %param.25) | copy-start | bytes 1572868
  24.4 9.7 %copy-start.2 = (bf16[1024,3072]{1,0:T(8,128)(2,1)S(1)}, bf16[1024,3072]{1,0:T(8,128)(2,1)}, u32[]{:S(2)}) copy-start(bf16[1024,3072]{1,0:T(8,128)(2,1)} %weight_ref.3) | copy-start | bytes 18874372
  26.7 9.8 %copy-start.5 = (bf16[1024,1024]{1,0:T(8,128)(2,1)S(1)}, bf16[1024,1024]{1,0:T(8,128)(2,1)}, u32[]{:S(2)}) copy-start(bf16[1024,1024]{1,0:T(8,128)(2,1)} %out_hbm.1) | copy-start | bytes 6291460
  26.7 18.7 %collective-permute-start.6 = (bf16[64,2048]{1,0:T(8,128)(2,1)S(1)}, bf16[64,2048]{1,0:T(8,128)(2,1)S(1)}, u32[]{:S(2)}, u32[]{:S(2)}) collective-permute-start(bf16[64,2048]{1,0:T(8,128)(2,1)S(1)} %slice.84), channel_id=1, source_target_pairs={{2,1},{1,0},{6,5},{5,4},{10,9},{9,8},{14,13},{13,12},{18,17},{17,1... | collective-permute-start | bytes 786440 | tf_op jit(solution)/shard_map/ppermute | solution.py:346
  28.1 17.3 %collective-permute-start.5 = (bf16[64,2048]{1,0:T(8,128)(2,1)S(1)}, bf16[64,2048]{1,0:T(8,128)(2,1)S(1)}, u32[]{:S(2)}, u32[]{:S(2)}) collective-permute-start(bf16[64,2048]{1,0:T(8,128)(2,1)S(1)} %slice.83), channel_id=1, source_target_pairs={{1,2},{2,3},{5,6},{6,7},{9,10},{10,11},{13,14},{14,15},{17,18},{18... | collective-permute-start | bytes 786440 | tf_op jit(solution)/shard_map/ppermute | solution.py:345
  28.8 16.6 %collective-permute-start.4 = (bf16[64,2048]{1,0:T(8,128)(2,1)S(1)}, bf16[64,2048]{1,0:T(8,128)(2,1)S(1)}, u32[]{:S(2)}, u32[]{:S(2)}) collective-permute-start(bf16[64,2048]{1,0:T(8,128)(2,1)S(1)} %slice.82), channel_id=1, source_target_pairs={{0,3},{3,0},{4,7},{7,4},{8,11},{11,8},{12,15},{15,12},{16,19},{19,... | collective-permute-start | bytes 786440 | tf_op jit(solution)/shard_map/ppermute | solution.py:344
  34.1 2.4 %copy-start.3 = (bf16[1024,2048]{1,0:T(8,128)(2,1)S(1)}, bf16[1024,2048]{1,0:T(8,128)(2,1)}, u32[]{:S(2)}) copy-start(bf16[1024,2048]{1,0:T(8,128)(2,1)} %in_hbm.1) | copy-start | bytes 12582916
  34.1 2.9 %copy-start.4 = (bf16[1024,1024]{1,0:T(8,128)(2,1)S(1)}, bf16[1024,1024]{1,0:T(8,128)(2,1)}, u32[]{:S(2)}) copy-start(bf16[1024,1024]{1,0:T(8,128)(2,1)} %attn_hbm.1) | copy-start | bytes 6291460
  34.1 2.9 %copy-start.7 = (bf16[128,1024]{1,0:T(8,128)(2,1)S(1)}, bf16[128,1024]{1,0:T(8,128)(2,1)}, u32[]{:S(2)}) copy-start(bf16[128,1024]{1,0:T(8,128)(2,1)} %frames_ref.1) | copy-start | bytes 786436
  34.1 2.8 %copy-start.22 = (f32[1024]{0:T(1024)S(1)}, f32[1024]{0:T(1024)}, u32[]{:S(2)}) copy-start(f32[1024]{0:T(1024)} %param.21) | copy-start | bytes 12292
  45.6 15.4 %collective-permute-start.9 = (bf16[32,1024]{1,0:T(8,128)(2,1)S(1)}, bf16[32,1024]{1,0:T(8,128)(2,1)S(1)}, u32[]{:S(2)}, u32[]{:S(2)}) collective-permute-start(bf16[32,1024]{1,0:T(8,128)(2,1)S(1)} %get-tuple-element.48), channel_id=1, source_target_pairs={{0,1},{1,2},{2,3},{3,0},{4,5},{5,6},{6,7},{7,4},{8,9},{9,10},{10,1... | collective-permute-start | bytes 196616 | tf_op jit(solution)/shard_map/ppermute | solution.py:31
  46.6 12.2 %collective-permute-start.8 = (bf16[32,1024]{1,0:T(8,128)(2,1)S(1)}, bf16[32,1024]{1,0:T(8,128)(2,1)S(1)}, u32[]{:S(2)}, u32[]{:S(2)}) collective-permute-start(bf16[32,1024]{1,0:T(8,128)(2,1)S(1)} %get-tuple-element.48), channel_id=1, source_target_pairs={{0,2},{1,3},{2,0},{3,1},{4,6},{5,7},{6,4},{7,5},{8,10},{9,11},{10,... | collective-permute-start | bytes 196616 | tf_op jit(solution)/shard_map/ppermute | solution.py:31
  47.5 5.7 %collective-permute-start.7 = (bf16[32,1024]{1,0:T(8,128)(2,1)S(1)}, bf16[32,1024]{1,0:T(8,128)(2,1)S(1)}, u32[]{:S(2)}, u32[]{:S(2)}) collective-permute-start(bf16[32,1024]{1,0:T(8,128)(2,1)S(1)} %get-tuple-element.48), channel_id=1, source_target_pairs={{0,3},{1,0},{2,1},{3,2},{4,7},{5,4},{6,5},{7,6},{8,11},{9,8},{10,9... | collective-permute-start | bytes 196616 | tf_op jit(solution)/shard_map/ppermute | solution.py:31
  50.4 30.9 %collective-permute-start.19 = (bf16[64,2048]{1,0:T(8,128)(2,1)S(1)}, bf16[64,2048]{1,0:T(8,128)(2,1)S(1)}, u32[]{:S(2)}, u32[]{:S(2)}) collective-permute-start(bf16[64,2048]{1,0:T(8,128)(2,1)S(1)} %slice.87), channel_id=1, source_target_pairs={{2,1},{1,0},{6,5},{5,4},{10,9},{9,8},{14,13},{13,12},{18,17},{17,1... | collective-permute-start | bytes 786440 | tf_op jit(solution)/shard_map/ppermute | solution.py:346
  51.7 16.0 %collective-permute-start.18 = (bf16[64,2048]{1,0:T(8,128)(2,1)S(1)}, bf16[64,2048]{1,0:T(8,128)(2,1)S(1)}, u32[]{:S(2)}, u32[]{:S(2)}) collective-permute-start(bf16[64,2048]{1,0:T(8,128)(2,1)S(1)} %slice.86), channel_id=1, source_target_pairs={{1,2},{2,3},{5,6},{6,7},{9,10},{10,11},{13,14},{14,15},{17,18},{18... | collective-permute-start | bytes 786440 | tf_op jit(solution)/shard_map/ppermute | solution.py:345
  53.2 12.7 %collective-permute-start.17 = (bf16[64,2048]{1,0:T(8,128)(2,1)S(1)}, bf16[64,2048]{1,0:T(8,128)(2,1)S(1)}, u32[]{:S(2)}, u32[]{:S(2)}) collective-permute-start(bf16[64,2048]{1,0:T(8,128)(2,1)S(1)} %slice.85), channel_id=1, source_target_pairs={{0,3},{3,0},{4,7},{7,4},{8,11},{11,8},{12,15},{15,12},{16,19},{19,... | collective-permute-start | bytes 786440 | tf_op jit(solution)/shard_map/ppermute | solution.py:344
  58.8 24.1 %collective-permute-start.16 = (bf16[64,2048]{1,0:T(8,128)(2,1)S(1)}, bf16[64,2048]{1,0:T(8,128)(2,1)S(1)}, u32[]{:S(2)}, u32[]{:S(2)}) collective-permute-start(bf16[64,2048]{1,0:T(8,128)(2,1)S(1)} %get-tuple-element.78), channel_id=1, source_target_pairs={{0,24},{4,28},{8,16},{12,20},{16,8},{20,12},{24,0},{28,4},{1,25},{... | collective-permute-start | bytes 786440 | tf_op jit(solution)/shard_map/ppermute | solution.py:26
  61.2 13.5 %collective-permute-start.12 = (bf16[128,1024]{1,0:T(8,128)(2,1)S(1)}, bf16[128,1024]{1,0:T(8,128)(2,1)S(1)}, u32[]{:S(2)}, u32[]{:S(2)}) collective-permute-start(bf16[128,1024]{1,0:T(8,128)(2,1)S(1)} %get-tuple-element.73), channel_id=1, source_target_pairs={{0,24},{4,28},{8,16},{12,20},{16,8},{20,12},{24,0},{28,4},{1,25},{... | collective-permute-start | bytes 786440 | tf_op jit(solution)/shard_map/ppermute | solution.py:26
  66.0 12.8 %collective-permute-start.11 = (bf16[128,1024]{1,0:T(8,128)(2,1)S(1)}, bf16[128,1024]{1,0:T(8,128)(2,1)S(1)}, u32[]{:S(2)}, u32[]{:S(2)}) collective-permute-start(bf16[128,1024]{1,0:T(8,128)(2,1)S(1)} %get-tuple-element.73), channel_id=1, source_target_pairs={{0,16},{4,20},{8,24},{12,28},{16,0},{20,4},{24,8},{28,12},{1,17},{... | collective-permute-start | bytes 786440 | tf_op jit(solution)/shard_map/ppermute | solution.py:26
  67.7 13.4 %collective-permute-start.10 = (bf16[128,1024]{1,0:T(8,128)(2,1)S(1)}, bf16[128,1024]{1,0:T(8,128)(2,1)S(1)}, u32[]{:S(2)}, u32[]{:S(2)}) collective-permute-start(bf16[128,1024]{1,0:T(8,128)(2,1)S(1)} %get-tuple-element.73), channel_id=1, source_target_pairs={{0,8},{4,12},{8,0},{12,4},{16,24},{20,28},{24,16},{28,20},{1,9},{5... | collective-permute-start | bytes 786440 | tf_op jit(solution)/shard_map/ppermute | solution.py:26
  74.7 10.6 %collective-permute-start.15 = (bf16[64,2048]{1,0:T(8,128)(2,1)S(1)}, bf16[64,2048]{1,0:T(8,128)(2,1)S(1)}, u32[]{:S(2)}, u32[]{:S(2)}) collective-permute-start(bf16[64,2048]{1,0:T(8,128)(2,1)S(1)} %get-tuple-element.79), channel_id=1, source_target_pairs={{0,16},{4,20},{8,24},{12,28},{16,0},{20,4},{24,8},{28,12},{1,17},{... | collective-permute-start | bytes 786440 | tf_op jit(solution)/shard_map/ppermute | solution.py:26
  78.8 9.5 %collective-permute-start.14 = (bf16[64,2048]{1,0:T(8,128)(2,1)S(1)}, bf16[64,2048]{1,0:T(8,128)(2,1)S(1)}, u32[]{:S(2)}, u32[]{:S(2)}) collective-permute-start(bf16[64,2048]{1,0:T(8,128)(2,1)S(1)} %get-tuple-element.80), channel_id=1, source_target_pairs={{0,8},{4,12},{8,0},{12,4},{16,24},{20,28},{24,16},{28,20},{1,9},{5... | collective-permute-start | bytes 786440 | tf_op jit(solution)/shard_map/ppermute | solution.py:26
  81.2 2.7 %collective-permute-start.13 = (bf16[512,1024]{1,0:T(8,128)(2,1)S(1)}, bf16[512,1024]{1,0:T(8,128)(2,1)S(1)}, u32[]{:S(2)}, u32[]{:S(2)}) collective-permute-start(bf16[512,1024]{1,0:T(8,128)(2,1)S(1)} %pad_maximum_fusion.1), channel_id=1, source_target_pairs={{0,4},{4,0},{8,12},{12,8},{16,20},{20,16},{24,28},{28,24},{1,5},{5... | collective-permute-start | bytes 3145736 | tf_op jit(solution)/shard_map/ppermute | solution.py:26
  81.5 13.8 %collective-permute-start.22 = (bf16[64,2048]{1,0:T(8,128)(2,1)S(1)}, bf16[64,2048]{1,0:T(8,128)(2,1)S(1)}, u32[]{:S(2)}, u32[]{:S(2)}) collective-permute-start(bf16[64,2048]{1,0:T(8,128)(2,1)S(1)} %get-tuple-element.74), channel_id=1, source_target_pairs={{0,24},{4,28},{8,16},{12,20},{16,8},{20,12},{24,0},{28,4},{1,25},{... | collective-permute-start | bytes 786440 | tf_op jit(solution)/shard_map/ppermute | solution.py:26
  82.9 14.1 %collective-permute-start.21 = (bf16[64,2048]{1,0:T(8,128)(2,1)S(1)}, bf16[64,2048]{1,0:T(8,128)(2,1)S(1)}, u32[]{:S(2)}, u32[]{:S(2)}) collective-permute-start(bf16[64,2048]{1,0:T(8,128)(2,1)S(1)} %get-tuple-element.75), channel_id=1, source_target_pairs={{0,16},{4,20},{8,24},{12,28},{16,0},{20,4},{24,8},{28,12},{1,17},{... | collective-permute-start | bytes 786440 | tf_op jit(solution)/shard_map/ppermute | solution.py:26
  84.0 14.9 %collective-permute-start.20 = (bf16[64,2048]{1,0:T(8,128)(2,1)S(1)}, bf16[64,2048]{1,0:T(8,128)(2,1)S(1)}, u32[]{:S(2)}, u32[]{:S(2)}) collective-permute-start(bf16[64,2048]{1,0:T(8,128)(2,1)S(1)} %get-tuple-element.76), channel_id=1, source_target_pairs={{0,8},{4,12},{8,0},{12,4},{16,24},{20,28},{24,16},{28,20},{1,9},{5... | collective-permute-start | bytes 786440 | tf_op jit(solution)/shard_map/ppermute | solution.py:26
  85.3 16.5 %copy-start.23 = (bf16[1024,1024]{1,0:T(8,128)(2,1)}, bf16[1024,1024]{1,0:T(8,128)(2,1)S(1)}, u32[]{:S(2)}) copy-start(bf16[1024,1024]{1,0:T(8,128)(2,1)S(1)} %constant_dynamic-update-slice_fusion.8.refs_9_) | copy-start | bytes 6291460
  85.3 17.2 %copy-start.29 = (s32[8]{0:T(128)S(1)}, s32[8]{0:T(128)}, u32[]{:S(2)}) copy-start(s32[8]{0:T(128)} %param.17) | copy-start | bytes 100
  98.8 2.9 %copy-start.16 = (bf16[64,2048]{1,0:T(8,128)(2,1)}, bf16[64,2048]{1,0:T(8,128)(2,1)S(1)}, u32[]{:S(2)}) copy-start(bf16[64,2048]{1,0:T(8,128)(2,1)S(1)} %collective-permute-done.20.refs_5_) | copy-start | bytes 786436
  98.9 0.7 copy-start.8
  101.8 2.7 %collective-permute-start.23 = (bf16[512,1024]{1,0:T(8,128)(2,1)S(1)}, bf16[512,1024]{1,0:T(8,128)(2,1)S(1)}, u32[]{:S(2)}, u32[]{:S(2)}) collective-permute-start(bf16[512,1024]{1,0:T(8,128)(2,1)S(1)} %other_half.1), channel_id=1, source_target_pairs={{0,4},{4,0},{8,12},{12,8},{16,20},{20,16},{24,28},{28,24},{1,5},{5... | collective-permute-start | bytes 3145736 | tf_op jit(solution)/shard_map/ppermute | solution.py:26
  104.4 1.0 copy-start.9
  105.4 0.9 copy-start.11
  106.3 0.9 copy-start.13
  107.3 0.9 copy-start.15
  108.2 0.9 copy-start.17
  113.4 1.0 copy-start.31
  114.4 2.2 %copy-start.30 = (bf16[1024,2048]{1,0:T(8,128)(2,1)S(1)}, bf16[1024,2048]{1,0:T(8,128)(2,1)}, u32[]{:S(2)}) copy-start(bf16[1024,2048]{1,0:T(8,128)(2,1)} %param.27) | copy-start | bytes 12582916
  115.3 5.9 %collective-permute-start.30 = (bf16[512,640]{1,0:T(8,128)(2,1)S(1)}, bf16[512,640]{1,0:T(8,128)(2,1)S(1)}, u32[]{:S(2)}, u32[]{:S(2)}) collective-permute-start(bf16[512,640]{1,0:T(8,128)(2,1)S(1)} %slice.101), channel_id=1, source_target_pairs={{0,4},{4,0},{8,12},{12,8},{16,20},{20,16},{24,28},{28,24},{1,5},{5... | collective-permute-start | bytes 1966088 | tf_op jit(solution)/shard_map/ppermute | solution.py:26
  117.9 7.7 %collective-permute-start.24 = (bf16[512,1024]{1,0:T(8,128)(2,1)S(1)}, bf16[512,1024]{1,0:T(8,128)(2,1)S(1)}, u32[]{:S(2)}, u32[]{:S(2)}) collective-permute-start(bf16[512,1024]{1,0:T(8,128)(2,1)S(1)} %fusion.8), channel_id=1, source_target_pairs={{0,4},{4,0},{8,12},{12,8},{16,20},{20,16},{24,28},{28,24},{1,5},{5... | collective-permute-start | bytes 3145736 | tf_op jit(solution)/shard_map/ppermute | solution.py:26
  120.1 6.8 %collective-permute-start.27 = (bf16[512,1024]{1,0:T(8,128)(2,1)S(1)}, bf16[512,1024]{1,0:T(8,128)(2,1)S(1)}, u32[]{:S(2)}, u32[]{:S(2)}) collective-permute-start(bf16[512,1024]{1,0:T(8,128)(2,1)S(1)} %fusion.11), channel_id=1, source_target_pairs={{0,4},{4,0},{8,12},{12,8},{16,20},{20,16},{24,28},{28,24},{1,5},{5... | collective-permute-start | bytes 3145736 | tf_op jit(solution)/shard_map/ppermute | solution.py:26
  122.1 8.0 %collective-permute-start.33 = (bf16[128,640]{1,0:T(8,128)(2,1)S(1)}, bf16[128,640]{1,0:T(8,128)(2,1)S(1)}, u32[]{:S(2)}, u32[]{:S(2)}) collective-permute-start(bf16[128,640]{1,0:T(8,128)(2,1)S(1)} %get-tuple-element.84), channel_id=1, source_target_pairs={{0,24},{4,28},{8,16},{12,20},{16,8},{20,12},{24,0},{28,4},{1,25},{... | collective-permute-start | bytes 491528 | tf_op jit(solution)/shard_map/ppermute | solution.py:26
  123.4 9.3 %collective-permute-start.32 = (bf16[128,640]{1,0:T(8,128)(2,1)S(1)}, bf16[128,640]{1,0:T(8,128)(2,1)S(1)}, u32[]{:S(2)}, u32[]{:S(2)}) collective-permute-start(bf16[128,640]{1,0:T(8,128)(2,1)S(1)} %get-tuple-element.85), channel_id=1, source_target_pairs={{0,16},{4,20},{8,24},{12,28},{16,0},{20,4},{24,8},{28,12},{1,17},{... | collective-permute-start | bytes 491528 | tf_op jit(solution)/shard_map/ppermute | solution.py:26
  125.3 7.6 %collective-permute-start.31 = (bf16[128,640]{1,0:T(8,128)(2,1)S(1)}, bf16[128,640]{1,0:T(8,128)(2,1)S(1)}, u32[]{:S(2)}, u32[]{:S(2)}) collective-permute-start(bf16[128,640]{1,0:T(8,128)(2,1)S(1)} %get-tuple-element.86), channel_id=1, source_target_pairs={{0,8},{4,12},{8,0},{12,4},{16,24},{20,28},{24,16},{28,20},{1,9},{5... | collective-permute-start | bytes 491528 | tf_op jit(solution)/shard_map/ppermute | solution.py:26
  130.1 2.9 %copy-start.26 = (bf16[128,640]{1,0:T(8,128)(2,1)}, bf16[128,640]{1,0:T(8,128)(2,1)S(1)}, u32[]{:S(2)}) copy-start(bf16[128,640]{1,0:T(8,128)(2,1)S(1)} %collective-permute-done.33.refs_3_) | copy-start | bytes 491524
  135.7 5.9 %copy-start.25 = (bf16[128,512]{1,0:T(8,128)(2,1)S(1)}, bf16[128,512]{1,0:T(8,128)(2,1)}, u32[]{:S(2)}) copy-start(bf16[128,512]{1,0:T(8,128)(2,1)} %get-tuple-element.71) | copy-start | bytes 393220
  135.7 7.5 %collective-permute-start.36 = (bf16[128,512]{1,0:T(8,128)(2,1)}, bf16[128,512]{1,0:T(8,128)(2,1)S(1)}, u32[]{:S(2)}, u32[]{:S(2)}) collective-permute-start(bf16[128,512]{1,0:T(8,128)(2,1)} %get-tuple-element.71), channel_id=1, source_target_pairs={{0,24},{4,28},{8,16},{12,20},{16,8},{20,12},{24,0},{28,4},{1,25},{... | collective-permute-start | bytes 393224 | tf_op jit(solution)/shard_map/ppermute | solution.py:26
  137.3 7.7 %collective-permute-start.35 = (bf16[128,512]{1,0:T(8,128)(2,1)}, bf16[128,512]{1,0:T(8,128)(2,1)S(1)}, u32[]{:S(2)}, u32[]{:S(2)}) collective-permute-start(bf16[128,512]{1,0:T(8,128)(2,1)} %get-tuple-element.71), channel_id=1, source_target_pairs={{0,16},{4,20},{8,24},{12,28},{16,0},{20,4},{24,8},{28,12},{1,17},{... | collective-permute-start | bytes 393224 | tf_op jit(solution)/shard_map/ppermute | solution.py:26
  138.8 7.2 %collective-permute-start.34 = (bf16[128,512]{1,0:T(8,128)(2,1)}, bf16[128,512]{1,0:T(8,128)(2,1)S(1)}, u32[]{:S(2)}, u32[]{:S(2)}) collective-permute-start(bf16[128,512]{1,0:T(8,128)(2,1)} %get-tuple-element.71), channel_id=1, source_target_pairs={{0,8},{4,12},{8,0},{12,4},{16,24},{20,28},{24,16},{28,20},{1,9},{5... | collective-permute-start | bytes 393224 | tf_op jit(solution)/shard_map/ppermute | solution.py:26
  139.3 17.1 %collective-permute-start.25 = (bf16[2,128,1024]{2,1,0:T(8,128)(2,1)S(1)}, bf16[2,128,1024]{2,1,0:T(8,128)(2,1)S(1)}, u32[]{:S(2)}, u32[]{:S(2)}) collective-permute-start(bf16[2,128,1024]{2,1,0:T(8,128)(2,1)S(1)} %slice_bitcast_fusion), channel_id=1, source_target_pairs={{0,8},{4,12},{8,0},{12,4},{16,24},{20,28},{24,16},{28,20},{1,9},{5... | collective-permute-start | bytes 1572872 | tf_op jit(solution)/shard_map/ppermute | solution.py:26
  141.0 16.0 %collective-permute-start.28 = (bf16[2,128,1024]{2,1,0:T(8,128)(2,1)S(1)}, bf16[2,128,1024]{2,1,0:T(8,128)(2,1)S(1)}, u32[]{:S(2)}, u32[]{:S(2)}) collective-permute-start(bf16[2,128,1024]{2,1,0:T(8,128)(2,1)S(1)} %bitcast.99), channel_id=1, source_target_pairs={{0,16},{4,20},{8,24},{12,28},{16,0},{20,4},{24,8},{28,12},{1,17},{... | collective-permute-start | bytes 1572872 | tf_op jit(solution)/shard_map/ppermute | solution.py:26
  146.1 13.1 %collective-permute-start.37 = (bf16[512,512]{1,0:T(8,128)(2,1)S(1)}, bf16[512,512]{1,0:T(8,128)(2,1)S(1)}, u32[]{:S(2)}, u32[]{:S(2)}) collective-permute-start(bf16[512,512]{1,0:T(8,128)(2,1)S(1)} %pad_maximum_fusion.2), channel_id=1, source_target_pairs={{0,4},{4,0},{8,12},{12,8},{16,20},{20,16},{24,28},{28,24},{1,5},{5... | collective-permute-start | bytes 1572872 | tf_op jit(solution)/shard_map/ppermute | solution.py:26
  156.6 7.4 %collective-permute-start.26 = (bf16[128,1024]{1,0:T(8,128)(2,1)S(1)}, bf16[128,1024]{1,0:T(8,128)(2,1)S(1)}, u32[]{:S(2)}, u32[]{:S(2)}) collective-permute-start(bf16[128,1024]{1,0:T(8,128)(2,1)S(1)} %get-tuple-element.90), channel_id=1, source_target_pairs={{0,16},{4,20},{8,24},{12,28},{16,0},{20,4},{24,8},{28,12},{1,17},{... | collective-permute-start | bytes 786440 | tf_op jit(solution)/shard_map/ppermute | solution.py:26
  157.1 7.7 %copy-start.18 = (f32[128,128]{1,0:T(8,128)S(1)}, f32[128,128]{1,0:T(8,128)}, u32[]{:S(2)}) copy-start(f32[128,128]{1,0:T(8,128)} %pad_maximum_fusion.5.refs_5_.refs_6_) | copy-start | bytes 196612
  157.1 7.7 %copy-start.19 = (f32[128,128]{1,0:T(8,128)S(1)}, f32[128,128]{1,0:T(8,128)}, u32[]{:S(2)}) copy-start(f32[128,128]{1,0:T(8,128)} %pad_maximum_fusion.4.refs_4_.refs_5_) | copy-start | bytes 196612
  157.1 7.7 %copy-start.20 = (f32[128,128]{1,0:T(8,128)S(1)}, f32[128,128]{1,0:T(8,128)}, u32[]{:S(2)}) copy-start(f32[128,128]{1,0:T(8,128)} %get-tuple-element.70.refs_4_) | copy-start | bytes 196612
  157.3 7.4 %collective-permute-start.29 = (bf16[128,1024]{1,0:T(8,128)(2,1)S(1)}, bf16[128,1024]{1,0:T(8,128)(2,1)S(1)}, u32[]{:S(2)}, u32[]{:S(2)}) collective-permute-start(bf16[128,1024]{1,0:T(8,128)(2,1)S(1)} %get-tuple-element.88), channel_id=1, source_target_pairs={{0,8},{4,12},{8,0},{12,4},{16,24},{20,28},{24,16},{28,20},{1,9},{5... | collective-permute-start | bytes 786440 | tf_op jit(solution)/shard_map/ppermute | solution.py:26
  (6 other events, 4.1 us)

commit v3 on v2

--- a/solution.py
+++ b/solution.py
@@ -139,7 +139,7 @@
     return pl.pallas_call(
         kernel,
         out_shape=jax.ShapeDtypeStruct((rows, count * chunk_cols), jnp.bfloat16),
-        compiler_params=pltpu.CompilerParams(vmem_limit_bytes=40 << 20),
+        compiler_params=pltpu.CompilerParams(vmem_limit_bytes=(16 << 20) * max(1, tokens // 2048)),
         name="attend",
     )(*flat, scale, cosine, sine, query_place, key_place, key_real, kv)
 
@@ -171,7 +171,7 @@
         out_specs=pl.BlockSpec((rows, step), lambda i: (0, i)),
         out_shape=jax.ShapeDtypeStruct((rows, wide), jnp.bfloat16),
         scratch_shapes=[pltpu.VMEM((rows, width), jnp.bfloat16)],
-        compiler_params=pltpu.CompilerParams(vmem_limit_bytes=16 << 20),
+        compiler_params=pltpu.CompilerParams(vmem_limit_bytes=12 << 20),
         cost_estimate=pl.CostEstimate(
             flops=2 * rows * width * wide, bytes_accessed=2 * width * wide, transcendentals=0
         ),
@@ -179,32 +179,22 @@
     )(held, gain[None, :], w_qkv)
 
 
-def convolve(
-    frames, near, own_proj, before_proj, key_index, key_ids, key_real, w_attn_out, norm_conv,
-    w_point_in, w_depth, w_point_out,
+def gate_frames(
+    frames, own_proj, near_proj, key_row, query_col, w_attn_out, norm_conv, w_point_in, tail_rows
 ):
     frame_rows, width = frames.shape
-    before = before_proj.shape[0]
-    key_rows = before + frame_rows
-    near_rows = near.shape[0]
-    extra = before - near_rows
-    query_rows = extra + frame_rows
-    lead = key_rows - query_rows
+    near_rows = near_proj.shape[0]
+    key_rows = near_rows + frame_rows
     head_size = width // CH
-    pooled_rows = frame_rows // 4
-    taps = w_depth.shape[0]
     lanes = 2 * head_size
 
     def kernel(
-        frames_ref, near_ref, own_ref, before_ref, key_row_ref, query_col_ref, gain_ref, depth_ref,
-        attn_hbm, in_hbm, out_hbm, conf_ref, pooled_ref,
-        attn_w, in_w, out_w, context_ref, glu_ref, active_ref, sems,
+        frames_ref, own_ref, near_ref, key_row_ref, query_col_ref, gain_ref, attn_hbm, in_hbm,
+        mid_ref, glu_ref, tail_ref, attn_w, in_w, context_ref, sems,
     ):
         copies = [
-            pltpu.make_async_copy(source, target, sems.at[i])
-            for i, (source, target) in enumerate(
-                ((attn_hbm, attn_w), (in_hbm, in_w), (out_hbm, out_w))
-            )
+            pltpu.make_async_copy(attn_hbm, attn_w, sems.at[0]),
+            pltpu.make_async_copy(in_hbm, in_w, sems.at[1]),
         ]
         for copy in copies:
             copy.start()
@@ -213,14 +203,14 @@
         seen = (key_at <= at) & (key_id >= ids - 2) & ((key_live > 0) | (key_at == at))
         bias = jnp.where(seen, 0.0, masked_score)
         bias = jnp.concatenate([bias, bias], axis=0)
-        left = lax.broadcasted_iota(jnp.int32, (query_rows, lanes), 1) < head_size
+        left = lax.broadcasted_iota(jnp.int32, (frame_rows, lanes), 1) < head_size
         for pair in range(width // lanes):
 
             def both_rows(offset):
                 columns = pl.ds(offset + pair * lanes, lanes)
-                return jnp.concatenate([before_ref[:, columns], own_ref[:, columns]], axis=0)
-
-            query = both_rows(0)[lead:]
+                return jnp.concatenate([near_ref[:, columns], own_ref[:, columns]], axis=0)
+
+            query = own_ref[:, pl.ds(pair * lanes, lanes)]
             none = jnp.zeros_like(query)
             query = jnp.concatenate(
                 [jnp.where(left, query, none), jnp.where(left, none, query)], axis=0
@@ -237,13 +227,13 @@
             )
             context = summed / total
             context_ref[:, pl.ds(pair * lanes, lanes)] = jnp.where(
-                left, context[:query_rows], context[query_rows:]
+                left, context[:frame_rows], context[frame_rows:]
             ).astype(jnp.bfloat16)
-        inputs = jnp.concatenate([near_ref[near_rows - extra :], frames_ref[...]], axis=0)
         copies[0].wait()
-        mid = inputs.astype(jnp.float32) + jnp.dot(
+        mid = frames_ref[...].astype(jnp.float32) + jnp.dot(
             context_ref[...], attn_w[...], preferred_element_type=jnp.float32
         )
+        mid_ref[...] = mid
         conv_in = layer_norm(mid, gain_ref[...]).astype(jnp.bfloat16)
         copies[1].wait()
         part = 256
@@ -254,21 +244,63 @@
             gate = jnp.dot(
                 conv_in, in_w[:, pl.ds(width + start, part)], preferred_element_type=jnp.float32
             )
-            glu = jnp.where(live > 0, value * jax.nn.sigmoid(gate), 0.0)
-            glu_ref[:, pl.ds(start, part)] = glu.astype(jnp.bfloat16).astype(jnp.float32)
+            glu = jnp.where(live > 0, value * jax.nn.sigmoid(gate), 0.0).astype(jnp.bfloat16)
+            glu_ref[:, pl.ds(start, part)] = glu
+            tail_ref[:, pl.ds(start, part)] = glu[frame_rows - tail_rows :]
+
+    plain = pl.BlockSpec(memory_space=pltpu.VMEM)
+    apart = pl.BlockSpec(memory_space=pl.ANY)
+    return pl.pallas_call(
+        kernel,
+        in_specs=[plain] * 6 + [apart] * 2,
+        out_specs=(plain, plain, plain),
+        out_shape=(
+            jax.ShapeDtypeStruct((frame_rows, width), jnp.float32),
+            jax.ShapeDtypeStruct((frame_rows, width), jnp.bfloat16),
+            jax.ShapeDtypeStruct((tail_rows, width), jnp.bfloat16),
+        ),
+        scratch_shapes=[
+            pltpu.VMEM(w_attn_out.shape, jnp.bfloat16),
+            pltpu.VMEM(w_point_in.shape, jnp.bfloat16),
+            pltpu.VMEM((frame_rows, width), jnp.bfloat16),
+            pltpu.SemaphoreType.DMA((2,)),
+        ],
+        compiler_params=pltpu.CompilerParams(vmem_limit_bytes=16 << 20),
+        cost_estimate=pl.CostEstimate(
+            flops=2 * frame_rows * width * 3 * width,
+            bytes_accessed=6 * width * width,
+            transcendentals=CH * frame_rows * key_rows,
+        ),
+        name="gate_frames",
+    )(
+        frames, own_proj, near_proj, key_row, query_col, norm_conv[None, :], w_attn_out, w_point_in
+    )
+
+
+def finish_frames(mid, glu, rim, real_col, depth_weights, w_point_out):
+    frame_rows, width = mid.shape
+    extra = rim.shape[0]
+    pooled_rows = frame_rows // 4
+    taps = depth_weights.shape[0]
+
+    def kernel(
+        mid_ref, glu_ref, rim_ref, real_ref, depth_ref, out_ref, conf_ref, pooled_ref, held_ref,
+        active_ref,
+    ):
+        held_ref[:extra] = rim_ref[...].astype(jnp.float32)
+        held_ref[extra:] = glu_ref[...].astype(jnp.float32)
         for start in range(0, width, 128):
             columns = pl.ds(start, 128)
             depth = jnp.zeros((frame_rows, 128), jnp.float32)
             for tap in range(taps):
-                depth = depth + depth_ref[tap : tap + 1, columns] * glu_ref[
+                depth = depth + depth_ref[tap : tap + 1, columns] * held_ref[
                     pl.ds(extra - tap, frame_rows), columns
                 ]
             active_ref[:, columns] = jax.nn.silu(depth).astype(jnp.bfloat16)
-        copies[2].wait()
-        final = mid[extra:] + jnp.dot(
-            active_ref[...], out_w[...], preferred_element_type=jnp.float32
+        final = mid_ref[...] + jnp.dot(
+            active_ref[...], out_ref[...], preferred_element_type=jnp.float32
         )
-        conf = jnp.where(live[extra:] > 0, final, 0.0).astype(jnp.bfloat16)
+        conf = jnp.where(real_ref[...] > 0, final, 0.0).astype(jnp.bfloat16)
         conf_ref[...] = conf
         row = lax.broadcasted_iota(jnp.int32, (pooled_rows, frame_rows), 0)
         column = lax.broadcasted_iota(jnp.int32, (pooled_rows, frame_rows), 1)
@@ -277,56 +309,43 @@
             jnp.bfloat16
         )
 
-    key_row = jnp.stack([key_index, key_ids, key_real.astype(jnp.int32)])
-    query_col = jnp.transpose(key_row[:, lead:])
-    plain = pl.BlockSpec(memory_space=pltpu.VMEM)
-    apart = pl.BlockSpec(memory_space=pl.ANY)
-    flops = 2 * query_rows * width * 4 * width
     return pl.pallas_call(
         kernel,
-        in_specs=[plain] * 8 + [apart] * 3,
-        out_specs=(plain, plain),
         out_shape=(
             jax.ShapeDtypeStruct((frame_rows, width), jnp.bfloat16),
             jax.ShapeDtypeStruct((pooled_rows, width), jnp.bfloat16),
         ),
         scratch_shapes=[
-            pltpu.VMEM(w_attn_out.shape, jnp.bfloat16),
-            pltpu.VMEM(w_point_in.shape, jnp.bfloat16),
-            pltpu.VMEM(w_point_out.shape, jnp.bfloat16),
-            pltpu.VMEM((query_rows, width), jnp.bfloat16),
-            pltpu.VMEM((query_rows, width), jnp.float32),
+            pltpu.VMEM((extra + frame_rows, width), jnp.float32),
             pltpu.VMEM((frame_rows, width), jnp.bfloat16),
-            pltpu.SemaphoreType.DMA((3,)),
         ],
-        compiler_params=pltpu.CompilerParams(vmem_limit_bytes=32 << 20),
+        compiler_params=pltpu.CompilerParams(vmem_limit_bytes=8 << 20),
         cost_estimate=pl.CostEstimate(
-            flops=flops, bytes_accessed=8 * width * width, transcendentals=CH * query_rows * key_rows
-        ),
-        name="convolve",
-    )(
-        frames, near, own_proj, before_proj, key_row, query_col, norm_conv[None, :],
-        w_depth.astype(jnp.float32), w_attn_out, w_point_in, w_point_out,
-    )
+            flops=2 * frame_rows * width * width, bytes_accessed=2 * width * width, transcendentals=0
+        ),
+        name="finish_frames",
+    )(mid, glu, rim, real_col, depth_weights, w_point_out)
 
 
 def conformer(
-    frames, own_proj, near, far, first, block_ids, valid_counts, shard_frames, norm_attn, w_qkv,
-    w_attn_out, norm_conv, w_point_in, w_depth, w_point_out,
+    frames, own_proj, near, first, block_ids, valid_counts, shard_frames, norm_attn, w_qkv,
+    w_attn_out, norm_conv, w_point_in, depth_weights, w_point_out,
 ):
-    frame_rows = frames.shape[0]
-    before = near.shape[0] + far.shape[0]
-    key_rows = before + frame_rows
-    before_proj = project(jnp.concatenate([far, near], axis=0), norm_attn, w_qkv)
+    before = near.shape[0]
+    key_rows = before + frames.shape[0]
+    near_proj = project(near, norm_attn, w_qkv)
     key_index = first - before + jnp.arange(key_rows, dtype=jnp.int32)
     key_place, key_count = shard_count(key_index, valid_counts, shard_frames)
     key_real = (key_place < key_count) & (key_index >= 0)
     padded_ids = jnp.concatenate([jnp.full((before,), -100, jnp.int32), block_ids])
     key_ids = lax.dynamic_slice_in_dim(padded_ids, first, key_rows, 0)
-    return convolve(
-        frames, near, own_proj, before_proj, key_index, key_ids, key_real, w_attn_out, norm_conv,
-        w_point_in, w_depth, w_point_out,
-    )
+    key_row = jnp.stack([key_index, key_ids, key_real.astype(jnp.int32)])
+    query_col = jnp.transpose(key_row[:, before:])
+    mid, glu, tail = gate_frames(
+        frames, own_proj, near_proj, key_row, query_col, w_attn_out, norm_conv, w_point_in, 32
+    )
+    rim = shifted(tail, ("tm", "mp"), 1)
+    return finish_frames(mid, glu, rim, query_col[:, 2:3], depth_weights, w_point_out)
 
 
 def line_pieces(value, beside):
@@ -336,11 +355,14 @@
         return [jnp.stack(pieces)], lambda source: (place - source) % mp_count, beside
     below = lax.ppermute(value, "mp", [(0, 1), (1, 2), (2, 3)])
     above = lax.ppermute(value, "mp", [(1, 0), (2, 1), (3, 2)])
-    value, below, above, beside = lax.optimization_barrier((value, below, above, beside))
     half = value.shape[0] // 2
-    chunks, waiting = [], (value, below, above)
+    own, below, above, beside = lax.optimization_barrier(
+        ((value[:half], value[half:]), below, above, beside)
+    )
+    chunks, waiting = [], (own, below, above)
     for start in (0, half):
-        mine, lower, upper = [array[start : start + half] for array in waiting]
+        own, below, above = waiting
+        mine, lower, upper = own[start // half], below[start : start + half], above[start : start + half]
         far = lax.ppermute(mine, "mp", [(0, 3), (3, 0)])
         lower_2 = lax.ppermute(lower, "mp", [(1, 2), (2, 3)])
         upper_2 = lax.ppermute(upper, "mp", [(2, 1), (1, 0)])
@@ -373,36 +395,33 @@
     plain = pl.BlockSpec(memory_space=pltpu.VMEM)
     scalar = pl.BlockSpec(memory_space=pltpu.SMEM)
 
-    def other_half(place_ref, *refs):
-        columns = pl.ds(pl.multiple_of((1 - place_ref[0] % 2) * half, 128), half)
-        for i, ref in enumerate(refs[:-1]):
-            refs[-1][i * part : (i + 1) * part, :] = ref[:, columns]
-
-    given = pl.pallas_call(
-        other_half,
+    def halves(place_ref, *refs):
+        for away, out_ref in enumerate(refs[-2:]):
+            columns = pl.ds(pl.multiple_of((place_ref[0] + away) % 2 * half, 128), half)
+            for i, ref in enumerate(refs[:-2]):
+                out_ref[i * part : (i + 1) * part, :] = ref[:, columns]
+
+    mine, given = pl.pallas_call(
+        halves,
         in_specs=[scalar] + [plain] * len(flat),
-        out_specs=plain,
-        out_shape=jax.ShapeDtypeStruct((len(flat) * part, half), jnp.bfloat16),
-        compiler_params=pltpu.CompilerParams(vmem_limit_bytes=16 << 20),
-        name="other_half",
+        out_specs=(plain, plain),
+        out_shape=(jax.ShapeDtypeStruct((len(flat) * part, half), jnp.bfloat16),) * 2,
+        compiler_params=pltpu.CompilerParams(vmem_limit_bytes=4 << 20),
+        name="halves",
     )(place_word, *flat)
     taken = swapped(given, 1)
     step = min(256, tokens)
 
-    def kernel(place_ref, *refs):
-        near_refs = refs[: len(flat)]
-        taken_ref, pooled_ref, gain_ref, out_ref, word_ref, weight_ref = refs[len(flat) :]
+    def kernel(
+        place_ref, mine_ref, taken_ref, pooled_ref, gain_ref, out_ref, word_ref, weight_ref
+    ):
         place = place_ref[0]
-        columns = pl.ds(pl.multiple_of((place % 2) * half, 128), half)
-        for i, ref in enumerate(near_refs):
+        for i in range(len(flat)):
             chunk, other = i // (tm_count // 2), 2 * (i % (tm_count // 2))
-            for shift in (0, 1):
+            for shift, ref in enumerate((mine_ref, taken_ref)):
                 source = place ^ (other + shift)
                 row = pl.multiple_of(source * (part * len(near)) + chunk * part, part)
-                if shift:
-                    weight_ref[pl.ds(row, part), :] = taken_ref[i * part : (i + 1) * part]
-                else:
-                    weight_ref[pl.ds(row, part), :] = ref[:, columns]
+                weight_ref[pl.ds(row, part), :] = ref[i * part : (i + 1) * part]
         lane = lax.broadcasted_iota(jnp.int32, (step, HDIM), 1) // 32 - 2 * (place % 2)
         for start in range(0, tokens, step):
             rows = pl.ds(start, step)
@@ -417,16 +436,16 @@
 
     return pl.pallas_call(
         kernel,
-        in_specs=[scalar] + [plain] * (len(flat) + 3),
+        in_specs=[scalar] + [plain] * 4,
         out_specs=(plain, plain),
         out_shape=(
             jax.ShapeDtypeStruct((tokens, half), jnp.bfloat16),
             jax.ShapeDtypeStruct((tokens, HDIM), jnp.bfloat16),
         ),
         scratch_shapes=[pltpu.VMEM((depth, half), jnp.bfloat16)],
-        compiler_params=pltpu.CompilerParams(vmem_limit_bytes=48 << 20),
+        compiler_params=pltpu.CompilerParams(vmem_limit_bytes=16 << 20),
         name="adapt",
-    )(place_word, *flat, taken, pooled, gain[None, :])
+    )(place_word, mine, taken, pooled, gain[None, :])
 
 
 def spread_even(value):
@@ -491,23 +510,24 @@
     shard_frames = frame_rows * mp_count
     first = (time_place * mp_count + model_place) * frame_rows
     near = shifted(frames, ("tm", "mp"), 1)
-    far = shifted(frames[frame_rows - 32 :], ("tm", "mp"), 2)
     own_proj = project(frames, norm_attn, w_qkv)
-    stacked, row_of, (near, far, own_proj) = line_pieces(w_adapter, (near, far, own_proj))
+    depth_weights = w_depth.astype(jnp.float32)
+    w_adapter, own_proj = lax.optimization_barrier((w_adapter, own_proj))
     conf_out, pooled = conformer(
-        frames, own_proj, near, far, first, block_ids, valid_counts, shard_frames, norm_attn, w_qkv,
-        w_attn_out, norm_conv, w_point_in, w_depth, w_point_out,
-    )
-    pooled, stacked[0] = lax.optimization_barrier((pooled, stacked[0]))
+        frames, own_proj, near, first, block_ids, valid_counts, shard_frames, norm_attn, w_qkv,
+        w_attn_out, norm_conv, w_point_in, depth_weights, w_point_out,
+    )
+    stacked, row_of, pooled = line_pieces(w_adapter, pooled)
     piece = pooled.shape[0]
     shard_tokens = piece * mp_count
     cycle = [rotated(pooled, by) for by in range(mp_count - 1, 0, -1)] + [pooled]
     shard_pooled = lax.dynamic_slice_in_dim(
         jnp.concatenate(cycle + cycle, axis=0), (mp_count - 1 - model_place) * piece, shard_tokens, 0
     )
+    even_pooled, stacked[0] = lax.optimization_barrier((spread_even(shard_pooled), stacked[0]))
     all_pooled, near_columns = lax.optimization_barrier(
         (
-            spread(spread_even(shard_pooled)),
+            spread(even_pooled),
             [chip_adapter_columns(chunk, row_of) for chunk in stacked],
         )
     )

time: 171 us -> 159 us (0.930)
  starting transfers between devices: 61.6 us -> 56.7 us
  local copies, waits for them, and re-layouts: 18.9 us -> 15.9 us
  waiting for transfers between devices: 52.3 us -> 49.9 us
    ppermute x25, waiting for transfers between devices: 47.5 us -> 36.6 us  [swapped(): return lax.ppermute(value, 'tm', [(i, i ^ bits) for i in range(length)])]
    ppermute x2, waiting for transfers between devices: 0.01 us -> 9.22 us  [line_pieces(): upper_2 = lax.ppermute(upper, 'mp', [(2, 1), (1, 0)])]
    ppermute x25, starting transfers between devices: 26.6 us -> 23.8 us  [swapped(): return lax.ppermute(value, 'tm', [(i, i ^ bits) for i in range(length)])]
    unnamed x89 -> x77, local copies, waits for them, and re-layouts: 15 us -> 12.5 us
    ppermute x2, waiting for transfers between devices: 0.01 us -> 1.87 us  [shifted(): return lax.ppermute(value, axis, [(i, i + by) for i in range(length - by)])]
    ppermute x2, waiting for transfers between devices: 3.96 us -> 2.1 us  [line_pieces(): far = lax.ppermute(mine, 'mp', [(0, 3), (3, 0)])]
    ppermute x2, starting transfers between devices: 10.8 us -> 8.95 us  [line_pieces(): far = lax.ppermute(mine, 'mp', [(0, 3), (3, 0)])]
    pallas_call x3 -> x4, Pallas kernels: 12.7 us -> 11.5 us  [the longest x1 3.82 us: adapt(): pl.pallas_call(kernel, in_specs=[scalar] + [plain] * 4, out_specs=(plain,...]
  transfers between devices with their start and end apart: 38 -> 38, of which waited for: 19 -> 16; matrix products, arithmetic and copies ran while one was open for 8% -> 8% of each run, Pallas kernels for 8% -> 7%
where the time goes in v3:
time: 159 us; the launch traced here: 158 us
  starting transfers between devices  56.7 us (36%)
  waiting for transfers between devices  49.9 us (31%)
  Pallas kernels  23.2 us (15%)
  local copies, waits for them, and re-layouts  15.9 us (10%)
  matrix products  6.47 us (4%)
  other arithmetic  4.18 us (3%)
  between operations  1.7 us (1%)
    ppermute x25, waiting for transfers between devices, swapped(): return lax.ppermute(value, 'tm', [(i, i ^ bits) for i in range(length)])  36.6 us
    ppermute x25, starting transfers between devices, swapped(): return lax.ppermute(value, 'tm', [(i, i ^ bits) for i in range(length)])  23.8 us
    unnamed x77, local copies, waits for them, and re-layouts  12.5 us
    ppermute x2, starting transfers between devices, shifted(): return lax.ppermute(value, axis, [(i, i + by) for i in range(length - by)])  9.63 us
    ppermute x2, waiting for transfers between devices, line_pieces(): upper_2 = lax.ppermute(upper, 'mp', [(2, 1), (1, 0)])  9.22 us
    ppermute x2, starting transfers between devices, line_pieces(): far = lax.ppermute(mine, 'mp', [(0, 3), (3, 0)])  8.95 us
    ppermute x3, starting transfers between devices, rotated(): lax.ppermute(value, 'mp', [(i, (i + by) % length) for i in range(length)])  5.37 us
    pallas_call x1, Pallas kernels, attend(): pl.pallas_call(kernel, out_shape=jax.ShapeDtypeStruct((rows, count * chun...  5.34 us
  transfers between devices with their start and end apart: 38, of which 16 were waited for; matrix products, arithmetic and copies ran while one was open for 8% of the time, Pallas kernels for 7%

profile of v3, /device:TPU:0, one launch (start us, length us, event | category | flops | bytes accessed | tf_op | source)
XLA Modules:
  0.0 158.1 jit_solution(18269853887278209885)
XLA Ops:
  0.6 5.1 %collective-permute-start = (bf16[128,1024]{1,0:T(8,128)(2,1)}, bf16[128,1024]{1,0:T(8,128)(2,1)S(1)}, u32[]{:S(2)}, u32[]{:S(2)}) collective-permute-start(bf16[128,1024]{1,0:T(8,128)(2,1)} %frames_ref.1), channel_id=1, source_target_pairs={{0,1},{1,2},{2,3},{3,4},{4,5},{5,6},{6,7},{7,8},{8,9},{9,10},{10,1... | collective-permute-start | bytes 786440 | tf_op jit(solution)/shard_map/ppermute | solution.py:21
  5.7 2.8 %copy-done.2 = bf16[1024,3072]{1,0:T(8,128)(2,1)S(1)} copy-done((bf16[1024,3072]{1,0:T(8,128)(2,1)S(1)}, bf16[1024,3072]{1,0:T(8,128)(2,1)}, u32[]{:S(2)}) %copy-start.2) | copy-done | bytes 6291480
  8.5 0.9 copy-done.9
  10.2 2.1 %project.2.own_ref = bf16[128,3072]{1,0:T(8,128)(2,1)S(1)} custom-call(bf16[128,1024]{1,0:T(8,128)(2,1)S(1)} %copy-done.9, f32[1,1024]{1,0:T(1,128)S(1)} %bitcast.94, bf16[1024,3072]{1,0:T(8,128)(2,1)S(1)} %copy-done.2), custom_call_target="tpu_custom_call" | custom-call | flops 805306368 | bytes 6291456 | tf_op jit(solution)/shard_map/project/pallas_call | solution.py:163
  12.3 3.5 %collective-permute-start.2 = (bf16[128,2048]{1,0:T(8,128)(2,1)}, bf16[128,2048]{1,0:T(8,128)(2,1)S(1)}, u32[]{:S(2)}, u32[]{:S(2)}) collective-permute-start(bf16[128,2048]{1,0:T(8,128)(2,1)} %param.25), channel_id=1, source_target_pairs={{0,1},{1,2},{2,3},{4,5},{5,6},{6,7},{8,9},{9,10},{10,11},{12,13},{... | collective-permute-start | bytes 1572872 | tf_op jit(solution)/shard_map/ppermute | solution.py:356
  15.8 1.3 collective-permute-start.3
  17.1 1.1 fusion.30
  20.2 2.8 %copy-done.3 = bf16[1024,3072]{1,0:T(8,128)(2,1)S(1)} copy-done((bf16[1024,3072]{1,0:T(8,128)(2,1)S(1)}, bf16[1024,3072]{1,0:T(8,128)(2,1)}, u32[]{:S(2)}) %copy-start.3) | copy-done | bytes 6291480
  22.9 2.1 %project.3.near_ref = bf16[128,3072]{1,0:T(8,128)(2,1)S(1)} custom-call(bf16[128,1024]{1,0:T(8,128)(2,1)S(1)} %collective-permute-done.held_ref, f32[1,1024]{1,0:T(1,128)S(1)} %bitcast.95, bf16[1024,3072]{1,0:T(8,128)(2,1)S(1)} %copy-done.3), custom_call_target="tpu_custom_call" | custom-call | flops 805306368 | bytes 6291456 | tf_op jit(solution)/shard_map/project/pallas_call | solution.py:163
  25.8 3.0 %gate_frames.1 = (f32[128,1024]{1,0:T(8,128)S(1)}, bf16[128,1024]{1,0:T(8,128)(2,1)S(1)}, bf16[32,1024]{1,0:T(8,128)(2,1)S(1)}) custom-call(bf16[128,1024]{1,0:T(8,128)(2,1)S(1)} %copy-done.10, bf16[128,3072]{1,0:T(8,128)(2,1)S(1)} %project.2.own_ref, bf16[128,3072]{1,0:T(8,128)(2,1)S(1)} %project.3.near_ref, s32[3,256]{1,0:T(4,128)S(1)} %pad_add_fusion.key_row_ref, ...), custom_call_target="tpu_custom_call" | custom-call | flops 805306368 | bytes 6291456 | tf_op jit(solution)/shard_map/gate_frames/pallas_call | solution.py:253
  28.8 4.6 %collective-permute-start.1 = (bf16[32,1024]{1,0:T(8,128)(2,1)S(1)}, bf16[32,1024]{1,0:T(8,128)(2,1)S(1)}, u32[]{:S(2)}, u32[]{:S(2)}) collective-permute-start(bf16[32,1024]{1,0:T(8,128)(2,1)S(1)} %get-tuple-element.46), channel_id=1, source_target_pairs={{0,1},{1,2},{2,3},{3,4},{4,5},{5,6},{6,7},{7,8},{8,9},{9,10},{10,1... | collective-permute-start | bytes 196616 | tf_op jit(solution)/shard_map/ppermute | solution.py:21
  33.4 1.9 %collective-permute-done.1.rim_ref = bf16[32,1024]{1,0:T(8,128)(2,1)S(1)} collective-permute-done((bf16[32,1024]{1,0:T(8,128)(2,1)S(1)}, bf16[32,1024]{1,0:T(8,128)(2,1)S(1)}, u32[]{:S(2)}, u32[]{:S(2)}) %collective-permute-start.1) | collective-permute-done | bytes 65568 | tf_op jit(solution)/shard_map/ppermute | solution.py:21
  35.3 3.5 %finish_frames.1 = (bf16[128,1024]{1,0:T(8,128)(2,1)}, bf16[32,1024]{1,0:T(8,128)(2,1)S(1)}) custom-call(f32[128,1024]{1,0:T(8,128)S(1)} %get-tuple-element.44.mid_ref, bf16[128,1024]{1,0:T(8,128)(2,1)S(1)} %get-tuple-element.45.glu_ref, bf16[32,1024]{1,0:T(8,128)(2,1)S(1)} %collective-permute-done.1.rim_ref, s32[128,1]{1,0:T(8,128)S(1)} %slice.107.real_ref, ...), custom_call_target="tpu_custom_call" | custom-call | flops 268435456 | bytes 2097152 | tf_op jit(solution)/shard_map/finish_frames/pallas_call | solution.py:312
  38.8 3.2 %collective-permute-start.4 = (bf16[32,1024]{1,0:T(8,128)(2,1)S(1)}, bf16[32,1024]{1,0:T(8,128)(2,1)S(1)}, u32[]{:S(2)}, u32[]{:S(2)}) collective-permute-start(bf16[32,1024]{1,0:T(8,128)(2,1)S(1)} %get-tuple-element.50), channel_id=1, source_target_pairs={{0,3},{1,0},{2,1},{3,2},{4,7},{5,4},{6,5},{7,6},{8,11},{9,8},{10,9... | collective-permute-start | bytes 196616 | tf_op jit(solution)/shard_map/ppermute | solution.py:31
  42.7 1.6 collective-permute-start.6
  44.9 1.3 collective-permute-start.12
  46.3 4.5 %collective-permute-start.10 = (bf16[64,2048]{1,0:T(8,128)(2,1)S(1)}, bf16[64,2048]{1,0:T(8,128)(2,1)S(1)}, u32[]{:S(2)}, u32[]{:S(2)}) collective-permute-start(bf16[64,2048]{1,0:T(8,128)(2,1)S(1)} %get-tuple-element.51), channel_id=1, source_target_pairs={{0,3},{3,0},{4,7},{7,4},{8,11},{11,8},{12,15},{15,12},{16,19},{19,... | collective-permute-start | bytes 786440 | tf_op jit(solution)/shard_map/ppermute | solution.py:366
  50.9 1.5 collective-permute-start.7
  52.5 1.2 collective-permute-start.8
  53.7 0.8 collective-permute-start.9
  54.5 6.0 %collective-permute-done.12 = bf16[64,2048]{1,0:T(8,128)(2,1)S(1)} collective-permute-done((bf16[64,2048]{1,0:T(8,128)(2,1)S(1)}, bf16[64,2048]{1,0:T(8,128)(2,1)S(1)}, u32[]{:S(2)}, u32[]{:S(2)}) %collective-permute-start.12) | collective-permute-done | bytes 262176 | tf_op jit(solution)/shard_map/ppermute | solution.py:368
  60.5 4.4 %collective-permute-start.17 = (bf16[64,2048]{1,0:T(8,128)(2,1)S(1)}, bf16[64,2048]{1,0:T(8,128)(2,1)S(1)}, u32[]{:S(2)}, u32[]{:S(2)}) collective-permute-start(bf16[64,2048]{1,0:T(8,128)(2,1)S(1)} %get-tuple-element.60), channel_id=1, source_target_pairs={{0,3},{3,0},{4,7},{7,4},{8,11},{11,8},{12,15},{15,12},{16,19},{19,... | collective-permute-start | bytes 786440 | tf_op jit(solution)/shard_map/ppermute | solution.py:366
  65.9 1.5 collective-permute-start.19
  67.6 1.8 %collective-permute-start.14 = (bf16[64,2048]{1,0:T(8,128)(2,1)S(1)}, bf16[64,2048]{1,0:T(8,128)(2,1)S(1)}, u32[]{:S(2)}, u32[]{:S(2)}) collective-permute-start(bf16[64,2048]{1,0:T(8,128)(2,1)S(1)} %get-tuple-element.90), channel_id=1, source_target_pairs={{0,8},{4,12},{8,0},{12,4},{16,24},{20,28},{24,16},{28,20},{1,9},{5... | collective-permute-start | bytes 786440 | tf_op jit(solution)/shard_map/ppermute | solution.py:26
  69.5 2.1 %collective-permute-done.17 = bf16[64,2048]{1,0:T(8,128)(2,1)S(1)} collective-permute-done((bf16[64,2048]{1,0:T(8,128)(2,1)S(1)}, bf16[64,2048]{1,0:T(8,128)(2,1)S(1)}, u32[]{:S(2)}, u32[]{:S(2)}) %collective-permute-start.17) | collective-permute-done | bytes 262176 | tf_op jit(solution)/shard_map/ppermute | solution.py:366
  71.6 2.0 %collective-permute-start.16 = (bf16[64,2048]{1,0:T(8,128)(2,1)S(1)}, bf16[64,2048]{1,0:T(8,128)(2,1)S(1)}, u32[]{:S(2)}, u32[]{:S(2)}) collective-permute-start(bf16[64,2048]{1,0:T(8,128)(2,1)S(1)} %get-tuple-element.88), channel_id=1, source_target_pairs={{0,24},{4,28},{8,16},{12,20},{16,8},{20,12},{24,0},{28,4},{1,25},{... | collective-permute-start | bytes 786440 | tf_op jit(solution)/shard_map/ppermute | solution.py:26
  73.8 3.2 %collective-permute-done.19 = bf16[64,2048]{1,0:T(8,128)(2,1)S(1)} collective-permute-done((bf16[64,2048]{1,0:T(8,128)(2,1)S(1)}, bf16[64,2048]{1,0:T(8,128)(2,1)S(1)}, u32[]{:S(2)}, u32[]{:S(2)}) %collective-permute-start.19) | collective-permute-done | bytes 262176 | tf_op jit(solution)/shard_map/ppermute | solution.py:368
  77.1 1.5 collective-permute-start.20
  78.6 1.2 collective-permute-start.21
  79.8 0.9 collective-permute-start.22
  80.9 1.0 collective-permute-done.15.refs_2_
  81.9 4.4 %collective-permute-done.20.refs_5_ = bf16[64,2048]{1,0:T(8,128)(2,1)S(1)} collective-permute-done((bf16[64,2048]{1,0:T(8,128)(2,1)S(1)}, bf16[64,2048]{1,0:T(8,128)(2,1)S(1)}, u32[]{:S(2)}, u32[]{:S(2)}) %collective-permute-start.20) | collective-permute-done | bytes 262176 | tf_op jit(solution)/shard_map/ppermute | solution.py:26
  86.4 6.2 %collective-permute-done.21.refs_6_ = bf16[64,2048]{1,0:T(8,128)(2,1)S(1)} collective-permute-done((bf16[64,2048]{1,0:T(8,128)(2,1)S(1)}, bf16[64,2048]{1,0:T(8,128)(2,1)S(1)}, u32[]{:S(2)}, u32[]{:S(2)}) %collective-permute-start.21) | collective-permute-done | bytes 262176 | tf_op jit(solution)/shard_map/ppermute | solution.py:26
  92.6 1.2 halves.1
  93.7 1.0 copy-done.7
  95.9 1.8 %collective-permute-done.23.taken_ref = bf16[512,1024]{1,0:T(8,128)(2,1)} collective-permute-done((bf16[512,1024]{1,0:T(8,128)(2,1)}, bf16[512,1024]{1,0:T(8,128)(2,1)}, u32[]{:S(2)}, u32[]{:S(2)}) %collective-permute-start.23) | collective-permute-done | bytes 1048608 | tf_op jit(solution)/shard_map/ppermute | solution.py:26
  97.7 1.2 copy-done.8
  99.0 3.8 %adapt.1 = (bf16[1024,1024]{1,0:T(8,128)(2,1)S(1)}, bf16[1024,128]{1,0:T(8,128)(2,1)S(1)}) custom-call(s32[1]{0:T(128)} %bitcast.5.place_ref, bf16[512,1024]{1,0:T(8,128)(2,1)S(1)} %copy-done.8, bf16[512,1024]{1,0:T(8,128)(2,1)} %collective-permute-done.23.taken_ref, bf16[1024,1024]{1,0:T(8,128)(2,1)S(1)} %pad_maximum_fusion.pooled_ref, f32[1,1024]{1,0:T(1,128)S(1)} %bitcast.96), custom_call_target="tpu_custom_call" | custom-call | tf_op jit(solution)/shard_map/adapt/pallas_call | solution.py:437
  102.8 0.7 convolution_convert_fusion
  103.8 0.7 convolution_convert_fusion.1
  105.0 1.1 copy-done.26
  106.0 1.3 fusion.11
  107.5 0.7 pad_maximum_fusion.4.refs_4_.refs_5_
  108.2 1.3 fusion.8
  109.9 0.7 pad_maximum_fusion.5.refs_5_.refs_6_
  110.8 0.7 fusion.29
  111.9 1.4 collective-permute-start.32
  113.3 1.7 %collective-permute-start.33 = (bf16[128,640]{1,0:T(8,128)(2,1)S(1)}, bf16[128,640]{1,0:T(8,128)(2,1)S(1)}, u32[]{:S(2)}, u32[]{:S(2)}) collective-permute-start(bf16[128,640]{1,0:T(8,128)(2,1)S(1)} %get-tuple-element.94), channel_id=1, source_target_pairs={{0,24},{4,28},{8,16},{12,20},{16,8},{20,12},{24,0},{28,4},{1,25},{... | collective-permute-start | bytes 491528 | tf_op jit(solution)/shard_map/ppermute | solution.py:26
  115.0 1.3 add_convert_fusion
  116.3 1.3 add_convert_fusion.1
  117.6 1.0 collective-permute-done.31.refs_1_
  118.7 2.7 %collective-permute-done.33.refs_3_ = bf16[128,640]{1,0:T(8,128)(2,1)S(1)} collective-permute-done((bf16[128,640]{1,0:T(8,128)(2,1)S(1)}, bf16[128,640]{1,0:T(8,128)(2,1)S(1)}, u32[]{:S(2)}, u32[]{:S(2)}) %collective-permute-start.33) | collective-permute-done | bytes 163872 | tf_op jit(solution)/shard_map/ppermute | solution.py:26
  122.1 2.1 %finish_keys.1 = (bf16[128,512]{1,0:T(8,128)(2,1)}, f32[128,128]{1,0:T(8,128)}) custom-call(bf16[128,640]{1,0:T(8,128)(2,1)} %get-tuple-element.78.refs_0_, bf16[128,640]{1,0:T(8,128)(2,1)} %copy-done.18, bf16[128,640]{1,0:T(8,128)(2,1)} %copy-done.19, bf16[128,640]{1,0:T(8,128)(2,1)} %copy-done.20, f32[128,128]{1,0:T(8,128)} %pad_maximum_fusion.4.refs_4_.refs_5_, ...), custom_call_target="tpu_custom_call" | custom-call | tf_op jit(solution)/shard_map/finish_keys/pallas_call | solution.py:86
  124.2 1.7 %collective-permute-start.34 = (bf16[128,512]{1,0:T(8,128)(2,1)}, bf16[128,512]{1,0:T(8,128)(2,1)S(1)}, u32[]{:S(2)}, u32[]{:S(2)}) collective-permute-start(bf16[128,512]{1,0:T(8,128)(2,1)} %get-tuple-element.83), channel_id=1, source_target_pairs={{0,8},{4,12},{8,0},{12,4},{16,24},{20,28},{24,16},{28,20},{1,9},{5... | collective-permute-start | bytes 393224 | tf_op jit(solution)/shard_map/ppermute | solution.py:26
  126.6 1.1 collective-permute-start.36
  127.7 1.4 collective-permute-start.28
  129.2 1.1 collective-permute-start.25
  130.5 4.0 %collective-permute-done.35 = bf16[128,512]{1,0:T(8,128)(2,1)S(1)} collective-permute-done((bf16[128,512]{1,0:T(8,128)(2,1)}, bf16[128,512]{1,0:T(8,128)(2,1)S(1)}, u32[]{:S(2)}, u32[]{:S(2)}) %collective-permute-start.35) | collective-permute-done | bytes 131104 | tf_op jit(solution)/shard_map/ppermute | solution.py:26
  134.6 9.4 %collective-permute-done.28 = bf16[2,128,1024]{2,1,0:T(8,128)(2,1)S(1)} collective-permute-done((bf16[2,128,1024]{2,1,0:T(8,128)(2,1)S(1)}, bf16[2,128,1024]{2,1,0:T(8,128)(2,1)S(1)}, u32[]{:S(2)}, u32[]{:S(2)}) %collective-permute-start.28) | collective-permute-done | bytes 524320 | tf_op jit(solution)/shard_map/ppermute | solution.py:26
  144.3 1.5 collective-permute-start.29
  146.0 0.9 collective-permute-start.26
  147.0 4.0 %collective-permute-done.29.refs_3_ = bf16[128,1024]{1,0:T(8,128)(2,1)S(1)} collective-permute-done((bf16[128,1024]{1,0:T(8,128)(2,1)S(1)}, bf16[128,1024]{1,0:T(8,128)(2,1)S(1)}, u32[]{:S(2)}, u32[]{:S(2)}) %collective-permute-start.29) | collective-permute-done | bytes 262176 | tf_op jit(solution)/shard_map/ppermute | solution.py:26
  151.0 1.8 %collective-permute-done.26.refs_1_ = bf16[128,1024]{1,0:T(8,128)(2,1)S(1)} collective-permute-done((bf16[128,1024]{1,0:T(8,128)(2,1)S(1)}, bf16[128,1024]{1,0:T(8,128)(2,1)S(1)}, u32[]{:S(2)}, u32[]{:S(2)}) %collective-permute-start.26) | collective-permute-done | bytes 262176 | tf_op jit(solution)/shard_map/ppermute | solution.py:26
  152.8 5.3 %attend.1 = bf16[128,2048]{1,0:T(8,128)(2,1)} custom-call(bf16[128,1024]{1,0:T(8,128)(2,1)S(1)} %get-tuple-element.101.refs_0_, bf16[128,1024]{1,0:T(8,128)(2,1)S(1)} %collective-permute-done.26.refs_1_, bf16[128,1024]{1,0:T(8,128)(2,1)S(1)} %get-tuple-element.99.refs_2_, bf16[128,1024]{1,0:T(8,128)(2,1)S(1)} %collective-permute-done.29.refs_3_, ...), custom_call_target="tpu_custom_call" | custom-call | tf_op jit(solution)/shard_map/attend/pallas_call | solution.py:139
  (164 shorter events, 11.4 us)
Async XLA Ops:
  0.6 102.2 %copy-start = (bf16[1024,256]{1,0:T(8,128)(2,1)S(1)}, bf16[1024,256]{1,0:T(8,128)(2,1)}, u32[]{:S(2)}) copy-start(bf16[1024,256]{1,0:T(8,128)(2,1)} %param.29) | copy-start | bytes 1572868
  0.6 19.5 %collective-permute-start = (bf16[128,1024]{1,0:T(8,128)(2,1)}, bf16[128,1024]{1,0:T(8,128)(2,1)S(1)}, u32[]{:S(2)}, u32[]{:S(2)}) collective-permute-start(bf16[128,1024]{1,0:T(8,128)(2,1)} %frames_ref.1), channel_id=1, source_target_pairs={{0,1},{1,2},{2,3},{3,4},{4,5},{5,6},{6,7},{7,8},{8,9},{9,10},{10,1... | collective-permute-start | bytes 786440 | tf_op jit(solution)/shard_map/ppermute | solution.py:21
  5.7 2.8 %copy-start.2 = (bf16[1024,3072]{1,0:T(8,128)(2,1)S(1)}, bf16[1024,3072]{1,0:T(8,128)(2,1)}, u32[]{:S(2)}) copy-start(bf16[1024,3072]{1,0:T(8,128)(2,1)} %weight_ref.3) | copy-start | bytes 18874372
  8.5 0.9 copy-start.9
  10.2 8.7 %copy-start.23 = (s32[8]{0:T(128)S(1)}, s32[8]{0:T(128)}, u32[]{:S(2)}) copy-start(s32[8]{0:T(128)} %param.17) | copy-start | bytes 100
  10.2 9.4 %copy-start.22 = (s32[4096]{0:T(1024)S(1)}, s32[4096]{0:T(1024)}, u32[]{:S(2)}) copy-start(s32[4096]{0:T(1024)} %param.16) | copy-start | bytes 49156
  10.2 9.9 %copy-start.21 = (bf16[31,1024]{1,0:T(8,128)(2,1)S(1)}, bf16[31,1024]{1,0:T(8,128)(2,1)}, u32[]{:S(2)}) copy-start(bf16[31,1024]{1,0:T(8,128)(2,1)} %param.23) | copy-start | bytes 190468
  10.2 10.0 %copy-start.15 = (f32[1024]{0:T(1024)S(1)}, f32[1024]{0:T(1024)}, u32[]{:S(2)}) copy-start(f32[1024]{0:T(1024)} %param.18) | copy-start | bytes 12292
  12.3 26.5 %collective-permute-start.2 = (bf16[128,2048]{1,0:T(8,128)(2,1)}, bf16[128,2048]{1,0:T(8,128)(2,1)S(1)}, u32[]{:S(2)}, u32[]{:S(2)}) collective-permute-start(bf16[128,2048]{1,0:T(8,128)(2,1)} %param.25), channel_id=1, source_target_pairs={{0,1},{1,2},{2,3},{4,5},{5,6},{6,7},{8,9},{9,10},{10,11},{12,13},{... | collective-permute-start | bytes 1572872 | tf_op jit(solution)/shard_map/ppermute | solution.py:356
  15.8 23.0 %collective-permute-start.3 = (bf16[128,2048]{1,0:T(8,128)(2,1)}, bf16[128,2048]{1,0:T(8,128)(2,1)S(1)}, u32[]{:S(2)}, u32[]{:S(2)}) collective-permute-start(bf16[128,2048]{1,0:T(8,128)(2,1)} %param.25), channel_id=1, source_target_pairs={{1,0},{2,1},{3,2},{5,4},{6,5},{7,6},{9,8},{10,9},{11,10},{13,12},{... | collective-permute-start | bytes 1572872 | tf_op jit(solution)/shard_map/ppermute | solution.py:357
  20.1 2.8 %copy-start.3 = (bf16[1024,3072]{1,0:T(8,128)(2,1)S(1)}, bf16[1024,3072]{1,0:T(8,128)(2,1)}, u32[]{:S(2)}) copy-start(bf16[1024,3072]{1,0:T(8,128)(2,1)} %weight_ref.3) | copy-start | bytes 18874372
  22.9 2.2 %copy-start.4 = (bf16[1024,2048]{1,0:T(8,128)(2,1)S(1)}, bf16[1024,2048]{1,0:T(8,128)(2,1)}, u32[]{:S(2)}) copy-start(bf16[1024,2048]{1,0:T(8,128)(2,1)} %in_hbm.1) | copy-start | bytes 12582916
  22.9 2.9 %copy-start.5 = (bf16[1024,1024]{1,0:T(8,128)(2,1)S(1)}, bf16[1024,1024]{1,0:T(8,128)(2,1)}, u32[]{:S(2)}) copy-start(bf16[1024,1024]{1,0:T(8,128)(2,1)} %attn_hbm.1) | copy-start | bytes 6291460
  22.9 2.9 %copy-start.10 = (bf16[128,1024]{1,0:T(8,128)(2,1)S(1)}, bf16[128,1024]{1,0:T(8,128)(2,1)}, u32[]{:S(2)}) copy-start(bf16[128,1024]{1,0:T(8,128)(2,1)} %frames_ref.1) | copy-start | bytes 786436
  22.9 2.9 %copy-start.16 = (f32[1024]{0:T(1024)S(1)}, f32[1024]{0:T(1024)}, u32[]{:S(2)}) copy-start(f32[1024]{0:T(1024)} %param.21) | copy-start | bytes 12292
  25.8 9.5 %copy-start.6 = (bf16[1024,1024]{1,0:T(8,128)(2,1)S(1)}, bf16[1024,1024]{1,0:T(8,128)(2,1)}, u32[]{:S(2)}) copy-start(bf16[1024,1024]{1,0:T(8,128)(2,1)} %out_ref.1) | copy-start | bytes 6291460
  28.8 6.4 %collective-permute-start.1 = (bf16[32,1024]{1,0:T(8,128)(2,1)S(1)}, bf16[32,1024]{1,0:T(8,128)(2,1)S(1)}, u32[]{:S(2)}, u32[]{:S(2)}) collective-permute-start(bf16[32,1024]{1,0:T(8,128)(2,1)S(1)} %get-tuple-element.46), channel_id=1, source_target_pairs={{0,1},{1,2},{2,3},{3,4},{4,5},{5,6},{6,7},{7,8},{8,9},{9,10},{10,1... | collective-permute-start | bytes 196616 | tf_op jit(solution)/shard_map/ppermute | solution.py:21
  38.8 7.4 %collective-permute-start.4 = (bf16[32,1024]{1,0:T(8,128)(2,1)S(1)}, bf16[32,1024]{1,0:T(8,128)(2,1)S(1)}, u32[]{:S(2)}, u32[]{:S(2)}) collective-permute-start(bf16[32,1024]{1,0:T(8,128)(2,1)S(1)} %get-tuple-element.50), channel_id=1, source_target_pairs={{0,3},{1,0},{2,1},{3,2},{4,7},{5,4},{6,5},{7,6},{8,11},{9,8},{10,9... | collective-permute-start | bytes 196616 | tf_op jit(solution)/shard_map/ppermute | solution.py:31
  42.1 8.7 %collective-permute-start.5 = (bf16[32,1024]{1,0:T(8,128)(2,1)S(1)}, bf16[32,1024]{1,0:T(8,128)(2,1)S(1)}, u32[]{:S(2)}, u32[]{:S(2)}) collective-permute-start(bf16[32,1024]{1,0:T(8,128)(2,1)S(1)} %get-tuple-element.50), channel_id=1, source_target_pairs={{0,2},{1,3},{2,0},{3,1},{4,6},{5,7},{6,4},{7,5},{8,10},{9,11},{10,... | collective-permute-start | bytes 196616 | tf_op jit(solution)/shard_map/ppermute | solution.py:31
  42.7 8.2 %collective-permute-start.6 = (bf16[32,1024]{1,0:T(8,128)(2,1)S(1)}, bf16[32,1024]{1,0:T(8,128)(2,1)S(1)}, u32[]{:S(2)}, u32[]{:S(2)}) collective-permute-start(bf16[32,1024]{1,0:T(8,128)(2,1)S(1)} %get-tuple-element.50), channel_id=1, source_target_pairs={{0,1},{1,2},{2,3},{3,0},{4,5},{5,6},{6,7},{7,4},{8,9},{9,10},{10,1... | collective-permute-start | bytes 196616 | tf_op jit(solution)/shard_map/ppermute | solution.py:31
  44.2 9.5 %collective-permute-start.11 = (bf16[64,2048]{1,0:T(8,128)(2,1)S(1)}, bf16[64,2048]{1,0:T(8,128)(2,1)S(1)}, u32[]{:S(2)}, u32[]{:S(2)}) collective-permute-start(bf16[64,2048]{1,0:T(8,128)(2,1)S(1)} %slice.84), channel_id=1, source_target_pairs={{1,2},{2,3},{5,6},{6,7},{9,10},{10,11},{13,14},{14,15},{17,18},{18... | collective-permute-start | bytes 786440 | tf_op jit(solution)/shard_map/ppermute | solution.py:367
  44.9 15.6 %collective-permute-start.12 = (bf16[64,2048]{1,0:T(8,128)(2,1)S(1)}, bf16[64,2048]{1,0:T(8,128)(2,1)S(1)}, u32[]{:S(2)}, u32[]{:S(2)}) collective-permute-start(bf16[64,2048]{1,0:T(8,128)(2,1)S(1)} %slice.85), channel_id=1, source_target_pairs={{2,1},{1,0},{6,5},{5,4},{10,9},{9,8},{14,13},{13,12},{18,17},{17,1... | collective-permute-start | bytes 786440 | tf_op jit(solution)/shard_map/ppermute | solution.py:368
  46.3 14.3 %collective-permute-start.10 = (bf16[64,2048]{1,0:T(8,128)(2,1)S(1)}, bf16[64,2048]{1,0:T(8,128)(2,1)S(1)}, u32[]{:S(2)}, u32[]{:S(2)}) collective-permute-start(bf16[64,2048]{1,0:T(8,128)(2,1)S(1)} %get-tuple-element.51), channel_id=1, source_target_pairs={{0,3},{3,0},{4,7},{7,4},{8,11},{11,8},{12,15},{15,12},{16,19},{19,... | collective-permute-start | bytes 786440 | tf_op jit(solution)/shard_map/ppermute | solution.py:366
  50.9 15.0 %collective-permute-start.7 = (bf16[128,1024]{1,0:T(8,128)(2,1)S(1)}, bf16[128,1024]{1,0:T(8,128)(2,1)S(1)}, u32[]{:S(2)}, u32[]{:S(2)}) collective-permute-start(bf16[128,1024]{1,0:T(8,128)(2,1)S(1)} %constant_dynamic-slice_fusion), channel_id=1, source_target_pairs={{0,8},{4,12},{8,0},{12,4},{16,24},{20,28},{24,16},{28,20},{1,9},{5... | collective-permute-start | bytes 786440 | tf_op jit(solution)/shard_map/ppermute | solution.py:26
  52.5 14.9 %collective-permute-start.8 = (bf16[128,1024]{1,0:T(8,128)(2,1)S(1)}, bf16[128,1024]{1,0:T(8,128)(2,1)S(1)}, u32[]{:S(2)}, u32[]{:S(2)}) collective-permute-start(bf16[128,1024]{1,0:T(8,128)(2,1)S(1)} %constant_dynamic-slice_fusion), channel_id=1, source_target_pairs={{0,16},{4,20},{8,24},{12,28},{16,0},{20,4},{24,8},{28,12},{1,17},{... | collective-permute-start | bytes 786440 | tf_op jit(solution)/shard_map/ppermute | solution.py:26
  53.7 13.7 %collective-permute-start.9 = (bf16[128,1024]{1,0:T(8,128)(2,1)S(1)}, bf16[128,1024]{1,0:T(8,128)(2,1)S(1)}, u32[]{:S(2)}, u32[]{:S(2)}) collective-permute-start(bf16[128,1024]{1,0:T(8,128)(2,1)S(1)} %constant_dynamic-slice_fusion), channel_id=1, source_target_pairs={{0,24},{4,28},{8,16},{12,20},{16,8},{20,12},{24,0},{28,4},{1,25},{... | collective-permute-start | bytes 786440 | tf_op jit(solution)/shard_map/ppermute | solution.py:26
  60.5 11.0 %collective-permute-start.17 = (bf16[64,2048]{1,0:T(8,128)(2,1)S(1)}, bf16[64,2048]{1,0:T(8,128)(2,1)S(1)}, u32[]{:S(2)}, u32[]{:S(2)}) collective-permute-start(bf16[64,2048]{1,0:T(8,128)(2,1)S(1)} %get-tuple-element.60), channel_id=1, source_target_pairs={{0,3},{3,0},{4,7},{7,4},{8,11},{11,8},{12,15},{15,12},{16,19},{19,... | collective-permute-start | bytes 786440 | tf_op jit(solution)/shard_map/ppermute | solution.py:366
  65.0 8.6 %collective-permute-start.18 = (bf16[64,2048]{1,0:T(8,128)(2,1)S(1)}, bf16[64,2048]{1,0:T(8,128)(2,1)S(1)}, u32[]{:S(2)}, u32[]{:S(2)}) collective-permute-start(bf16[64,2048]{1,0:T(8,128)(2,1)S(1)} %slice.86), channel_id=1, source_target_pairs={{1,2},{2,3},{5,6},{6,7},{9,10},{10,11},{13,14},{14,15},{17,18},{18... | collective-permute-start | bytes 786440 | tf_op jit(solution)/shard_map/ppermute | solution.py:367
  65.9 11.1 %collective-permute-start.19 = (bf16[64,2048]{1,0:T(8,128)(2,1)S(1)}, bf16[64,2048]{1,0:T(8,128)(2,1)S(1)}, u32[]{:S(2)}, u32[]{:S(2)}) collective-permute-start(bf16[64,2048]{1,0:T(8,128)(2,1)S(1)} %slice.87), channel_id=1, source_target_pairs={{2,1},{1,0},{6,5},{5,4},{10,9},{9,8},{14,13},{13,12},{18,17},{17,1... | collective-permute-start | bytes 786440 | tf_op jit(solution)/shard_map/ppermute | solution.py:368
  67.6 11.0 %collective-permute-start.14 = (bf16[64,2048]{1,0:T(8,128)(2,1)S(1)}, bf16[64,2048]{1,0:T(8,128)(2,1)S(1)}, u32[]{:S(2)}, u32[]{:S(2)}) collective-permute-start(bf16[64,2048]{1,0:T(8,128)(2,1)S(1)} %get-tuple-element.90), channel_id=1, source_target_pairs={{0,8},{4,12},{8,0},{12,4},{16,24},{20,28},{24,16},{28,20},{1,9},{5... | collective-permute-start | bytes 786440 | tf_op jit(solution)/shard_map/ppermute | solution.py:26
  69.4 12.5 %collective-permute-start.15 = (bf16[64,2048]{1,0:T(8,128)(2,1)S(1)}, bf16[64,2048]{1,0:T(8,128)(2,1)S(1)}, u32[]{:S(2)}, u32[]{:S(2)}) collective-permute-start(bf16[64,2048]{1,0:T(8,128)(2,1)S(1)} %get-tuple-element.89), channel_id=1, source_target_pairs={{0,16},{4,20},{8,24},{12,28},{16,0},{20,4},{24,8},{28,12},{1,17},{... | collective-permute-start | bytes 786440 | tf_op jit(solution)/shard_map/ppermute | solution.py:26
  71.6 10.4 %collective-permute-start.16 = (bf16[64,2048]{1,0:T(8,128)(2,1)S(1)}, bf16[64,2048]{1,0:T(8,128)(2,1)S(1)}, u32[]{:S(2)}, u32[]{:S(2)}) collective-permute-start(bf16[64,2048]{1,0:T(8,128)(2,1)S(1)} %get-tuple-element.88), channel_id=1, source_target_pairs={{0,24},{4,28},{8,16},{12,20},{16,8},{20,12},{24,0},{28,4},{1,25},{... | collective-permute-start | bytes 786440 | tf_op jit(solution)/shard_map/ppermute | solution.py:26
  73.6 6.2 %collective-permute-start.13 = (bf16[512,1024]{1,0:T(8,128)(2,1)S(1)}, bf16[512,1024]{1,0:T(8,128)(2,1)S(1)}, u32[]{:S(2)}, u32[]{:S(2)}) collective-permute-start(bf16[512,1024]{1,0:T(8,128)(2,1)S(1)} %pad_maximum_fusion.2), channel_id=1, source_target_pairs={{0,4},{4,0},{8,12},{12,8},{16,20},{20,16},{24,28},{28,24},{1,5},{5... | collective-permute-start | bytes 3145736 | tf_op jit(solution)/shard_map/ppermute | solution.py:26
  77.1 9.2 %collective-permute-start.20 = (bf16[64,2048]{1,0:T(8,128)(2,1)S(1)}, bf16[64,2048]{1,0:T(8,128)(2,1)S(1)}, u32[]{:S(2)}, u32[]{:S(2)}) collective-permute-start(bf16[64,2048]{1,0:T(8,128)(2,1)S(1)} %get-tuple-element.86), channel_id=1, source_target_pairs={{0,8},{4,12},{8,0},{12,4},{16,24},{20,28},{24,16},{28,20},{1,9},{5... | collective-permute-start | bytes 786440 | tf_op jit(solution)/shard_map/ppermute | solution.py:26
  78.6 14.0 %collective-permute-start.21 = (bf16[64,2048]{1,0:T(8,128)(2,1)S(1)}, bf16[64,2048]{1,0:T(8,128)(2,1)S(1)}, u32[]{:S(2)}, u32[]{:S(2)}) collective-permute-start(bf16[64,2048]{1,0:T(8,128)(2,1)S(1)} %get-tuple-element.85), channel_id=1, source_target_pairs={{0,16},{4,20},{8,24},{12,28},{16,0},{20,4},{24,8},{28,12},{1,17},{... | collective-permute-start | bytes 786440 | tf_op jit(solution)/shard_map/ppermute | solution.py:26
  79.8 12.8 %collective-permute-start.22 = (bf16[64,2048]{1,0:T(8,128)(2,1)S(1)}, bf16[64,2048]{1,0:T(8,128)(2,1)S(1)}, u32[]{:S(2)}, u32[]{:S(2)}) collective-permute-start(bf16[64,2048]{1,0:T(8,128)(2,1)S(1)} %get-tuple-element.84), channel_id=1, source_target_pairs={{0,24},{4,28},{8,16},{12,20},{16,8},{20,12},{24,0},{28,4},{1,25},{... | collective-permute-start | bytes 786440 | tf_op jit(solution)/shard_map/ppermute | solution.py:26
  80.9 14.7 %copy-start.24 = (f32[64]{0:T(128)S(1)}, f32[64]{0:T(128)}, u32[]{:S(2)}) copy-start(f32[64]{0:T(128)} %multiply_power_fusion) | copy-start | bytes 772
  80.9 14.7 %copy-start.25 = (f32[128]{0:T(128)S(1)}, f32[128]{0:T(128)}, u32[]{:S(2)}) copy-start(f32[128]{0:T(128)} %get-tuple-element.108) | copy-start | bytes 1540
  93.7 1.0 copy-start.7
  94.7 3.0 %collective-permute-start.23 = (bf16[512,1024]{1,0:T(8,128)(2,1)}, bf16[512,1024]{1,0:T(8,128)(2,1)}, u32[]{:S(2)}, u32[]{:S(2)}) collective-permute-start(bf16[512,1024]{1,0:T(8,128)(2,1)} %get-tuple-element.72), channel_id=1, source_target_pairs={{0,4},{4,0},{8,12},{12,8},{16,20},{20,16},{24,28},{28,24},{1,5},{5... | collective-permute-start | bytes 3145736 | tf_op jit(solution)/shard_map/ppermute | solution.py:26
  97.7 1.2 copy-start.8
  102.8 1.0 copy-start.27
  103.8 2.2 %copy-start.26 = (bf16[1024,2048]{1,0:T(8,128)(2,1)S(1)}, bf16[1024,2048]{1,0:T(8,128)(2,1)}, u32[]{:S(2)}) copy-start(bf16[1024,2048]{1,0:T(8,128)(2,1)} %param.27) | copy-start | bytes 12582916
  104.8 5.9 %collective-permute-start.30 = (bf16[512,640]{1,0:T(8,128)(2,1)S(1)}, bf16[512,640]{1,0:T(8,128)(2,1)S(1)}, u32[]{:S(2)}, u32[]{:S(2)}) collective-permute-start(bf16[512,640]{1,0:T(8,128)(2,1)S(1)} %slice.101), channel_id=1, source_target_pairs={{0,4},{4,0},{8,12},{12,8},{16,20},{20,16},{24,28},{28,24},{1,5},{5... | collective-permute-start | bytes 1966088 | tf_op jit(solution)/shard_map/ppermute | solution.py:26
  107.3 7.7 %collective-permute-start.27 = (bf16[512,1024]{1,0:T(8,128)(2,1)S(1)}, bf16[512,1024]{1,0:T(8,128)(2,1)S(1)}, u32[]{:S(2)}, u32[]{:S(2)}) collective-permute-start(bf16[512,1024]{1,0:T(8,128)(2,1)S(1)} %fusion.11), channel_id=1, source_target_pairs={{0,4},{4,0},{8,12},{12,8},{16,20},{20,16},{24,28},{28,24},{1,5},{5... | collective-permute-start | bytes 3145736 | tf_op jit(solution)/shard_map/ppermute | solution.py:26
  109.5 6.8 %collective-permute-start.24 = (bf16[512,1024]{1,0:T(8,128)(2,1)S(1)}, bf16[512,1024]{1,0:T(8,128)(2,1)S(1)}, u32[]{:S(2)}, u32[]{:S(2)}) collective-permute-start(bf16[512,1024]{1,0:T(8,128)(2,1)S(1)} %fusion.8), channel_id=1, source_target_pairs={{0,4},{4,0},{8,12},{12,8},{16,20},{20,16},{24,28},{28,24},{1,5},{5... | collective-permute-start | bytes 3145736 | tf_op jit(solution)/shard_map/ppermute | solution.py:26
  111.5 7.0 %collective-permute-start.31 = (bf16[128,640]{1,0:T(8,128)(2,1)S(1)}, bf16[128,640]{1,0:T(8,128)(2,1)S(1)}, u32[]{:S(2)}, u32[]{:S(2)}) collective-permute-start(bf16[128,640]{1,0:T(8,128)(2,1)S(1)} %get-tuple-element.96), channel_id=1, source_target_pairs={{0,8},{4,12},{8,0},{12,4},{16,24},{20,28},{24,16},{28,20},{1,9},{5... | collective-permute-start | bytes 491528 | tf_op jit(solution)/shard_map/ppermute | solution.py:26
  111.9 6.8 %collective-permute-start.32 = (bf16[128,640]{1,0:T(8,128)(2,1)S(1)}, bf16[128,640]{1,0:T(8,128)(2,1)S(1)}, u32[]{:S(2)}, u32[]{:S(2)}) collective-permute-start(bf16[128,640]{1,0:T(8,128)(2,1)S(1)} %get-tuple-element.95), channel_id=1, source_target_pairs={{0,16},{4,20},{8,24},{12,28},{16,0},{20,4},{24,8},{28,12},{1,17},{... | collective-permute-start | bytes 491528 | tf_op jit(solution)/shard_map/ppermute | solution.py:26
  113.3 8.1 %collective-permute-start.33 = (bf16[128,640]{1,0:T(8,128)(2,1)S(1)}, bf16[128,640]{1,0:T(8,128)(2,1)S(1)}, u32[]{:S(2)}, u32[]{:S(2)}) collective-permute-start(bf16[128,640]{1,0:T(8,128)(2,1)S(1)} %get-tuple-element.94), channel_id=1, source_target_pairs={{0,24},{4,28},{8,16},{12,20},{16,8},{20,12},{24,0},{28,4},{1,25},{... | collective-permute-start | bytes 491528 | tf_op jit(solution)/shard_map/ppermute | solution.py:26
  118.6 2.8 %copy-start.18 = (bf16[128,640]{1,0:T(8,128)(2,1)}, bf16[128,640]{1,0:T(8,128)(2,1)S(1)}, u32[]{:S(2)}) copy-start(bf16[128,640]{1,0:T(8,128)(2,1)S(1)} %collective-permute-done.31.refs_1_) | copy-start | bytes 491524
  118.7 2.7 %copy-start.19 = (bf16[128,640]{1,0:T(8,128)(2,1)}, bf16[128,640]{1,0:T(8,128)(2,1)S(1)}, u32[]{:S(2)}) copy-start(bf16[128,640]{1,0:T(8,128)(2,1)S(1)} %collective-permute-done.32.refs_2_) | copy-start | bytes 491524
  124.2 6.1 %copy-start.17 = (bf16[128,512]{1,0:T(8,128)(2,1)S(1)}, bf16[128,512]{1,0:T(8,128)(2,1)}, u32[]{:S(2)}) copy-start(bf16[128,512]{1,0:T(8,128)(2,1)} %get-tuple-element.83) | copy-start | bytes 393220
  124.2 6.3 %collective-permute-start.34 = (bf16[128,512]{1,0:T(8,128)(2,1)}, bf16[128,512]{1,0:T(8,128)(2,1)S(1)}, u32[]{:S(2)}, u32[]{:S(2)}) collective-permute-start(bf16[128,512]{1,0:T(8,128)(2,1)} %get-tuple-element.83), channel_id=1, source_target_pairs={{0,8},{4,12},{8,0},{12,4},{16,24},{20,28},{24,16},{28,20},{1,9},{5... | collective-permute-start | bytes 393224 | tf_op jit(solution)/shard_map/ppermute | solution.py:26
  125.9 8.6 %collective-permute-start.35 = (bf16[128,512]{1,0:T(8,128)(2,1)}, bf16[128,512]{1,0:T(8,128)(2,1)S(1)}, u32[]{:S(2)}, u32[]{:S(2)}) collective-permute-start(bf16[128,512]{1,0:T(8,128)(2,1)} %get-tuple-element.83), channel_id=1, source_target_pairs={{0,16},{4,20},{8,24},{12,28},{16,0},{20,4},{24,8},{28,12},{1,17},{... | collective-permute-start | bytes 393224 | tf_op jit(solution)/shard_map/ppermute | solution.py:26
  126.6 7.9 %collective-permute-start.36 = (bf16[128,512]{1,0:T(8,128)(2,1)}, bf16[128,512]{1,0:T(8,128)(2,1)S(1)}, u32[]{:S(2)}, u32[]{:S(2)}) collective-permute-start(bf16[128,512]{1,0:T(8,128)(2,1)} %get-tuple-element.83), channel_id=1, source_target_pairs={{0,24},{4,28},{8,16},{12,20},{16,8},{20,12},{24,0},{28,4},{1,25},{... | collective-permute-start | bytes 393224 | tf_op jit(solution)/shard_map/ppermute | solution.py:26
  127.7 16.3 %collective-permute-start.28 = (bf16[2,128,1024]{2,1,0:T(8,128)(2,1)S(1)}, bf16[2,128,1024]{2,1,0:T(8,128)(2,1)S(1)}, u32[]{:S(2)}, u32[]{:S(2)}) collective-permute-start(bf16[2,128,1024]{2,1,0:T(8,128)(2,1)S(1)} %bitcast.102), channel_id=1, source_target_pairs={{0,16},{4,20},{8,24},{12,28},{16,0},{20,4},{24,8},{28,12},{1,17},{... | collective-permute-start | bytes 1572872 | tf_op jit(solution)/shard_map/ppermute | solution.py:26
  129.2 16.6 %collective-permute-start.25 = (bf16[2,128,1024]{2,1,0:T(8,128)(2,1)S(1)}, bf16[2,128,1024]{2,1,0:T(8,128)(2,1)S(1)}, u32[]{:S(2)}, u32[]{:S(2)}) collective-permute-start(bf16[2,128,1024]{2,1,0:T(8,128)(2,1)S(1)} %slice_bitcast_fusion), channel_id=1, source_target_pairs={{0,8},{4,12},{8,0},{12,4},{16,24},{20,28},{24,16},{28,20},{1,9},{5... | collective-permute-start | bytes 1572872 | tf_op jit(solution)/shard_map/ppermute | solution.py:26
  134.5 12.4 %collective-permute-start.37 = (bf16[512,512]{1,0:T(8,128)(2,1)S(1)}, bf16[512,512]{1,0:T(8,128)(2,1)S(1)}, u32[]{:S(2)}, u32[]{:S(2)}) collective-permute-start(bf16[512,512]{1,0:T(8,128)(2,1)S(1)} %pad_maximum_fusion.3), channel_id=1, source_target_pairs={{0,4},{4,0},{8,12},{12,8},{16,20},{20,16},{24,28},{28,24},{1,5},{5... | collective-permute-start | bytes 1572872 | tf_op jit(solution)/shard_map/ppermute | solution.py:26
  144.2 8.5 %copy-start.11 = (f32[128,128]{1,0:T(8,128)S(1)}, f32[128,128]{1,0:T(8,128)}, u32[]{:S(2)}) copy-start(f32[128,128]{1,0:T(8,128)} %pad_maximum_fusion.5.refs_5_.refs_6_) | copy-start | bytes 196612
  144.2 8.5 %copy-start.12 = (f32[128,128]{1,0:T(8,128)S(1)}, f32[128,128]{1,0:T(8,128)}, u32[]{:S(2)}) copy-start(f32[128,128]{1,0:T(8,128)} %pad_maximum_fusion.4.refs_4_.refs_5_) | copy-start | bytes 196612
  144.3 8.5 %copy-start.13 = (f32[128,128]{1,0:T(8,128)S(1)}, f32[128,128]{1,0:T(8,128)}, u32[]{:S(2)}) copy-start(f32[128,128]{1,0:T(8,128)} %get-tuple-element.82.refs_4_) | copy-start | bytes 196612
  144.3 6.7 %collective-permute-start.29 = (bf16[128,1024]{1,0:T(8,128)(2,1)S(1)}, bf16[128,1024]{1,0:T(8,128)(2,1)S(1)}, u32[]{:S(2)}, u32[]{:S(2)}) collective-permute-start(bf16[128,1024]{1,0:T(8,128)(2,1)S(1)} %get-tuple-element.98), channel_id=1, source_target_pairs={{0,8},{4,12},{8,0},{12,4},{16,24},{20,28},{24,16},{28,20},{1,9},{5... | collective-permute-start | bytes 786440 | tf_op jit(solution)/shard_map/ppermute | solution.py:26
  146.0 6.7 %collective-permute-start.26 = (bf16[128,1024]{1,0:T(8,128)(2,1)S(1)}, bf16[128,1024]{1,0:T(8,128)(2,1)S(1)}, u32[]{:S(2)}, u32[]{:S(2)}) collective-permute-start(bf16[128,1024]{1,0:T(8,128)(2,1)S(1)} %get-tuple-element.100), channel_id=1, source_target_pairs={{0,16},{4,20},{8,24},{12,28},{16,0},{20,4},{24,8},{28,12},{1,17},{... | collective-permute-start | bytes 786440 | tf_op jit(solution)/shard_map/ppermute | solution.py:26
  146.9 11.2 %copy-start.1 = (bf16[1024,256]{1,0:T(8,128)(2,1)S(1)}, bf16[1024,256]{1,0:T(8,128)(2,1)}, u32[]{:S(2)}) copy-start(bf16[1024,256]{1,0:T(8,128)(2,1)} %param.29) | copy-start | bytes 1572868
  (2 other events, 1.3 us)

commit v4 on v3

--- a/solution.py
+++ b/solution.py
@@ -144,52 +144,41 @@
     )(*flat, scale, cosine, sine, query_place, key_place, key_real, kv)
 
 
-def project(held, gain, w_qkv):
-    rows, width = held.shape
+def project(near, frames, gain, w_qkv):
+    rows, width = frames.shape
+    both = near.shape[0] + rows
     wide = w_qkv.shape[1]
-    step = width
-
-    def kernel(held_ref, gain_ref, weight_ref, out_ref, normed_ref):
-        @pl.when(pl.program_id(0) == 0)
-        def _():
-            normed_ref[...] = layer_norm(held_ref[...].astype(jnp.float32), gain_ref[...]).astype(
-                jnp.bfloat16
-            )
-
-        out_ref[...] = jnp.dot(
-            normed_ref[...], weight_ref[...], preferred_element_type=jnp.float32
-        ).astype(jnp.bfloat16)
+
+    def kernel(near_ref, frames_ref, gain_ref, weight_ref, out_ref):
+        held = jnp.concatenate([near_ref[...], frames_ref[...]], axis=0).astype(jnp.float32)
+        normed = layer_norm(held, gain_ref[...]).astype(jnp.bfloat16)
+        for start in range(0, wide, width):
+            columns = pl.ds(start, width)
+            out_ref[:, columns] = jnp.dot(
+                normed, weight_ref[:, columns], preferred_element_type=jnp.float32
+            ).astype(jnp.bfloat16)
 
     return pl.pallas_call(
         kernel,
-        grid=(wide // step,),
-        in_specs=[
-            pl.BlockSpec((rows, width), lambda i: (0, 0)),
-            pl.BlockSpec((1, width), lambda i: (0, 0)),
-            pl.BlockSpec((width, step), lambda i: (0, i)),
-        ],
-        out_specs=pl.BlockSpec((rows, step), lambda i: (0, i)),
-        out_shape=jax.ShapeDtypeStruct((rows, wide), jnp.bfloat16),
-        scratch_shapes=[pltpu.VMEM((rows, width), jnp.bfloat16)],
-        compiler_params=pltpu.CompilerParams(vmem_limit_bytes=12 << 20),
+        out_shape=jax.ShapeDtypeStruct((both, wide), jnp.bfloat16),
+        compiler_params=pltpu.CompilerParams(vmem_limit_bytes=16 << 20),
         cost_estimate=pl.CostEstimate(
-            flops=2 * rows * width * wide, bytes_accessed=2 * width * wide, transcendentals=0
+            flops=2 * both * width * wide, bytes_accessed=2 * width * wide, transcendentals=0
         ),
         name="project",
-    )(held, gain[None, :], w_qkv)
+    )(near, frames, gain[None, :], w_qkv)
 
 
 def gate_frames(
-    frames, own_proj, near_proj, key_row, query_col, w_attn_out, norm_conv, w_point_in, tail_rows
+    frames, proj, key_row, query_col, w_attn_out, norm_conv, w_point_in, tail_rows
 ):
     frame_rows, width = frames.shape
-    near_rows = near_proj.shape[0]
-    key_rows = near_rows + frame_rows
+    key_rows = proj.shape[0]
     head_size = width // CH
     lanes = 2 * head_size
 
     def kernel(
-        frames_ref, own_ref, near_ref, key_row_ref, query_col_ref, gain_ref, attn_hbm, in_hbm,
+        frames_ref, proj_ref, key_row_ref, query_col_ref, gain_ref, attn_hbm, in_hbm,
         mid_ref, glu_ref, tail_ref, attn_w, in_w, context_ref, sems,
     ):
         copies = [
@@ -208,9 +197,9 @@
 
             def both_rows(offset):
                 columns = pl.ds(offset + pair * lanes, lanes)
-                return jnp.concatenate([near_ref[:, columns], own_ref[:, columns]], axis=0)
-
-            query = own_ref[:, pl.ds(pair * lanes, lanes)]
+                return proj_ref[:, columns]
+
+            query = proj_ref[key_rows - frame_rows :, pl.ds(pair * lanes, lanes)]
             none = jnp.zeros_like(query)
             query = jnp.concatenate(
                 [jnp.where(left, query, none), jnp.where(left, none, query)], axis=0
@@ -249,10 +238,10 @@
             tail_ref[:, pl.ds(start, part)] = glu[frame_rows - tail_rows :]
 
     plain = pl.BlockSpec(memory_space=pltpu.VMEM)
-    apart = pl.BlockSpec(memory_space=pl.ANY)
+    apart = pl.BlockSpec(memory_space=pltpu.HBM)
     return pl.pallas_call(
         kernel,
-        in_specs=[plain] * 6 + [apart] * 2,
+        in_specs=[plain] * 5 + [apart] * 2,
         out_specs=(plain, plain, plain),
         out_shape=(
             jax.ShapeDtypeStruct((frame_rows, width), jnp.float32),
@@ -273,30 +262,59 @@
         ),
         name="gate_frames",
     )(
-        frames, own_proj, near_proj, key_row, query_col, norm_conv[None, :], w_attn_out, w_point_in
-    )
-
-
-def finish_frames(mid, glu, rim, real_col, depth_weights, w_point_out):
+        frames, proj, key_row, query_col, norm_conv[None, :], w_attn_out, w_point_in
+    )
+
+
+def convolve_late(glu, depth_weights, extra):
+    frame_rows, width = glu.shape
+    taps = depth_weights.shape[0]
+    late = frame_rows - extra
+
+    def kernel(glu_ref, depth_ref, out_ref, held_ref):
+        held_ref[...] = glu_ref[...].astype(jnp.float32)
+        for start in range(0, width, 128):
+            columns = pl.ds(start, 128)
+            depth = jnp.zeros((late, 128), jnp.float32)
+            for tap in range(taps):
+                depth = depth + depth_ref[tap : tap + 1, columns] * held_ref[
+                    pl.ds(extra - tap, late), columns
+                ]
+            out_ref[:, columns] = jax.nn.silu(depth).astype(jnp.bfloat16)
+
+    return pl.pallas_call(
+        kernel,
+        out_shape=jax.ShapeDtypeStruct((late, width), jnp.bfloat16),
+        scratch_shapes=[pltpu.VMEM((frame_rows, width), jnp.float32)],
+        compiler_params=pltpu.CompilerParams(vmem_limit_bytes=8 << 20),
+        cost_estimate=pl.CostEstimate(
+            flops=2 * taps * late * width, bytes_accessed=4 * late * width, transcendentals=0
+        ),
+        name="convolve_late",
+    )(glu, depth_weights)
+
+
+def finish_frames(mid, glu, active, rim, real_col, depth_weights, w_point_out):
     frame_rows, width = mid.shape
     extra = rim.shape[0]
     pooled_rows = frame_rows // 4
     taps = depth_weights.shape[0]
 
     def kernel(
-        mid_ref, glu_ref, rim_ref, real_ref, depth_ref, out_ref, conf_ref, pooled_ref, held_ref,
-        active_ref,
+        mid_ref, glu_ref, late_ref, rim_ref, real_ref, depth_ref, out_ref, conf_ref, pooled_ref,
+        held_ref, active_ref,
     ):
         held_ref[:extra] = rim_ref[...].astype(jnp.float32)
-        held_ref[extra:] = glu_ref[...].astype(jnp.float32)
+        held_ref[extra:] = glu_ref[:extra].astype(jnp.float32)
+        active_ref[extra:] = late_ref[...]
         for start in range(0, width, 128):
             columns = pl.ds(start, 128)
-            depth = jnp.zeros((frame_rows, 128), jnp.float32)
+            depth = jnp.zeros((extra, 128), jnp.float32)
             for tap in range(taps):
                 depth = depth + depth_ref[tap : tap + 1, columns] * held_ref[
-                    pl.ds(extra - tap, frame_rows), columns
+                    pl.ds(extra - tap, extra), columns
                 ]
-            active_ref[:, columns] = jax.nn.silu(depth).astype(jnp.bfloat16)
+            active_ref[:extra, columns] = jax.nn.silu(depth).astype(jnp.bfloat16)
         final = mid_ref[...] + jnp.dot(
             active_ref[...], out_ref[...], preferred_element_type=jnp.float32
         )
@@ -316,7 +334,7 @@
             jax.ShapeDtypeStruct((pooled_rows, width), jnp.bfloat16),
         ),
         scratch_shapes=[
-            pltpu.VMEM((extra + frame_rows, width), jnp.float32),
+            pltpu.VMEM((2 * extra, width), jnp.float32),
             pltpu.VMEM((frame_rows, width), jnp.bfloat16),
         ],
         compiler_params=pltpu.CompilerParams(vmem_limit_bytes=8 << 20),
@@ -324,16 +342,16 @@
             flops=2 * frame_rows * width * width, bytes_accessed=2 * width * width, transcendentals=0
         ),
         name="finish_frames",
-    )(mid, glu, rim, real_col, depth_weights, w_point_out)
+    )(mid, glu, active, rim, real_col, depth_weights, w_point_out)
 
 
 def conformer(
-    frames, own_proj, near, first, block_ids, valid_counts, shard_frames, norm_attn, w_qkv,
+    frames, near, first, block_ids, valid_counts, shard_frames, norm_attn, w_qkv,
     w_attn_out, norm_conv, w_point_in, depth_weights, w_point_out,
 ):
     before = near.shape[0]
     key_rows = before + frames.shape[0]
-    near_proj = project(near, norm_attn, w_qkv)
+    proj = project(near, frames, norm_attn, w_qkv)
     key_index = first - before + jnp.arange(key_rows, dtype=jnp.int32)
     key_place, key_count = shard_count(key_index, valid_counts, shard_frames)
     key_real = (key_place < key_count) & (key_index >= 0)
@@ -342,10 +360,11 @@
     key_row = jnp.stack([key_index, key_ids, key_real.astype(jnp.int32)])
     query_col = jnp.transpose(key_row[:, before:])
     mid, glu, tail = gate_frames(
-        frames, own_proj, near_proj, key_row, query_col, w_attn_out, norm_conv, w_point_in, 32
+        frames, proj, key_row, query_col, w_attn_out, norm_conv, w_point_in, 32
     )
     rim = shifted(tail, ("tm", "mp"), 1)
-    return finish_frames(mid, glu, rim, query_col[:, 2:3], depth_weights, w_point_out)
+    active = convolve_late(glu, depth_weights, 32)
+    return finish_frames(mid, glu, active, rim, query_col[:, 2:3], depth_weights, w_point_out)
 
 
 def line_pieces(value, beside):
@@ -385,7 +404,7 @@
     return kept
 
 
-def adapt(pooled, near, gain):
+def adapt(pooled, near, gain, w_key, w_value):
     tm_count, time_place = lax.axis_size("tm"), lax.axis_index("tm")
     part, cols = near[0][0].shape
     half = cols // 2
@@ -410,10 +429,11 @@
         name="halves",
     )(place_word, *flat)
     taken = swapped(given, 1)
-    step = min(256, tokens)
+    step, key_cols = min(256, tokens), w_key.shape[1]
 
     def kernel(
-        place_ref, mine_ref, taken_ref, pooled_ref, gain_ref, out_ref, word_ref, weight_ref
+        place_ref, mine_ref, taken_ref, pooled_ref, gain_ref, key_ref, value_ref, out_ref, kv_ref,
+        weight_ref,
     ):
         place = place_ref[0]
         for i in range(len(flat)):
@@ -428,24 +448,29 @@
             adapted = jnp.dot(
                 pooled_ref[rows, :], weight_ref[...], preferred_element_type=jnp.float32
             )
-            out_ref[rows, :] = (adapted * gain_ref[...]).astype(jnp.bfloat16)
+            scaled = (adapted * gain_ref[...]).astype(jnp.bfloat16)
+            out_ref[rows, :] = scaled
+            for i, ref in enumerate((key_ref, value_ref)):
+                kv_ref[rows, pl.ds(i * key_cols, key_cols)] = jnp.dot(
+                    scaled, ref[...], preferred_element_type=jnp.float32
+                ).astype(jnp.bfloat16)
             squares = jnp.sum(adapted * adapted, axis=-1, keepdims=True)
             high = squares.astype(jnp.bfloat16).astype(jnp.float32)
             words = jnp.where(lane == 0, high, jnp.where(lane == 1, squares - high, 0.0))
-            word_ref[rows, :] = words.astype(jnp.bfloat16)
+            kv_ref[rows, pl.ds(2 * key_cols, HDIM)] = words.astype(jnp.bfloat16)
 
     return pl.pallas_call(
         kernel,
-        in_specs=[scalar] + [plain] * 4,
+        in_specs=[scalar] + [plain] * 6,
         out_specs=(plain, plain),
         out_shape=(
             jax.ShapeDtypeStruct((tokens, half), jnp.bfloat16),
-            jax.ShapeDtypeStruct((tokens, HDIM), jnp.bfloat16),
+            jax.ShapeDtypeStruct((tokens, 2 * key_cols + HDIM), jnp.bfloat16),
         ),
         scratch_shapes=[pltpu.VMEM((depth, half), jnp.bfloat16)],
-        compiler_params=pltpu.CompilerParams(vmem_limit_bytes=16 << 20),
+        compiler_params=pltpu.CompilerParams(vmem_limit_bytes=18 << 20),
         name="adapt",
-    )(place_word, mine, taken, pooled, gain[None, :])
+    )(place_word, mine, taken, pooled, gain[None, :], w_key, w_value)
 
 
 def spread_even(value):
@@ -510,11 +535,10 @@
     shard_frames = frame_rows * mp_count
     first = (time_place * mp_count + model_place) * frame_rows
     near = shifted(frames, ("tm", "mp"), 1)
-    own_proj = project(frames, norm_attn, w_qkv)
     depth_weights = w_depth.astype(jnp.float32)
-    w_adapter, own_proj = lax.optimization_barrier((w_adapter, own_proj))
+    w_adapter, near = lax.optimization_barrier((w_adapter, near))
     conf_out, pooled = conformer(
-        frames, own_proj, near, first, block_ids, valid_counts, shard_frames, norm_attn, w_qkv,
+        frames, near, first, block_ids, valid_counts, shard_frames, norm_attn, w_qkv,
         w_attn_out, norm_conv, w_point_in, depth_weights, w_point_out,
     )
     stacked, row_of, pooled = line_pieces(w_adapter, pooled)
@@ -534,13 +558,8 @@
     tokens = all_pooled.shape[0]
     block = w_adapter.shape[1] * mp_count // tm_count
     gain = lax.dynamic_slice_in_dim(llm_gain, time_place * block, block, 0)
-    scaled, words = adapt(all_pooled, near_columns, gain)
-    raw_keys = jnp.dot(scaled, w_key, preferred_element_type=jnp.float32).astype(jnp.bfloat16)
-    raw_values = jnp.dot(scaled, w_value, preferred_element_type=jnp.float32).astype(jnp.bfloat16)
+    scaled, kv_raw = adapt(all_pooled, near_columns, gain, w_key, w_value)
     key_cols, half_cols = w_key.shape[1], w_query.shape[1] // 2
-    kv_raw, scaled = lax.optimization_barrier(
-        (jnp.concatenate([raw_keys, raw_values, words], axis=1), scaled)
-    )
     kv_parts = direct_parts(kv_raw)
     bits = list(range(tm_count.bit_length() - 2))
     left, right = scaled[: tokens // 2], scaled[tokens // 2 :]

time: 159 us -> 155 us (0.975)
  local copies, waits for them, and re-layouts: 15.9 us -> 11.3 us
  waiting for transfers between devices: 49.9 us -> 52.7 us
    unnamed x77 -> x59, local copies, waits for them, and re-layouts: 12.5 us -> 8.24 us
    pallas_call x1, Pallas kernels: 3.52 us -> 1.82 us  [finish_frames(): pl.pallas_call(kernel, out_shape=(jax.ShapeDtypeStruct((frame_rows, width...]
  transfers between devices with their start and end apart: 38 -> 38, of which waited for: 16 -> 18; matrix products, arithmetic and copies ran while one was open for 8% -> 8% of each run, Pallas kernels for 7% -> 6%
where the time goes in v4:
time: 155 us
  starting transfers between devices  57.5 us (37%)
  waiting for transfers between devices  52.7 us (34%)
  Pallas kernels  22.2 us (14%)
  local copies, waits for them, and re-layouts  11.3 us (7%)
  matrix products  5.04 us (3%)
  other arithmetic  4.55 us (3%)
  between operations  1.6 us (1%)
    ppermute x25, waiting for transfers between devices, swapped(): return lax.ppermute(value, 'tm', [(i, i ^ bits) for i in range(length)])  36.6 us
    ppermute x25, starting transfers between devices, swapped(): return lax.ppermute(value, 'tm', [(i, i ^ bits) for i in range(length)])  23.4 us
    ppermute x2, waiting for transfers between devices, line_pieces(): upper_2 = lax.ppermute(upper, 'mp', [(2, 1), (1, 0)])  10.2 us
    ppermute x2, starting transfers between devices, line_pieces(): far = lax.ppermute(mine, 'mp', [(0, 3), (3, 0)])  9.55 us
    ppermute x2, starting transfers between devices, shifted(): return lax.ppermute(value, axis, [(i, i + by) for i in range(length - by)])  9.5 us
    unnamed x59, local copies, waits for them, and re-layouts  8.24 us
    ppermute x3, starting transfers between devices, rotated(): lax.ppermute(value, 'mp', [(i, (i + by) % length) for i in range(length)])  5.37 us
    pallas_call x1, Pallas kernels, attend(): pl.pallas_call(kernel, out_shape=jax.ShapeDtypeStruct((rows, count * chun...  5.34 us
  transfers between devices with their start and end apart: 38, of which 18 were waited for; matrix products, arithmetic and copies ran while one was open for 8% of the time, Pallas kernels for 6%

profile of v4, /device:TPU:0, one launch (start us, length us, event | category | flops | bytes accessed | tf_op | source)
XLA Modules:
  0.0 154.8 jit_solution(13913600562470523090)
XLA Ops:
  0.6 4.9 %collective-permute-start = (bf16[128,1024]{1,0:T(8,128)(2,1)}, bf16[128,1024]{1,0:T(8,128)(2,1)S(1)}, u32[]{:S(2)}, u32[]{:S(2)}) collective-permute-start(bf16[128,1024]{1,0:T(8,128)(2,1)} %frames_ref.3), channel_id=1, source_target_pairs={{0,1},{1,2},{2,3},{3,4},{4,5},{5,6},{6,7},{7,8},{8,9},{9,10},{10,1... | collective-permute-start | bytes 786440 | tf_op jit(solution)/shard_map/ppermute | solution.py:21
  5.7 0.7 select_reduce_fusion.1
  6.5 0.8 pad_dynamic-slice_fusion
  7.6 0.8 convert_element_type.82.depth_ref
  8.6 2.8 %collective-permute-done.near_ref = bf16[128,1024]{1,0:T(8,128)(2,1)S(1)} collective-permute-done((bf16[128,1024]{1,0:T(8,128)(2,1)}, bf16[128,1024]{1,0:T(8,128)(2,1)S(1)}, u32[]{:S(2)}, u32[]{:S(2)}) %collective-permute-start) | collective-permute-done | bytes 262176 | tf_op jit(solution)/shard_map/ppermute | solution.py:21
  11.4 4.3 %collective-permute-start.2 = (bf16[128,2048]{1,0:T(8,128)(2,1)}, bf16[128,2048]{1,0:T(8,128)(2,1)S(1)}, u32[]{:S(2)}, u32[]{:S(2)}) collective-permute-start(bf16[128,2048]{1,0:T(8,128)(2,1)} %param.25), channel_id=1, source_target_pairs={{0,1},{1,2},{2,3},{4,5},{5,6},{6,7},{8,9},{9,10},{10,11},{12,13},{... | collective-permute-start | bytes 1572872 | tf_op jit(solution)/shard_map/ppermute | solution.py:375
  15.7 1.3 collective-permute-start.3
  17.1 2.8 %copy-done = bf16[1024,3072]{1,0:T(8,128)(2,1)S(1)} copy-done((bf16[1024,3072]{1,0:T(8,128)(2,1)S(1)}, bf16[1024,3072]{1,0:T(8,128)(2,1)}, u32[]{:S(2)}) %copy-start) | copy-done | bytes 6291480
  19.8 0.9 copy-done.4
  21.5 2.1 %project.1.proj_ref = bf16[256,3072]{1,0:T(8,128)(2,1)S(1)} custom-call(bf16[128,1024]{1,0:T(8,128)(2,1)S(1)} %collective-permute-done.near_ref, bf16[128,1024]{1,0:T(8,128)(2,1)S(1)} %copy-done.4, f32[1,1024]{1,0:T(1,128)S(1)} %bitcast.92, bf16[1024,3072]{1,0:T(8,128)(2,1)S(1)} %copy-done), custom_call_target="tpu_custom_call" | custom-call | flops 1610612736 | bytes 6291456 | tf_op jit(solution)/shard_map/project/pallas_call | solution.py:161
  24.3 3.0 %gate_frames.1 = (f32[128,1024]{1,0:T(8,128)S(1)}, bf16[128,1024]{1,0:T(8,128)(2,1)S(1)}, bf16[32,1024]{1,0:T(8,128)(2,1)S(1)}) custom-call(bf16[128,1024]{1,0:T(8,128)(2,1)S(1)} %copy-done.4, bf16[256,3072]{1,0:T(8,128)(2,1)S(1)} %project.1.proj_ref, s32[3,256]{1,0:T(4,128)S(1)} %pad_add_fusion.key_row_ref, s32[128,3]{1,0:T(8,128)S(1)} %bitcast.89, ...), custom_call_target="tpu_custom_call" | custom-call | flops 805306368 | bytes 6291456 | tf_op jit(solution)/shard_map/gate_frames/pallas_call | solution.py:242
  27.4 4.6 %collective-permute-start.1 = (bf16[32,1024]{1,0:T(8,128)(2,1)S(1)}, bf16[32,1024]{1,0:T(8,128)(2,1)S(1)}, u32[]{:S(2)}, u32[]{:S(2)}) collective-permute-start(bf16[32,1024]{1,0:T(8,128)(2,1)S(1)} %get-tuple-element.44), channel_id=1, source_target_pairs={{0,1},{1,2},{2,3},{3,4},{4,5},{5,6},{6,7},{7,8},{8,9},{9,10},{10,1... | collective-permute-start | bytes 196616 | tf_op jit(solution)/shard_map/ppermute | solution.py:21
  32.0 1.6 %convolve_late.1.late_ref = bf16[96,1024]{1,0:T(8,128)(2,1)S(1)} custom-call(bf16[128,1024]{1,0:T(8,128)(2,1)S(1)} %get-tuple-element.43.glu_ref, f32[31,1024]{1,0:T(8,128)S(1)} %convert_element_type.82.depth_ref), custom_call_target="tpu_custom_call" | custom-call | flops 6094848 | bytes 393216 | tf_op jit(solution)/shard_map/convolve_late/pallas_call | solution.py:285
  33.8 1.8 %finish_frames.1 = (bf16[128,1024]{1,0:T(8,128)(2,1)}, bf16[32,1024]{1,0:T(8,128)(2,1)S(1)}) custom-call(f32[128,1024]{1,0:T(8,128)S(1)} %get-tuple-element.42.mid_ref, bf16[128,1024]{1,0:T(8,128)(2,1)S(1)} %get-tuple-element.43.glu_ref, bf16[96,1024]{1,0:T(8,128)(2,1)S(1)} %convolve_late.1.late_ref, bf16[32,1024]{1,0:T(8,128)(2,1)S(1)} %collective-permute-done.1.rim_ref, ...), custom_call_target="tpu_custom_call" | custom-call | flops 268435456 | bytes 2097152 | tf_op jit(solution)/shard_map/finish_frames/pallas_call | solution.py:330
  35.7 4.4 %collective-permute-start.4 = (bf16[32,1024]{1,0:T(8,128)(2,1)S(1)}, bf16[32,1024]{1,0:T(8,128)(2,1)S(1)}, u32[]{:S(2)}, u32[]{:S(2)}) collective-permute-start(bf16[32,1024]{1,0:T(8,128)(2,1)S(1)} %get-tuple-element.48), channel_id=1, source_target_pairs={{0,3},{1,0},{2,1},{3,2},{4,7},{5,4},{6,5},{7,6},{8,11},{9,8},{10,9... | collective-permute-start | bytes 196616 | tf_op jit(solution)/shard_map/ppermute | solution.py:31
  40.1 1.0 collective-permute-start.6
  41.8 1.3 collective-permute-start.12
  43.1 5.1 %collective-permute-start.10 = (bf16[64,2048]{1,0:T(8,128)(2,1)S(1)}, bf16[64,2048]{1,0:T(8,128)(2,1)S(1)}, u32[]{:S(2)}, u32[]{:S(2)}) collective-permute-start(bf16[64,2048]{1,0:T(8,128)(2,1)S(1)} %get-tuple-element.49), channel_id=1, source_target_pairs={{0,3},{3,0},{4,7},{7,4},{8,11},{11,8},{12,15},{15,12},{16,19},{19,... | collective-permute-start | bytes 786440 | tf_op jit(solution)/shard_map/ppermute | solution.py:385
  48.4 1.7 %collective-permute-start.7 = (bf16[128,1024]{1,0:T(8,128)(2,1)S(1)}, bf16[128,1024]{1,0:T(8,128)(2,1)S(1)}, u32[]{:S(2)}, u32[]{:S(2)}) collective-permute-start(bf16[128,1024]{1,0:T(8,128)(2,1)S(1)} %constant_dynamic-slice_fusion), channel_id=1, source_target_pairs={{0,8},{4,12},{8,0},{12,4},{16,24},{20,28},{24,16},{28,20},{1,9},{5... | collective-permute-start | bytes 786440 | tf_op jit(solution)/shard_map/ppermute | solution.py:26
  50.1 1.3 collective-permute-start.8
  52.0 7.0 %collective-permute-done.12 = bf16[64,2048]{1,0:T(8,128)(2,1)S(1)} collective-permute-done((bf16[64,2048]{1,0:T(8,128)(2,1)S(1)}, bf16[64,2048]{1,0:T(8,128)(2,1)S(1)}, u32[]{:S(2)}, u32[]{:S(2)}) %collective-permute-start.12) | collective-permute-done | bytes 262176 | tf_op jit(solution)/shard_map/ppermute | solution.py:387
  58.9 4.4 %collective-permute-start.17 = (bf16[64,2048]{1,0:T(8,128)(2,1)S(1)}, bf16[64,2048]{1,0:T(8,128)(2,1)S(1)}, u32[]{:S(2)}, u32[]{:S(2)}) collective-permute-start(bf16[64,2048]{1,0:T(8,128)(2,1)S(1)} %get-tuple-element.58), channel_id=1, source_target_pairs={{0,3},{3,0},{4,7},{7,4},{8,11},{11,8},{12,15},{15,12},{16,19},{19,... | collective-permute-start | bytes 786440 | tf_op jit(solution)/shard_map/ppermute | solution.py:385
  64.3 1.5 collective-permute-start.19
  65.9 1.2 collective-permute-start.14
  67.4 2.8 %collective-permute-done.17 = bf16[64,2048]{1,0:T(8,128)(2,1)S(1)} collective-permute-done((bf16[64,2048]{1,0:T(8,128)(2,1)S(1)}, bf16[64,2048]{1,0:T(8,128)(2,1)S(1)}, u32[]{:S(2)}, u32[]{:S(2)}) %collective-permute-start.17) | collective-permute-done | bytes 262176 | tf_op jit(solution)/shard_map/ppermute | solution.py:385
  70.2 2.0 %collective-permute-start.16 = (bf16[64,2048]{1,0:T(8,128)(2,1)S(1)}, bf16[64,2048]{1,0:T(8,128)(2,1)S(1)}, u32[]{:S(2)}, u32[]{:S(2)}) collective-permute-start(bf16[64,2048]{1,0:T(8,128)(2,1)S(1)} %get-tuple-element.84), channel_id=1, source_target_pairs={{0,24},{4,28},{8,16},{12,20},{16,8},{20,12},{24,0},{28,4},{1,25},{... | collective-permute-start | bytes 786440 | tf_op jit(solution)/shard_map/ppermute | solution.py:26
  72.5 3.2 %collective-permute-done.19 = bf16[64,2048]{1,0:T(8,128)(2,1)S(1)} collective-permute-done((bf16[64,2048]{1,0:T(8,128)(2,1)S(1)}, bf16[64,2048]{1,0:T(8,128)(2,1)S(1)}, u32[]{:S(2)}, u32[]{:S(2)}) %collective-permute-start.19) | collective-permute-done | bytes 262176 | tf_op jit(solution)/shard_map/ppermute | solution.py:387
  75.8 1.1 collective-permute-start.20
  76.9 1.5 collective-permute-start.21
  78.4 1.0 collective-permute-start.22
  79.7 5.4 %collective-permute-done.20.refs_5_ = bf16[64,2048]{1,0:T(8,128)(2,1)S(1)} collective-permute-done((bf16[64,2048]{1,0:T(8,128)(2,1)S(1)}, bf16[64,2048]{1,0:T(8,128)(2,1)S(1)}, u32[]{:S(2)}, u32[]{:S(2)}) %collective-permute-start.20) | collective-permute-done | bytes 262176 | tf_op jit(solution)/shard_map/ppermute | solution.py:26
  85.1 4.4 %collective-permute-done.21.refs_6_ = bf16[64,2048]{1,0:T(8,128)(2,1)S(1)} collective-permute-done((bf16[64,2048]{1,0:T(8,128)(2,1)S(1)}, bf16[64,2048]{1,0:T(8,128)(2,1)S(1)}, u32[]{:S(2)}, u32[]{:S(2)}) %collective-permute-start.21) | collective-permute-done | bytes 262176 | tf_op jit(solution)/shard_map/ppermute | solution.py:26
  89.5 1.1 collective-permute-done.22.refs_7_
  90.6 1.2 halves.1
  92.9 1.8 %collective-permute-done.23.taken_ref = bf16[512,1024]{1,0:T(8,128)(2,1)} collective-permute-done((bf16[512,1024]{1,0:T(8,128)(2,1)}, bf16[512,1024]{1,0:T(8,128)(2,1)}, u32[]{:S(2)}, u32[]{:S(2)}) %collective-permute-start.23) | collective-permute-done | bytes 1048608 | tf_op jit(solution)/shard_map/ppermute | solution.py:26
  94.7 1.0 copy-done.7
  95.8 1.0 copy-done.8
  96.8 5.0 %adapt.1 = (bf16[1024,1024]{1,0:T(8,128)(2,1)S(1)}, bf16[1024,640]{1,0:T(8,128)(2,1)S(1)}) custom-call(s32[1]{0:T(128)} %bitcast.5.place_ref, bf16[512,1024]{1,0:T(8,128)(2,1)S(1)} %get-tuple-element.69.mine_ref, bf16[512,1024]{1,0:T(8,128)(2,1)} %collective-permute-done.23.taken_ref, bf16[1024,1024]{1,0:T(8,128)(2,1)S(1)} %pad_maximum_fusion.pooled_ref, ...), custom_call_target="tpu_custom_call" | custom-call | tf_op jit(solution)/shard_map/adapt/pallas_call | solution.py:462
  102.1 1.3 fusion.11
  103.8 0.7 pad_maximum_fusion.3.refs_4_.refs_5_
  104.5 1.3 fusion.8
  106.0 0.7 pad_maximum_fusion.4.refs_5_.refs_6_
  106.9 0.7 fusion.29
  107.6 1.1 collective-permute-start.31
  108.7 1.2 collective-permute-start.32
  110.0 1.2 collective-permute-start.33
  111.1 1.3 add_convert_fusion
  112.4 1.3 add_convert_fusion.1
  113.7 1.0 collective-permute-done.31.refs_1_
  114.7 2.5 %collective-permute-done.32.refs_2_ = bf16[128,640]{1,0:T(8,128)(2,1)S(1)} collective-permute-done((bf16[128,640]{1,0:T(8,128)(2,1)S(1)}, bf16[128,640]{1,0:T(8,128)(2,1)S(1)}, u32[]{:S(2)}, u32[]{:S(2)}) %collective-permute-start.32) | collective-permute-done | bytes 163872 | tf_op jit(solution)/shard_map/ppermute | solution.py:26
  117.2 1.2 collective-permute-done.33.refs_3_
  119.1 2.1 %finish_keys.1 = (bf16[128,512]{1,0:T(8,128)(2,1)}, f32[128,128]{1,0:T(8,128)}) custom-call(bf16[128,640]{1,0:T(8,128)(2,1)} %get-tuple-element.74.refs_0_, bf16[128,640]{1,0:T(8,128)(2,1)} %copy-done.14, bf16[128,640]{1,0:T(8,128)(2,1)} %copy-done.15, bf16[128,640]{1,0:T(8,128)(2,1)} %copy-done.16, f32[128,128]{1,0:T(8,128)} %pad_maximum_fusion.3.refs_4_.refs_5_, ...), custom_call_target="tpu_custom_call" | custom-call | tf_op jit(solution)/shard_map/finish_keys/pallas_call | solution.py:86
  121.2 0.9 collective-permute-start.34
  122.1 1.5 collective-permute-start.35
  123.6 1.1 collective-permute-start.36
  124.8 1.3 collective-permute-start.28
  126.2 1.2 collective-permute-start.25
  127.5 3.8 %collective-permute-done.35 = bf16[128,512]{1,0:T(8,128)(2,1)S(1)} collective-permute-done((bf16[128,512]{1,0:T(8,128)(2,1)}, bf16[128,512]{1,0:T(8,128)(2,1)S(1)}, u32[]{:S(2)}, u32[]{:S(2)}) %collective-permute-start.35) | collective-permute-done | bytes 131104 | tf_op jit(solution)/shard_map/ppermute | solution.py:26
  131.5 9.8 %collective-permute-done.28 = bf16[2,128,1024]{2,1,0:T(8,128)(2,1)S(1)} collective-permute-done((bf16[2,128,1024]{2,1,0:T(8,128)(2,1)S(1)}, bf16[2,128,1024]{2,1,0:T(8,128)(2,1)S(1)}, u32[]{:S(2)}, u32[]{:S(2)}) %collective-permute-start.28) | collective-permute-done | bytes 524320 | tf_op jit(solution)/shard_map/ppermute | solution.py:26
  141.5 1.0 collective-permute-start.29
  142.8 1.3 collective-permute-start.26
  144.1 4.5 %collective-permute-done.29.refs_3_ = bf16[128,1024]{1,0:T(8,128)(2,1)S(1)} collective-permute-done((bf16[128,1024]{1,0:T(8,128)(2,1)S(1)}, bf16[128,1024]{1,0:T(8,128)(2,1)S(1)}, u32[]{:S(2)}, u32[]{:S(2)}) %collective-permute-start.29) | collective-permute-done | bytes 262176 | tf_op jit(solution)/shard_map/ppermute | solution.py:26
  148.6 0.9 collective-permute-done.26.refs_1_
  149.5 5.3 %attend.1 = bf16[128,2048]{1,0:T(8,128)(2,1)} custom-call(bf16[128,1024]{1,0:T(8,128)(2,1)S(1)} %get-tuple-element.97.refs_0_, bf16[128,1024]{1,0:T(8,128)(2,1)S(1)} %collective-permute-done.26.refs_1_, bf16[128,1024]{1,0:T(8,128)(2,1)S(1)} %get-tuple-element.95.refs_2_, bf16[128,1024]{1,0:T(8,128)(2,1)S(1)} %collective-permute-done.29.refs_3_, ...), custom_call_target="tpu_custom_call" | custom-call | tf_op jit(solution)/shard_map/attend/pallas_call | solution.py:139
  (143 shorter events, 9.2 us)
Async XLA Ops:
  0.6 10.8 %collective-permute-start = (bf16[128,1024]{1,0:T(8,128)(2,1)}, bf16[128,1024]{1,0:T(8,128)(2,1)S(1)}, u32[]{:S(2)}, u32[]{:S(2)}) collective-permute-start(bf16[128,1024]{1,0:T(8,128)(2,1)} %frames_ref.3), channel_id=1, source_target_pairs={{0,1},{1,2},{2,3},{3,4},{4,5},{5,6},{6,7},{7,8},{8,9},{9,10},{10,1... | collective-permute-start | bytes 786440 | tf_op jit(solution)/shard_map/ppermute | solution.py:21
  11.4 24.2 %collective-permute-start.2 = (bf16[128,2048]{1,0:T(8,128)(2,1)}, bf16[128,2048]{1,0:T(8,128)(2,1)S(1)}, u32[]{:S(2)}, u32[]{:S(2)}) collective-permute-start(bf16[128,2048]{1,0:T(8,128)(2,1)} %param.25), channel_id=1, source_target_pairs={{0,1},{1,2},{2,3},{4,5},{5,6},{6,7},{8,9},{9,10},{10,11},{12,13},{... | collective-permute-start | bytes 1572872 | tf_op jit(solution)/shard_map/ppermute | solution.py:375
  15.7 19.9 %collective-permute-start.3 = (bf16[128,2048]{1,0:T(8,128)(2,1)}, bf16[128,2048]{1,0:T(8,128)(2,1)S(1)}, u32[]{:S(2)}, u32[]{:S(2)}) collective-permute-start(bf16[128,2048]{1,0:T(8,128)(2,1)} %param.25), channel_id=1, source_target_pairs={{1,0},{2,1},{3,2},{5,4},{6,5},{7,6},{9,8},{10,9},{11,10},{13,12},{... | collective-permute-start | bytes 1572872 | tf_op jit(solution)/shard_map/ppermute | solution.py:376
  17.0 2.8 %copy-start = (bf16[1024,3072]{1,0:T(8,128)(2,1)S(1)}, bf16[1024,3072]{1,0:T(8,128)(2,1)}, u32[]{:S(2)}) copy-start(bf16[1024,3072]{1,0:T(8,128)(2,1)} %weight_ref.1) | copy-start | bytes 18874372
  19.8 0.9 copy-start.4
  20.8 0.7 copy-start.10
  21.5 2.2 %copy-start.1 = (bf16[1024,2048]{1,0:T(8,128)(2,1)S(1)}, bf16[1024,2048]{1,0:T(8,128)(2,1)}, u32[]{:S(2)}) copy-start(bf16[1024,2048]{1,0:T(8,128)(2,1)} %in_hbm.1) | copy-start | bytes 12582916
  21.5 2.9 %copy-start.2 = (bf16[1024,1024]{1,0:T(8,128)(2,1)S(1)}, bf16[1024,1024]{1,0:T(8,128)(2,1)}, u32[]{:S(2)}) copy-start(bf16[1024,1024]{1,0:T(8,128)(2,1)} %attn_hbm.1) | copy-start | bytes 6291460
  21.5 2.9 %copy-start.11 = (f32[1024]{0:T(1024)S(1)}, f32[1024]{0:T(1024)}, u32[]{:S(2)}) copy-start(f32[1024]{0:T(1024)} %param.21) | copy-start | bytes 12292
  24.3 7.6 %copy-start.12 = (bf16[128,2048]{1,0:T(8,128)(2,1)S(1)}, bf16[128,2048]{1,0:T(8,128)(2,1)}, u32[]{:S(2)}) copy-start(bf16[128,2048]{1,0:T(8,128)(2,1)} %param.25) | copy-start | bytes 1572868
  24.3 9.5 %copy-start.3 = (bf16[1024,1024]{1,0:T(8,128)(2,1)S(1)}, bf16[1024,1024]{1,0:T(8,128)(2,1)}, u32[]{:S(2)}) copy-start(bf16[1024,1024]{1,0:T(8,128)(2,1)} %out_ref.1) | copy-start | bytes 6291460
  27.4 6.4 %collective-permute-start.1 = (bf16[32,1024]{1,0:T(8,128)(2,1)S(1)}, bf16[32,1024]{1,0:T(8,128)(2,1)S(1)}, u32[]{:S(2)}, u32[]{:S(2)}) collective-permute-start(bf16[32,1024]{1,0:T(8,128)(2,1)S(1)} %get-tuple-element.44), channel_id=1, source_target_pairs={{0,1},{1,2},{2,3},{3,4},{4,5},{5,6},{6,7},{7,8},{8,9},{9,10},{10,1... | collective-permute-start | bytes 196616 | tf_op jit(solution)/shard_map/ppermute | solution.py:21
  35.7 7.4 %collective-permute-start.4 = (bf16[32,1024]{1,0:T(8,128)(2,1)S(1)}, bf16[32,1024]{1,0:T(8,128)(2,1)S(1)}, u32[]{:S(2)}, u32[]{:S(2)}) collective-permute-start(bf16[32,1024]{1,0:T(8,128)(2,1)S(1)} %get-tuple-element.48), channel_id=1, source_target_pairs={{0,3},{1,0},{2,1},{3,2},{4,7},{5,4},{6,5},{7,6},{8,11},{9,8},{10,9... | collective-permute-start | bytes 196616 | tf_op jit(solution)/shard_map/ppermute | solution.py:31
  40.1 8.2 %collective-permute-start.5 = (bf16[32,1024]{1,0:T(8,128)(2,1)S(1)}, bf16[32,1024]{1,0:T(8,128)(2,1)S(1)}, u32[]{:S(2)}, u32[]{:S(2)}) collective-permute-start(bf16[32,1024]{1,0:T(8,128)(2,1)S(1)} %get-tuple-element.48), channel_id=1, source_target_pairs={{0,2},{1,3},{2,0},{3,1},{4,6},{5,7},{6,4},{7,5},{8,10},{9,11},{10,... | collective-permute-start | bytes 196616 | tf_op jit(solution)/shard_map/ppermute | solution.py:31
  40.1 8.2 %collective-permute-start.6 = (bf16[32,1024]{1,0:T(8,128)(2,1)S(1)}, bf16[32,1024]{1,0:T(8,128)(2,1)S(1)}, u32[]{:S(2)}, u32[]{:S(2)}) collective-permute-start(bf16[32,1024]{1,0:T(8,128)(2,1)S(1)} %get-tuple-element.48), channel_id=1, source_target_pairs={{0,1},{1,2},{2,3},{3,0},{4,5},{5,6},{6,7},{7,4},{8,9},{9,10},{10,1... | collective-permute-start | bytes 196616 | tf_op jit(solution)/shard_map/ppermute | solution.py:31
  41.1 10.4 %collective-permute-start.11 = (bf16[64,2048]{1,0:T(8,128)(2,1)S(1)}, bf16[64,2048]{1,0:T(8,128)(2,1)S(1)}, u32[]{:S(2)}, u32[]{:S(2)}) collective-permute-start(bf16[64,2048]{1,0:T(8,128)(2,1)S(1)} %slice.84), channel_id=1, source_target_pairs={{1,2},{2,3},{5,6},{6,7},{9,10},{10,11},{13,14},{14,15},{17,18},{18... | collective-permute-start | bytes 786440 | tf_op jit(solution)/shard_map/ppermute | solution.py:386
  41.8 17.1 %collective-permute-start.12 = (bf16[64,2048]{1,0:T(8,128)(2,1)S(1)}, bf16[64,2048]{1,0:T(8,128)(2,1)S(1)}, u32[]{:S(2)}, u32[]{:S(2)}) collective-permute-start(bf16[64,2048]{1,0:T(8,128)(2,1)S(1)} %slice.85), channel_id=1, source_target_pairs={{2,1},{1,0},{6,5},{5,4},{10,9},{9,8},{14,13},{13,12},{18,17},{17,1... | collective-permute-start | bytes 786440 | tf_op jit(solution)/shard_map/ppermute | solution.py:387
  43.1 15.8 %collective-permute-start.10 = (bf16[64,2048]{1,0:T(8,128)(2,1)S(1)}, bf16[64,2048]{1,0:T(8,128)(2,1)S(1)}, u32[]{:S(2)}, u32[]{:S(2)}) collective-permute-start(bf16[64,2048]{1,0:T(8,128)(2,1)S(1)} %get-tuple-element.49), channel_id=1, source_target_pairs={{0,3},{3,0},{4,7},{7,4},{8,11},{11,8},{12,15},{15,12},{16,19},{19,... | collective-permute-start | bytes 786440 | tf_op jit(solution)/shard_map/ppermute | solution.py:385
  48.4 15.8 %collective-permute-start.7 = (bf16[128,1024]{1,0:T(8,128)(2,1)S(1)}, bf16[128,1024]{1,0:T(8,128)(2,1)S(1)}, u32[]{:S(2)}, u32[]{:S(2)}) collective-permute-start(bf16[128,1024]{1,0:T(8,128)(2,1)S(1)} %constant_dynamic-slice_fusion), channel_id=1, source_target_pairs={{0,8},{4,12},{8,0},{12,4},{16,24},{20,28},{24,16},{28,20},{1,9},{5... | collective-permute-start | bytes 786440 | tf_op jit(solution)/shard_map/ppermute | solution.py:26
  50.1 15.6 %collective-permute-start.8 = (bf16[128,1024]{1,0:T(8,128)(2,1)S(1)}, bf16[128,1024]{1,0:T(8,128)(2,1)S(1)}, u32[]{:S(2)}, u32[]{:S(2)}) collective-permute-start(bf16[128,1024]{1,0:T(8,128)(2,1)S(1)} %constant_dynamic-slice_fusion), channel_id=1, source_target_pairs={{0,16},{4,20},{8,24},{12,28},{16,0},{20,4},{24,8},{28,12},{1,17},{... | collective-permute-start | bytes 786440 | tf_op jit(solution)/shard_map/ppermute | solution.py:26
  51.4 14.3 %collective-permute-start.9 = (bf16[128,1024]{1,0:T(8,128)(2,1)S(1)}, bf16[128,1024]{1,0:T(8,128)(2,1)S(1)}, u32[]{:S(2)}, u32[]{:S(2)}) collective-permute-start(bf16[128,1024]{1,0:T(8,128)(2,1)S(1)} %constant_dynamic-slice_fusion), channel_id=1, source_target_pairs={{0,24},{4,28},{8,16},{12,20},{16,8},{20,12},{24,0},{28,4},{1,25},{... | collective-permute-start | bytes 786440 | tf_op jit(solution)/shard_map/ppermute | solution.py:26
  58.9 11.3 %collective-permute-start.17 = (bf16[64,2048]{1,0:T(8,128)(2,1)S(1)}, bf16[64,2048]{1,0:T(8,128)(2,1)S(1)}, u32[]{:S(2)}, u32[]{:S(2)}) collective-permute-start(bf16[64,2048]{1,0:T(8,128)(2,1)S(1)} %get-tuple-element.58), channel_id=1, source_target_pairs={{0,3},{3,0},{4,7},{7,4},{8,11},{11,8},{12,15},{15,12},{16,19},{19,... | collective-permute-start | bytes 786440 | tf_op jit(solution)/shard_map/ppermute | solution.py:385
  63.4 8.9 %collective-permute-start.18 = (bf16[64,2048]{1,0:T(8,128)(2,1)S(1)}, bf16[64,2048]{1,0:T(8,128)(2,1)S(1)}, u32[]{:S(2)}, u32[]{:S(2)}) collective-permute-start(bf16[64,2048]{1,0:T(8,128)(2,1)S(1)} %slice.86), channel_id=1, source_target_pairs={{1,2},{2,3},{5,6},{6,7},{9,10},{10,11},{13,14},{14,15},{17,18},{18... | collective-permute-start | bytes 786440 | tf_op jit(solution)/shard_map/ppermute | solution.py:386
  64.3 11.4 %collective-permute-start.19 = (bf16[64,2048]{1,0:T(8,128)(2,1)S(1)}, bf16[64,2048]{1,0:T(8,128)(2,1)S(1)}, u32[]{:S(2)}, u32[]{:S(2)}) collective-permute-start(bf16[64,2048]{1,0:T(8,128)(2,1)S(1)} %slice.87), channel_id=1, source_target_pairs={{2,1},{1,0},{6,5},{5,4},{10,9},{9,8},{14,13},{13,12},{18,17},{17,1... | collective-permute-start | bytes 786440 | tf_op jit(solution)/shard_map/ppermute | solution.py:387
  65.9 11.0 %collective-permute-start.14 = (bf16[64,2048]{1,0:T(8,128)(2,1)S(1)}, bf16[64,2048]{1,0:T(8,128)(2,1)S(1)}, u32[]{:S(2)}, u32[]{:S(2)}) collective-permute-start(bf16[64,2048]{1,0:T(8,128)(2,1)S(1)} %get-tuple-element.86), channel_id=1, source_target_pairs={{0,8},{4,12},{8,0},{12,4},{16,24},{20,28},{24,16},{28,20},{1,9},{5... | collective-permute-start | bytes 786440 | tf_op jit(solution)/shard_map/ppermute | solution.py:26
  67.1 12.6 %collective-permute-start.15 = (bf16[64,2048]{1,0:T(8,128)(2,1)S(1)}, bf16[64,2048]{1,0:T(8,128)(2,1)S(1)}, u32[]{:S(2)}, u32[]{:S(2)}) collective-permute-start(bf16[64,2048]{1,0:T(8,128)(2,1)S(1)} %get-tuple-element.85), channel_id=1, source_target_pairs={{0,16},{4,20},{8,24},{12,28},{16,0},{20,4},{24,8},{28,12},{1,17},{... | collective-permute-start | bytes 786440 | tf_op jit(solution)/shard_map/ppermute | solution.py:26
  70.2 9.5 %collective-permute-start.16 = (bf16[64,2048]{1,0:T(8,128)(2,1)S(1)}, bf16[64,2048]{1,0:T(8,128)(2,1)S(1)}, u32[]{:S(2)}, u32[]{:S(2)}) collective-permute-start(bf16[64,2048]{1,0:T(8,128)(2,1)S(1)} %get-tuple-element.84), channel_id=1, source_target_pairs={{0,24},{4,28},{8,16},{12,20},{16,8},{20,12},{24,0},{28,4},{1,25},{... | collective-permute-start | bytes 786440 | tf_op jit(solution)/shard_map/ppermute | solution.py:26
  72.3 6.2 %collective-permute-start.13 = (bf16[512,1024]{1,0:T(8,128)(2,1)S(1)}, bf16[512,1024]{1,0:T(8,128)(2,1)S(1)}, u32[]{:S(2)}, u32[]{:S(2)}) collective-permute-start(bf16[512,1024]{1,0:T(8,128)(2,1)S(1)} %pad_maximum_fusion.1), channel_id=1, source_target_pairs={{0,4},{4,0},{8,12},{12,8},{16,20},{20,16},{24,28},{28,24},{1,5},{5... | collective-permute-start | bytes 3145736 | tf_op jit(solution)/shard_map/ppermute | solution.py:26
  75.8 9.2 %collective-permute-start.20 = (bf16[64,2048]{1,0:T(8,128)(2,1)S(1)}, bf16[64,2048]{1,0:T(8,128)(2,1)S(1)}, u32[]{:S(2)}, u32[]{:S(2)}) collective-permute-start(bf16[64,2048]{1,0:T(8,128)(2,1)S(1)} %get-tuple-element.82), channel_id=1, source_target_pairs={{0,8},{4,12},{8,0},{12,4},{16,24},{20,28},{24,16},{28,20},{1,9},{5... | collective-permute-start | bytes 786440 | tf_op jit(solution)/shard_map/ppermute | solution.py:26
  76.9 12.6 %collective-permute-start.21 = (bf16[64,2048]{1,0:T(8,128)(2,1)S(1)}, bf16[64,2048]{1,0:T(8,128)(2,1)S(1)}, u32[]{:S(2)}, u32[]{:S(2)}) collective-permute-start(bf16[64,2048]{1,0:T(8,128)(2,1)S(1)} %get-tuple-element.81), channel_id=1, source_target_pairs={{0,16},{4,20},{8,24},{12,28},{16,0},{20,4},{24,8},{28,12},{1,17},{... | collective-permute-start | bytes 786440 | tf_op jit(solution)/shard_map/ppermute | solution.py:26
  78.4 12.1 %collective-permute-start.22 = (bf16[64,2048]{1,0:T(8,128)(2,1)S(1)}, bf16[64,2048]{1,0:T(8,128)(2,1)S(1)}, u32[]{:S(2)}, u32[]{:S(2)}) collective-permute-start(bf16[64,2048]{1,0:T(8,128)(2,1)S(1)} %get-tuple-element.80), channel_id=1, source_target_pairs={{0,24},{4,28},{8,16},{12,20},{16,8},{20,12},{24,0},{28,4},{1,25},{... | collective-permute-start | bytes 786440 | tf_op jit(solution)/shard_map/ppermute | solution.py:26
  79.7 12.8 %copy-start.17 = (s32[8]{0:T(128)S(1)}, s32[8]{0:T(128)}, u32[]{:S(2)}) copy-start(s32[8]{0:T(128)} %param.17) | copy-start | bytes 100
  91.7 3.0 %collective-permute-start.23 = (bf16[512,1024]{1,0:T(8,128)(2,1)}, bf16[512,1024]{1,0:T(8,128)(2,1)}, u32[]{:S(2)}, u32[]{:S(2)}) collective-permute-start(bf16[512,1024]{1,0:T(8,128)(2,1)} %get-tuple-element.70), channel_id=1, source_target_pairs={{0,4},{4,0},{8,12},{12,8},{16,20},{20,16},{24,28},{28,24},{1,5},{5... | collective-permute-start | bytes 3145736 | tf_op jit(solution)/shard_map/ppermute | solution.py:26
  94.7 1.0 copy-start.7
  95.8 1.0 copy-start.8
  96.8 5.3 %copy-start.18 = (bf16[1024,2048]{1,0:T(8,128)(2,1)S(1)}, bf16[1024,2048]{1,0:T(8,128)(2,1)}, u32[]{:S(2)}) copy-start(bf16[1024,2048]{1,0:T(8,128)(2,1)} %param.27) | copy-start | bytes 12582916
  101.9 4.8 %collective-permute-start.30 = (bf16[512,640]{1,0:T(8,128)(2,1)S(1)}, bf16[512,640]{1,0:T(8,128)(2,1)S(1)}, u32[]{:S(2)}, u32[]{:S(2)}) collective-permute-start(bf16[512,640]{1,0:T(8,128)(2,1)S(1)} %slice.101), channel_id=1, source_target_pairs={{0,4},{4,0},{8,12},{12,8},{16,20},{20,16},{24,28},{28,24},{1,5},{5... | collective-permute-start | bytes 1966088 | tf_op jit(solution)/shard_map/ppermute | solution.py:26
  103.4 7.7 %collective-permute-start.27 = (bf16[512,1024]{1,0:T(8,128)(2,1)S(1)}, bf16[512,1024]{1,0:T(8,128)(2,1)S(1)}, u32[]{:S(2)}, u32[]{:S(2)}) collective-permute-start(bf16[512,1024]{1,0:T(8,128)(2,1)S(1)} %fusion.11), channel_id=1, source_target_pairs={{0,4},{4,0},{8,12},{12,8},{16,20},{20,16},{24,28},{28,24},{1,5},{5... | collective-permute-start | bytes 3145736 | tf_op jit(solution)/shard_map/ppermute | solution.py:26
  105.8 6.6 %collective-permute-start.24 = (bf16[512,1024]{1,0:T(8,128)(2,1)S(1)}, bf16[512,1024]{1,0:T(8,128)(2,1)S(1)}, u32[]{:S(2)}, u32[]{:S(2)}) collective-permute-start(bf16[512,1024]{1,0:T(8,128)(2,1)S(1)} %fusion.8), channel_id=1, source_target_pairs={{0,4},{4,0},{8,12},{12,8},{16,20},{20,16},{24,28},{28,24},{1,5},{5... | collective-permute-start | bytes 3145736 | tf_op jit(solution)/shard_map/ppermute | solution.py:26
  107.6 7.0 %collective-permute-start.31 = (bf16[128,640]{1,0:T(8,128)(2,1)S(1)}, bf16[128,640]{1,0:T(8,128)(2,1)S(1)}, u32[]{:S(2)}, u32[]{:S(2)}) collective-permute-start(bf16[128,640]{1,0:T(8,128)(2,1)S(1)} %get-tuple-element.92), channel_id=1, source_target_pairs={{0,8},{4,12},{8,0},{12,4},{16,24},{20,28},{24,16},{28,20},{1,9},{5... | collective-permute-start | bytes 491528 | tf_op jit(solution)/shard_map/ppermute | solution.py:26
  108.7 8.5 %collective-permute-start.32 = (bf16[128,640]{1,0:T(8,128)(2,1)S(1)}, bf16[128,640]{1,0:T(8,128)(2,1)S(1)}, u32[]{:S(2)}, u32[]{:S(2)}) collective-permute-start(bf16[128,640]{1,0:T(8,128)(2,1)S(1)} %get-tuple-element.91), channel_id=1, source_target_pairs={{0,16},{4,20},{8,24},{12,28},{16,0},{20,4},{24,8},{28,12},{1,17},{... | collective-permute-start | bytes 491528 | tf_op jit(solution)/shard_map/ppermute | solution.py:26
  110.0 8.5 %collective-permute-start.33 = (bf16[128,640]{1,0:T(8,128)(2,1)S(1)}, bf16[128,640]{1,0:T(8,128)(2,1)S(1)}, u32[]{:S(2)}, u32[]{:S(2)}) collective-permute-start(bf16[128,640]{1,0:T(8,128)(2,1)S(1)} %get-tuple-element.90), channel_id=1, source_target_pairs={{0,24},{4,28},{8,16},{12,20},{16,8},{20,12},{24,0},{28,4},{1,25},{... | collective-permute-start | bytes 491528 | tf_op jit(solution)/shard_map/ppermute | solution.py:26
  114.7 3.8 %copy-start.14 = (bf16[128,640]{1,0:T(8,128)(2,1)}, bf16[128,640]{1,0:T(8,128)(2,1)S(1)}, u32[]{:S(2)}) copy-start(bf16[128,640]{1,0:T(8,128)(2,1)S(1)} %collective-permute-done.31.refs_1_) | copy-start | bytes 491524
  117.2 1.3 copy-start.15
  118.4 0.7 copy-start.16
  121.2 6.1 %copy-start.13 = (bf16[128,512]{1,0:T(8,128)(2,1)S(1)}, bf16[128,512]{1,0:T(8,128)(2,1)}, u32[]{:S(2)}) copy-start(bf16[128,512]{1,0:T(8,128)(2,1)} %get-tuple-element.79) | copy-start | bytes 393220
  121.2 6.3 %collective-permute-start.34 = (bf16[128,512]{1,0:T(8,128)(2,1)}, bf16[128,512]{1,0:T(8,128)(2,1)S(1)}, u32[]{:S(2)}, u32[]{:S(2)}) collective-permute-start(bf16[128,512]{1,0:T(8,128)(2,1)} %get-tuple-element.79), channel_id=1, source_target_pairs={{0,8},{4,12},{8,0},{12,4},{16,24},{20,28},{24,16},{28,20},{1,9},{5... | collective-permute-start | bytes 393224 | tf_op jit(solution)/shard_map/ppermute | solution.py:26
  122.1 9.1 %collective-permute-start.35 = (bf16[128,512]{1,0:T(8,128)(2,1)}, bf16[128,512]{1,0:T(8,128)(2,1)S(1)}, u32[]{:S(2)}, u32[]{:S(2)}) collective-permute-start(bf16[128,512]{1,0:T(8,128)(2,1)} %get-tuple-element.79), channel_id=1, source_target_pairs={{0,16},{4,20},{8,24},{12,28},{16,0},{20,4},{24,8},{28,12},{1,17},{... | collective-permute-start | bytes 393224 | tf_op jit(solution)/shard_map/ppermute | solution.py:26
  123.6 7.7 %collective-permute-start.36 = (bf16[128,512]{1,0:T(8,128)(2,1)}, bf16[128,512]{1,0:T(8,128)(2,1)S(1)}, u32[]{:S(2)}, u32[]{:S(2)}) collective-permute-start(bf16[128,512]{1,0:T(8,128)(2,1)} %get-tuple-element.79), channel_id=1, source_target_pairs={{0,24},{4,28},{8,16},{12,20},{16,8},{20,12},{24,0},{28,4},{1,25},{... | collective-permute-start | bytes 393224 | tf_op jit(solution)/shard_map/ppermute | solution.py:26
  124.8 16.5 %collective-permute-start.28 = (bf16[2,128,1024]{2,1,0:T(8,128)(2,1)S(1)}, bf16[2,128,1024]{2,1,0:T(8,128)(2,1)S(1)}, u32[]{:S(2)}, u32[]{:S(2)}) collective-permute-start(bf16[2,128,1024]{2,1,0:T(8,128)(2,1)S(1)} %bitcast.97), channel_id=1, source_target_pairs={{0,16},{4,20},{8,24},{12,28},{16,0},{20,4},{24,8},{28,12},{1,17},{... | collective-permute-start | bytes 1572872 | tf_op jit(solution)/shard_map/ppermute | solution.py:26
  126.2 16.4 %collective-permute-start.25 = (bf16[2,128,1024]{2,1,0:T(8,128)(2,1)S(1)}, bf16[2,128,1024]{2,1,0:T(8,128)(2,1)S(1)}, u32[]{:S(2)}, u32[]{:S(2)}) collective-permute-start(bf16[2,128,1024]{2,1,0:T(8,128)(2,1)S(1)} %slice_bitcast_fusion), channel_id=1, source_target_pairs={{0,8},{4,12},{8,0},{12,4},{16,24},{20,28},{24,16},{28,20},{1,9},{5... | collective-permute-start | bytes 1572872 | tf_op jit(solution)/shard_map/ppermute | solution.py:26
  131.4 12.7 %collective-permute-start.37 = (bf16[512,512]{1,0:T(8,128)(2,1)S(1)}, bf16[512,512]{1,0:T(8,128)(2,1)S(1)}, u32[]{:S(2)}, u32[]{:S(2)}) collective-permute-start(bf16[512,512]{1,0:T(8,128)(2,1)S(1)} %pad_maximum_fusion.2), channel_id=1, source_target_pairs={{0,4},{4,0},{8,12},{12,8},{16,20},{20,16},{24,28},{28,24},{1,5},{5... | collective-permute-start | bytes 1572872 | tf_op jit(solution)/shard_map/ppermute | solution.py:26
  141.5 8.0 %copy-start.5 = (f32[128,128]{1,0:T(8,128)S(1)}, f32[128,128]{1,0:T(8,128)}, u32[]{:S(2)}) copy-start(f32[128,128]{1,0:T(8,128)} %pad_maximum_fusion.4.refs_5_.refs_6_) | copy-start | bytes 196612
  141.5 8.0 %copy-start.6 = (f32[128,128]{1,0:T(8,128)S(1)}, f32[128,128]{1,0:T(8,128)}, u32[]{:S(2)}) copy-start(f32[128,128]{1,0:T(8,128)} %pad_maximum_fusion.3.refs_4_.refs_5_) | copy-start | bytes 196612
  141.5 8.0 %copy-start.9 = (f32[128,128]{1,0:T(8,128)S(1)}, f32[128,128]{1,0:T(8,128)}, u32[]{:S(2)}) copy-start(f32[128,128]{1,0:T(8,128)} %get-tuple-element.78.refs_4_) | copy-start | bytes 196612
  141.5 7.1 %collective-permute-start.29 = (bf16[128,1024]{1,0:T(8,128)(2,1)S(1)}, bf16[128,1024]{1,0:T(8,128)(2,1)S(1)}, u32[]{:S(2)}, u32[]{:S(2)}) collective-permute-start(bf16[128,1024]{1,0:T(8,128)(2,1)S(1)} %get-tuple-element.94), channel_id=1, source_target_pairs={{0,8},{4,12},{8,0},{12,4},{16,24},{20,28},{24,16},{28,20},{1,9},{5... | collective-permute-start | bytes 786440 | tf_op jit(solution)/shard_map/ppermute | solution.py:26
  142.8 6.7 %collective-permute-start.26 = (bf16[128,1024]{1,0:T(8,128)(2,1)S(1)}, bf16[128,1024]{1,0:T(8,128)(2,1)S(1)}, u32[]{:S(2)}, u32[]{:S(2)}) collective-permute-start(bf16[128,1024]{1,0:T(8,128)(2,1)S(1)} %get-tuple-element.96), channel_id=1, source_target_pairs={{0,16},{4,20},{8,24},{12,28},{16,0},{20,4},{24,8},{28,12},{1,17},{... | collective-permute-start | bytes 786440 | tf_op jit(solution)/shard_map/ppermute | solution.py:26

commit v5 on v4

--- a/solution.py
+++ b/solution.py
@@ -166,7 +166,31 @@
             flops=2 * both * width * wide, bytes_accessed=2 * width * wide, transcendentals=0
         ),
         name="project",
-    )(near, frames, gain[None, :], w_qkv)
+    )(near, frames, gain, w_qkv)
+
+
+def staged(*arrays):
+    count = len(arrays)
+
+    def kernel(*refs):
+        sems = refs[-1]
+        copies = [
+            pltpu.make_async_copy(refs[i], refs[count + i], sems.at[i]) for i in range(count)
+        ]
+        for copy in copies:
+            copy.start()
+        for copy in copies:
+            copy.wait()
+
+    return pl.pallas_call(
+        kernel,
+        in_specs=[pl.BlockSpec(memory_space=pltpu.HBM)] * count,
+        out_specs=(pl.BlockSpec(memory_space=pltpu.VMEM),) * count,
+        out_shape=tuple(jax.ShapeDtypeStruct(array.shape, array.dtype) for array in arrays),
+        scratch_shapes=[pltpu.SemaphoreType.DMA((count,))],
+        compiler_params=pltpu.CompilerParams(vmem_limit_bytes=12 << 20),
+        name="staged",
+    )(*arrays)
 
 
 def gate_frames(
@@ -351,7 +375,6 @@
 ):
     before = near.shape[0]
     key_rows = before + frames.shape[0]
-    proj = project(near, frames, norm_attn, w_qkv)
     key_index = first - before + jnp.arange(key_rows, dtype=jnp.int32)
     key_place, key_count = shard_count(key_index, valid_counts, shard_frames)
     key_real = (key_place < key_count) & (key_index >= 0)
@@ -359,6 +382,11 @@
     key_ids = lax.dynamic_slice_in_dim(padded_ids, first, key_rows, 0)
     key_row = jnp.stack([key_index, key_ids, key_real.astype(jnp.int32)])
     query_col = jnp.transpose(key_row[:, before:])
+    w_qkv, key_row, query_col, depth_weights = lax.optimization_barrier(
+        (w_qkv, key_row, query_col, depth_weights)
+    )
+    held_frames, held_gain, held_weight = staged(frames, norm_attn[None, :], w_qkv)
+    proj = project(near, held_frames, held_gain, held_weight)
     mid, glu, tail = gate_frames(
         frames, proj, key_row, query_col, w_attn_out, norm_conv, w_point_in, 32
     )
@@ -542,6 +570,7 @@
         w_attn_out, norm_conv, w_point_in, depth_weights, w_point_out,
     )
     stacked, row_of, pooled = line_pieces(w_adapter, pooled)
+    pooled, late_place, late_counts = lax.optimization_barrier((pooled, time_place, valid_counts))
     piece = pooled.shape[0]
     shard_tokens = piece * mp_count
     cycle = [rotated(pooled, by) for by in range(mp_count - 1, 0, -1)] + [pooled]
@@ -577,12 +606,12 @@
         query_chunks.append((keep, taken))
     order = list(range(0, tm_count, 2)) + list(range(1, tm_count, 2))
     within = jnp.arange(shard_tokens, dtype=jnp.int32)
-    own_place = time_place * shard_tokens + within
+    own_place = late_place * shard_tokens + within
     cosine, sine = rotary_tables(own_place, HDIM)
     kv, scale = finish_keys(kv_parts, cosine, sine, key_cols, block * tm_count)
     all_kv = spread(spread_even(kv))
-    key_place = jnp.concatenate([(time_place ^ other) * shard_tokens + within for other in order])
-    place_in, counts = shard_count(key_place, valid_counts, shard_tokens)
+    key_place = jnp.concatenate([(late_place ^ other) * shard_tokens + within for other in order])
+    place_in, counts = shard_count(key_place, late_counts, shard_tokens)
     key_real = (place_in * 4 < counts).astype(jnp.int32)
     attended = attend(
         query_chunks, all_kv, scale, cosine, sine, own_place[:, None], key_place[None, :],

time: 155 us -> 152 us (0.981)
  waiting for transfers between devices: 52.7 us -> 49.1 us
  local copies, waits for them, and re-layouts: 11.3 us -> 14.7 us
  Pallas kernels: 22.2 us -> 20.3 us
    unnamed x59 -> x65, local copies, waits for them, and re-layouts: 8.24 us -> 11.7 us
    ppermute x2, waiting for transfers between devices: 3.04 us -> 0.24 us  [shifted(): return lax.ppermute(value, axis, [(i, i + by) for i in range(length - by)])]
  transfers between devices with their start and end apart: 38 -> 38, of which waited for: 18 -> 15; matrix products, arithmetic and copies ran while one was open for 8% -> 8% of each run, Pallas kernels for 6% -> 6%
where the time goes in v5:
time: 152 us; the launch traced here: 151 us
  starting transfers between devices  56.4 us (37%)
  waiting for transfers between devices  49.1 us (32%)
  Pallas kernels  20.3 us (13%)
  local copies, waits for them, and re-layouts  14.7 us (10%)
  matrix products  5.06 us (3%)
  other arithmetic  4.48 us (3%)
    ppermute x25, waiting for transfers between devices, swapped(): return lax.ppermute(value, 'tm', [(i, i ^ bits) for i in range(length)])  37.9 us
    ppermute x25, starting transfers between devices, swapped(): return lax.ppermute(value, 'tm', [(i, i ^ bits) for i in range(length)])  23.8 us
    unnamed x65, local copies, waits for them, and re-layouts  11.7 us
    ppermute x2, starting transfers between devices, shifted(): return lax.ppermute(value, axis, [(i, i + by) for i in range(length - by)])  9.49 us
    ppermute x2, waiting for transfers between devices, line_pieces(): upper_2 = lax.ppermute(upper, 'mp', [(2, 1), (1, 0)])  9.2 us
    ppermute x2, starting transfers between devices, line_pieces(): far = lax.ppermute(mine, 'mp', [(0, 3), (3, 0)])  8.74 us
    ppermute x3, starting transfers between devices, rotated(): lax.ppermute(value, 'mp', [(i, (i + by) % length) for i in range(length)])  5.38 us
    pallas_call x1, Pallas kernels, attend(): pl.pallas_call(kernel, out_shape=jax.ShapeDtypeStruct((rows, count * chun...  5.33 us
  transfers between devices with their start and end apart: 38, of which 15 were waited for; matrix products, arithmetic and copies ran while one was open for 8% of the time, Pallas kernels for 6%

profile of v5, /device:TPU:0, one launch (start us, length us, event | category | flops | bytes accessed | tf_op | source)
XLA Modules:
  0.0 151.5 jit_solution(11377382405697954216)
XLA Ops:
  0.6 4.9 %collective-permute-start = (bf16[128,1024]{1,0:T(8,128)(2,1)}, bf16[128,1024]{1,0:T(8,128)(2,1)S(1)}, u32[]{:S(2)}, u32[]{:S(2)}) collective-permute-start(bf16[128,1024]{1,0:T(8,128)(2,1)} %frames_ref.1), channel_id=1, source_target_pairs={{0,1},{1,2},{2,3},{3,4},{4,5},{5,6},{6,7},{7,8},{8,9},{9,10},{10,1... | collective-permute-start | bytes 786440 | tf_op jit(solution)/shard_map/ppermute | solution.py:21
  5.6 0.7 select_reduce_fusion.1
  6.4 0.8 pad_dynamic-slice_fusion
  7.3 0.8 convert_element_type.82.depth_ref
  8.2 2.8 %copy-done = bf16[1024,3072]{1,0:T(8,128)(2,1)S(1)} copy-done((bf16[1024,3072]{1,0:T(8,128)(2,1)S(1)}, bf16[1024,3072]{1,0:T(8,128)(2,1)}, u32[]{:S(2)}) %copy-start) | copy-done | bytes 6291480
  11.0 0.9 copy-done.6
  12.0 0.7 copy-done.14
  13.2 2.6 %copy-done.1 = bf16[1024,3072]{1,0:T(8,128)(2,1)} copy-done((bf16[1024,3072]{1,0:T(8,128)(2,1)}, bf16[1024,3072]{1,0:T(8,128)(2,1)S(1)}, u32[]{:S(2)}) %copy-start.1) | copy-done | bytes 6291480
  15.8 0.7 dynamic_slice.44
  16.5 3.5 %collective-permute-start.2 = (bf16[128,2048]{1,0:T(8,128)(2,1)S(1)}, bf16[128,2048]{1,0:T(8,128)(2,1)S(1)}, u32[]{:S(2)}, u32[]{:S(2)}) collective-permute-start(bf16[128,2048]{1,0:T(8,128)(2,1)S(1)} %copy-done.15), channel_id=1, source_target_pairs={{0,1},{1,2},{2,3},{4,5},{5,6},{6,7},{8,9},{9,10},{10,11},{12,13},{... | collective-permute-start | bytes 1572872 | tf_op jit(solution)/shard_map/ppermute | solution.py:403
  20.0 1.3 collective-permute-start.3
  21.3 2.8 %copy-done.2 = bf16[1024,3072]{1,0:T(8,128)(2,1)S(1)} copy-done((bf16[1024,3072]{1,0:T(8,128)(2,1)S(1)}, bf16[1024,3072]{1,0:T(8,128)(2,1)}, u32[]{:S(2)}) %copy-start.2) | copy-done | bytes 6291480
  24.1 2.1 %project.1.proj_ref = bf16[256,3072]{1,0:T(8,128)(2,1)S(1)} custom-call(bf16[128,1024]{1,0:T(8,128)(2,1)S(1)} %collective-permute-done.near_ref, bf16[128,1024]{1,0:T(8,128)(2,1)S(1)} %get-tuple-element.53.frames_ref, f32[1,1024]{1,0:T(1,128)S(1)} %get-tuple-element.54.gain_ref, bf16[1024,3072]{1,0:T(8,128)(2,1)S(1)} %copy-done.2), custom_call_target="tpu_custom_call" | custom-call | flops 1610612736 | bytes 6291456 | tf_op jit(solution)/shard_map/project/pallas_call | solution.py:161
  26.3 0.7 copy-done.4
  27.0 3.1 %gate_frames.1 = (f32[128,1024]{1,0:T(8,128)S(1)}, bf16[128,1024]{1,0:T(8,128)(2,1)S(1)}, bf16[32,1024]{1,0:T(8,128)(2,1)S(1)}) custom-call(bf16[128,1024]{1,0:T(8,128)(2,1)S(1)} %copy-done.7, bf16[256,3072]{1,0:T(8,128)(2,1)S(1)} %project.1.proj_ref, s32[3,256]{1,0:T(4,128)S(1)} %pad_add_fusion.key_row_ref, s32[128,3]{1,0:T(8,128)S(1)} %bitcast.89, ...), custom_call_target="tpu_custom_call" | custom-call | flops 805306368 | bytes 6291456 | tf_op jit(solution)/shard_map/gate_frames/pallas_call | solution.py:266
  30.0 4.5 %collective-permute-start.1 = (bf16[32,1024]{1,0:T(8,128)(2,1)S(1)}, bf16[32,1024]{1,0:T(8,128)(2,1)S(1)}, u32[]{:S(2)}, u32[]{:S(2)}) collective-permute-start(bf16[32,1024]{1,0:T(8,128)(2,1)S(1)} %get-tuple-element.61), channel_id=1, source_target_pairs={{0,1},{1,2},{2,3},{3,4},{4,5},{5,6},{6,7},{7,8},{8,9},{9,10},{10,1... | collective-permute-start | bytes 196616 | tf_op jit(solution)/shard_map/ppermute | solution.py:21
  34.6 1.6 %convolve_late.1.late_ref = bf16[96,1024]{1,0:T(8,128)(2,1)S(1)} custom-call(bf16[128,1024]{1,0:T(8,128)(2,1)S(1)} %get-tuple-element.59.glu_ref, f32[31,1024]{1,0:T(8,128)S(1)} %convert_element_type.82.depth_ref), custom_call_target="tpu_custom_call" | custom-call | flops 6094848 | bytes 393216 | tf_op jit(solution)/shard_map/convolve_late/pallas_call | solution.py:309
  36.5 1.8 %finish_frames.1 = (bf16[128,1024]{1,0:T(8,128)(2,1)}, bf16[32,1024]{1,0:T(8,128)(2,1)S(1)}) custom-call(f32[128,1024]{1,0:T(8,128)S(1)} %get-tuple-element.58.mid_ref, bf16[128,1024]{1,0:T(8,128)(2,1)S(1)} %get-tuple-element.59.glu_ref, bf16[96,1024]{1,0:T(8,128)(2,1)S(1)} %convolve_late.1.late_ref, bf16[32,1024]{1,0:T(8,128)(2,1)S(1)} %collective-permute-done.1.rim_ref, ...), custom_call_target="tpu_custom_call" | custom-call | flops 268435456 | bytes 2097152 | tf_op jit(solution)/shard_map/finish_frames/pallas_call | solution.py:354
  38.3 3.3 %collective-permute-start.4 = (bf16[32,1024]{1,0:T(8,128)(2,1)S(1)}, bf16[32,1024]{1,0:T(8,128)(2,1)S(1)}, u32[]{:S(2)}, u32[]{:S(2)}) collective-permute-start(bf16[32,1024]{1,0:T(8,128)(2,1)S(1)} %get-tuple-element.66), channel_id=1, source_target_pairs={{0,3},{1,0},{2,1},{3,2},{4,7},{5,4},{6,5},{7,6},{8,11},{9,8},{10,9... | collective-permute-start | bytes 196616 | tf_op jit(solution)/shard_map/ppermute | solution.py:31
  42.1 1.6 %collective-permute-start.6 = (bf16[32,1024]{1,0:T(8,128)(2,1)S(1)}, bf16[32,1024]{1,0:T(8,128)(2,1)S(1)}, u32[]{:S(2)}, u32[]{:S(2)}) collective-permute-start(bf16[32,1024]{1,0:T(8,128)(2,1)S(1)} %get-tuple-element.66), channel_id=1, source_target_pairs={{0,1},{1,2},{2,3},{3,0},{4,5},{5,6},{6,7},{7,4},{8,9},{9,10},{10,1... | collective-permute-start | bytes 196616 | tf_op jit(solution)/shard_map/ppermute | solution.py:31
  43.7 0.7 collective-permute-start.11
  44.4 1.3 collective-permute-start.12
  45.9 4.3 %collective-permute-start.10 = (bf16[64,2048]{1,0:T(8,128)(2,1)S(1)}, bf16[64,2048]{1,0:T(8,128)(2,1)S(1)}, u32[]{:S(2)}, u32[]{:S(2)}) collective-permute-start(bf16[64,2048]{1,0:T(8,128)(2,1)S(1)} %get-tuple-element.67), channel_id=1, source_target_pairs={{0,3},{3,0},{4,7},{7,4},{8,11},{11,8},{12,15},{15,12},{16,19},{19,... | collective-permute-start | bytes 786440 | tf_op jit(solution)/shard_map/ppermute | solution.py:413
  50.4 1.6 %collective-permute-start.7 = (bf16[128,1024]{1,0:T(8,128)(2,1)S(1)}, bf16[128,1024]{1,0:T(8,128)(2,1)S(1)}, u32[]{:S(2)}, u32[]{:S(2)}) collective-permute-start(bf16[128,1024]{1,0:T(8,128)(2,1)S(1)} %constant_dynamic-slice_fusion), channel_id=1, source_target_pairs={{0,8},{4,12},{8,0},{12,4},{16,24},{20,28},{24,16},{28,20},{1,9},{5... | collective-permute-start | bytes 786440 | tf_op jit(solution)/shard_map/ppermute | solution.py:26
  52.0 1.4 collective-permute-start.8
  54.0 6.0 %collective-permute-done.12 = bf16[64,2048]{1,0:T(8,128)(2,1)S(1)} collective-permute-done((bf16[64,2048]{1,0:T(8,128)(2,1)S(1)}, bf16[64,2048]{1,0:T(8,128)(2,1)S(1)}, u32[]{:S(2)}, u32[]{:S(2)}) %collective-permute-start.12) | collective-permute-done | bytes 262176 | tf_op jit(solution)/shard_map/ppermute | solution.py:415
  60.0 4.4 %collective-permute-start.17 = (bf16[64,2048]{1,0:T(8,128)(2,1)S(1)}, bf16[64,2048]{1,0:T(8,128)(2,1)S(1)}, u32[]{:S(2)}, u32[]{:S(2)}) collective-permute-start(bf16[64,2048]{1,0:T(8,128)(2,1)S(1)} %get-tuple-element.76), channel_id=1, source_target_pairs={{0,3},{3,0},{4,7},{7,4},{8,11},{11,8},{12,15},{15,12},{16,19},{19,... | collective-permute-start | bytes 786440 | tf_op jit(solution)/shard_map/ppermute | solution.py:413
  64.5 0.7 collective-permute-start.18
  65.4 1.5 collective-permute-start.19
  67.0 2.0 %collective-permute-start.14 = (bf16[64,2048]{1,0:T(8,128)(2,1)S(1)}, bf16[64,2048]{1,0:T(8,128)(2,1)S(1)}, u32[]{:S(2)}, u32[]{:S(2)}) collective-permute-start(bf16[64,2048]{1,0:T(8,128)(2,1)S(1)} %get-tuple-element.106), channel_id=1, source_target_pairs={{0,8},{4,12},{8,0},{12,4},{16,24},{20,28},{24,16},{28,20},{1,9},{5... | collective-permute-start | bytes 786440 | tf_op jit(solution)/shard_map/ppermute | solution.py:26
  69.0 1.8 %collective-permute-done.17 = bf16[64,2048]{1,0:T(8,128)(2,1)S(1)} collective-permute-done((bf16[64,2048]{1,0:T(8,128)(2,1)S(1)}, bf16[64,2048]{1,0:T(8,128)(2,1)S(1)}, u32[]{:S(2)}, u32[]{:S(2)}) %collective-permute-start.17) | collective-permute-done | bytes 262176 | tf_op jit(solution)/shard_map/ppermute | solution.py:413
  70.8 2.0 %collective-permute-start.16 = (bf16[64,2048]{1,0:T(8,128)(2,1)S(1)}, bf16[64,2048]{1,0:T(8,128)(2,1)S(1)}, u32[]{:S(2)}, u32[]{:S(2)}) collective-permute-start(bf16[64,2048]{1,0:T(8,128)(2,1)S(1)} %get-tuple-element.104), channel_id=1, source_target_pairs={{0,24},{4,28},{8,16},{12,20},{16,8},{20,12},{24,0},{28,4},{1,25},{... | collective-permute-start | bytes 786440 | tf_op jit(solution)/shard_map/ppermute | solution.py:26
  73.1 3.2 %collective-permute-done.19 = bf16[64,2048]{1,0:T(8,128)(2,1)S(1)} collective-permute-done((bf16[64,2048]{1,0:T(8,128)(2,1)S(1)}, bf16[64,2048]{1,0:T(8,128)(2,1)S(1)}, u32[]{:S(2)}, u32[]{:S(2)}) %collective-permute-start.19) | collective-permute-done | bytes 262176 | tf_op jit(solution)/shard_map/ppermute | solution.py:415
  76.4 2.1 %collective-permute-start.20 = (bf16[64,2048]{1,0:T(8,128)(2,1)S(1)}, bf16[64,2048]{1,0:T(8,128)(2,1)S(1)}, u32[]{:S(2)}, u32[]{:S(2)}) collective-permute-start(bf16[64,2048]{1,0:T(8,128)(2,1)S(1)} %get-tuple-element.102), channel_id=1, source_target_pairs={{0,8},{4,12},{8,0},{12,4},{16,24},{20,28},{24,16},{28,20},{1,9},{5... | collective-permute-start | bytes 786440 | tf_op jit(solution)/shard_map/ppermute | solution.py:26
  79.0 1.0 collective-permute-start.22
  80.2 0.8 collective-permute-done.15.refs_2_
  81.0 4.5 %collective-permute-done.20.refs_5_ = bf16[64,2048]{1,0:T(8,128)(2,1)S(1)} collective-permute-done((bf16[64,2048]{1,0:T(8,128)(2,1)S(1)}, bf16[64,2048]{1,0:T(8,128)(2,1)S(1)}, u32[]{:S(2)}, u32[]{:S(2)}) %collective-permute-start.20) | collective-permute-done | bytes 262176 | tf_op jit(solution)/shard_map/ppermute | solution.py:26
  85.6 6.6 %collective-permute-done.21.refs_6_ = bf16[64,2048]{1,0:T(8,128)(2,1)S(1)} collective-permute-done((bf16[64,2048]{1,0:T(8,128)(2,1)S(1)}, bf16[64,2048]{1,0:T(8,128)(2,1)S(1)}, u32[]{:S(2)}, u32[]{:S(2)}) %collective-permute-start.21) | collective-permute-done | bytes 262176 | tf_op jit(solution)/shard_map/ppermute | solution.py:26
  92.9 2.1 %collective-permute-done.23.taken_ref = bf16[512,1024]{1,0:T(8,128)(2,1)S(1)} collective-permute-done((bf16[512,1024]{1,0:T(8,128)(2,1)S(1)}, bf16[512,1024]{1,0:T(8,128)(2,1)S(1)}, u32[]{:S(2)}, u32[]{:S(2)}) %collective-permute-start.23) | collective-permute-done | bytes 1048608 | tf_op jit(solution)/shard_map/ppermute | solution.py:26
  95.0 3.7 %adapt.1 = (bf16[1024,1024]{1,0:T(8,128)(2,1)S(1)}, bf16[1024,640]{1,0:T(8,128)(2,1)S(1)}) custom-call(s32[1]{0:T(128)} %bitcast.5.place_ref, bf16[512,1024]{1,0:T(8,128)(2,1)S(1)} %get-tuple-element.87.mine_ref, bf16[512,1024]{1,0:T(8,128)(2,1)S(1)} %collective-permute-done.23.taken_ref, bf16[1024,1024]{1,0:T(8,128)(2,1)S(1)} %pad_maximum_fusion.pooled_ref, ...), custom_call_target="tpu_custom_call" | custom-call | tf_op jit(solution)/shard_map/adapt/pallas_call | solution.py:490
  99.0 1.3 fusion.11
  100.7 0.7 pad_maximum_fusion.3.refs_4_.refs_5_
  101.4 1.3 fusion.8
  102.8 0.7 pad_maximum_fusion.4.refs_5_.refs_6_
  103.7 0.7 fusion.29
  104.8 1.4 collective-permute-start.32
  106.2 1.7 %collective-permute-start.33 = (bf16[128,640]{1,0:T(8,128)(2,1)S(1)}, bf16[128,640]{1,0:T(8,128)(2,1)S(1)}, u32[]{:S(2)}, u32[]{:S(2)}) collective-permute-start(bf16[128,640]{1,0:T(8,128)(2,1)S(1)} %get-tuple-element.110), channel_id=1, source_target_pairs={{0,24},{4,28},{8,16},{12,20},{16,8},{20,12},{24,0},{28,4},{1,25},{... | collective-permute-start | bytes 491528 | tf_op jit(solution)/shard_map/ppermute | solution.py:26
  108.0 1.3 add_convert_fusion
  109.3 1.3 add_convert_fusion.1
  110.5 1.0 collective-permute-done.31.refs_1_
  111.5 3.0 %collective-permute-done.32.refs_2_ = bf16[128,640]{1,0:T(8,128)(2,1)S(1)} collective-permute-done((bf16[128,640]{1,0:T(8,128)(2,1)S(1)}, bf16[128,640]{1,0:T(8,128)(2,1)S(1)}, u32[]{:S(2)}, u32[]{:S(2)}) %collective-permute-start.32) | collective-permute-done | bytes 163872 | tf_op jit(solution)/shard_map/ppermute | solution.py:26
  114.6 0.7 copy-done.18
  115.3 2.1 %finish_keys.1 = (bf16[128,512]{1,0:T(8,128)(2,1)}, f32[128,128]{1,0:T(8,128)}) custom-call(bf16[128,640]{1,0:T(8,128)(2,1)} %get-tuple-element.92.refs_0_, bf16[128,640]{1,0:T(8,128)(2,1)} %copy-done.17, bf16[128,640]{1,0:T(8,128)(2,1)} %copy-done.18, bf16[128,640]{1,0:T(8,128)(2,1)} %copy-done.19, f32[128,128]{1,0:T(8,128)} %pad_maximum_fusion.3.refs_4_.refs_5_, ...), custom_call_target="tpu_custom_call" | custom-call | tf_op jit(solution)/shard_map/finish_keys/pallas_call | solution.py:86
  117.4 1.7 %collective-permute-start.34 = (bf16[128,512]{1,0:T(8,128)(2,1)}, bf16[128,512]{1,0:T(8,128)(2,1)S(1)}, u32[]{:S(2)}, u32[]{:S(2)}) collective-permute-start(bf16[128,512]{1,0:T(8,128)(2,1)} %get-tuple-element.99), channel_id=1, source_target_pairs={{0,8},{4,12},{8,0},{12,4},{16,24},{20,28},{24,16},{28,20},{1,9},{5... | collective-permute-start | bytes 393224 | tf_op jit(solution)/shard_map/ppermute | solution.py:26
  119.4 1.4 collective-permute-start.36
  121.0 1.4 collective-permute-start.28
  122.4 0.8 collective-permute-start.25
  123.5 4.5 %collective-permute-done.35 = bf16[128,512]{1,0:T(8,128)(2,1)S(1)} collective-permute-done((bf16[128,512]{1,0:T(8,128)(2,1)}, bf16[128,512]{1,0:T(8,128)(2,1)S(1)}, u32[]{:S(2)}, u32[]{:S(2)}) %collective-permute-start.35) | collective-permute-done | bytes 131104 | tf_op jit(solution)/shard_map/ppermute | solution.py:26
  128.1 9.3 %collective-permute-done.28 = bf16[2,128,1024]{2,1,0:T(8,128)(2,1)S(1)} collective-permute-done((bf16[2,128,1024]{2,1,0:T(8,128)(2,1)S(1)}, bf16[2,128,1024]{2,1,0:T(8,128)(2,1)S(1)}, u32[]{:S(2)}, u32[]{:S(2)}) %collective-permute-start.28) | collective-permute-done | bytes 524320 | tf_op jit(solution)/shard_map/ppermute | solution.py:26
  137.7 1.3 collective-permute-start.29
  139.2 1.1 collective-permute-start.26
  140.4 4.0 %collective-permute-done.29.refs_3_ = bf16[128,1024]{1,0:T(8,128)(2,1)S(1)} collective-permute-done((bf16[128,1024]{1,0:T(8,128)(2,1)S(1)}, bf16[128,1024]{1,0:T(8,128)(2,1)S(1)}, u32[]{:S(2)}, u32[]{:S(2)}) %collective-permute-start.29) | collective-permute-done | bytes 262176 | tf_op jit(solution)/shard_map/ppermute | solution.py:26
  144.4 1.8 %collective-permute-done.26.refs_1_ = bf16[128,1024]{1,0:T(8,128)(2,1)S(1)} collective-permute-done((bf16[128,1024]{1,0:T(8,128)(2,1)S(1)}, bf16[128,1024]{1,0:T(8,128)(2,1)S(1)}, u32[]{:S(2)}, u32[]{:S(2)}) %collective-permute-start.26) | collective-permute-done | bytes 262176 | tf_op jit(solution)/shard_map/ppermute | solution.py:26
  146.2 5.3 %attend.1 = bf16[128,2048]{1,0:T(8,128)(2,1)} custom-call(bf16[128,1024]{1,0:T(8,128)(2,1)S(1)} %get-tuple-element.117.refs_0_, bf16[128,1024]{1,0:T(8,128)(2,1)S(1)} %collective-permute-done.26.refs_1_, bf16[128,1024]{1,0:T(8,128)(2,1)S(1)} %get-tuple-element.115.refs_2_, bf16[128,1024]{1,0:T(8,128)(2,1)S(1)} %collective-permute-done.29.refs_3_, ...), custom_call_target="tpu_custom_call" | custom-call | tf_op jit(solution)/shard_map/attend/pallas_call | solution.py:139
  (150 shorter events, 7.6 us)
Async XLA Ops:
  0.6 15.8 %collective-permute-start = (bf16[128,1024]{1,0:T(8,128)(2,1)}, bf16[128,1024]{1,0:T(8,128)(2,1)S(1)}, u32[]{:S(2)}, u32[]{:S(2)}) collective-permute-start(bf16[128,1024]{1,0:T(8,128)(2,1)} %frames_ref.1), channel_id=1, source_target_pairs={{0,1},{1,2},{2,3},{3,4},{4,5},{5,6},{6,7},{7,8},{8,9},{9,10},{10,1... | collective-permute-start | bytes 786440 | tf_op jit(solution)/shard_map/ppermute | solution.py:21
  8.2 2.8 %copy-start = (bf16[1024,3072]{1,0:T(8,128)(2,1)S(1)}, bf16[1024,3072]{1,0:T(8,128)(2,1)}, u32[]{:S(2)}) copy-start(bf16[1024,3072]{1,0:T(8,128)(2,1)} %refs_2_) | copy-start | bytes 18874372
  11.0 0.9 copy-start.6
  12.0 0.7 copy-start.14
  12.7 3.8 %copy-start.15 = (bf16[128,2048]{1,0:T(8,128)(2,1)S(1)}, bf16[128,2048]{1,0:T(8,128)(2,1)}, u32[]{:S(2)}) copy-start(bf16[128,2048]{1,0:T(8,128)(2,1)} %param.25) | copy-start | bytes 1572868
  13.1 2.6 %copy-start.1 = (bf16[1024,3072]{1,0:T(8,128)(2,1)}, bf16[1024,3072]{1,0:T(8,128)(2,1)S(1)}, u32[]{:S(2)}) copy-start(bf16[1024,3072]{1,0:T(8,128)(2,1)S(1)} %get-tuple-element.55.weight_ref) | copy-start | bytes 18874372
  16.5 21.8 %collective-permute-start.2 = (bf16[128,2048]{1,0:T(8,128)(2,1)S(1)}, bf16[128,2048]{1,0:T(8,128)(2,1)S(1)}, u32[]{:S(2)}, u32[]{:S(2)}) collective-permute-start(bf16[128,2048]{1,0:T(8,128)(2,1)S(1)} %copy-done.15), channel_id=1, source_target_pairs={{0,1},{1,2},{2,3},{4,5},{5,6},{6,7},{8,9},{9,10},{10,11},{12,13},{... | collective-permute-start | bytes 1572872 | tf_op jit(solution)/shard_map/ppermute | solution.py:403
  20.0 18.3 %collective-permute-start.3 = (bf16[128,2048]{1,0:T(8,128)(2,1)S(1)}, bf16[128,2048]{1,0:T(8,128)(2,1)S(1)}, u32[]{:S(2)}, u32[]{:S(2)}) collective-permute-start(bf16[128,2048]{1,0:T(8,128)(2,1)S(1)} %copy-done.15), channel_id=1, source_target_pairs={{1,0},{2,1},{3,2},{5,4},{6,5},{7,6},{9,8},{10,9},{11,10},{13,12},{... | collective-permute-start | bytes 1572872 | tf_op jit(solution)/shard_map/ppermute | solution.py:404
  21.3 2.8 %copy-start.2 = (bf16[1024,3072]{1,0:T(8,128)(2,1)S(1)}, bf16[1024,3072]{1,0:T(8,128)(2,1)}, u32[]{:S(2)}) copy-start(bf16[1024,3072]{1,0:T(8,128)(2,1)} %copy-done.1) | copy-start | bytes 18874372
  24.1 2.2 %copy-start.3 = (bf16[1024,2048]{1,0:T(8,128)(2,1)S(1)}, bf16[1024,2048]{1,0:T(8,128)(2,1)}, u32[]{:S(2)}) copy-start(bf16[1024,2048]{1,0:T(8,128)(2,1)} %in_hbm.1) | copy-start | bytes 12582916
  24.1 2.9 %copy-start.4 = (bf16[1024,1024]{1,0:T(8,128)(2,1)S(1)}, bf16[1024,1024]{1,0:T(8,128)(2,1)}, u32[]{:S(2)}) copy-start(bf16[1024,1024]{1,0:T(8,128)(2,1)} %attn_hbm.1) | copy-start | bytes 6291460
  24.1 2.9 %copy-start.7 = (bf16[128,1024]{1,0:T(8,128)(2,1)S(1)}, bf16[128,1024]{1,0:T(8,128)(2,1)}, u32[]{:S(2)}) copy-start(bf16[128,1024]{1,0:T(8,128)(2,1)} %frames_ref.1) | copy-start | bytes 786436
  24.1 2.9 %copy-start.13 = (f32[1024]{0:T(1024)S(1)}, f32[1024]{0:T(1024)}, u32[]{:S(2)}) copy-start(f32[1024]{0:T(1024)} %param.21) | copy-start | bytes 12292
  27.0 9.5 %copy-start.5 = (bf16[1024,1024]{1,0:T(8,128)(2,1)S(1)}, bf16[1024,1024]{1,0:T(8,128)(2,1)}, u32[]{:S(2)}) copy-start(bf16[1024,1024]{1,0:T(8,128)(2,1)} %out_ref.1) | copy-start | bytes 6291460
  30.0 6.4 %collective-permute-start.1 = (bf16[32,1024]{1,0:T(8,128)(2,1)S(1)}, bf16[32,1024]{1,0:T(8,128)(2,1)S(1)}, u32[]{:S(2)}, u32[]{:S(2)}) collective-permute-start(bf16[32,1024]{1,0:T(8,128)(2,1)S(1)} %get-tuple-element.61), channel_id=1, source_target_pairs={{0,1},{1,2},{2,3},{3,4},{4,5},{5,6},{6,7},{7,8},{8,9},{9,10},{10,1... | collective-permute-start | bytes 196616 | tf_op jit(solution)/shard_map/ppermute | solution.py:21
  38.3 7.6 %collective-permute-start.4 = (bf16[32,1024]{1,0:T(8,128)(2,1)S(1)}, bf16[32,1024]{1,0:T(8,128)(2,1)S(1)}, u32[]{:S(2)}, u32[]{:S(2)}) collective-permute-start(bf16[32,1024]{1,0:T(8,128)(2,1)S(1)} %get-tuple-element.66), channel_id=1, source_target_pairs={{0,3},{1,0},{2,1},{3,2},{4,7},{5,4},{6,5},{7,6},{8,11},{9,8},{10,9... | collective-permute-start | bytes 196616 | tf_op jit(solution)/shard_map/ppermute | solution.py:31
  41.6 8.7 %collective-permute-start.5 = (bf16[32,1024]{1,0:T(8,128)(2,1)S(1)}, bf16[32,1024]{1,0:T(8,128)(2,1)S(1)}, u32[]{:S(2)}, u32[]{:S(2)}) collective-permute-start(bf16[32,1024]{1,0:T(8,128)(2,1)S(1)} %get-tuple-element.66), channel_id=1, source_target_pairs={{0,2},{1,3},{2,0},{3,1},{4,6},{5,7},{6,4},{7,5},{8,10},{9,11},{10,... | collective-permute-start | bytes 196616 | tf_op jit(solution)/shard_map/ppermute | solution.py:31
  42.1 8.2 %collective-permute-start.6 = (bf16[32,1024]{1,0:T(8,128)(2,1)S(1)}, bf16[32,1024]{1,0:T(8,128)(2,1)S(1)}, u32[]{:S(2)}, u32[]{:S(2)}) collective-permute-start(bf16[32,1024]{1,0:T(8,128)(2,1)S(1)} %get-tuple-element.66), channel_id=1, source_target_pairs={{0,1},{1,2},{2,3},{3,0},{4,5},{5,6},{6,7},{7,4},{8,9},{9,10},{10,1... | collective-permute-start | bytes 196616 | tf_op jit(solution)/shard_map/ppermute | solution.py:31
  43.7 9.6 %collective-permute-start.11 = (bf16[64,2048]{1,0:T(8,128)(2,1)S(1)}, bf16[64,2048]{1,0:T(8,128)(2,1)S(1)}, u32[]{:S(2)}, u32[]{:S(2)}) collective-permute-start(bf16[64,2048]{1,0:T(8,128)(2,1)S(1)} %slice.84), channel_id=1, source_target_pairs={{1,2},{2,3},{5,6},{6,7},{9,10},{10,11},{13,14},{14,15},{17,18},{18... | collective-permute-start | bytes 786440 | tf_op jit(solution)/shard_map/ppermute | solution.py:414
  44.4 15.6 %collective-permute-start.12 = (bf16[64,2048]{1,0:T(8,128)(2,1)S(1)}, bf16[64,2048]{1,0:T(8,128)(2,1)S(1)}, u32[]{:S(2)}, u32[]{:S(2)}) collective-permute-start(bf16[64,2048]{1,0:T(8,128)(2,1)S(1)} %slice.85), channel_id=1, source_target_pairs={{2,1},{1,0},{6,5},{5,4},{10,9},{9,8},{14,13},{13,12},{18,17},{17,1... | collective-permute-start | bytes 786440 | tf_op jit(solution)/shard_map/ppermute | solution.py:415
  45.9 14.1 %collective-permute-start.10 = (bf16[64,2048]{1,0:T(8,128)(2,1)S(1)}, bf16[64,2048]{1,0:T(8,128)(2,1)S(1)}, u32[]{:S(2)}, u32[]{:S(2)}) collective-permute-start(bf16[64,2048]{1,0:T(8,128)(2,1)S(1)} %get-tuple-element.67), channel_id=1, source_target_pairs={{0,3},{3,0},{4,7},{7,4},{8,11},{11,8},{12,15},{15,12},{16,19},{19,... | collective-permute-start | bytes 786440 | tf_op jit(solution)/shard_map/ppermute | solution.py:413
  50.4 14.9 %collective-permute-start.7 = (bf16[128,1024]{1,0:T(8,128)(2,1)S(1)}, bf16[128,1024]{1,0:T(8,128)(2,1)S(1)}, u32[]{:S(2)}, u32[]{:S(2)}) collective-permute-start(bf16[128,1024]{1,0:T(8,128)(2,1)S(1)} %constant_dynamic-slice_fusion), channel_id=1, source_target_pairs={{0,8},{4,12},{8,0},{12,4},{16,24},{20,28},{24,16},{28,20},{1,9},{5... | collective-permute-start | bytes 786440 | tf_op jit(solution)/shard_map/ppermute | solution.py:26
  52.0 14.9 %collective-permute-start.8 = (bf16[128,1024]{1,0:T(8,128)(2,1)S(1)}, bf16[128,1024]{1,0:T(8,128)(2,1)S(1)}, u32[]{:S(2)}, u32[]{:S(2)}) collective-permute-start(bf16[128,1024]{1,0:T(8,128)(2,1)S(1)} %constant_dynamic-slice_fusion), channel_id=1, source_target_pairs={{0,16},{4,20},{8,24},{12,28},{16,0},{20,4},{24,8},{28,12},{1,17},{... | collective-permute-start | bytes 786440 | tf_op jit(solution)/shard_map/ppermute | solution.py:26
  53.3 13.5 %collective-permute-start.9 = (bf16[128,1024]{1,0:T(8,128)(2,1)S(1)}, bf16[128,1024]{1,0:T(8,128)(2,1)S(1)}, u32[]{:S(2)}, u32[]{:S(2)}) collective-permute-start(bf16[128,1024]{1,0:T(8,128)(2,1)S(1)} %constant_dynamic-slice_fusion), channel_id=1, source_target_pairs={{0,24},{4,28},{8,16},{12,20},{16,8},{20,12},{24,0},{28,4},{1,25},{... | collective-permute-start | bytes 786440 | tf_op jit(solution)/shard_map/ppermute | solution.py:26
  60.0 10.8 %collective-permute-start.17 = (bf16[64,2048]{1,0:T(8,128)(2,1)S(1)}, bf16[64,2048]{1,0:T(8,128)(2,1)S(1)}, u32[]{:S(2)}, u32[]{:S(2)}) collective-permute-start(bf16[64,2048]{1,0:T(8,128)(2,1)S(1)} %get-tuple-element.76), channel_id=1, source_target_pairs={{0,3},{3,0},{4,7},{7,4},{8,11},{11,8},{12,15},{15,12},{16,19},{19,... | collective-permute-start | bytes 786440 | tf_op jit(solution)/shard_map/ppermute | solution.py:413
  64.5 8.4 %collective-permute-start.18 = (bf16[64,2048]{1,0:T(8,128)(2,1)S(1)}, bf16[64,2048]{1,0:T(8,128)(2,1)S(1)}, u32[]{:S(2)}, u32[]{:S(2)}) collective-permute-start(bf16[64,2048]{1,0:T(8,128)(2,1)S(1)} %slice.86), channel_id=1, source_target_pairs={{1,2},{2,3},{5,6},{6,7},{9,10},{10,11},{13,14},{14,15},{17,18},{18... | collective-permute-start | bytes 786440 | tf_op jit(solution)/shard_map/ppermute | solution.py:414
  65.4 10.9 %collective-permute-start.19 = (bf16[64,2048]{1,0:T(8,128)(2,1)S(1)}, bf16[64,2048]{1,0:T(8,128)(2,1)S(1)}, u32[]{:S(2)}, u32[]{:S(2)}) collective-permute-start(bf16[64,2048]{1,0:T(8,128)(2,1)S(1)} %slice.87), channel_id=1, source_target_pairs={{2,1},{1,0},{6,5},{5,4},{10,9},{9,8},{14,13},{13,12},{18,17},{17,1... | collective-permute-start | bytes 786440 | tf_op jit(solution)/shard_map/ppermute | solution.py:415
  67.0 11.4 %collective-permute-start.14 = (bf16[64,2048]{1,0:T(8,128)(2,1)S(1)}, bf16[64,2048]{1,0:T(8,128)(2,1)S(1)}, u32[]{:S(2)}, u32[]{:S(2)}) collective-permute-start(bf16[64,2048]{1,0:T(8,128)(2,1)S(1)} %get-tuple-element.106), channel_id=1, source_target_pairs={{0,8},{4,12},{8,0},{12,4},{16,24},{20,28},{24,16},{28,20},{1,9},{5... | collective-permute-start | bytes 786440 | tf_op jit(solution)/shard_map/ppermute | solution.py:26
  69.0 12.0 %collective-permute-start.15 = (bf16[64,2048]{1,0:T(8,128)(2,1)S(1)}, bf16[64,2048]{1,0:T(8,128)(2,1)S(1)}, u32[]{:S(2)}, u32[]{:S(2)}) collective-permute-start(bf16[64,2048]{1,0:T(8,128)(2,1)S(1)} %get-tuple-element.105), channel_id=1, source_target_pairs={{0,16},{4,20},{8,24},{12,28},{16,0},{20,4},{24,8},{28,12},{1,17},{... | collective-permute-start | bytes 786440 | tf_op jit(solution)/shard_map/ppermute | solution.py:26
  70.8 10.2 %collective-permute-start.16 = (bf16[64,2048]{1,0:T(8,128)(2,1)S(1)}, bf16[64,2048]{1,0:T(8,128)(2,1)S(1)}, u32[]{:S(2)}, u32[]{:S(2)}) collective-permute-start(bf16[64,2048]{1,0:T(8,128)(2,1)S(1)} %get-tuple-element.104), channel_id=1, source_target_pairs={{0,24},{4,28},{8,16},{12,20},{16,8},{20,12},{24,0},{28,4},{1,25},{... | collective-permute-start | bytes 786440 | tf_op jit(solution)/shard_map/ppermute | solution.py:26
  72.9 6.2 %collective-permute-start.13 = (bf16[512,1024]{1,0:T(8,128)(2,1)S(1)}, bf16[512,1024]{1,0:T(8,128)(2,1)S(1)}, u32[]{:S(2)}, u32[]{:S(2)}) collective-permute-start(bf16[512,1024]{1,0:T(8,128)(2,1)S(1)} %pad_maximum_fusion.1), channel_id=1, source_target_pairs={{0,4},{4,0},{8,12},{12,8},{16,20},{20,16},{24,28},{28,24},{1,5},{5... | collective-permute-start | bytes 3145736 | tf_op jit(solution)/shard_map/ppermute | solution.py:26
  76.4 9.2 %collective-permute-start.20 = (bf16[64,2048]{1,0:T(8,128)(2,1)S(1)}, bf16[64,2048]{1,0:T(8,128)(2,1)S(1)}, u32[]{:S(2)}, u32[]{:S(2)}) collective-permute-start(bf16[64,2048]{1,0:T(8,128)(2,1)S(1)} %get-tuple-element.102), channel_id=1, source_target_pairs={{0,8},{4,12},{8,0},{12,4},{16,24},{20,28},{24,16},{28,20},{1,9},{5... | collective-permute-start | bytes 786440 | tf_op jit(solution)/shard_map/ppermute | solution.py:26
  78.4 13.7 %collective-permute-start.21 = (bf16[64,2048]{1,0:T(8,128)(2,1)S(1)}, bf16[64,2048]{1,0:T(8,128)(2,1)S(1)}, u32[]{:S(2)}, u32[]{:S(2)}) collective-permute-start(bf16[64,2048]{1,0:T(8,128)(2,1)S(1)} %get-tuple-element.101), channel_id=1, source_target_pairs={{0,16},{4,20},{8,24},{12,28},{16,0},{20,4},{24,8},{28,12},{1,17},{... | collective-permute-start | bytes 786440 | tf_op jit(solution)/shard_map/ppermute | solution.py:26
  79.0 13.1 %collective-permute-start.22 = (bf16[64,2048]{1,0:T(8,128)(2,1)S(1)}, bf16[64,2048]{1,0:T(8,128)(2,1)S(1)}, u32[]{:S(2)}, u32[]{:S(2)}) collective-permute-start(bf16[64,2048]{1,0:T(8,128)(2,1)S(1)} %get-tuple-element.100), channel_id=1, source_target_pairs={{0,24},{4,28},{8,16},{12,20},{16,8},{20,12},{24,0},{28,4},{1,25},{... | collective-permute-start | bytes 786440 | tf_op jit(solution)/shard_map/ppermute | solution.py:26
  80.2 12.2 %copy-start.20 = (s32[8]{0:T(128)S(1)}, s32[8]{0:T(128)}, u32[]{:S(2)}) copy-start(s32[8]{0:T(128)} %param.17) | copy-start | bytes 100
  80.2 14.8 %copy-start.10 = (bf16[1024,256]{1,0:T(8,128)(2,1)S(1)}, bf16[1024,256]{1,0:T(8,128)(2,1)}, u32[]{:S(2)}) copy-start(bf16[1024,256]{1,0:T(8,128)(2,1)} %key_ref.1) | copy-start | bytes 1572868
  80.2 14.8 %copy-start.11 = (bf16[1024,256]{1,0:T(8,128)(2,1)S(1)}, bf16[1024,256]{1,0:T(8,128)(2,1)}, u32[]{:S(2)}) copy-start(bf16[1024,256]{1,0:T(8,128)(2,1)} %value_ref.1) | copy-start | bytes 1572868
  92.3 2.7 %collective-permute-start.23 = (bf16[512,1024]{1,0:T(8,128)(2,1)S(1)}, bf16[512,1024]{1,0:T(8,128)(2,1)S(1)}, u32[]{:S(2)}, u32[]{:S(2)}) collective-permute-start(bf16[512,1024]{1,0:T(8,128)(2,1)S(1)} %get-tuple-element.88), channel_id=1, source_target_pairs={{0,4},{4,0},{8,12},{12,8},{16,20},{20,16},{24,28},{28,24},{1,5},{5... | collective-permute-start | bytes 3145736 | tf_op jit(solution)/shard_map/ppermute | solution.py:26
  95.0 3.9 %copy-start.21 = (bf16[1024,2048]{1,0:T(8,128)(2,1)S(1)}, bf16[1024,2048]{1,0:T(8,128)(2,1)}, u32[]{:S(2)}) copy-start(bf16[1024,2048]{1,0:T(8,128)(2,1)} %param.27) | copy-start | bytes 12582916
  98.8 4.8 %collective-permute-start.30 = (bf16[512,640]{1,0:T(8,128)(2,1)S(1)}, bf16[512,640]{1,0:T(8,128)(2,1)S(1)}, u32[]{:S(2)}, u32[]{:S(2)}) collective-permute-start(bf16[512,640]{1,0:T(8,128)(2,1)S(1)} %slice.101), channel_id=1, source_target_pairs={{0,4},{4,0},{8,12},{12,8},{16,20},{20,16},{24,28},{28,24},{1,5},{5... | collective-permute-start | bytes 1966088 | tf_op jit(solution)/shard_map/ppermute | solution.py:26
  100.2 7.7 %collective-permute-start.27 = (bf16[512,1024]{1,0:T(8,128)(2,1)S(1)}, bf16[512,1024]{1,0:T(8,128)(2,1)S(1)}, u32[]{:S(2)}, u32[]{:S(2)}) collective-permute-start(bf16[512,1024]{1,0:T(8,128)(2,1)S(1)} %fusion.11), channel_id=1, source_target_pairs={{0,4},{4,0},{8,12},{12,8},{16,20},{20,16},{24,28},{28,24},{1,5},{5... | collective-permute-start | bytes 3145736 | tf_op jit(solution)/shard_map/ppermute | solution.py:26
  102.6 6.6 %collective-permute-start.24 = (bf16[512,1024]{1,0:T(8,128)(2,1)S(1)}, bf16[512,1024]{1,0:T(8,128)(2,1)S(1)}, u32[]{:S(2)}, u32[]{:S(2)}) collective-permute-start(bf16[512,1024]{1,0:T(8,128)(2,1)S(1)} %fusion.8), channel_id=1, source_target_pairs={{0,4},{4,0},{8,12},{12,8},{16,20},{20,16},{24,28},{28,24},{1,5},{5... | collective-permute-start | bytes 3145736 | tf_op jit(solution)/shard_map/ppermute | solution.py:26
  104.5 7.0 %collective-permute-start.31 = (bf16[128,640]{1,0:T(8,128)(2,1)S(1)}, bf16[128,640]{1,0:T(8,128)(2,1)S(1)}, u32[]{:S(2)}, u32[]{:S(2)}) collective-permute-start(bf16[128,640]{1,0:T(8,128)(2,1)S(1)} %get-tuple-element.112), channel_id=1, source_target_pairs={{0,8},{4,12},{8,0},{12,4},{16,24},{20,28},{24,16},{28,20},{1,9},{5... | collective-permute-start | bytes 491528 | tf_op jit(solution)/shard_map/ppermute | solution.py:26
  104.8 9.7 %collective-permute-start.32 = (bf16[128,640]{1,0:T(8,128)(2,1)S(1)}, bf16[128,640]{1,0:T(8,128)(2,1)S(1)}, u32[]{:S(2)}, u32[]{:S(2)}) collective-permute-start(bf16[128,640]{1,0:T(8,128)(2,1)S(1)} %get-tuple-element.111), channel_id=1, source_target_pairs={{0,16},{4,20},{8,24},{12,28},{16,0},{20,4},{24,8},{28,12},{1,17},{... | collective-permute-start | bytes 491528 | tf_op jit(solution)/shard_map/ppermute | solution.py:26
  106.2 8.3 %collective-permute-start.33 = (bf16[128,640]{1,0:T(8,128)(2,1)S(1)}, bf16[128,640]{1,0:T(8,128)(2,1)S(1)}, u32[]{:S(2)}, u32[]{:S(2)}) collective-permute-start(bf16[128,640]{1,0:T(8,128)(2,1)S(1)} %get-tuple-element.110), channel_id=1, source_target_pairs={{0,24},{4,28},{8,16},{12,20},{16,8},{20,12},{24,0},{28,4},{1,25},{... | collective-permute-start | bytes 491528 | tf_op jit(solution)/shard_map/ppermute | solution.py:26
  111.5 3.1 %copy-start.17 = (bf16[128,640]{1,0:T(8,128)(2,1)}, bf16[128,640]{1,0:T(8,128)(2,1)S(1)}, u32[]{:S(2)}) copy-start(bf16[128,640]{1,0:T(8,128)(2,1)S(1)} %collective-permute-done.31.refs_1_) | copy-start | bytes 491524
  114.5 0.7 copy-start.18
  114.5 0.7 copy-start.19
  117.4 5.8 %copy-start.16 = (bf16[128,512]{1,0:T(8,128)(2,1)S(1)}, bf16[128,512]{1,0:T(8,128)(2,1)}, u32[]{:S(2)}) copy-start(bf16[128,512]{1,0:T(8,128)(2,1)} %get-tuple-element.99) | copy-start | bytes 393220
  117.4 6.1 %collective-permute-start.34 = (bf16[128,512]{1,0:T(8,128)(2,1)}, bf16[128,512]{1,0:T(8,128)(2,1)S(1)}, u32[]{:S(2)}, u32[]{:S(2)}) collective-permute-start(bf16[128,512]{1,0:T(8,128)(2,1)} %get-tuple-element.99), channel_id=1, source_target_pairs={{0,8},{4,12},{8,0},{12,4},{16,24},{20,28},{24,16},{28,20},{1,9},{5... | collective-permute-start | bytes 393224 | tf_op jit(solution)/shard_map/ppermute | solution.py:26
  119.1 8.9 %collective-permute-start.35 = (bf16[128,512]{1,0:T(8,128)(2,1)}, bf16[128,512]{1,0:T(8,128)(2,1)S(1)}, u32[]{:S(2)}, u32[]{:S(2)}) collective-permute-start(bf16[128,512]{1,0:T(8,128)(2,1)} %get-tuple-element.99), channel_id=1, source_target_pairs={{0,16},{4,20},{8,24},{12,28},{16,0},{20,4},{24,8},{28,12},{1,17},{... | collective-permute-start | bytes 393224 | tf_op jit(solution)/shard_map/ppermute | solution.py:26
  119.4 8.5 %collective-permute-start.36 = (bf16[128,512]{1,0:T(8,128)(2,1)}, bf16[128,512]{1,0:T(8,128)(2,1)S(1)}, u32[]{:S(2)}, u32[]{:S(2)}) collective-permute-start(bf16[128,512]{1,0:T(8,128)(2,1)} %get-tuple-element.99), channel_id=1, source_target_pairs={{0,24},{4,28},{8,16},{12,20},{16,8},{20,12},{24,0},{28,4},{1,25},{... | collective-permute-start | bytes 393224 | tf_op jit(solution)/shard_map/ppermute | solution.py:26
  121.0 16.4 %collective-permute-start.28 = (bf16[2,128,1024]{2,1,0:T(8,128)(2,1)S(1)}, bf16[2,128,1024]{2,1,0:T(8,128)(2,1)S(1)}, u32[]{:S(2)}, u32[]{:S(2)}) collective-permute-start(bf16[2,128,1024]{2,1,0:T(8,128)(2,1)S(1)} %bitcast.97), channel_id=1, source_target_pairs={{0,16},{4,20},{8,24},{12,28},{16,0},{20,4},{24,8},{28,12},{1,17},{... | collective-permute-start | bytes 1572872 | tf_op jit(solution)/shard_map/ppermute | solution.py:26
  122.4 16.6 %collective-permute-start.25 = (bf16[2,128,1024]{2,1,0:T(8,128)(2,1)S(1)}, bf16[2,128,1024]{2,1,0:T(8,128)(2,1)S(1)}, u32[]{:S(2)}, u32[]{:S(2)}) collective-permute-start(bf16[2,128,1024]{2,1,0:T(8,128)(2,1)S(1)} %slice_bitcast_fusion), channel_id=1, source_target_pairs={{0,8},{4,12},{8,0},{12,4},{16,24},{20,28},{24,16},{28,20},{1,9},{5... | collective-permute-start | bytes 1572872 | tf_op jit(solution)/shard_map/ppermute | solution.py:26
  128.0 12.4 %collective-permute-start.37 = (bf16[512,512]{1,0:T(8,128)(2,1)S(1)}, bf16[512,512]{1,0:T(8,128)(2,1)S(1)}, u32[]{:S(2)}, u32[]{:S(2)}) collective-permute-start(bf16[512,512]{1,0:T(8,128)(2,1)S(1)} %pad_maximum_fusion.2), channel_id=1, source_target_pairs={{0,4},{4,0},{8,12},{12,8},{16,20},{20,16},{24,28},{28,24},{1,5},{5... | collective-permute-start | bytes 1572872 | tf_op jit(solution)/shard_map/ppermute | solution.py:26
  137.7 8.5 %copy-start.8 = (f32[128,128]{1,0:T(8,128)S(1)}, f32[128,128]{1,0:T(8,128)}, u32[]{:S(2)}) copy-start(f32[128,128]{1,0:T(8,128)} %pad_maximum_fusion.4.refs_5_.refs_6_) | copy-start | bytes 196612
  137.7 8.5 %copy-start.9 = (f32[128,128]{1,0:T(8,128)S(1)}, f32[128,128]{1,0:T(8,128)}, u32[]{:S(2)}) copy-start(f32[128,128]{1,0:T(8,128)} %pad_maximum_fusion.3.refs_4_.refs_5_) | copy-start | bytes 196612
  137.7 8.5 %copy-start.12 = (f32[128,128]{1,0:T(8,128)S(1)}, f32[128,128]{1,0:T(8,128)}, u32[]{:S(2)}) copy-start(f32[128,128]{1,0:T(8,128)} %get-tuple-element.97.refs_4_) | copy-start | bytes 196612
  137.7 6.7 %collective-permute-start.29 = (bf16[128,1024]{1,0:T(8,128)(2,1)S(1)}, bf16[128,1024]{1,0:T(8,128)(2,1)S(1)}, u32[]{:S(2)}, u32[]{:S(2)}) collective-permute-start(bf16[128,1024]{1,0:T(8,128)(2,1)S(1)} %get-tuple-element.114), channel_id=1, source_target_pairs={{0,8},{4,12},{8,0},{12,4},{16,24},{20,28},{24,16},{28,20},{1,9},{5... | collective-permute-start | bytes 786440 | tf_op jit(solution)/shard_map/ppermute | solution.py:26
  139.2 6.9 %collective-permute-start.26 = (bf16[128,1024]{1,0:T(8,128)(2,1)S(1)}, bf16[128,1024]{1,0:T(8,128)(2,1)S(1)}, u32[]{:S(2)}, u32[]{:S(2)}) collective-permute-start(bf16[128,1024]{1,0:T(8,128)(2,1)S(1)} %get-tuple-element.116), channel_id=1, source_target_pairs={{0,16},{4,20},{8,24},{12,28},{16,0},{20,4},{24,8},{28,12},{1,17},{... | collective-permute-start | bytes 786440 | tf_op jit(solution)/shard_map/ppermute | solution.py:26

commit v6 on v5

--- a/solution.py
+++ b/solution.py
@@ -99,7 +99,7 @@
     tokens = kv.shape[0]
     chunk_heads = chunk_cols // HDIM
     group = count * chunk_heads // kv_heads
-    step = 2 if chunk_heads % 2 == 0 and tokens <= 2048 else 1
+    step = 4 if chunk_heads % 4 == 0 and tokens <= 1024 else 1
     factor = HDIM**-0.5
 
     def kernel(*refs):

time: 152 us -> 152 us (level)
  no operation moved by 1% of the time
where the time goes in v6:
time: 152 us
  starting transfers between devices  56.4 us (37%)
  waiting for transfers between devices  49.1 us (32%)
  Pallas kernels  20.6 us (14%)
  local copies, waits for them, and re-layouts  14.7 us (10%)
  matrix products  5.06 us (3%)
  other arithmetic  4.48 us (3%)
    ppermute x25, waiting for transfers between devices, swapped(): return lax.ppermute(value, 'tm', [(i, i ^ bits) for i in range(length)])  37.9 us
    ppermute x25, starting transfers between devices, swapped(): return lax.ppermute(value, 'tm', [(i, i ^ bits) for i in range(length)])  23.8 us
    unnamed x65, local copies, waits for them, and re-layouts  11.7 us
    ppermute x2, starting transfers between devices, shifted(): return lax.ppermute(value, axis, [(i, i + by) for i in range(length - by)])  9.49 us
    ppermute x2, waiting for transfers between devices, line_pieces(): upper_2 = lax.ppermute(upper, 'mp', [(2, 1), (1, 0)])  9.2 us
    ppermute x2, starting transfers between devices, line_pieces(): far = lax.ppermute(mine, 'mp', [(0, 3), (3, 0)])  8.74 us
    pallas_call x1, Pallas kernels, attend(): pl.pallas_call(kernel, out_shape=jax.ShapeDtypeStruct((rows, count * chun...  5.62 us
    ppermute x3, starting transfers between devices, rotated(): lax.ppermute(value, 'mp', [(i, (i + by) % length) for i in range(length)])  5.38 us
  transfers between devices with their start and end apart: 38, of which 15 were waited for; matrix products, arithmetic and copies ran while one was open for 8% of the time, Pallas kernels for 6%

profile of v6, /device:TPU:0, one launch (start us, length us, event | category | flops | bytes accessed | tf_op | source)
XLA Modules:
  0.0 151.8 jit_solution(16590350035315052262)
XLA Ops:
  0.6 4.9 %collective-permute-start = (bf16[128,1024]{1,0:T(8,128)(2,1)}, bf16[128,1024]{1,0:T(8,128)(2,1)S(1)}, u32[]{:S(2)}, u32[]{:S(2)}) collective-permute-start(bf16[128,1024]{1,0:T(8,128)(2,1)} %frames_ref.1), channel_id=1, source_target_pairs={{0,1},{1,2},{2,3},{3,4},{4,5},{5,6},{6,7},{7,8},{8,9},{9,10},{10,1... | collective-permute-start | bytes 786440 | tf_op jit(solution)/shard_map/ppermute | solution.py:21
  5.6 0.7 select_reduce_fusion.1
  6.4 0.8 pad_dynamic-slice_fusion
  7.3 0.8 convert_element_type.82.depth_ref
  8.2 2.8 %copy-done = bf16[1024,3072]{1,0:T(8,128)(2,1)S(1)} copy-done((bf16[1024,3072]{1,0:T(8,128)(2,1)S(1)}, bf16[1024,3072]{1,0:T(8,128)(2,1)}, u32[]{:S(2)}) %copy-start) | copy-done | bytes 6291480
  11.0 0.9 copy-done.6
  12.0 0.7 copy-done.14
  13.2 2.6 %copy-done.1 = bf16[1024,3072]{1,0:T(8,128)(2,1)} copy-done((bf16[1024,3072]{1,0:T(8,128)(2,1)}, bf16[1024,3072]{1,0:T(8,128)(2,1)S(1)}, u32[]{:S(2)}) %copy-start.1) | copy-done | bytes 6291480
  15.8 0.7 dynamic_slice.44
  16.5 3.5 %collective-permute-start.2 = (bf16[128,2048]{1,0:T(8,128)(2,1)S(1)}, bf16[128,2048]{1,0:T(8,128)(2,1)S(1)}, u32[]{:S(2)}, u32[]{:S(2)}) collective-permute-start(bf16[128,2048]{1,0:T(8,128)(2,1)S(1)} %copy-done.15), channel_id=1, source_target_pairs={{0,1},{1,2},{2,3},{4,5},{5,6},{6,7},{8,9},{9,10},{10,11},{12,13},{... | collective-permute-start | bytes 1572872 | tf_op jit(solution)/shard_map/ppermute | solution.py:403
  20.0 1.3 collective-permute-start.3
  21.3 2.8 %copy-done.2 = bf16[1024,3072]{1,0:T(8,128)(2,1)S(1)} copy-done((bf16[1024,3072]{1,0:T(8,128)(2,1)S(1)}, bf16[1024,3072]{1,0:T(8,128)(2,1)}, u32[]{:S(2)}) %copy-start.2) | copy-done | bytes 6291480
  24.1 2.1 %project.1.proj_ref = bf16[256,3072]{1,0:T(8,128)(2,1)S(1)} custom-call(bf16[128,1024]{1,0:T(8,128)(2,1)S(1)} %collective-permute-done.near_ref, bf16[128,1024]{1,0:T(8,128)(2,1)S(1)} %get-tuple-element.53.frames_ref, f32[1,1024]{1,0:T(1,128)S(1)} %get-tuple-element.54.gain_ref, bf16[1024,3072]{1,0:T(8,128)(2,1)S(1)} %copy-done.2), custom_call_target="tpu_custom_call" | custom-call | flops 1610612736 | bytes 6291456 | tf_op jit(solution)/shard_map/project/pallas_call | solution.py:161
  26.3 0.7 copy-done.4
  27.0 3.1 %gate_frames.1 = (f32[128,1024]{1,0:T(8,128)S(1)}, bf16[128,1024]{1,0:T(8,128)(2,1)S(1)}, bf16[32,1024]{1,0:T(8,128)(2,1)S(1)}) custom-call(bf16[128,1024]{1,0:T(8,128)(2,1)S(1)} %copy-done.7, bf16[256,3072]{1,0:T(8,128)(2,1)S(1)} %project.1.proj_ref, s32[3,256]{1,0:T(4,128)S(1)} %pad_add_fusion.key_row_ref, s32[128,3]{1,0:T(8,128)S(1)} %bitcast.89, ...), custom_call_target="tpu_custom_call" | custom-call | flops 805306368 | bytes 6291456 | tf_op jit(solution)/shard_map/gate_frames/pallas_call | solution.py:266
  30.0 4.5 %collective-permute-start.1 = (bf16[32,1024]{1,0:T(8,128)(2,1)S(1)}, bf16[32,1024]{1,0:T(8,128)(2,1)S(1)}, u32[]{:S(2)}, u32[]{:S(2)}) collective-permute-start(bf16[32,1024]{1,0:T(8,128)(2,1)S(1)} %get-tuple-element.61), channel_id=1, source_target_pairs={{0,1},{1,2},{2,3},{3,4},{4,5},{5,6},{6,7},{7,8},{8,9},{9,10},{10,1... | collective-permute-start | bytes 196616 | tf_op jit(solution)/shard_map/ppermute | solution.py:21
  34.6 1.6 %convolve_late.1.late_ref = bf16[96,1024]{1,0:T(8,128)(2,1)S(1)} custom-call(bf16[128,1024]{1,0:T(8,128)(2,1)S(1)} %get-tuple-element.59.glu_ref, f32[31,1024]{1,0:T(8,128)S(1)} %convert_element_type.82.depth_ref), custom_call_target="tpu_custom_call" | custom-call | flops 6094848 | bytes 393216 | tf_op jit(solution)/shard_map/convolve_late/pallas_call | solution.py:309
  36.5 1.8 %finish_frames.1 = (bf16[128,1024]{1,0:T(8,128)(2,1)}, bf16[32,1024]{1,0:T(8,128)(2,1)S(1)}) custom-call(f32[128,1024]{1,0:T(8,128)S(1)} %get-tuple-element.58.mid_ref, bf16[128,1024]{1,0:T(8,128)(2,1)S(1)} %get-tuple-element.59.glu_ref, bf16[96,1024]{1,0:T(8,128)(2,1)S(1)} %convolve_late.1.late_ref, bf16[32,1024]{1,0:T(8,128)(2,1)S(1)} %collective-permute-done.1.rim_ref, ...), custom_call_target="tpu_custom_call" | custom-call | flops 268435456 | bytes 2097152 | tf_op jit(solution)/shard_map/finish_frames/pallas_call | solution.py:354
  38.3 3.3 %collective-permute-start.4 = (bf16[32,1024]{1,0:T(8,128)(2,1)S(1)}, bf16[32,1024]{1,0:T(8,128)(2,1)S(1)}, u32[]{:S(2)}, u32[]{:S(2)}) collective-permute-start(bf16[32,1024]{1,0:T(8,128)(2,1)S(1)} %get-tuple-element.66), channel_id=1, source_target_pairs={{0,3},{1,0},{2,1},{3,2},{4,7},{5,4},{6,5},{7,6},{8,11},{9,8},{10,9... | collective-permute-start | bytes 196616 | tf_op jit(solution)/shard_map/ppermute | solution.py:31
  42.1 1.6 %collective-permute-start.6 = (bf16[32,1024]{1,0:T(8,128)(2,1)S(1)}, bf16[32,1024]{1,0:T(8,128)(2,1)S(1)}, u32[]{:S(2)}, u32[]{:S(2)}) collective-permute-start(bf16[32,1024]{1,0:T(8,128)(2,1)S(1)} %get-tuple-element.66), channel_id=1, source_target_pairs={{0,1},{1,2},{2,3},{3,0},{4,5},{5,6},{6,7},{7,4},{8,9},{9,10},{10,1... | collective-permute-start | bytes 196616 | tf_op jit(solution)/shard_map/ppermute | solution.py:31
  43.7 0.7 collective-permute-start.11
  44.4 1.3 collective-permute-start.12
  45.9 4.3 %collective-permute-start.10 = (bf16[64,2048]{1,0:T(8,128)(2,1)S(1)}, bf16[64,2048]{1,0:T(8,128)(2,1)S(1)}, u32[]{:S(2)}, u32[]{:S(2)}) collective-permute-start(bf16[64,2048]{1,0:T(8,128)(2,1)S(1)} %get-tuple-element.67), channel_id=1, source_target_pairs={{0,3},{3,0},{4,7},{7,4},{8,11},{11,8},{12,15},{15,12},{16,19},{19,... | collective-permute-start | bytes 786440 | tf_op jit(solution)/shard_map/ppermute | solution.py:413
  50.4 1.6 %collective-permute-start.7 = (bf16[128,1024]{1,0:T(8,128)(2,1)S(1)}, bf16[128,1024]{1,0:T(8,128)(2,1)S(1)}, u32[]{:S(2)}, u32[]{:S(2)}) collective-permute-start(bf16[128,1024]{1,0:T(8,128)(2,1)S(1)} %constant_dynamic-slice_fusion), channel_id=1, source_target_pairs={{0,8},{4,12},{8,0},{12,4},{16,24},{20,28},{24,16},{28,20},{1,9},{5... | collective-permute-start | bytes 786440 | tf_op jit(solution)/shard_map/ppermute | solution.py:26
  52.0 1.4 collective-permute-start.8
  54.0 6.0 %collective-permute-done.12 = bf16[64,2048]{1,0:T(8,128)(2,1)S(1)} collective-permute-done((bf16[64,2048]{1,0:T(8,128)(2,1)S(1)}, bf16[64,2048]{1,0:T(8,128)(2,1)S(1)}, u32[]{:S(2)}, u32[]{:S(2)}) %collective-permute-start.12) | collective-permute-done | bytes 262176 | tf_op jit(solution)/shard_map/ppermute | solution.py:415
  60.0 4.4 %collective-permute-start.17 = (bf16[64,2048]{1,0:T(8,128)(2,1)S(1)}, bf16[64,2048]{1,0:T(8,128)(2,1)S(1)}, u32[]{:S(2)}, u32[]{:S(2)}) collective-permute-start(bf16[64,2048]{1,0:T(8,128)(2,1)S(1)} %get-tuple-element.76), channel_id=1, source_target_pairs={{0,3},{3,0},{4,7},{7,4},{8,11},{11,8},{12,15},{15,12},{16,19},{19,... | collective-permute-start | bytes 786440 | tf_op jit(solution)/shard_map/ppermute | solution.py:413
  64.5 0.7 collective-permute-start.18
  65.4 1.5 collective-permute-start.19
  67.0 2.0 %collective-permute-start.14 = (bf16[64,2048]{1,0:T(8,128)(2,1)S(1)}, bf16[64,2048]{1,0:T(8,128)(2,1)S(1)}, u32[]{:S(2)}, u32[]{:S(2)}) collective-permute-start(bf16[64,2048]{1,0:T(8,128)(2,1)S(1)} %get-tuple-element.106), channel_id=1, source_target_pairs={{0,8},{4,12},{8,0},{12,4},{16,24},{20,28},{24,16},{28,20},{1,9},{5... | collective-permute-start | bytes 786440 | tf_op jit(solution)/shard_map/ppermute | solution.py:26
  69.0 1.8 %collective-permute-done.17 = bf16[64,2048]{1,0:T(8,128)(2,1)S(1)} collective-permute-done((bf16[64,2048]{1,0:T(8,128)(2,1)S(1)}, bf16[64,2048]{1,0:T(8,128)(2,1)S(1)}, u32[]{:S(2)}, u32[]{:S(2)}) %collective-permute-start.17) | collective-permute-done | bytes 262176 | tf_op jit(solution)/shard_map/ppermute | solution.py:413
  70.8 2.0 %collective-permute-start.16 = (bf16[64,2048]{1,0:T(8,128)(2,1)S(1)}, bf16[64,2048]{1,0:T(8,128)(2,1)S(1)}, u32[]{:S(2)}, u32[]{:S(2)}) collective-permute-start(bf16[64,2048]{1,0:T(8,128)(2,1)S(1)} %get-tuple-element.104), channel_id=1, source_target_pairs={{0,24},{4,28},{8,16},{12,20},{16,8},{20,12},{24,0},{28,4},{1,25},{... | collective-permute-start | bytes 786440 | tf_op jit(solution)/shard_map/ppermute | solution.py:26
  73.1 3.2 %collective-permute-done.19 = bf16[64,2048]{1,0:T(8,128)(2,1)S(1)} collective-permute-done((bf16[64,2048]{1,0:T(8,128)(2,1)S(1)}, bf16[64,2048]{1,0:T(8,128)(2,1)S(1)}, u32[]{:S(2)}, u32[]{:S(2)}) %collective-permute-start.19) | collective-permute-done | bytes 262176 | tf_op jit(solution)/shard_map/ppermute | solution.py:415
  76.4 2.1 %collective-permute-start.20 = (bf16[64,2048]{1,0:T(8,128)(2,1)S(1)}, bf16[64,2048]{1,0:T(8,128)(2,1)S(1)}, u32[]{:S(2)}, u32[]{:S(2)}) collective-permute-start(bf16[64,2048]{1,0:T(8,128)(2,1)S(1)} %get-tuple-element.102), channel_id=1, source_target_pairs={{0,8},{4,12},{8,0},{12,4},{16,24},{20,28},{24,16},{28,20},{1,9},{5... | collective-permute-start | bytes 786440 | tf_op jit(solution)/shard_map/ppermute | solution.py:26
  79.0 1.0 collective-permute-start.22
  80.2 0.8 collective-permute-done.15.refs_2_
  81.0 4.5 %collective-permute-done.20.refs_5_ = bf16[64,2048]{1,0:T(8,128)(2,1)S(1)} collective-permute-done((bf16[64,2048]{1,0:T(8,128)(2,1)S(1)}, bf16[64,2048]{1,0:T(8,128)(2,1)S(1)}, u32[]{:S(2)}, u32[]{:S(2)}) %collective-permute-start.20) | collective-permute-done | bytes 262176 | tf_op jit(solution)/shard_map/ppermute | solution.py:26
  85.6 6.6 %collective-permute-done.21.refs_6_ = bf16[64,2048]{1,0:T(8,128)(2,1)S(1)} collective-permute-done((bf16[64,2048]{1,0:T(8,128)(2,1)S(1)}, bf16[64,2048]{1,0:T(8,128)(2,1)S(1)}, u32[]{:S(2)}, u32[]{:S(2)}) %collective-permute-start.21) | collective-permute-done | bytes 262176 | tf_op jit(solution)/shard_map/ppermute | solution.py:26
  92.9 2.1 %collective-permute-done.23.taken_ref = bf16[512,1024]{1,0:T(8,128)(2,1)S(1)} collective-permute-done((bf16[512,1024]{1,0:T(8,128)(2,1)S(1)}, bf16[512,1024]{1,0:T(8,128)(2,1)S(1)}, u32[]{:S(2)}, u32[]{:S(2)}) %collective-permute-start.23) | collective-permute-done | bytes 1048608 | tf_op jit(solution)/shard_map/ppermute | solution.py:26
  95.0 3.7 %adapt.1 = (bf16[1024,1024]{1,0:T(8,128)(2,1)S(1)}, bf16[1024,640]{1,0:T(8,128)(2,1)S(1)}) custom-call(s32[1]{0:T(128)} %bitcast.5.place_ref, bf16[512,1024]{1,0:T(8,128)(2,1)S(1)} %get-tuple-element.87.mine_ref, bf16[512,1024]{1,0:T(8,128)(2,1)S(1)} %collective-permute-done.23.taken_ref, bf16[1024,1024]{1,0:T(8,128)(2,1)S(1)} %pad_maximum_fusion.pooled_ref, ...), custom_call_target="tpu_custom_call" | custom-call | tf_op jit(solution)/shard_map/adapt/pallas_call | solution.py:490
  99.0 1.3 fusion.11
  100.7 0.7 pad_maximum_fusion.3.refs_4_.refs_5_
  101.4 1.3 fusion.8
  102.8 0.7 pad_maximum_fusion.4.refs_5_.refs_6_
  103.7 0.7 fusion.29
  104.8 1.4 collective-permute-start.32
  106.2 1.7 %collective-permute-start.33 = (bf16[128,640]{1,0:T(8,128)(2,1)S(1)}, bf16[128,640]{1,0:T(8,128)(2,1)S(1)}, u32[]{:S(2)}, u32[]{:S(2)}) collective-permute-start(bf16[128,640]{1,0:T(8,128)(2,1)S(1)} %get-tuple-element.110), channel_id=1, source_target_pairs={{0,24},{4,28},{8,16},{12,20},{16,8},{20,12},{24,0},{28,4},{1,25},{... | collective-permute-start | bytes 491528 | tf_op jit(solution)/shard_map/ppermute | solution.py:26
  108.0 1.3 add_convert_fusion
  109.3 1.3 add_convert_fusion.1
  110.5 1.0 collective-permute-done.31.refs_1_
  111.5 3.0 %collective-permute-done.32.refs_2_ = bf16[128,640]{1,0:T(8,128)(2,1)S(1)} collective-permute-done((bf16[128,640]{1,0:T(8,128)(2,1)S(1)}, bf16[128,640]{1,0:T(8,128)(2,1)S(1)}, u32[]{:S(2)}, u32[]{:S(2)}) %collective-permute-start.32) | collective-permute-done | bytes 163872 | tf_op jit(solution)/shard_map/ppermute | solution.py:26
  114.6 0.7 copy-done.18
  115.3 2.1 %finish_keys.1 = (bf16[128,512]{1,0:T(8,128)(2,1)}, f32[128,128]{1,0:T(8,128)}) custom-call(bf16[128,640]{1,0:T(8,128)(2,1)} %get-tuple-element.92.refs_0_, bf16[128,640]{1,0:T(8,128)(2,1)} %copy-done.17, bf16[128,640]{1,0:T(8,128)(2,1)} %copy-done.18, bf16[128,640]{1,0:T(8,128)(2,1)} %copy-done.19, f32[128,128]{1,0:T(8,128)} %pad_maximum_fusion.3.refs_4_.refs_5_, ...), custom_call_target="tpu_custom_call" | custom-call | tf_op jit(solution)/shard_map/finish_keys/pallas_call | solution.py:86
  117.4 1.7 %collective-permute-start.34 = (bf16[128,512]{1,0:T(8,128)(2,1)}, bf16[128,512]{1,0:T(8,128)(2,1)S(1)}, u32[]{:S(2)}, u32[]{:S(2)}) collective-permute-start(bf16[128,512]{1,0:T(8,128)(2,1)} %get-tuple-element.99), channel_id=1, source_target_pairs={{0,8},{4,12},{8,0},{12,4},{16,24},{20,28},{24,16},{28,20},{1,9},{5... | collective-permute-start | bytes 393224 | tf_op jit(solution)/shard_map/ppermute | solution.py:26
  119.4 1.4 collective-permute-start.36
  121.0 1.4 collective-permute-start.28
  122.4 0.8 collective-permute-start.25
  123.5 4.5 %collective-permute-done.35 = bf16[128,512]{1,0:T(8,128)(2,1)S(1)} collective-permute-done((bf16[128,512]{1,0:T(8,128)(2,1)}, bf16[128,512]{1,0:T(8,128)(2,1)S(1)}, u32[]{:S(2)}, u32[]{:S(2)}) %collective-permute-start.35) | collective-permute-done | bytes 131104 | tf_op jit(solution)/shard_map/ppermute | solution.py:26
  128.1 9.3 %collective-permute-done.28 = bf16[2,128,1024]{2,1,0:T(8,128)(2,1)S(1)} collective-permute-done((bf16[2,128,1024]{2,1,0:T(8,128)(2,1)S(1)}, bf16[2,128,1024]{2,1,0:T(8,128)(2,1)S(1)}, u32[]{:S(2)}, u32[]{:S(2)}) %collective-permute-start.28) | collective-permute-done | bytes 524320 | tf_op jit(solution)/shard_map/ppermute | solution.py:26
  137.7 1.3 collective-permute-start.29
  139.2 1.1 collective-permute-start.26
  140.4 4.0 %collective-permute-done.29.refs_3_ = bf16[128,1024]{1,0:T(8,128)(2,1)S(1)} collective-permute-done((bf16[128,1024]{1,0:T(8,128)(2,1)S(1)}, bf16[128,1024]{1,0:T(8,128)(2,1)S(1)}, u32[]{:S(2)}, u32[]{:S(2)}) %collective-permute-start.29) | collective-permute-done | bytes 262176 | tf_op jit(solution)/shard_map/ppermute | solution.py:26
  144.4 1.8 %collective-permute-done.26.refs_1_ = bf16[128,1024]{1,0:T(8,128)(2,1)S(1)} collective-permute-done((bf16[128,1024]{1,0:T(8,128)(2,1)S(1)}, bf16[128,1024]{1,0:T(8,128)(2,1)S(1)}, u32[]{:S(2)}, u32[]{:S(2)}) %collective-permute-start.26) | collective-permute-done | bytes 262176 | tf_op jit(solution)/shard_map/ppermute | solution.py:26
  146.2 5.6 %attend.1 = bf16[128,2048]{1,0:T(8,128)(2,1)} custom-call(bf16[128,1024]{1,0:T(8,128)(2,1)S(1)} %get-tuple-element.117.refs_0_, bf16[128,1024]{1,0:T(8,128)(2,1)S(1)} %collective-permute-done.26.refs_1_, bf16[128,1024]{1,0:T(8,128)(2,1)S(1)} %get-tuple-element.115.refs_2_, bf16[128,1024]{1,0:T(8,128)(2,1)S(1)} %collective-permute-done.29.refs_3_, ...), custom_call_target="tpu_custom_call" | custom-call | tf_op jit(solution)/shard_map/attend/pallas_call | solution.py:139
  (150 shorter events, 7.6 us)
Async XLA Ops:
  0.6 15.8 %collective-permute-start = (bf16[128,1024]{1,0:T(8,128)(2,1)}, bf16[128,1024]{1,0:T(8,128)(2,1)S(1)}, u32[]{:S(2)}, u32[]{:S(2)}) collective-permute-start(bf16[128,1024]{1,0:T(8,128)(2,1)} %frames_ref.1), channel_id=1, source_target_pairs={{0,1},{1,2},{2,3},{3,4},{4,5},{5,6},{6,7},{7,8},{8,9},{9,10},{10,1... | collective-permute-start | bytes 786440 | tf_op jit(solution)/shard_map/ppermute | solution.py:21
  8.2 2.8 %copy-start = (bf16[1024,3072]{1,0:T(8,128)(2,1)S(1)}, bf16[1024,3072]{1,0:T(8,128)(2,1)}, u32[]{:S(2)}) copy-start(bf16[1024,3072]{1,0:T(8,128)(2,1)} %refs_2_) | copy-start | bytes 18874372
  11.0 0.9 copy-start.6
  12.0 0.7 copy-start.14
  12.7 3.8 %copy-start.15 = (bf16[128,2048]{1,0:T(8,128)(2,1)S(1)}, bf16[128,2048]{1,0:T(8,128)(2,1)}, u32[]{:S(2)}) copy-start(bf16[128,2048]{1,0:T(8,128)(2,1)} %param.25) | copy-start | bytes 1572868
  13.1 2.6 %copy-start.1 = (bf16[1024,3072]{1,0:T(8,128)(2,1)}, bf16[1024,3072]{1,0:T(8,128)(2,1)S(1)}, u32[]{:S(2)}) copy-start(bf16[1024,3072]{1,0:T(8,128)(2,1)S(1)} %get-tuple-element.55.weight_ref) | copy-start | bytes 18874372
  16.5 21.8 %collective-permute-start.2 = (bf16[128,2048]{1,0:T(8,128)(2,1)S(1)}, bf16[128,2048]{1,0:T(8,128)(2,1)S(1)}, u32[]{:S(2)}, u32[]{:S(2)}) collective-permute-start(bf16[128,2048]{1,0:T(8,128)(2,1)S(1)} %copy-done.15), channel_id=1, source_target_pairs={{0,1},{1,2},{2,3},{4,5},{5,6},{6,7},{8,9},{9,10},{10,11},{12,13},{... | collective-permute-start | bytes 1572872 | tf_op jit(solution)/shard_map/ppermute | solution.py:403
  20.0 18.3 %collective-permute-start.3 = (bf16[128,2048]{1,0:T(8,128)(2,1)S(1)}, bf16[128,2048]{1,0:T(8,128)(2,1)S(1)}, u32[]{:S(2)}, u32[]{:S(2)}) collective-permute-start(bf16[128,2048]{1,0:T(8,128)(2,1)S(1)} %copy-done.15), channel_id=1, source_target_pairs={{1,0},{2,1},{3,2},{5,4},{6,5},{7,6},{9,8},{10,9},{11,10},{13,12},{... | collective-permute-start | bytes 1572872 | tf_op jit(solution)/shard_map/ppermute | solution.py:404
  21.3 2.8 %copy-start.2 = (bf16[1024,3072]{1,0:T(8,128)(2,1)S(1)}, bf16[1024,3072]{1,0:T(8,128)(2,1)}, u32[]{:S(2)}) copy-start(bf16[1024,3072]{1,0:T(8,128)(2,1)} %copy-done.1) | copy-start | bytes 18874372
  24.1 2.2 %copy-start.3 = (bf16[1024,2048]{1,0:T(8,128)(2,1)S(1)}, bf16[1024,2048]{1,0:T(8,128)(2,1)}, u32[]{:S(2)}) copy-start(bf16[1024,2048]{1,0:T(8,128)(2,1)} %in_hbm.1) | copy-start | bytes 12582916
  24.1 2.9 %copy-start.4 = (bf16[1024,1024]{1,0:T(8,128)(2,1)S(1)}, bf16[1024,1024]{1,0:T(8,128)(2,1)}, u32[]{:S(2)}) copy-start(bf16[1024,1024]{1,0:T(8,128)(2,1)} %attn_hbm.1) | copy-start | bytes 6291460
  24.1 2.9 %copy-start.7 = (bf16[128,1024]{1,0:T(8,128)(2,1)S(1)}, bf16[128,1024]{1,0:T(8,128)(2,1)}, u32[]{:S(2)}) copy-start(bf16[128,1024]{1,0:T(8,128)(2,1)} %frames_ref.1) | copy-start | bytes 786436
  24.1 2.9 %copy-start.13 = (f32[1024]{0:T(1024)S(1)}, f32[1024]{0:T(1024)}, u32[]{:S(2)}) copy-start(f32[1024]{0:T(1024)} %param.21) | copy-start | bytes 12292
  27.0 9.5 %copy-start.5 = (bf16[1024,1024]{1,0:T(8,128)(2,1)S(1)}, bf16[1024,1024]{1,0:T(8,128)(2,1)}, u32[]{:S(2)}) copy-start(bf16[1024,1024]{1,0:T(8,128)(2,1)} %out_ref.1) | copy-start | bytes 6291460
  30.0 6.4 %collective-permute-start.1 = (bf16[32,1024]{1,0:T(8,128)(2,1)S(1)}, bf16[32,1024]{1,0:T(8,128)(2,1)S(1)}, u32[]{:S(2)}, u32[]{:S(2)}) collective-permute-start(bf16[32,1024]{1,0:T(8,128)(2,1)S(1)} %get-tuple-element.61), channel_id=1, source_target_pairs={{0,1},{1,2},{2,3},{3,4},{4,5},{5,6},{6,7},{7,8},{8,9},{9,10},{10,1... | collective-permute-start | bytes 196616 | tf_op jit(solution)/shard_map/ppermute | solution.py:21
  38.3 7.6 %collective-permute-start.4 = (bf16[32,1024]{1,0:T(8,128)(2,1)S(1)}, bf16[32,1024]{1,0:T(8,128)(2,1)S(1)}, u32[]{:S(2)}, u32[]{:S(2)}) collective-permute-start(bf16[32,1024]{1,0:T(8,128)(2,1)S(1)} %get-tuple-element.66), channel_id=1, source_target_pairs={{0,3},{1,0},{2,1},{3,2},{4,7},{5,4},{6,5},{7,6},{8,11},{9,8},{10,9... | collective-permute-start | bytes 196616 | tf_op jit(solution)/shard_map/ppermute | solution.py:31
  41.6 8.7 %collective-permute-start.5 = (bf16[32,1024]{1,0:T(8,128)(2,1)S(1)}, bf16[32,1024]{1,0:T(8,128)(2,1)S(1)}, u32[]{:S(2)}, u32[]{:S(2)}) collective-permute-start(bf16[32,1024]{1,0:T(8,128)(2,1)S(1)} %get-tuple-element.66), channel_id=1, source_target_pairs={{0,2},{1,3},{2,0},{3,1},{4,6},{5,7},{6,4},{7,5},{8,10},{9,11},{10,... | collective-permute-start | bytes 196616 | tf_op jit(solution)/shard_map/ppermute | solution.py:31
  42.1 8.2 %collective-permute-start.6 = (bf16[32,1024]{1,0:T(8,128)(2,1)S(1)}, bf16[32,1024]{1,0:T(8,128)(2,1)S(1)}, u32[]{:S(2)}, u32[]{:S(2)}) collective-permute-start(bf16[32,1024]{1,0:T(8,128)(2,1)S(1)} %get-tuple-element.66), channel_id=1, source_target_pairs={{0,1},{1,2},{2,3},{3,0},{4,5},{5,6},{6,7},{7,4},{8,9},{9,10},{10,1... | collective-permute-start | bytes 196616 | tf_op jit(solution)/shard_map/ppermute | solution.py:31
  43.7 9.6 %collective-permute-start.11 = (bf16[64,2048]{1,0:T(8,128)(2,1)S(1)}, bf16[64,2048]{1,0:T(8,128)(2,1)S(1)}, u32[]{:S(2)}, u32[]{:S(2)}) collective-permute-start(bf16[64,2048]{1,0:T(8,128)(2,1)S(1)} %slice.84), channel_id=1, source_target_pairs={{1,2},{2,3},{5,6},{6,7},{9,10},{10,11},{13,14},{14,15},{17,18},{18... | collective-permute-start | bytes 786440 | tf_op jit(solution)/shard_map/ppermute | solution.py:414
  44.4 15.6 %collective-permute-start.12 = (bf16[64,2048]{1,0:T(8,128)(2,1)S(1)}, bf16[64,2048]{1,0:T(8,128)(2,1)S(1)}, u32[]{:S(2)}, u32[]{:S(2)}) collective-permute-start(bf16[64,2048]{1,0:T(8,128)(2,1)S(1)} %slice.85), channel_id=1, source_target_pairs={{2,1},{1,0},{6,5},{5,4},{10,9},{9,8},{14,13},{13,12},{18,17},{17,1... | collective-permute-start | bytes 786440 | tf_op jit(solution)/shard_map/ppermute | solution.py:415
  45.9 14.1 %collective-permute-start.10 = (bf16[64,2048]{1,0:T(8,128)(2,1)S(1)}, bf16[64,2048]{1,0:T(8,128)(2,1)S(1)}, u32[]{:S(2)}, u32[]{:S(2)}) collective-permute-start(bf16[64,2048]{1,0:T(8,128)(2,1)S(1)} %get-tuple-element.67), channel_id=1, source_target_pairs={{0,3},{3,0},{4,7},{7,4},{8,11},{11,8},{12,15},{15,12},{16,19},{19,... | collective-permute-start | bytes 786440 | tf_op jit(solution)/shard_map/ppermute | solution.py:413
  50.4 14.9 %collective-permute-start.7 = (bf16[128,1024]{1,0:T(8,128)(2,1)S(1)}, bf16[128,1024]{1,0:T(8,128)(2,1)S(1)}, u32[]{:S(2)}, u32[]{:S(2)}) collective-permute-start(bf16[128,1024]{1,0:T(8,128)(2,1)S(1)} %constant_dynamic-slice_fusion), channel_id=1, source_target_pairs={{0,8},{4,12},{8,0},{12,4},{16,24},{20,28},{24,16},{28,20},{1,9},{5... | collective-permute-start | bytes 786440 | tf_op jit(solution)/shard_map/ppermute | solution.py:26
  52.0 14.9 %collective-permute-start.8 = (bf16[128,1024]{1,0:T(8,128)(2,1)S(1)}, bf16[128,1024]{1,0:T(8,128)(2,1)S(1)}, u32[]{:S(2)}, u32[]{:S(2)}) collective-permute-start(bf16[128,1024]{1,0:T(8,128)(2,1)S(1)} %constant_dynamic-slice_fusion), channel_id=1, source_target_pairs={{0,16},{4,20},{8,24},{12,28},{16,0},{20,4},{24,8},{28,12},{1,17},{... | collective-permute-start | bytes 786440 | tf_op jit(solution)/shard_map/ppermute | solution.py:26
  53.3 13.5 %collective-permute-start.9 = (bf16[128,1024]{1,0:T(8,128)(2,1)S(1)}, bf16[128,1024]{1,0:T(8,128)(2,1)S(1)}, u32[]{:S(2)}, u32[]{:S(2)}) collective-permute-start(bf16[128,1024]{1,0:T(8,128)(2,1)S(1)} %constant_dynamic-slice_fusion), channel_id=1, source_target_pairs={{0,24},{4,28},{8,16},{12,20},{16,8},{20,12},{24,0},{28,4},{1,25},{... | collective-permute-start | bytes 786440 | tf_op jit(solution)/shard_map/ppermute | solution.py:26
  60.0 10.8 %collective-permute-start.17 = (bf16[64,2048]{1,0:T(8,128)(2,1)S(1)}, bf16[64,2048]{1,0:T(8,128)(2,1)S(1)}, u32[]{:S(2)}, u32[]{:S(2)}) collective-permute-start(bf16[64,2048]{1,0:T(8,128)(2,1)S(1)} %get-tuple-element.76), channel_id=1, source_target_pairs={{0,3},{3,0},{4,7},{7,4},{8,11},{11,8},{12,15},{15,12},{16,19},{19,... | collective-permute-start | bytes 786440 | tf_op jit(solution)/shard_map/ppermute | solution.py:413
  64.5 8.4 %collective-permute-start.18 = (bf16[64,2048]{1,0:T(8,128)(2,1)S(1)}, bf16[64,2048]{1,0:T(8,128)(2,1)S(1)}, u32[]{:S(2)}, u32[]{:S(2)}) collective-permute-start(bf16[64,2048]{1,0:T(8,128)(2,1)S(1)} %slice.86), channel_id=1, source_target_pairs={{1,2},{2,3},{5,6},{6,7},{9,10},{10,11},{13,14},{14,15},{17,18},{18... | collective-permute-start | bytes 786440 | tf_op jit(solution)/shard_map/ppermute | solution.py:414
  65.4 10.9 %collective-permute-start.19 = (bf16[64,2048]{1,0:T(8,128)(2,1)S(1)}, bf16[64,2048]{1,0:T(8,128)(2,1)S(1)}, u32[]{:S(2)}, u32[]{:S(2)}) collective-permute-start(bf16[64,2048]{1,0:T(8,128)(2,1)S(1)} %slice.87), channel_id=1, source_target_pairs={{2,1},{1,0},{6,5},{5,4},{10,9},{9,8},{14,13},{13,12},{18,17},{17,1... | collective-permute-start | bytes 786440 | tf_op jit(solution)/shard_map/ppermute | solution.py:415
  67.0 11.4 %collective-permute-start.14 = (bf16[64,2048]{1,0:T(8,128)(2,1)S(1)}, bf16[64,2048]{1,0:T(8,128)(2,1)S(1)}, u32[]{:S(2)}, u32[]{:S(2)}) collective-permute-start(bf16[64,2048]{1,0:T(8,128)(2,1)S(1)} %get-tuple-element.106), channel_id=1, source_target_pairs={{0,8},{4,12},{8,0},{12,4},{16,24},{20,28},{24,16},{28,20},{1,9},{5... | collective-permute-start | bytes 786440 | tf_op jit(solution)/shard_map/ppermute | solution.py:26
  69.0 12.0 %collective-permute-start.15 = (bf16[64,2048]{1,0:T(8,128)(2,1)S(1)}, bf16[64,2048]{1,0:T(8,128)(2,1)S(1)}, u32[]{:S(2)}, u32[]{:S(2)}) collective-permute-start(bf16[64,2048]{1,0:T(8,128)(2,1)S(1)} %get-tuple-element.105), channel_id=1, source_target_pairs={{0,16},{4,20},{8,24},{12,28},{16,0},{20,4},{24,8},{28,12},{1,17},{... | collective-permute-start | bytes 786440 | tf_op jit(solution)/shard_map/ppermute | solution.py:26
  70.8 10.2 %collective-permute-start.16 = (bf16[64,2048]{1,0:T(8,128)(2,1)S(1)}, bf16[64,2048]{1,0:T(8,128)(2,1)S(1)}, u32[]{:S(2)}, u32[]{:S(2)}) collective-permute-start(bf16[64,2048]{1,0:T(8,128)(2,1)S(1)} %get-tuple-element.104), channel_id=1, source_target_pairs={{0,24},{4,28},{8,16},{12,20},{16,8},{20,12},{24,0},{28,4},{1,25},{... | collective-permute-start | bytes 786440 | tf_op jit(solution)/shard_map/ppermute | solution.py:26
  72.9 6.2 %collective-permute-start.13 = (bf16[512,1024]{1,0:T(8,128)(2,1)S(1)}, bf16[512,1024]{1,0:T(8,128)(2,1)S(1)}, u32[]{:S(2)}, u32[]{:S(2)}) collective-permute-start(bf16[512,1024]{1,0:T(8,128)(2,1)S(1)} %pad_maximum_fusion.1), channel_id=1, source_target_pairs={{0,4},{4,0},{8,12},{12,8},{16,20},{20,16},{24,28},{28,24},{1,5},{5... | collective-permute-start | bytes 3145736 | tf_op jit(solution)/shard_map/ppermute | solution.py:26
  76.4 9.2 %collective-permute-start.20 = (bf16[64,2048]{1,0:T(8,128)(2,1)S(1)}, bf16[64,2048]{1,0:T(8,128)(2,1)S(1)}, u32[]{:S(2)}, u32[]{:S(2)}) collective-permute-start(bf16[64,2048]{1,0:T(8,128)(2,1)S(1)} %get-tuple-element.102), channel_id=1, source_target_pairs={{0,8},{4,12},{8,0},{12,4},{16,24},{20,28},{24,16},{28,20},{1,9},{5... | collective-permute-start | bytes 786440 | tf_op jit(solution)/shard_map/ppermute | solution.py:26
  78.4 13.7 %collective-permute-start.21 = (bf16[64,2048]{1,0:T(8,128)(2,1)S(1)}, bf16[64,2048]{1,0:T(8,128)(2,1)S(1)}, u32[]{:S(2)}, u32[]{:S(2)}) collective-permute-start(bf16[64,2048]{1,0:T(8,128)(2,1)S(1)} %get-tuple-element.101), channel_id=1, source_target_pairs={{0,16},{4,20},{8,24},{12,28},{16,0},{20,4},{24,8},{28,12},{1,17},{... | collective-permute-start | bytes 786440 | tf_op jit(solution)/shard_map/ppermute | solution.py:26
  79.0 13.1 %collective-permute-start.22 = (bf16[64,2048]{1,0:T(8,128)(2,1)S(1)}, bf16[64,2048]{1,0:T(8,128)(2,1)S(1)}, u32[]{:S(2)}, u32[]{:S(2)}) collective-permute-start(bf16[64,2048]{1,0:T(8,128)(2,1)S(1)} %get-tuple-element.100), channel_id=1, source_target_pairs={{0,24},{4,28},{8,16},{12,20},{16,8},{20,12},{24,0},{28,4},{1,25},{... | collective-permute-start | bytes 786440 | tf_op jit(solution)/shard_map/ppermute | solution.py:26
  80.2 12.2 %copy-start.20 = (s32[8]{0:T(128)S(1)}, s32[8]{0:T(128)}, u32[]{:S(2)}) copy-start(s32[8]{0:T(128)} %param.17) | copy-start | bytes 100
  80.2 14.8 %copy-start.10 = (bf16[1024,256]{1,0:T(8,128)(2,1)S(1)}, bf16[1024,256]{1,0:T(8,128)(2,1)}, u32[]{:S(2)}) copy-start(bf16[1024,256]{1,0:T(8,128)(2,1)} %key_ref.1) | copy-start | bytes 1572868
  80.2 14.8 %copy-start.11 = (bf16[1024,256]{1,0:T(8,128)(2,1)S(1)}, bf16[1024,256]{1,0:T(8,128)(2,1)}, u32[]{:S(2)}) copy-start(bf16[1024,256]{1,0:T(8,128)(2,1)} %value_ref.1) | copy-start | bytes 1572868
  92.3 2.7 %collective-permute-start.23 = (bf16[512,1024]{1,0:T(8,128)(2,1)S(1)}, bf16[512,1024]{1,0:T(8,128)(2,1)S(1)}, u32[]{:S(2)}, u32[]{:S(2)}) collective-permute-start(bf16[512,1024]{1,0:T(8,128)(2,1)S(1)} %get-tuple-element.88), channel_id=1, source_target_pairs={{0,4},{4,0},{8,12},{12,8},{16,20},{20,16},{24,28},{28,24},{1,5},{5... | collective-permute-start | bytes 3145736 | tf_op jit(solution)/shard_map/ppermute | solution.py:26
  95.0 3.9 %copy-start.21 = (bf16[1024,2048]{1,0:T(8,128)(2,1)S(1)}, bf16[1024,2048]{1,0:T(8,128)(2,1)}, u32[]{:S(2)}) copy-start(bf16[1024,2048]{1,0:T(8,128)(2,1)} %param.27) | copy-start | bytes 12582916
  98.8 4.8 %collective-permute-start.30 = (bf16[512,640]{1,0:T(8,128)(2,1)S(1)}, bf16[512,640]{1,0:T(8,128)(2,1)S(1)}, u32[]{:S(2)}, u32[]{:S(2)}) collective-permute-start(bf16[512,640]{1,0:T(8,128)(2,1)S(1)} %slice.101), channel_id=1, source_target_pairs={{0,4},{4,0},{8,12},{12,8},{16,20},{20,16},{24,28},{28,24},{1,5},{5... | collective-permute-start | bytes 1966088 | tf_op jit(solution)/shard_map/ppermute | solution.py:26
  100.2 7.7 %collective-permute-start.27 = (bf16[512,1024]{1,0:T(8,128)(2,1)S(1)}, bf16[512,1024]{1,0:T(8,128)(2,1)S(1)}, u32[]{:S(2)}, u32[]{:S(2)}) collective-permute-start(bf16[512,1024]{1,0:T(8,128)(2,1)S(1)} %fusion.11), channel_id=1, source_target_pairs={{0,4},{4,0},{8,12},{12,8},{16,20},{20,16},{24,28},{28,24},{1,5},{5... | collective-permute-start | bytes 3145736 | tf_op jit(solution)/shard_map/ppermute | solution.py:26
  102.6 6.6 %collective-permute-start.24 = (bf16[512,1024]{1,0:T(8,128)(2,1)S(1)}, bf16[512,1024]{1,0:T(8,128)(2,1)S(1)}, u32[]{:S(2)}, u32[]{:S(2)}) collective-permute-start(bf16[512,1024]{1,0:T(8,128)(2,1)S(1)} %fusion.8), channel_id=1, source_target_pairs={{0,4},{4,0},{8,12},{12,8},{16,20},{20,16},{24,28},{28,24},{1,5},{5... | collective-permute-start | bytes 3145736 | tf_op jit(solution)/shard_map/ppermute | solution.py:26
  104.5 7.0 %collective-permute-start.31 = (bf16[128,640]{1,0:T(8,128)(2,1)S(1)}, bf16[128,640]{1,0:T(8,128)(2,1)S(1)}, u32[]{:S(2)}, u32[]{:S(2)}) collective-permute-start(bf16[128,640]{1,0:T(8,128)(2,1)S(1)} %get-tuple-element.112), channel_id=1, source_target_pairs={{0,8},{4,12},{8,0},{12,4},{16,24},{20,28},{24,16},{28,20},{1,9},{5... | collective-permute-start | bytes 491528 | tf_op jit(solution)/shard_map/ppermute | solution.py:26
  104.8 9.7 %collective-permute-start.32 = (bf16[128,640]{1,0:T(8,128)(2,1)S(1)}, bf16[128,640]{1,0:T(8,128)(2,1)S(1)}, u32[]{:S(2)}, u32[]{:S(2)}) collective-permute-start(bf16[128,640]{1,0:T(8,128)(2,1)S(1)} %get-tuple-element.111), channel_id=1, source_target_pairs={{0,16},{4,20},{8,24},{12,28},{16,0},{20,4},{24,8},{28,12},{1,17},{... | collective-permute-start | bytes 491528 | tf_op jit(solution)/shard_map/ppermute | solution.py:26
  106.2 8.3 %collective-permute-start.33 = (bf16[128,640]{1,0:T(8,128)(2,1)S(1)}, bf16[128,640]{1,0:T(8,128)(2,1)S(1)}, u32[]{:S(2)}, u32[]{:S(2)}) collective-permute-start(bf16[128,640]{1,0:T(8,128)(2,1)S(1)} %get-tuple-element.110), channel_id=1, source_target_pairs={{0,24},{4,28},{8,16},{12,20},{16,8},{20,12},{24,0},{28,4},{1,25},{... | collective-permute-start | bytes 491528 | tf_op jit(solution)/shard_map/ppermute | solution.py:26
  111.5 3.1 %copy-start.17 = (bf16[128,640]{1,0:T(8,128)(2,1)}, bf16[128,640]{1,0:T(8,128)(2,1)S(1)}, u32[]{:S(2)}) copy-start(bf16[128,640]{1,0:T(8,128)(2,1)S(1)} %collective-permute-done.31.refs_1_) | copy-start | bytes 491524
  114.5 0.7 copy-start.18
  114.5 0.7 copy-start.19
  117.4 5.8 %copy-start.16 = (bf16[128,512]{1,0:T(8,128)(2,1)S(1)}, bf16[128,512]{1,0:T(8,128)(2,1)}, u32[]{:S(2)}) copy-start(bf16[128,512]{1,0:T(8,128)(2,1)} %get-tuple-element.99) | copy-start | bytes 393220
  117.4 6.1 %collective-permute-start.34 = (bf16[128,512]{1,0:T(8,128)(2,1)}, bf16[128,512]{1,0:T(8,128)(2,1)S(1)}, u32[]{:S(2)}, u32[]{:S(2)}) collective-permute-start(bf16[128,512]{1,0:T(8,128)(2,1)} %get-tuple-element.99), channel_id=1, source_target_pairs={{0,8},{4,12},{8,0},{12,4},{16,24},{20,28},{24,16},{28,20},{1,9},{5... | collective-permute-start | bytes 393224 | tf_op jit(solution)/shard_map/ppermute | solution.py:26
  119.1 8.9 %collective-permute-start.35 = (bf16[128,512]{1,0:T(8,128)(2,1)}, bf16[128,512]{1,0:T(8,128)(2,1)S(1)}, u32[]{:S(2)}, u32[]{:S(2)}) collective-permute-start(bf16[128,512]{1,0:T(8,128)(2,1)} %get-tuple-element.99), channel_id=1, source_target_pairs={{0,16},{4,20},{8,24},{12,28},{16,0},{20,4},{24,8},{28,12},{1,17},{... | collective-permute-start | bytes 393224 | tf_op jit(solution)/shard_map/ppermute | solution.py:26
  119.4 8.5 %collective-permute-start.36 = (bf16[128,512]{1,0:T(8,128)(2,1)}, bf16[128,512]{1,0:T(8,128)(2,1)S(1)}, u32[]{:S(2)}, u32[]{:S(2)}) collective-permute-start(bf16[128,512]{1,0:T(8,128)(2,1)} %get-tuple-element.99), channel_id=1, source_target_pairs={{0,24},{4,28},{8,16},{12,20},{16,8},{20,12},{24,0},{28,4},{1,25},{... | collective-permute-start | bytes 393224 | tf_op jit(solution)/shard_map/ppermute | solution.py:26
  121.0 16.4 %collective-permute-start.28 = (bf16[2,128,1024]{2,1,0:T(8,128)(2,1)S(1)}, bf16[2,128,1024]{2,1,0:T(8,128)(2,1)S(1)}, u32[]{:S(2)}, u32[]{:S(2)}) collective-permute-start(bf16[2,128,1024]{2,1,0:T(8,128)(2,1)S(1)} %bitcast.97), channel_id=1, source_target_pairs={{0,16},{4,20},{8,24},{12,28},{16,0},{20,4},{24,8},{28,12},{1,17},{... | collective-permute-start | bytes 1572872 | tf_op jit(solution)/shard_map/ppermute | solution.py:26
  122.4 16.6 %collective-permute-start.25 = (bf16[2,128,1024]{2,1,0:T(8,128)(2,1)S(1)}, bf16[2,128,1024]{2,1,0:T(8,128)(2,1)S(1)}, u32[]{:S(2)}, u32[]{:S(2)}) collective-permute-start(bf16[2,128,1024]{2,1,0:T(8,128)(2,1)S(1)} %slice_bitcast_fusion), channel_id=1, source_target_pairs={{0,8},{4,12},{8,0},{12,4},{16,24},{20,28},{24,16},{28,20},{1,9},{5... | collective-permute-start | bytes 1572872 | tf_op jit(solution)/shard_map/ppermute | solution.py:26
  128.0 12.4 %collective-permute-start.37 = (bf16[512,512]{1,0:T(8,128)(2,1)S(1)}, bf16[512,512]{1,0:T(8,128)(2,1)S(1)}, u32[]{:S(2)}, u32[]{:S(2)}) collective-permute-start(bf16[512,512]{1,0:T(8,128)(2,1)S(1)} %pad_maximum_fusion.2), channel_id=1, source_target_pairs={{0,4},{4,0},{8,12},{12,8},{16,20},{20,16},{24,28},{28,24},{1,5},{5... | collective-permute-start | bytes 1572872 | tf_op jit(solution)/shard_map/ppermute | solution.py:26
  137.7 8.5 %copy-start.8 = (f32[128,128]{1,0:T(8,128)S(1)}, f32[128,128]{1,0:T(8,128)}, u32[]{:S(2)}) copy-start(f32[128,128]{1,0:T(8,128)} %pad_maximum_fusion.4.refs_5_.refs_6_) | copy-start | bytes 196612
  137.7 8.5 %copy-start.9 = (f32[128,128]{1,0:T(8,128)S(1)}, f32[128,128]{1,0:T(8,128)}, u32[]{:S(2)}) copy-start(f32[128,128]{1,0:T(8,128)} %pad_maximum_fusion.3.refs_4_.refs_5_) | copy-start | bytes 196612
  137.7 8.5 %copy-start.12 = (f32[128,128]{1,0:T(8,128)S(1)}, f32[128,128]{1,0:T(8,128)}, u32[]{:S(2)}) copy-start(f32[128,128]{1,0:T(8,128)} %get-tuple-element.97.refs_4_) | copy-start | bytes 196612
  137.7 6.7 %collective-permute-start.29 = (bf16[128,1024]{1,0:T(8,128)(2,1)S(1)}, bf16[128,1024]{1,0:T(8,128)(2,1)S(1)}, u32[]{:S(2)}, u32[]{:S(2)}) collective-permute-start(bf16[128,1024]{1,0:T(8,128)(2,1)S(1)} %get-tuple-element.114), channel_id=1, source_target_pairs={{0,8},{4,12},{8,0},{12,4},{16,24},{20,28},{24,16},{28,20},{1,9},{5... | collective-permute-start | bytes 786440 | tf_op jit(solution)/shard_map/ppermute | solution.py:26
  139.2 6.9 %collective-permute-start.26 = (bf16[128,1024]{1,0:T(8,128)(2,1)S(1)}, bf16[128,1024]{1,0:T(8,128)(2,1)S(1)}, u32[]{:S(2)}, u32[]{:S(2)}) collective-permute-start(bf16[128,1024]{1,0:T(8,128)(2,1)S(1)} %get-tuple-element.116), channel_id=1, source_target_pairs={{0,16},{4,20},{8,24},{12,28},{16,0},{20,4},{24,8},{28,12},{1,17},{... | collective-permute-start | bytes 786440 | tf_op jit(solution)/shard_map/ppermute | solution.py:26
